TPU v7x, 32 devices: a whole 2x2x4 slice. The times are simulated.
32 devices in a mesh: dp: 4 (over z), row: 4 (over x, core), col: 2 (over y).
Axes of the slice: x: 2, y: 2, z: 4, core: 2. Of those that a mesh axis runs over, the one named last changes fastest.
Arguments:
- tokens: bfloat16 [8, 4096, 1024], P('dp', ('row', 'col')), may hold values from -6 to 6
- cotangent: bfloat16 [8, 4096, 1024], P('dp', ('row', 'col')), may hold values from -6 to 6
- branch: int32 [8, 8], P('dp'), may hold values from 256 to 2048
- ln1_gain: float32 [1024], replicated, may hold values from 0.5 to 1.5
- ln1_bias: float32 [1024], replicated, may hold values from -1.2 to 1.2
- qkv_weight: bfloat16 [1024, 3, 1024], P('row', None, 'col'), may hold values from -0.1875 to 0.1875
- qv_bias: float32 [2, 1024], P(None, 'col'), may hold values from -1.2 to 1.2
- out_weight: bfloat16 [1024, 1024], P('col', 'row'), may hold values from -1.5 to 1.5
- out_bias: float32 [1024], replicated, may hold values from -1.2 to 1.2
- ln2_gain: float32 [1024], replicated, may hold values from 0.5 to 1.5
- ln2_bias: float32 [1024], replicated, may hold values from -1.2 to 1.2
- fc_weight: bfloat16 [1024, 4096], P('row', 'col'), may hold values from -0.1875 to 0.1875
- fc_bias: float32 [4096], P('col'), may hold values from -1.8 to 1.8
- proj_weight: bfloat16 [4096, 1024], P('col', 'row'), may hold values from -0.09375 to 0.09375
- proj_bias: float32 [1024], replicated, may hold values from -1.2 to 1.2
Outputs:
- block_out: bfloat16 [8, 4096, 1024], P('dp', ('row', 'col'))
- input_grad: float32 [8, 4096, 1024], P('dp', ('row', 'col'))
- d_ln1_gain: float32 [1024], replicated
- d_ln1_bias: float32 [1024], replicated
- d_qkv_weight: float32 [1024, 3, 1024], P(('dp', 'row'), None, 'col')
- d_qv_bias: float32 [2, 1024], replicated
- d_out_weight: float32 [1024, 1024], P('col', ('dp', 'row'))
- d_out_bias: float32 [1024], replicated
- d_ln2_gain: float32 [1024], replicated
- d_ln2_bias: float32 [1024], replicated
- d_fc_weight: float32 [1024, 4096], P(('dp', 'row'), 'col')
- d_fc_bias: float32 [4096], replicated
- d_proj_weight: float32 [4096, 1024], P('col', ('dp', 'row'))
- d_proj_bias: float32 [1024], replicated
Inputs may be any that keep to these rules, and one draw needn't show every extreme that they name: branch[g, c] is the number of leading prompt tokens that continuation c of group g sees.
All inputs are finite; a program needn't handle non-finite values.
Results may differ from a plain program's by a relative error of at most 0.015.
Values may be sent and summed in bfloat16 or wider, within the bound.
No kernel may reach another device: no remote copies, remote signals or barrier semaphores. Data moves between devices by JAX's collectives and lax.ppermute only.
A program may use at most 328 MiB of HBM per device.

v0:
```python
import jax
import jax.numpy as jnp
from jax import lax
from jax.sharding import PartitionSpec as P

HEAD = 64
PLEN = 2048
CLEN = 256
CONTS = 8


EPSILON = 1e-05
MASKED_SCORE = -1e30


def normalize(values, gain, shift):
    center = values - jnp.mean(values, axis=-1, keepdims=True)
    spread = jnp.mean(center * center, axis=-1, keepdims=True)
    return center * lax.rsqrt(spread + EPSILON) * gain + shift


def gelu_tanh(values):
    return jax.nn.gelu(values, approximate=True)


def allowed_keys(row_pos, col_pos, branch_cut):
    row_seg = jnp.where(row_pos >= PLEN, (row_pos - PLEN) // CLEN, -1)
    col_seg = jnp.where(col_pos >= PLEN, (col_pos - PLEN) // CLEN, -1)
    picked = (row_seg[:, None] == jnp.arange(CONTS, dtype=jnp.int32)[None, :]).astype(jnp.int32)
    row_cut = jnp.sum(picked * branch_cut[None, :], axis=1)
    causal = col_pos[None, :] <= row_pos[:, None]
    same_seq = col_seg[None, :] == row_seg[:, None]
    in_prefix = (
        (row_seg[:, None] >= 0) & (col_seg[None, :] < 0) & (col_pos[None, :] < row_cut[:, None])
    )
    return same_seq & causal | in_prefix


def add_trees(first, second):
    return jax.tree.map(lambda total, extra: total + extra, first, second)


def body(
    tokens,
    cotangent,
    branch,
    ln1_gain,
    ln1_bias,
    qkv_weight,
    qv_bias,
    out_weight,
    out_bias,
    ln2_gain,
    ln2_bias,
    fc_weight,
    fc_bias,
    proj_weight,
    proj_bias,
):
    scale = HEAD ** (-0.5)
    width = tokens.shape[2]
    local_rows = tokens.shape[1]
    head_cols = qv_bias.shape[1]
    head_count = head_cols // HEAD
    ff_local = fc_bias.shape[0]
    col_count = lax.axis_size("col")
    row_count = lax.axis_size("row")
    row_rows = local_rows * col_count
    group_rows = row_rows * row_count
    q_block = min(512, row_rows)
    block_count = row_rows // q_block
    row_base = lax.axis_index("row") * row_rows
    col_index = lax.axis_index("col")
    bias_three = jnp.stack([qv_bias[0], jnp.zeros_like(qv_bias[0]), qv_bias[1]])
    key_pos = jnp.arange(group_rows, dtype=jnp.int32)
    block_starts = jnp.arange(block_count, dtype=jnp.int32) * q_block

    def spread_rows(values):
        return lax.all_gather(values, "col", axis=0, tiled=True)

    def spread_grads(values):
        return lax.all_gather(values, "col", axis=0, tiled=True)

    def sum_branch(values):
        return lax.psum_scatter(values, "col", scatter_dimension=0, tiled=True)

    def sum_inputs(values):
        return lax.psum_scatter(values, "col", scatter_dimension=0, tiled=True)

    kept_weights = (
        lax.all_gather(qkv_weight, "row", axis=0, tiled=True),
        lax.all_gather(out_weight, "row", axis=1, tiled=True),
        lax.all_gather(fc_weight, "row", axis=0, tiled=True),
        lax.all_gather(proj_weight, "row", axis=1, tiled=True),
    )

    def block_scores(queries3, keys3, offset, branch_cut):
        q_part = lax.dynamic_slice_in_dim(queries3, offset, q_block, 0)
        row_pos = row_base + offset + jnp.arange(q_block, dtype=jnp.int32)
        allowed = allowed_keys(row_pos, key_pos, branch_cut)
        scores = (
            jnp.einsum("qhd,khd->hqk", q_part, keys3, preferred_element_type=jnp.float32) * scale
        )
        return (q_part, jnp.where(allowed[None], scores, MASKED_SCORE))

    def micro_step(carry, micro_item):
        grads_acc, small_acc = carry
        tok_rows, cot_rows, branch_cut = micro_item
        w_qkv, w_out, w_fc, w_proj = kept_weights
        residual = tok_rows.astype(jnp.float32)
        normed = normalize(residual, ln1_gain, ln1_bias).astype(jnp.bfloat16)
        normed_all = spread_rows(normed)
        projected = jnp.einsum("td,dsf->tsf", normed_all, w_qkv, preferred_element_type=jnp.float32)
        projected = (projected + bias_three[None]).astype(jnp.bfloat16)
        key_rows, value_rows = (
            lax.all_gather(projected[:, 1], "row", axis=0, tiled=True),
            lax.all_gather(projected[:, 2], "row", axis=0, tiled=True),
        )
        queries3 = projected[:, 0].reshape(row_rows, head_count, HEAD)
        keys3 = key_rows.reshape(group_rows, head_count, HEAD)
        values3 = value_rows.reshape(group_rows, head_count, HEAD)

        def attend(offset):
            q_part, scores = block_scores(queries3, keys3, offset, branch_cut)
            row_peak = jnp.max(scores, axis=-1, keepdims=True)
            exponent = jnp.exp(scores - row_peak)
            row_total = jnp.sum(exponent, axis=-1, keepdims=True)
            probs_low = (exponent / row_total).astype(jnp.bfloat16)
            mixed_rows = jnp.einsum(
                "hqk,khd->qhd", probs_low, values3, preferred_element_type=jnp.float32
            )
            return (mixed_rows, (row_peak + jnp.log(row_total))[..., 0])

        attended, log_totals = lax.map(attend, block_starts)
        attended = attended.reshape(row_rows, head_cols).astype(jnp.bfloat16)
        branch_part = jnp.dot(attended, w_out, preferred_element_type=jnp.float32)
        middle = residual + sum_branch(branch_part) + out_bias
        normed_two = normalize(middle, ln2_gain, ln2_bias).astype(jnp.bfloat16)
        normed_two_all = spread_rows(normed_two)
        hidden = jnp.dot(normed_two_all, w_fc, preferred_element_type=jnp.float32) + fc_bias
        active = gelu_tanh(hidden).astype(jnp.bfloat16)
        ffn_part = jnp.dot(active, w_proj, preferred_element_type=jnp.float32)
        output_rows = (middle + sum_branch(ffn_part) + proj_bias).astype(jnp.bfloat16)
        cot_all = spread_grads(cot_rows)
        grad_proj = jnp.einsum("tf,td->fd", active, cot_all, preferred_element_type=jnp.float32)
        grad_proj_bias = jnp.sum(cot_rows.astype(jnp.float32), axis=0)
        grad_active = jnp.einsum("td,fd->tf", cot_all, w_proj, preferred_element_type=jnp.float32)
        grad_hidden = jax.vjp(gelu_tanh, hidden)[1](grad_active)[0].astype(jnp.bfloat16)
        grad_fc = jnp.einsum(
            "td,tf->df", normed_two_all, grad_hidden, preferred_element_type=jnp.float32
        )
        grad_fc_bias = jnp.sum(grad_hidden.astype(jnp.float32), axis=0)
        grad_normed_two = sum_inputs(
            jnp.einsum("tf,df->td", grad_hidden, w_fc, preferred_element_type=jnp.float32)
        )
        back_middle, grad_gain_two, grad_bias_two = jax.vjp(normalize, middle, ln2_gain, ln2_bias)[
            1
        ](grad_normed_two)
        grad_middle = cot_rows.astype(jnp.float32) + back_middle
        grad_out_rows = grad_middle.astype(jnp.bfloat16)
        grad_out_all = spread_grads(grad_out_rows)
        grad_out = jnp.einsum(
            "tc,td->cd", attended, grad_out_all, preferred_element_type=jnp.float32
        )
        grad_out_bias = jnp.sum(grad_out_rows.astype(jnp.float32), axis=0)
        grad_att = jnp.einsum("td,cd->tc", grad_out_all, w_out, preferred_element_type=jnp.float32)
        grad_att = grad_att.astype(jnp.bfloat16).reshape(row_rows, head_count, HEAD)

        def attend_back(acc_pair, block_item):
            offset, log_total = block_item
            grad_keys_acc, grad_values_acc = acc_pair
            q_part, scores = block_scores(queries3, keys3, offset, branch_cut)
            probs = jnp.exp(scores - log_total[..., None])
            probs_low = probs.astype(jnp.bfloat16)
            grad_part = lax.dynamic_slice_in_dim(grad_att, offset, q_block, 0)
            grad_values_acc = grad_values_acc + jnp.einsum(
                "hqk,qhd->khd", probs_low, grad_part, preferred_element_type=jnp.float32
            )
            grad_probs = jnp.einsum(
                "qhd,khd->hqk", grad_part, values3, preferred_element_type=jnp.float32
            )
            center = jnp.sum(grad_probs * probs, axis=-1, keepdims=True)
            grad_scores = (probs * (grad_probs - center)).astype(jnp.bfloat16)
            grad_keys_acc = (
                grad_keys_acc
                + jnp.einsum(
                    "hqk,qhd->khd", grad_scores, q_part, preferred_element_type=jnp.float32
                )
                * scale
            )
            grad_query = (
                jnp.einsum("hqk,khd->qhd", grad_scores, keys3, preferred_element_type=jnp.float32)
                * scale
            )
            return ((grad_keys_acc, grad_values_acc), grad_query)

        empty_keys = jnp.zeros((group_rows, head_count, HEAD), jnp.float32)
        (grad_keys, grad_values), grad_queries = lax.scan(
            attend_back, (empty_keys, empty_keys), (block_starts, log_totals)
        )
        own_keys, own_values = (
            lax.psum_scatter(
                grad_keys.reshape(group_rows, head_cols).astype(jnp.bfloat16),
                "row",
                scatter_dimension=0,
                tiled=True,
            ).astype(jnp.float32),
            lax.psum_scatter(
                grad_values.reshape(group_rows, head_cols).astype(jnp.bfloat16),
                "row",
                scatter_dimension=0,
                tiled=True,
            ).astype(jnp.float32),
        )
        grad_projected = jnp.stack(
            [grad_queries.reshape(row_rows, head_cols), own_keys, own_values], axis=1
        ).astype(jnp.bfloat16)
        grad_qkv = jnp.einsum(
            "td,tsf->dsf", normed_all, grad_projected, preferred_element_type=jnp.float32
        )
        grad_qkv_bias = jnp.sum(grad_projected.astype(jnp.float32), axis=0)
        grad_normed = sum_inputs(
            jnp.einsum("tsf,dsf->td", grad_projected, w_qkv, preferred_element_type=jnp.float32)
        )
        back_input, grad_gain_one, grad_bias_one = jax.vjp(normalize, residual, ln1_gain, ln1_bias)[
            1
        ](grad_normed)
        input_rows = grad_middle + back_input
        weight_terms = (grad_qkv, grad_out, grad_fc, grad_proj)
        small_terms = (
            grad_gain_one,
            grad_bias_one,
            grad_qkv_bias,
            grad_out_bias,
            grad_gain_two,
            grad_bias_two,
            grad_fc_bias,
            grad_proj_bias,
        )
        return (
            (add_trees(grads_acc, weight_terms), add_trees(small_acc, small_terms)),
            (output_rows, input_rows),
        )

    grads_init = (
        jnp.zeros((width, 3, head_cols), jnp.float32),
        jnp.zeros((head_cols, width), jnp.float32),
        jnp.zeros((width, ff_local), jnp.float32),
        jnp.zeros((ff_local, width), jnp.float32),
    )
    vector_zero = jnp.zeros((width,), jnp.float32)
    small_init = (
        vector_zero,
        vector_zero,
        jnp.zeros((3, head_cols), jnp.float32),
        vector_zero,
        vector_zero,
        vector_zero,
        jnp.zeros((ff_local,), jnp.float32),
        vector_zero,
    )
    (grads_acc, small_acc), (block_out, input_grad) = lax.scan(
        micro_step, (grads_init, small_init), (tokens, cotangent, branch)
    )
    (
        gain_one,
        bias_one,
        qkv_bias_acc,
        out_bias_acc,
        gain_two,
        bias_two,
        fc_bias_acc,
        proj_bias_acc,
    ) = small_acc
    qv_full = lax.dynamic_update_slice(
        jnp.zeros((2, width), jnp.float32),
        jnp.stack([qkv_bias_acc[0], qkv_bias_acc[2]]),
        (jnp.int32(0), col_index * head_cols),
    )
    fc_full = lax.dynamic_update_slice(
        jnp.zeros((ff_local * col_count,), jnp.float32), fc_bias_acc, (col_index * ff_local,)
    )
    summed = lax.psum(
        (gain_one, bias_one, qv_full, out_bias_acc, gain_two, bias_two, fc_full, proj_bias_acc),
        ("dp", "row", "col"),
    )
    return (
        block_out,
        input_grad,
        summed[0],
        summed[1],
        lax.psum_scatter(
            grads_acc[0].astype(jnp.bfloat16), ("dp", "row"), scatter_dimension=0, tiled=True
        ).astype(jnp.float32),
        summed[2],
        lax.psum_scatter(
            grads_acc[1].astype(jnp.bfloat16), ("dp", "row"), scatter_dimension=1, tiled=True
        ).astype(jnp.float32),
        summed[3],
        summed[4],
        summed[5],
        lax.psum_scatter(
            grads_acc[2].astype(jnp.bfloat16), ("dp", "row"), scatter_dimension=0, tiled=True
        ).astype(jnp.float32),
        summed[6],
        lax.psum_scatter(
            grads_acc[3].astype(jnp.bfloat16), ("dp", "row"), scatter_dimension=1, tiled=True
        ).astype(jnp.float32),
        summed[7],
    )


def solution(mesh):
    placed = (
        P("dp", ("row", "col"), None),
        P("dp", ("row", "col"), None),
        P("dp", None),
        P(),
        P(),
        P("row", None, "col"),
        P(None, "col"),
        P("col", "row"),
        P(),
        P(),
        P(),
        P("row", "col"),
        P("col"),
        P("col", "row"),
        P(),
    )
    return jax.shard_map(
        body,
        mesh=mesh,
        in_specs=placed,
        out_specs=(
            P("dp", ("row", "col"), None),
            P("dp", ("row", "col"), None),
            P(),
            P(),
            P(("dp", "row"), None, "col"),
            P(),
            P("col", ("dp", "row")),
            P(),
            P(),
            P(),
            P(("dp", "row"), "col"),
            P(),
            P("col", ("dp", "row")),
            P(),
        ),
        check_vma=False,
    )
```

profile of v0, /device:TPU:0, one launch (start us, length us, event | category | flops | bytes accessed | tf_op | source)
XLA Modules:
  0.0 2760.7 jit_solution(3911327315650754905)
XLA Ops:
  29.1 30.1 %all-gather.23.cloned.1.call-done = bf16[1024,3,512]{2,0,1:T(8,128)(2,1)} async-done(((bf16[256,3,512]{2,0,1:T(8,128)(2,1)}), bf16[1024,3,512]{2,0,1:T(8,128)(2,1)}) %all-gather.23.cloned.1.call-update) | async-done | bytes 3145744 | tf_op jit(solution)/shard_map/all_gather | solution.py:91
  59.2 36.1 %all-gather.29.cloned.1.call-done = bf16[1024,2048]{1,0:T(8,128)(2,1)} async-done(((bf16[256,2048]{1,0:T(8,128)(2,1)}), bf16[1024,2048]{1,0:T(8,128)(2,1)}) %all-gather.29.cloned.1.call-update) | async-done | bytes 4194320 | tf_op jit(solution)/shard_map/all_gather | solution.py:93
  95.3 36.4 %all-gather.25.cloned.1.call-done = bf16[2048,1024]{1,0:T(8,128)(2,1)} async-done(((bf16[2048,256]{1,0:T(8,128)(2,1)}), bf16[2048,1024]{1,0:T(8,128)(2,1)}) %all-gather.25.cloned.1.call-update) | async-done | bytes 4194320 | tf_op jit(solution)/shard_map/all_gather | solution.py:94
  131.7 2337.8 %while.107 = (s32[]{:T(128)}, f32[1024,3,512]{2,0,1:T(8,128)}, f32[512,1024]{1,0:T(8,128)}, f32[1024,2048]{1,0:T(8,128)}, f32[2048,1024]{1,0:T(8,128)}, /*index=...) while((s32[]{:T(128)}, f32[1024,3,512]{2,0,1:T(8,128)}, ...), condition=%wide.region_32.33_spmd.clone.clone, body=%wide.region_0.32_spmd.clone.clone.sunk | while | flops 54250668032 | bytes 1470284544 | solution.py:262
  138.8 33.2 %all-gather.31.cloned.1.call-done = bf16[1024,1024]{1,0:T(8,128)(2,1)} async-done(((bf16[512,1024]{1,0:T(8,128)(2,1)}), bf16[1024,1024]{1,0:T(8,128)(2,1)}) %all-gather.31.cloned.1.call-update) | async-done | bytes 2097168 | tf_op jit(solution)/shard_map/while/body/eval_jaxpr/all_gather | solution.py:79
  180.2 33.6 %all-gather.33.cloned.1.call-done = bf16[4096,1,512]{0,2,1:T(8,128)(2,1)} async-done(((bf16[1024,1,512]{0,2,1:T(8,128)(2,1)}), bf16[4096,1,512]{0,2,1:T(8,128)(2,1)}) %all-gather.33.cloned.1.call-update) | async-done | bytes 4194320 | tf_op jit(solution)/shard_map/while/body/eval_jaxpr/all_gather | solution.py:116
  213.8 36.0 %all-gather.35.cloned.1.call-done = bf16[4096,1,512]{0,2,1:T(8,128)(2,1)} async-done(((bf16[1024,1,512]{0,2,1:T(8,128)(2,1)}), bf16[4096,1,512]{0,2,1:T(8,128)(2,1)}) %all-gather.35.cloned.1.call-update) | async-done | bytes 4194320 | tf_op jit(solution)/shard_map/while/body/eval_jaxpr/all_gather | solution.py:117
  251.0 166.1 %while.108 = (s32[]{:T(128)}, bf16[2,512,8,64]{1,3,2,0:T(8,128)(2,1)}, f32[2,8,512]{2,1,0:T(8,128)S(1)}, s32[4096]{0:T(1024)S(1)}, s32[2]{0:T(128)S(1)}, /*index...) while((s32[]{:T(128)}, ...), condition=%wide.region_7.7_spmd.clone, body=%wide.region_3.6_spmd.clone.sunk | while | flops 4511079424 | bytes 219897072 | solution.py:134
  306.0 27.8 %fusion.204 = bf16[2,512,8,64]{1,3,2,0:T(8,128)(2,1)} fusion(bf16[2,512,8,64]{1,3,2,0:T(8,128)(2,1)} %get-tuple-element.1847, s32[]{:T(128)S(6)} %copy.76, bf16[4096,8,64]{0,2,1:T(8,128)(2,1)} %get-tuple-element.1868, f32[8,512,4096]{2,1,0:T(8,128)} %get-tuple-element.1812, f32[8,512]{1,0:T(8,128)S(1)} %fusion.203, ...), kind=kOutput, calls=%fused_computation.10.clone.1 | convolution fusion | flops 2231369728 | bytes 74481664 | tf_op jit(solution)/shard_map/while/body/eval_jaxpr/while/body/eval_jaxpr/hqk,khd->qhd/dot_general | solution.py:129
  388.8 27.8 %fusion.204 = bf16[2,512,8,64]{1,3,2,0:T(8,128)(2,1)} fusion(bf16[2,512,8,64]{1,3,2,0:T(8,128)(2,1)} %get-tuple-element.1847, s32[]{:T(128)S(6)} %copy.76, bf16[4096,8,64]{0,2,1:T(8,128)(2,1)} %get-tuple-element.1868, f32[8,512,4096]{2,1,0:T(8,128)} %get-tuple-element.1812, f32[8,512]{1,0:T(8,128)S(1)} %fusion.203, ...), kind=kOutput, calls=%fused_computation.10.clone.1 | convolution fusion | flops 2231369728 | bytes 74481664 | tf_op jit(solution)/shard_map/while/body/eval_jaxpr/while/body/eval_jaxpr/hqk,khd->qhd/dot_general | solution.py:129
  424.1 54.5 %reduce-scatter.19.cloned.1.call-done = f32[512,1024]{1,0:T(8,128)} async-done(((f32[1024,1024]{1,0:T(8,128)}), f32[512,1024]{1,0:T(8,128)}) %reduce-scatter.19.cloned.1.call-update) | async-done | bytes 2097168 | tf_op jit(solution)/shard_map/while/body/eval_jaxpr/reduce_scatter | solution.py:85
  485.7 30.1 %all-gather.37.cloned.1.call-done = bf16[1024,1024]{1,0:T(8,128)(2,1)} async-done(((bf16[512,1024]{1,0:T(8,128)(2,1)}), bf16[1024,1024]{1,0:T(8,128)(2,1)}) %all-gather.37.cloned.1.call-update) | async-done | bytes 2097168 | tf_op jit(solution)/shard_map/while/body/eval_jaxpr/all_gather | solution.py:79
  572.4 54.5 %reduce-scatter.21.cloned.1.call-done = f32[512,1024]{1,0:T(8,128)} async-done(((f32[1024,1024]{1,0:T(8,128)}), f32[512,1024]{1,0:T(8,128)}) %reduce-scatter.21.cloned.1.call-update) | async-done | bytes 2097168 | tf_op jit(solution)/shard_map/while/body/eval_jaxpr/reduce_scatter | solution.py:88
  634.2 33.2 %all-gather.41.cloned.1.call-done = bf16[1024,1024]{1,0:T(8,128)(2,1)} async-done(((bf16[512,1024]{1,0:T(8,128)(2,1)}), bf16[1024,1024]{1,0:T(8,128)(2,1)}) %all-gather.41.cloned.1.call-update) | async-done | bytes 2097168 | tf_op jit(solution)/shard_map/while/body/eval_jaxpr/all_gather | solution.py:82
  672.4 396.0 %while.109 = (s32[]{:T(128)}, f32[4096,8,64]{0,2,1:T(8,128)}, f32[4096,8,64]{0,2,1:T(8,128)}, bf16[2,512,8,64]{1,3,2,0:T(8,128)(2,1)}, s32[2]{0:T(128)S(1)}, /*i...) while((s32[]{:T(128)}, f32[4096,8,64]{0,2,1:T(8,128)}, ...), condition=%wide.region_17.17_spmd.clone.clone, body=%wide.region_14.16_spmd.clone.clone.sunk | while | flops 10913946624 | bytes 590913280 | solution.py:198
  679.8 28.7 %subtract_exponential_fusion.3 = f32[8,512,4096]{2,1,0:T(8,128)} fusion(bf16[4096,8,64]{0,2,1:T(8,128)(2,1)} %get-tuple-element.1913, f32[8,512]{1,0:T(8,128)S(1)} %dynamic-slice_bitcast_fusion.2, pred[512,4096]{1,0:T(8,128)(4,1)S(1)} %and_or_fusion.5, bf16[1024,8,64]{0,2,1:T(8,128)(2,1)S(1)} %get-tuple-element.1909, s32[]{:T(128)S(6)} %select_n.260), kind=kOutput, calls=%fused_computation.40.clone.1 | convolution fusion | flops 2197815296 | bytes 73940992 | tf_op jit(solution)/shard_map/while/body/eval_jaxpr/while/body/eval_jaxpr/qhd,khd->hqk/dot_general | solution.py:102
  734.5 43.6 %multiply_reduce_fusion.9 = (f32[8,512]{1,0:T(8,128)S(1)}, f32[8,512,4096]{2,1,0:T(8,128)}) fusion(f32[8,512,4096]{2,1,0:T(8,128)} %subtract_exponential_fusion.3, bf16[4096,8,64]{0,2,1:T(8,128)(2,1)S(1)} %copy-done, bf16[1024,8,64]{0,2,1:T(8,128)(2,1)} %get-tuple-element.1915, s32[]{:T(128)S(6)} %select_n.260), kind=kOutput, calls=%fused_computation.39.clone.2 | convolution fusion | flops 2181033984 | bytes 138952704 | tf_op jit(solution)/shard_map/while/body/eval_jaxpr/while/body/eval_jaxpr/qhd,khd->hqk/dot_general | solution.py:179
  778.1 53.0 %multiply_convert_fusion.9 = bf16[8,512,4096]{2,1,0:T(8,128)(2,1)} fusion(f32[8,512,4096]{2,1,0:T(8,128)} %subtract_exponential_fusion.3, f32[8,512,4096]{2,1,0:T(8,128)} %get-tuple-element.1831, f32[8,512]{1,0:T(8,128)S(1)} %get-tuple-element.1832), kind=kLoop, calls=%fused_computation.38.clone.1 | loop fusion | flops 50331648 | bytes 167788544 | tf_op jit(solution)/shard_map/while/body/eval_jaxpr/while/body/eval_jaxpr/convert_element_type | solution.py:183
  875.2 28.7 %subtract_exponential_fusion.3 = f32[8,512,4096]{2,1,0:T(8,128)} fusion(bf16[4096,8,64]{0,2,1:T(8,128)(2,1)} %get-tuple-element.1913, f32[8,512]{1,0:T(8,128)S(1)} %dynamic-slice_bitcast_fusion.2, pred[512,4096]{1,0:T(8,128)(4,1)S(1)} %and_or_fusion.5, bf16[1024,8,64]{0,2,1:T(8,128)(2,1)S(1)} %get-tuple-element.1909, s32[]{:T(128)S(6)} %select_n.260), kind=kOutput, calls=%fused_computation.40.clone.1 | convolution fusion | flops 2197815296 | bytes 73940992 | tf_op jit(solution)/shard_map/while/body/eval_jaxpr/while/body/eval_jaxpr/qhd,khd->hqk/dot_general | solution.py:102
  903.9 28.3 %bitcast_add_fusion.5 = f32[4096,8,64]{0,2,1:T(8,128)} fusion(f32[4096,8,64]{0,2,1:T(8,128)} %get-tuple-element.1890, f32[8,512,4096]{2,1,0:T(8,128)} %subtract_exponential_fusion.3, pred[]{:T(512)S(6)} %compare.79, bf16[1024,8,64]{0,2,1:T(8,128)(2,1)} %get-tuple-element.1915, s32[]{:T(128)S(6)} %select_n.260), kind=kOutput, calls=%fused_computation.43.clone.1 | convolution fusion | flops 2168455168 | bytes 84410376 | tf_op jit(solution)/shard_map/while/body/eval_jaxpr/while/body/eval_jaxpr/hqk,qhd->khd/dot_general | solution.py:176
  932.2 43.6 %multiply_reduce_fusion.9 = (f32[8,512]{1,0:T(8,128)S(1)}, f32[8,512,4096]{2,1,0:T(8,128)}) fusion(f32[8,512,4096]{2,1,0:T(8,128)} %subtract_exponential_fusion.3, bf16[4096,8,64]{0,2,1:T(8,128)(2,1)S(1)} %copy-done, bf16[1024,8,64]{0,2,1:T(8,128)(2,1)} %get-tuple-element.1915, s32[]{:T(128)S(6)} %select_n.260), kind=kOutput, calls=%fused_computation.39.clone.2 | convolution fusion | flops 2181033984 | bytes 138952704 | tf_op jit(solution)/shard_map/while/body/eval_jaxpr/while/body/eval_jaxpr/qhd,khd->hqk/dot_general | solution.py:179
  975.8 53.0 %multiply_convert_fusion.9 = bf16[8,512,4096]{2,1,0:T(8,128)(2,1)} fusion(f32[8,512,4096]{2,1,0:T(8,128)} %subtract_exponential_fusion.3, f32[8,512,4096]{2,1,0:T(8,128)} %get-tuple-element.1831, f32[8,512]{1,0:T(8,128)S(1)} %get-tuple-element.1832), kind=kLoop, calls=%fused_computation.38.clone.1 | loop fusion | flops 50331648 | bytes 167788544 | tf_op jit(solution)/shard_map/while/body/eval_jaxpr/while/body/eval_jaxpr/convert_element_type | solution.py:183
  1125.6 47.0 %reduce-scatter.23.cloned.1.call-done = bf16[1024,512]{1,0:T(8,128)(2,1)} async-done(((bf16[4096,512]{1,0:T(8,128)(2,1)}), bf16[1024,512]{1,0:T(8,128)(2,1)}) %reduce-scatter.23.cloned.1.call-update) | async-done | bytes 1048592 | tf_op jit(solution)/shard_map/while/body/eval_jaxpr/reduce_scatter | solution.py:208
  1241.5 44.2 %reduce-scatter.27.cloned.1.call-done = f32[512,1024]{1,0:T(8,128)} async-done(((f32[1024,1024]{1,0:T(8,128)}), f32[512,1024]{1,0:T(8,128)}) %reduce-scatter.27.cloned.1.call-update) | async-done | bytes 2097168 | tf_op jit(solution)/shard_map/while/body/eval_jaxpr/reduce_scatter | solution.py:88
  1300.4 33.2 %all-gather.31.cloned.1.call-done = bf16[1024,1024]{1,0:T(8,128)(2,1)} async-done(((bf16[512,1024]{1,0:T(8,128)(2,1)}), bf16[1024,1024]{1,0:T(8,128)(2,1)}) %all-gather.31.cloned.1.call-update) | async-done | bytes 2097168 | tf_op jit(solution)/shard_map/while/body/eval_jaxpr/all_gather | solution.py:79
  1342.0 33.4 %all-gather.33.cloned.1.call-done = bf16[4096,1,512]{0,2,1:T(8,128)(2,1)} async-done(((bf16[1024,1,512]{0,2,1:T(8,128)(2,1)}), bf16[4096,1,512]{0,2,1:T(8,128)(2,1)}) %all-gather.33.cloned.1.call-update) | async-done | bytes 4194320 | tf_op jit(solution)/shard_map/while/body/eval_jaxpr/all_gather | solution.py:116
  1375.4 36.0 %all-gather.35.cloned.1.call-done = bf16[4096,1,512]{0,2,1:T(8,128)(2,1)} async-done(((bf16[1024,1,512]{0,2,1:T(8,128)(2,1)}), bf16[4096,1,512]{0,2,1:T(8,128)(2,1)}) %all-gather.35.cloned.1.call-update) | async-done | bytes 4194320 | tf_op jit(solution)/shard_map/while/body/eval_jaxpr/all_gather | solution.py:117
  1412.5 177.5 %while.108 = (s32[]{:T(128)}, bf16[2,512,8,64]{1,3,2,0:T(8,128)(2,1)}, f32[2,8,512]{2,1,0:T(8,128)S(1)}, s32[4096]{0:T(1024)S(1)}, s32[2]{0:T(128)S(1)}, /*index...) while((s32[]{:T(128)}, ...), condition=%wide.region_7.7_spmd.clone, body=%wide.region_3.6_spmd.clone.sunk | while | flops 4511079424 | bytes 219897072 | solution.py:134
  1467.5 27.8 %fusion.204 = bf16[2,512,8,64]{1,3,2,0:T(8,128)(2,1)} fusion(bf16[2,512,8,64]{1,3,2,0:T(8,128)(2,1)} %get-tuple-element.1847, s32[]{:T(128)S(6)} %copy.76, bf16[4096,8,64]{0,2,1:T(8,128)(2,1)} %get-tuple-element.1868, f32[8,512,4096]{2,1,0:T(8,128)} %get-tuple-element.1812, f32[8,512]{1,0:T(8,128)S(1)} %fusion.203, ...), kind=kOutput, calls=%fused_computation.10.clone.1 | convolution fusion | flops 2231369728 | bytes 74481664 | tf_op jit(solution)/shard_map/while/body/eval_jaxpr/while/body/eval_jaxpr/hqk,khd->qhd/dot_general | solution.py:129
  1550.4 27.8 %fusion.204 = bf16[2,512,8,64]{1,3,2,0:T(8,128)(2,1)} fusion(bf16[2,512,8,64]{1,3,2,0:T(8,128)(2,1)} %get-tuple-element.1847, s32[]{:T(128)S(6)} %copy.76, bf16[4096,8,64]{0,2,1:T(8,128)(2,1)} %get-tuple-element.1868, f32[8,512,4096]{2,1,0:T(8,128)} %get-tuple-element.1812, f32[8,512]{1,0:T(8,128)S(1)} %fusion.203, ...), kind=kOutput, calls=%fused_computation.10.clone.1 | convolution fusion | flops 2231369728 | bytes 74481664 | tf_op jit(solution)/shard_map/while/body/eval_jaxpr/while/body/eval_jaxpr/hqk,khd->qhd/dot_general | solution.py:129
  1597.1 54.5 %reduce-scatter.19.cloned.1.call-done = f32[512,1024]{1,0:T(8,128)} async-done(((f32[1024,1024]{1,0:T(8,128)}), f32[512,1024]{1,0:T(8,128)}) %reduce-scatter.19.cloned.1.call-update) | async-done | bytes 2097168 | tf_op jit(solution)/shard_map/while/body/eval_jaxpr/reduce_scatter | solution.py:85
  1658.7 30.1 %all-gather.37.cloned.1.call-done = bf16[1024,1024]{1,0:T(8,128)(2,1)} async-done(((bf16[512,1024]{1,0:T(8,128)(2,1)}), bf16[1024,1024]{1,0:T(8,128)(2,1)}) %all-gather.37.cloned.1.call-update) | async-done | bytes 2097168 | tf_op jit(solution)/shard_map/while/body/eval_jaxpr/all_gather | solution.py:79
  1745.5 54.5 %reduce-scatter.21.cloned.1.call-done = f32[512,1024]{1,0:T(8,128)} async-done(((f32[1024,1024]{1,0:T(8,128)}), f32[512,1024]{1,0:T(8,128)}) %reduce-scatter.21.cloned.1.call-update) | async-done | bytes 2097168 | tf_op jit(solution)/shard_map/while/body/eval_jaxpr/reduce_scatter | solution.py:88
  1807.3 33.2 %all-gather.41.cloned.1.call-done = bf16[1024,1024]{1,0:T(8,128)(2,1)} async-done(((bf16[512,1024]{1,0:T(8,128)(2,1)}), bf16[1024,1024]{1,0:T(8,128)(2,1)}) %all-gather.41.cloned.1.call-update) | async-done | bytes 2097168 | tf_op jit(solution)/shard_map/while/body/eval_jaxpr/all_gather | solution.py:82
  1845.5 396.0 %while.109 = (s32[]{:T(128)}, f32[4096,8,64]{0,2,1:T(8,128)}, f32[4096,8,64]{0,2,1:T(8,128)}, bf16[2,512,8,64]{1,3,2,0:T(8,128)(2,1)}, s32[2]{0:T(128)S(1)}, /*i...) while((s32[]{:T(128)}, f32[4096,8,64]{0,2,1:T(8,128)}, ...), condition=%wide.region_17.17_spmd.clone.clone, body=%wide.region_14.16_spmd.clone.clone.sunk | while | flops 10913946624 | bytes 590913280 | solution.py:198
  1853.1 28.7 %subtract_exponential_fusion.3 = f32[8,512,4096]{2,1,0:T(8,128)} fusion(bf16[4096,8,64]{0,2,1:T(8,128)(2,1)} %get-tuple-element.1913, f32[8,512]{1,0:T(8,128)S(1)} %dynamic-slice_bitcast_fusion.2, pred[512,4096]{1,0:T(8,128)(4,1)S(1)} %and_or_fusion.5, bf16[1024,8,64]{0,2,1:T(8,128)(2,1)S(1)} %get-tuple-element.1909, s32[]{:T(128)S(6)} %select_n.260), kind=kOutput, calls=%fused_computation.40.clone.1 | convolution fusion | flops 2197815296 | bytes 73940992 | tf_op jit(solution)/shard_map/while/body/eval_jaxpr/while/body/eval_jaxpr/qhd,khd->hqk/dot_general | solution.py:102
  1907.8 43.6 %multiply_reduce_fusion.9 = (f32[8,512]{1,0:T(8,128)S(1)}, f32[8,512,4096]{2,1,0:T(8,128)}) fusion(f32[8,512,4096]{2,1,0:T(8,128)} %subtract_exponential_fusion.3, bf16[4096,8,64]{0,2,1:T(8,128)(2,1)S(1)} %copy-done, bf16[1024,8,64]{0,2,1:T(8,128)(2,1)} %get-tuple-element.1915, s32[]{:T(128)S(6)} %select_n.260), kind=kOutput, calls=%fused_computation.39.clone.2 | convolution fusion | flops 2181033984 | bytes 138952704 | tf_op jit(solution)/shard_map/while/body/eval_jaxpr/while/body/eval_jaxpr/qhd,khd->hqk/dot_general | solution.py:179
  1951.4 53.0 %multiply_convert_fusion.9 = bf16[8,512,4096]{2,1,0:T(8,128)(2,1)} fusion(f32[8,512,4096]{2,1,0:T(8,128)} %subtract_exponential_fusion.3, f32[8,512,4096]{2,1,0:T(8,128)} %get-tuple-element.1831, f32[8,512]{1,0:T(8,128)S(1)} %get-tuple-element.1832), kind=kLoop, calls=%fused_computation.38.clone.1 | loop fusion | flops 50331648 | bytes 167788544 | tf_op jit(solution)/shard_map/while/body/eval_jaxpr/while/body/eval_jaxpr/convert_element_type | solution.py:183
  2048.5 28.7 %subtract_exponential_fusion.3 = f32[8,512,4096]{2,1,0:T(8,128)} fusion(bf16[4096,8,64]{0,2,1:T(8,128)(2,1)} %get-tuple-element.1913, f32[8,512]{1,0:T(8,128)S(1)} %dynamic-slice_bitcast_fusion.2, pred[512,4096]{1,0:T(8,128)(4,1)S(1)} %and_or_fusion.5, bf16[1024,8,64]{0,2,1:T(8,128)(2,1)S(1)} %get-tuple-element.1909, s32[]{:T(128)S(6)} %select_n.260), kind=kOutput, calls=%fused_computation.40.clone.1 | convolution fusion | flops 2197815296 | bytes 73940992 | tf_op jit(solution)/shard_map/while/body/eval_jaxpr/while/body/eval_jaxpr/qhd,khd->hqk/dot_general | solution.py:102
  2077.2 28.3 %bitcast_add_fusion.5 = f32[4096,8,64]{0,2,1:T(8,128)} fusion(f32[4096,8,64]{0,2,1:T(8,128)} %get-tuple-element.1890, f32[8,512,4096]{2,1,0:T(8,128)} %subtract_exponential_fusion.3, pred[]{:T(512)S(6)} %compare.79, bf16[1024,8,64]{0,2,1:T(8,128)(2,1)} %get-tuple-element.1915, s32[]{:T(128)S(6)} %select_n.260), kind=kOutput, calls=%fused_computation.43.clone.1 | convolution fusion | flops 2168455168 | bytes 84410376 | tf_op jit(solution)/shard_map/while/body/eval_jaxpr/while/body/eval_jaxpr/hqk,qhd->khd/dot_general | solution.py:176
  2105.6 43.6 %multiply_reduce_fusion.9 = (f32[8,512]{1,0:T(8,128)S(1)}, f32[8,512,4096]{2,1,0:T(8,128)}) fusion(f32[8,512,4096]{2,1,0:T(8,128)} %subtract_exponential_fusion.3, bf16[4096,8,64]{0,2,1:T(8,128)(2,1)S(1)} %copy-done, bf16[1024,8,64]{0,2,1:T(8,128)(2,1)} %get-tuple-element.1915, s32[]{:T(128)S(6)} %select_n.260), kind=kOutput, calls=%fused_computation.39.clone.2 | convolution fusion | flops 2181033984 | bytes 138952704 | tf_op jit(solution)/shard_map/while/body/eval_jaxpr/while/body/eval_jaxpr/qhd,khd->hqk/dot_general | solution.py:179
  2149.1 53.0 %multiply_convert_fusion.9 = bf16[8,512,4096]{2,1,0:T(8,128)(2,1)} fusion(f32[8,512,4096]{2,1,0:T(8,128)} %subtract_exponential_fusion.3, f32[8,512,4096]{2,1,0:T(8,128)} %get-tuple-element.1831, f32[8,512]{1,0:T(8,128)S(1)} %get-tuple-element.1832), kind=kLoop, calls=%fused_computation.38.clone.1 | loop fusion | flops 50331648 | bytes 167788544 | tf_op jit(solution)/shard_map/while/body/eval_jaxpr/while/body/eval_jaxpr/convert_element_type | solution.py:183
  2298.7 47.0 %reduce-scatter.23.cloned.1.call-done = bf16[1024,512]{1,0:T(8,128)(2,1)} async-done(((bf16[4096,512]{1,0:T(8,128)(2,1)}), bf16[1024,512]{1,0:T(8,128)(2,1)}) %reduce-scatter.23.cloned.1.call-update) | async-done | bytes 1048592 | tf_op jit(solution)/shard_map/while/body/eval_jaxpr/reduce_scatter | solution.py:208
  2416.9 42.1 %reduce-scatter.27.cloned.1.call-done = f32[512,1024]{1,0:T(8,128)} async-done(((f32[1024,1024]{1,0:T(8,128)}), f32[512,1024]{1,0:T(8,128)}) %reduce-scatter.27.cloned.1.call-update) | async-done | bytes 2097168 | tf_op jit(solution)/shard_map/while/body/eval_jaxpr/reduce_scatter | solution.py:88
  2491.7 40.9 %all-reduce = (f32[1024]{0:T(1024)}, f32[1024]{0:T(1024)}, f32[2,1024]{1,0:T(2,128)}, f32[1024]{0:T(1024)}, f32[1024]{0:T(1024)}, /*index=5*/f32[1024]{0:T(1024)}, f32[4096]{0:T(1024)}, f32[1024]{0:T(1024)}) all-reduce(f32[1024]{0:T(1024)S(1)} %copy-done.69, ...), channel_id=1, replica_groups=mesh['dp'=4,'row'=4,'col'=2] {'dp','row','col'}, use_global_device_ids=true, to_apply=%region_33.34 | all-reduce | flops 12288 | bytes 98304 | tf_op jit(solution)/shard_map/psum | solution.py:283
  2534.1 66.8 %reduce-scatter.11.cloned.1.call-done = bf16[64,3,512]{2,0,1:T(8,128)(2,1)} async-done(((bf16[1024,3,512]{2,0,1:T(8,128)(2,1)}), bf16[64,3,512]{2,0,1:T(8,128)(2,1)}) %reduce-scatter.11.cloned.1.call-update) | async-done | bytes 196624 | tf_op jit(solution)/shard_map/reduce_scatter | solution.py:292
  2602.6 73.7 %reduce-scatter.15.cloned.1.call-done = bf16[64,2048]{1,0:T(8,128)(2,1)} async-done(((bf16[1024,2048]{1,0:T(8,128)(2,1)}), bf16[64,2048]{1,0:T(8,128)(2,1)}) %reduce-scatter.15.cloned.1.call-update) | async-done | bytes 262160 | tf_op jit(solution)/shard_map/reduce_scatter | solution.py:302
  2678.2 73.9 %reduce-scatter.17.cloned.1.call-done = bf16[2048,64]{0,1:T(8,128)(2,1)} async-done(((bf16[2048,1024]{0,1:T(8,128)(2,1)}), bf16[2048,64]{0,1:T(8,128)(2,1)}) %reduce-scatter.17.cloned.1.call-update) | async-done | bytes 262160 | tf_op jit(solution)/shard_map/reduce_scatter | solution.py:306
  (668 shorter events, 949.3 us)
Async XLA Ops:
  7.2 21.9 all-gather.27.cloned.1.call-start
  7.9 51.3 %all-gather.23.cloned.1.call-start = ((), (), s32[]{:S(2)}) async-start(), calls=%async_computation.10 | async-start | bytes 3932160 | tf_op jit(solution)/shard_map/all_gather | solution.py:91
  8.7 86.6 %all-gather.29.cloned.1.call-start = ((), (), s32[]{:S(2)}) async-start(), calls=%async_computation.13 | async-start | bytes 5242880 | tf_op jit(solution)/shard_map/all_gather | solution.py:93
  9.4 122.3 %all-gather.25.cloned.1.call-start = ((), (), s32[]{:S(2)}) async-start(), calls=%async_computation.11 | async-start | bytes 5242880 | tf_op jit(solution)/shard_map/all_gather | solution.py:94
  131.7 40.3 %all-gather.31.cloned.1.call-start = ((), (), s32[]{:S(2)}) async-start(), calls=%async_computation.18 | async-start | bytes 3145728 | tf_op jit(solution)/shard_map/while/body/eval_jaxpr/all_gather | solution.py:79
  138.8 75.0 %all-gather.33.cloned.1.call-start = ((), (), s32[]{:S(2)}) async-start(), calls=%async_computation.19 | async-start | bytes 5242880 | tf_op jit(solution)/shard_map/while/body/eval_jaxpr/all_gather | solution.py:116
  179.2 70.7 %all-gather.35.cloned.1.call-start = ((), (), s32[]{:S(2)}) async-start(), calls=%async_computation.20 | async-start | bytes 5242880 | tf_op jit(solution)/shard_map/while/body/eval_jaxpr/all_gather | solution.py:117
  179.9 298.6 %reduce-scatter.19.cloned.1.call-start = ((), (), s32[]{:S(2)}) async-start(), calls=%async_computation.21 | async-start | bytes 6291456 | tf_op jit(solution)/shard_map/while/body/eval_jaxpr/reduce_scatter | solution.py:85
  420.7 57.9 %copy-start.72 = (f32[1024]{0:T(1024)S(1)}, f32[1024]{0:T(1024)}, u32[]{:S(2)}) copy-start(f32[1024]{0:T(1024)} %get-tuple-element.2025) | copy-start | bytes 12292 | tf_op jit(solution)/shard_map/while
  424.0 57.1 %copy-start.34 = (f32[1024]{0:T(1024)S(1)}, f32[1024]{0:T(1024)}, u32[]{:S(2)}) copy-start(f32[1024]{0:T(1024)} %get-tuple-element.2026) | copy-start | bytes 12292 | tf_op jit(solution)/shard_map/while
  424.1 57.1 %copy-start.70 = (f32[1024]{0:T(1024)S(1)}, f32[1024]{0:T(1024)}, u32[]{:S(2)}) copy-start(f32[1024]{0:T(1024)} %get-tuple-element.2027) | copy-start | bytes 12292 | tf_op jit(solution)/shard_map/while
  424.1 91.8 %all-gather.37.cloned.1.call-start = ((), (), s32[]{:S(2)}) async-start(), calls=%async_computation.22 | async-start | bytes 3145728 | tf_op jit(solution)/shard_map/while/body/eval_jaxpr/all_gather | solution.py:79
  480.8 149.2 %copy-start.1 = (f32[512,1024]{1,0:T(8,128)}, f32[512,1024]{1,0:T(8,128)S(1)}, u32[]{:S(2)}) copy-start(f32[512,1024]{1,0:T(8,128)S(1)} %get-tuple-element.1774) | copy-start | bytes 6291460 | tf_op jit(solution)/shard_map/while
  482.6 67.8 %all-gather.39.cloned.1.call-start = ((), (), s32[]{:S(2)}) async-start(), calls=%async_computation.23 | async-start | bytes 3145728 | tf_op jit(solution)/shard_map/while/body/eval_jaxpr/all_gather | solution.py:82
  485.7 141.2 %reduce-scatter.21.cloned.1.call-start = ((), (), s32[]{:S(2)}) async-start(), calls=%async_computation.24 | async-start | bytes 6291456 | tf_op jit(solution)/shard_map/while/body/eval_jaxpr/reduce_scatter | solution.py:88
  572.4 95.0 %all-gather.41.cloned.1.call-start = ((), (), s32[]{:S(2)}) async-start(), calls=%async_computation.25 | async-start | bytes 3145728 | tf_op jit(solution)/shard_map/while/body/eval_jaxpr/all_gather | solution.py:82
  634.1 491.5 %reduce-scatter.25.cloned.1.call-start = ((), (), s32[]{:S(2)}) async-start(), calls=%async_computation.27 | async-start | bytes 5242880 | tf_op jit(solution)/shard_map/while/body/eval_jaxpr/reduce_scatter | solution.py:202
  778.1 53.0 %copy-start.18 = (bf16[2,512,8,64]{1,3,2,0:T(8,128)(2,1)S(1)}, bf16[2,512,8,64]{1,3,2,0:T(8,128)(2,1)}, u32[]{:S(2)}) copy-start(bf16[2,512,8,64]{1,3,2,0:T(8,128)(2,1)} %get-tuple-element.1891) | copy-start | bytes 3145732 | tf_op jit(solution)/shard_map/while/body/eval_jaxpr/while
  975.8 53.0 %copy-start.18 = (bf16[2,512,8,64]{1,3,2,0:T(8,128)(2,1)S(1)}, bf16[2,512,8,64]{1,3,2,0:T(8,128)(2,1)}, u32[]{:S(2)}) copy-start(bf16[2,512,8,64]{1,3,2,0:T(8,128)(2,1)} %get-tuple-element.1891) | copy-start | bytes 3145732 | tf_op jit(solution)/shard_map/while/body/eval_jaxpr/while
  1080.9 91.7 %reduce-scatter.23.cloned.1.call-start = ((), (), s32[]{:S(2)}) async-start(), calls=%async_computation.26 | async-start | bytes 5242880 | tf_op jit(solution)/shard_map/while/body/eval_jaxpr/reduce_scatter | solution.py:208
  1093.8 135.4 %reduce-scatter.29.cloned.1.call-start = ((), (), s32[]{:S(2)}) async-start(), calls=%async_computation.29 | async-start | bytes 6291456 | tf_op jit(solution)/shard_map/while/body/eval_jaxpr/reduce_scatter | solution.py:85
  1106.4 179.4 %reduce-scatter.27.cloned.1.call-start = ((), (), s32[]{:S(2)}) async-start(), calls=%async_computation.28 | async-start | bytes 6291456 | tf_op jit(solution)/shard_map/while/body/eval_jaxpr/reduce_scatter | solution.py:88
  1110.5 70.1 %copy-start.16 = (bf16[1024,1,512]{2,0,1:T(8,128)(2,1)}, bf16[1024,1,512]{2,0,1:T(8,128)(2,1)S(1)}, u32[]{:S(2)}) copy-start(bf16[1024,1,512]{2,0,1:T(8,128)(2,1)S(1)} %reshape.542) | copy-start | bytes 3145732 | tf_op jit(solution)/shard_map/while
  1293.2 40.4 %all-gather.31.cloned.1.call-start = ((), (), s32[]{:S(2)}) async-start(), calls=%async_computation.18 | async-start | bytes 3145728 | tf_op jit(solution)/shard_map/while/body/eval_jaxpr/all_gather | solution.py:79
  1300.4 75.0 %all-gather.33.cloned.1.call-start = ((), (), s32[]{:S(2)}) async-start(), calls=%async_computation.19 | async-start | bytes 5242880 | tf_op jit(solution)/shard_map/while/body/eval_jaxpr/all_gather | solution.py:116
  1340.7 70.7 %all-gather.35.cloned.1.call-start = ((), (), s32[]{:S(2)}) async-start(), calls=%async_computation.20 | async-start | bytes 5242880 | tf_op jit(solution)/shard_map/while/body/eval_jaxpr/all_gather | solution.py:117
  1341.5 310.0 %reduce-scatter.19.cloned.1.call-start = ((), (), s32[]{:S(2)}) async-start(), calls=%async_computation.21 | async-start | bytes 6291456 | tf_op jit(solution)/shard_map/while/body/eval_jaxpr/reduce_scatter | solution.py:85
  1593.7 57.9 %copy-start.72 = (f32[1024]{0:T(1024)S(1)}, f32[1024]{0:T(1024)}, u32[]{:S(2)}) copy-start(f32[1024]{0:T(1024)} %get-tuple-element.2025) | copy-start | bytes 12292 | tf_op jit(solution)/shard_map/while
  1597.0 57.1 %copy-start.34 = (f32[1024]{0:T(1024)S(1)}, f32[1024]{0:T(1024)}, u32[]{:S(2)}) copy-start(f32[1024]{0:T(1024)} %get-tuple-element.2026) | copy-start | bytes 12292 | tf_op jit(solution)/shard_map/while
  1597.0 57.1 %copy-start.70 = (f32[1024]{0:T(1024)S(1)}, f32[1024]{0:T(1024)}, u32[]{:S(2)}) copy-start(f32[1024]{0:T(1024)} %get-tuple-element.2027) | copy-start | bytes 12292 | tf_op jit(solution)/shard_map/while
  1597.0 91.8 %all-gather.37.cloned.1.call-start = ((), (), s32[]{:S(2)}) async-start(), calls=%async_computation.22 | async-start | bytes 3145728 | tf_op jit(solution)/shard_map/while/body/eval_jaxpr/all_gather | solution.py:79
  1653.8 149.4 %copy-start.1 = (f32[512,1024]{1,0:T(8,128)}, f32[512,1024]{1,0:T(8,128)S(1)}, u32[]{:S(2)}) copy-start(f32[512,1024]{1,0:T(8,128)S(1)} %get-tuple-element.1774) | copy-start | bytes 6291460 | tf_op jit(solution)/shard_map/while
  1655.5 67.9 %all-gather.39.cloned.1.call-start = ((), (), s32[]{:S(2)}) async-start(), calls=%async_computation.23 | async-start | bytes 3145728 | tf_op jit(solution)/shard_map/while/body/eval_jaxpr/all_gather | solution.py:82
  1658.6 141.4 %reduce-scatter.21.cloned.1.call-start = ((), (), s32[]{:S(2)}) async-start(), calls=%async_computation.24 | async-start | bytes 6291456 | tf_op jit(solution)/shard_map/while/body/eval_jaxpr/reduce_scatter | solution.py:88
  1745.5 95.0 %all-gather.41.cloned.1.call-start = ((), (), s32[]{:S(2)}) async-start(), calls=%async_computation.25 | async-start | bytes 3145728 | tf_op jit(solution)/shard_map/while/body/eval_jaxpr/all_gather | solution.py:82
  1807.2 491.5 %reduce-scatter.25.cloned.1.call-start = ((), (), s32[]{:S(2)}) async-start(), calls=%async_computation.27 | async-start | bytes 5242880 | tf_op jit(solution)/shard_map/while/body/eval_jaxpr/reduce_scatter | solution.py:202
  1951.4 53.0 %copy-start.18 = (bf16[2,512,8,64]{1,3,2,0:T(8,128)(2,1)S(1)}, bf16[2,512,8,64]{1,3,2,0:T(8,128)(2,1)}, u32[]{:S(2)}) copy-start(bf16[2,512,8,64]{1,3,2,0:T(8,128)(2,1)} %get-tuple-element.1891) | copy-start | bytes 3145732 | tf_op jit(solution)/shard_map/while/body/eval_jaxpr/while
  2149.1 53.0 %copy-start.18 = (bf16[2,512,8,64]{1,3,2,0:T(8,128)(2,1)S(1)}, bf16[2,512,8,64]{1,3,2,0:T(8,128)(2,1)}, u32[]{:S(2)}) copy-start(bf16[2,512,8,64]{1,3,2,0:T(8,128)(2,1)} %get-tuple-element.1891) | copy-start | bytes 3145732 | tf_op jit(solution)/shard_map/while/body/eval_jaxpr/while
  2254.0 91.7 %reduce-scatter.23.cloned.1.call-start = ((), (), s32[]{:S(2)}) async-start(), calls=%async_computation.26 | async-start | bytes 5242880 | tf_op jit(solution)/shard_map/while/body/eval_jaxpr/reduce_scatter | solution.py:208
  2266.9 135.4 %reduce-scatter.29.cloned.1.call-start = ((), (), s32[]{:S(2)}) async-start(), calls=%async_computation.29 | async-start | bytes 6291456 | tf_op jit(solution)/shard_map/while/body/eval_jaxpr/reduce_scatter | solution.py:85
  2279.5 179.5 %reduce-scatter.27.cloned.1.call-start = ((), (), s32[]{:S(2)}) async-start(), calls=%async_computation.28 | async-start | bytes 6291456 | tf_op jit(solution)/shard_map/while/body/eval_jaxpr/reduce_scatter | solution.py:88
  2283.6 70.1 %copy-start.16 = (bf16[1024,1,512]{2,0,1:T(8,128)(2,1)}, bf16[1024,1,512]{2,0,1:T(8,128)(2,1)S(1)}, u32[]{:S(2)}) copy-start(bf16[1024,1,512]{2,0,1:T(8,128)(2,1)S(1)} %reshape.542) | copy-start | bytes 3145732 | tf_op jit(solution)/shard_map/while
  2408.7 52.5 %copy-start.40 = (f32[512]{0:T(512)S(1)}, f32[512]{0:T(512)}, u32[]{:S(2)}) copy-start(f32[512]{0:T(512)} %copy-done.39) | copy-start | bytes 6148 | tf_op jit(solution)/shard_map/while
  2408.7 52.5 %copy-start.36 = (f32[512]{0:T(512)S(1)}, f32[512]{0:T(512)}, u32[]{:S(2)}) copy-start(f32[512]{0:T(512)} %copy-done.35) | copy-start | bytes 6148 | tf_op jit(solution)/shard_map/while
  2469.5 63.1 %reduce-scatter.13.cloned.1.call-start = ((), (), s32[]{:S(2)}) async-start(), calls=%async_computation.15 | async-start | bytes 1114112 | tf_op jit(solution)/shard_map/reduce_scatter | solution.py:296
  2472.2 128.7 %reduce-scatter.11.cloned.1.call-start = ((), (), s32[]{:S(2)}) async-start(), calls=%async_computation.14 | async-start | bytes 3342336 | tf_op jit(solution)/shard_map/reduce_scatter | solution.py:292
  2477.1 199.3 %reduce-scatter.15.cloned.1.call-start = ((), (), s32[]{:S(2)}) async-start(), calls=%async_computation.16 | async-start | bytes 4456448 | tf_op jit(solution)/shard_map/reduce_scatter | solution.py:302
  2483.2 268.8 %reduce-scatter.17.cloned.1.call-start = ((), (), s32[]{:S(2)}) async-start(), calls=%async_computation.17 | async-start | bytes 4456448 | tf_op jit(solution)/shard_map/reduce_scatter | solution.py:306
  (172 other events, 3074.6 us)
Sparse Core Ops, SparseCore 0:
  9.5 19.5 all-gather.26
  30.7 28.4 all-gather.22
  60.8 34.4 all-gather.28
  96.7 34.9 all-gather.24
  138.9 33.0 all-gather.30
  179.3 34.4 all-gather.32
  215.3 34.4 all-gather.34
  424.2 54.3 reduce-scatter.18
  482.7 33.0 all-gather.36
  517.2 33.0 all-gather.38
  572.5 54.3 reduce-scatter.20
  634.2 33.0 all-gather.40
  1081.0 44.5 reduce-scatter.24
  1128.0 44.5 reduce-scatter.22
  1174.7 54.3 reduce-scatter.28
  1231.3 54.3 reduce-scatter.26
  1300.5 33.0 all-gather.30
  1340.9 34.4 all-gather.32
  1376.9 34.4 all-gather.34
  1597.1 54.3 reduce-scatter.18
  1655.7 33.0 all-gather.36
  1690.3 33.0 all-gather.38
  1745.6 54.3 reduce-scatter.20
  1807.3 33.0 all-gather.40
  2254.1 44.5 reduce-scatter.24
  2301.1 44.5 reduce-scatter.22
  2347.9 54.3 reduce-scatter.28
  2404.6 54.3 reduce-scatter.26
  2474.0 57.7 reduce-scatter.12
  2535.4 65.4 reduce-scatter.10
  2604.8 71.5 reduce-scatter.14
  2680.2 71.7 reduce-scatter.16
where the time goes:
time: 2770 us; the launch traced here: 2760 us
  waiting for transfers between devices  1190 us (43%)
  matrix products  959 us (35%)
  other arithmetic  432 us (16%)
  local copies, waits for them, and re-layouts  83 us (3%)
  blocking collectives  40.9 us (1%)
  loops' own time  39.9 us (1%)
    dot_general x8, matrix products, block_scores(): jnp.einsum('qhd,khd->hqk', q_part, keys3, preferred_element_type=jnp.floa...  219 us
    convert_element_type x4, other arithmetic, attend_back(): grad_scores = (probs * (grad_probs - center)).astype(jnp.bfloat16)  212 us
    reduce_scatter x4, waiting for transfers between devices, sum_inputs(): return lax.psum_scatter(values, 'col', scatter_dimension=0, tiled=True)  195 us
    dot_general x4, matrix products, attend_back(): jnp.einsum('qhd,khd->hqk', grad_part, values3, preferred_element_type=jnp...  174 us
    reduce_scatter x4, waiting for transfers between devices, sum_branch(): return lax.psum_scatter(values, 'col', scatter_dimension=0, tiled=True)  152 us
    all_gather x4, waiting for transfers between devices, spread_rows(): return lax.all_gather(values, 'col', axis=0, tiled=True)  127 us
    all_gather x4, waiting for transfers between devices, spread_grads(): return lax.all_gather(values, 'col', axis=0, tiled=True)  114 us
    dot_general x4, matrix products, attend(): jnp.einsum('hqk,khd->qhd', probs_low, values3, preferred_element_type=jnp...  111 us
  transfers between devices with their start and end apart: 32, of which 31 were waited for; matrix products, arithmetic and copies ran while one was open for 7% of the time, Pallas kernels for 0%

commit v1 on v0

--- a/solution.py
+++ b/solution.py
@@ -1,6 +1,10 @@
+import functools
+
 import jax
 import jax.numpy as jnp
 from jax import lax
+from jax.experimental import pallas as pl
+from jax.experimental.pallas import tpu as pltpu
 from jax.sharding import PartitionSpec as P
 
 HEAD = 64
@@ -11,6 +15,16 @@
 
 EPSILON = 1e-05
 MASKED_SCORE = -1e30
+LOG2E = 1.4426950408889634
+PAIR = 2 * HEAD
+BQ = 256
+BK = 512
+BK_BACK = 512
+HIDDEN_TILE = 512
+VMEM_BYTES = 60 * 2**20
+NT = (((1,), (1,)), ((), ()))
+TN = (((0,), (0,)), ((), ()))
+MESH_AXES = ("row", "col")
 
 
 def normalize(values, gain, shift):
@@ -40,7 +54,7 @@
     return jax.tree.map(lambda total, extra: total + extra, first, second)
 
 
-def body(
+def gathered_body(
     tokens,
     cotangent,
     branch,
@@ -310,6 +324,796 @@
     )
 
 
+def dot(left, right):
+    return jnp.dot(left, right, preferred_element_type=jnp.float32)
+
+
+def dot_nt(left, right):
+    return lax.dot_general(left, right, NT, preferred_element_type=jnp.float32)
+
+
+def cost(flops, moved, exps=0):
+    return pl.CostEstimate(flops=int(flops), bytes_accessed=int(moved), transcendentals=int(exps))
+
+
+def params():
+    return pltpu.CompilerParams(vmem_limit_bytes=VMEM_BYTES)
+
+
+def fixed(shape):
+    return pl.BlockSpec(shape, lambda *_: (0,) * len(shape), pipeline_mode=pl.Buffered(1))
+
+
+def pair_rows(rows):
+    low = lax.broadcasted_iota(jnp.int32, rows.shape, 1) < HEAD
+    zero = jnp.zeros_like(rows)
+    return jnp.concatenate([jnp.where(low, rows, zero), jnp.where(low, zero, rows)], axis=0)
+
+
+def pick_lanes(stacked):
+    half = stacked.shape[0] // 2
+    low = lax.broadcasted_iota(jnp.int32, (half, stacked.shape[1]), 1) < HEAD
+    return jnp.where(low, stacked[:half], stacked[half:])
+
+
+def qkv_kernel(rows, groups, x_ref, w_ref, bias_ref, *out_refs):
+    depth = w_ref.shape[3]
+    for part in range(3):
+        weight = w_ref[:, 0, part].reshape(rows * depth, 2 * PAIR)
+        values = dot(x_ref[...], weight)
+        if part != 1:
+            values = values + bias_ref[0, 0 if part == 0 else 1]
+        if part == 0:
+            values = values * HEAD**-0.5
+        values = values.astype(jnp.bfloat16)
+        span = values.shape[0] // groups
+        for g in range(groups):
+            for half in range(2):
+                out_refs[g][half, 0, :, part * PAIR : (part + 1) * PAIR] = values[
+                    g * span : (g + 1) * span, half * PAIR : (half + 1) * PAIR
+                ]
+
+
+def project_qkv(normed, weight, bias, groups):
+    rows, cols, _, depth, width = weight.shape
+    tokens, model = normed.shape
+    span = tokens // groups
+    return pl.pallas_call(
+        functools.partial(qkv_kernel, rows, groups),
+        grid=(rows // 2, cols),
+        in_specs=[
+            fixed((tokens, model)),
+            pl.BlockSpec((rows, 1, 3, depth, 2 * PAIR), lambda i, c: (0, c, 0, 0, i)),
+            pl.BlockSpec((1, 2, 1, 2 * PAIR), lambda i, c: (c, 0, 0, i)),
+        ],
+        out_specs=[pl.BlockSpec((2, 1, span, 3 * PAIR), lambda i, c: (i, c, 0, 0))] * groups,
+        out_shape=[jax.ShapeDtypeStruct((rows, cols, span, 3 * PAIR), jnp.bfloat16)] * groups,
+        compiler_params=params(),
+        cost_estimate=cost(6 * tokens * model * model, 8 * tokens * model + 6 * model * model),
+        name="qkv",
+    )(normed, weight, bias)
+
+
+def attend_kernel(
+    bk, cut_ref, qkv_ref, o_ref, lse_ref, s_ref, own_ref, value_ref, peak_ref, acc_ref
+):
+    i = pl.program_id(0)
+    prompt_blocks = PLEN // BQ
+
+    @pl.when(i == 0)
+    def _():
+        value_ref[:, :PAIR] = qkv_ref[:, 2 * PAIR : 3 * PAIR]
+        value_ref[:, PAIR:] = jnp.ones((value_ref.shape[0], PAIR), value_ref.dtype)
+
+    start = pl.multiple_of(i * BQ, BQ)
+    queries = pair_rows(qkv_ref[pl.ds(start, BQ), 0:PAIR])
+    limit = jnp.where(i < prompt_blocks, start, cut_ref[jnp.maximum(i - prompt_blocks, 0)])
+    full = limit // bk
+    rest = limit - full * bk
+
+    def scores(first, count):
+        keys = qkv_ref[pl.ds(pl.multiple_of(first, BQ), count), PAIR : 2 * PAIR]
+        return dot_nt(queries, keys) * LOG2E
+
+    def lane_peak(values):
+        return functools.reduce(
+            jnp.maximum, [values[:, at : at + 128] for at in range(0, values.shape[1], 128)]
+        )
+
+    own = scores(start, BQ)
+    row = lax.broadcasted_iota(jnp.int32, own.shape, 0) & (BQ - 1)
+    own = jnp.where(lax.broadcasted_iota(jnp.int32, own.shape, 1) <= row, own, MASKED_SCORE)
+    own_ref[...] = own
+    peak_ref[...] = lane_peak(own)
+
+    def score_step(j, none):
+        values = scores(j * bk, bk)
+        s_ref[j] = values
+        peak_ref[...] = jnp.maximum(peak_ref[...], lane_peak(values))
+        return none
+
+    lax.fori_loop(0, full, score_step, 0)
+
+    @pl.when(rest > 0)
+    def _():
+        values = scores(full * bk, bk)
+        seen = lax.broadcasted_iota(jnp.int32, values.shape, 1) < rest
+        values = jnp.where(seen, values, MASKED_SCORE)
+        s_ref[full] = values
+        peak_ref[...] = jnp.maximum(peak_ref[...], lane_peak(values))
+
+    peak = jnp.max(peak_ref[...], axis=1, keepdims=True)
+    probs = jnp.exp2(own_ref[...] - peak).astype(jnp.bfloat16)
+    acc_ref[...] = dot(probs, value_ref[pl.ds(start, BQ), :])
+
+    def value_step(j, none):
+        probs = jnp.exp2(s_ref[j] - peak).astype(jnp.bfloat16)
+        acc_ref[...] += dot(probs, value_ref[pl.ds(pl.multiple_of(j * bk, bk), bk), :])
+        return none
+
+    lax.fori_loop(0, full + jnp.where(rest > 0, 1, 0), value_step, 0)
+    total = acc_ref[:, PAIR:]
+    o_ref[...] = pick_lanes(acc_ref[:, :PAIR] / total).astype(o_ref.dtype)
+    lse_ref[0] = jnp.transpose(peak + jnp.log2(total))[:8]
+
+
+def attend(cut, qkv):
+    tokens = qkv.shape[0]
+    blocks = tokens // BQ
+    pairs = 2 * tokens * tokens // 4
+    return pl.pallas_call(
+        functools.partial(attend_kernel, BK),
+        grid=(blocks,),
+        in_specs=[pl.BlockSpec(memory_space=pltpu.SMEM), fixed((tokens, 3 * PAIR))],
+        out_specs=[
+            pl.BlockSpec((BQ, PAIR), lambda i: (i, 0)),
+            pl.BlockSpec((1, 8, 2 * BQ), lambda i: (i, 0, 0)),
+        ],
+        out_shape=[
+            jax.ShapeDtypeStruct((tokens, PAIR), jnp.bfloat16),
+            jax.ShapeDtypeStruct((blocks, 8, 2 * BQ), jnp.float32),
+        ],
+        scratch_shapes=[
+            pltpu.VMEM((PLEN // BK, 2 * BQ, BK), jnp.float32),
+            pltpu.VMEM((2 * BQ, BQ), jnp.float32),
+            pltpu.VMEM((tokens, 2 * PAIR), jnp.bfloat16),
+            pltpu.VMEM((2 * BQ, PAIR), jnp.float32),
+            pltpu.VMEM((2 * BQ, 2 * PAIR), jnp.float32),
+        ],
+        compiler_params=params(),
+        cost_estimate=cost(8 * 2 * pairs * 256, 2 * tokens * 4 * PAIR, pairs),
+        name="attend",
+    )(cut, qkv)
+
+
+def attend_back_kernel(
+    bk, cut_ref, qkv_ref, o_ref, do_ref, lse_ref, out_ref, dk_ref, dv_ref, dq_ref
+):
+    i = pl.program_id(0)
+    prompt_blocks = PLEN // BQ
+
+    @pl.when(i == 0)
+    def _():
+        dk_ref[...] = jnp.zeros_like(dk_ref)
+        dv_ref[...] = jnp.zeros_like(dv_ref)
+
+    start = pl.multiple_of(i * BQ, BQ)
+    queries = pair_rows(qkv_ref[pl.ds(start, BQ), 0:PAIR])
+    grad = do_ref[pl.ds(start, BQ), :]
+    grads = pair_rows(grad)
+    mixed = jnp.transpose(
+        grad.astype(jnp.float32) * o_ref[pl.ds(start, BQ), :].astype(jnp.float32)
+    )
+    center = jnp.concatenate(
+        [
+            jnp.sum(mixed[:HEAD], axis=0, keepdims=True),
+            jnp.sum(mixed[HEAD:], axis=0, keepdims=True),
+        ],
+        axis=1,
+    )
+    log_total = lse_ref[0, 0:1, :]
+    limit = jnp.where(i < prompt_blocks, start, cut_ref[jnp.maximum(i - prompt_blocks, 0)])
+    full = limit // bk
+    rest = limit - full * bk
+
+    def block(first, count, keep, begin):
+        at = pl.ds(pl.multiple_of(first, BQ), count)
+        keys = qkv_ref[at, PAIR : 2 * PAIR]
+        values = qkv_ref[at, 2 * PAIR : 3 * PAIR]
+        probs = jnp.exp2(dot_nt(keys, queries) * LOG2E - log_total)
+        if keep is not None:
+            probs = jnp.where(keep(probs.shape), probs, 0.0)
+        dv_ref[at, :] += dot(probs.astype(jnp.bfloat16), grads)
+        grad_probs = dot_nt(values, grads)
+        grad_scores = (probs * (grad_probs - center)).astype(jnp.bfloat16)
+        dk_ref[at, :] += dot(grad_scores, queries)
+        part = lax.dot_general(keys, grad_scores, TN, preferred_element_type=jnp.float32)
+        dq_ref[...] = part if begin else dq_ref[...] + part
+
+    def causal(shape):
+        key = lax.broadcasted_iota(jnp.int32, shape, 0)
+        query = lax.broadcasted_iota(jnp.int32, shape, 1) & (BQ - 1)
+        return key <= query
+
+    block(start, BQ, causal, True)
+
+    def step(j, none):
+        block(j * bk, bk, None, False)
+        return none
+
+    lax.fori_loop(0, full, step, 0)
+
+    @pl.when(rest > 0)
+    def _():
+        block(full * bk, bk, lambda s: lax.broadcasted_iota(jnp.int32, s, 0) < rest, False)
+
+    grad_query = pick_lanes(jnp.transpose(dq_ref[...])) * HEAD**-0.5
+    out_ref[pl.ds(start, BQ), 0:PAIR] = grad_query.astype(out_ref.dtype)
+
+    @pl.when(i == pl.num_programs(0) - 1)
+    def _():
+        out_ref[:, PAIR : 2 * PAIR] = dk_ref[...].astype(out_ref.dtype)
+        out_ref[:, 2 * PAIR : 3 * PAIR] = dv_ref[...].astype(out_ref.dtype)
+
+
+def attend_back(cut, qkv, att, grad_att, log_totals):
+    tokens = qkv.shape[0]
+    pairs = 2 * tokens * tokens // 4
+    return pl.pallas_call(
+        functools.partial(attend_back_kernel, BK_BACK),
+        grid=(tokens // BQ,),
+        in_specs=[
+            pl.BlockSpec(memory_space=pltpu.SMEM),
+            fixed((tokens, 3 * PAIR)),
+            fixed((tokens, PAIR)),
+            fixed((tokens, PAIR)),
+            pl.BlockSpec((1, 8, 2 * BQ), lambda i: (i, 0, 0)),
+        ],
+        out_specs=fixed((tokens, 3 * PAIR)),
+        out_shape=jax.ShapeDtypeStruct((tokens, 3 * PAIR), jnp.bfloat16),
+        scratch_shapes=[
+            pltpu.VMEM((tokens, PAIR), jnp.float32),
+            pltpu.VMEM((tokens, PAIR), jnp.float32),
+            pltpu.VMEM((PAIR, 2 * BQ), jnp.float32),
+        ],
+        compiler_params=params(),
+        cost_estimate=cost(10 * 2 * pairs * 256, 2 * tokens * 8 * PAIR, pairs),
+        name="attend_back",
+    )(cut, qkv, att, grad_att, log_totals)
+
+
+def centered(values):
+    center = values - jnp.mean(values, axis=-1, keepdims=True)
+    spread = jnp.mean(center * center, axis=-1, keepdims=True)
+    inverse = lax.rsqrt(spread + EPSILON)
+    return center * inverse, inverse
+
+
+def norm_back(grad, gain, unit, inverse):
+    scaled = grad * gain
+    mean_one = jnp.mean(scaled, axis=-1, keepdims=True)
+    mean_two = jnp.mean(scaled * unit, axis=-1, keepdims=True)
+    return (scaled - mean_one - unit * mean_two) * inverse
+
+
+def middle_kernel(
+    rows, cols, tok_ref, att_ref, w_ref, vec_ref, middle_ref, normed_ref, turned_ref
+):
+    parts = []
+    for c in range(cols):
+        parts.append(jnp.concatenate([att_ref[r, c] for r in range(rows)], axis=1))
+    pieces = []
+    for r in range(rows):
+        total = dot(parts[0], w_ref[r, 0])
+        for c in range(1, cols):
+            total = total + dot(parts[c], w_ref[r, c])
+        pieces.append(total)
+    middle = tok_ref[0].astype(jnp.float32) + jnp.concatenate(pieces, axis=1) + vec_ref[0:1]
+    middle_ref[...] = middle
+    normed = (centered(middle)[0] * vec_ref[1:2] + vec_ref[2:3]).astype(jnp.bfloat16)
+    normed_ref[...] = normed
+    turned_ref[...] = jnp.transpose(normed)
+
+
+def project_out(tokens, att, weight, vectors, g):
+    rows, cols, span, _ = att.shape
+    model = tokens.shape[2]
+    tile = min(256, span)
+    return pl.pallas_call(
+        functools.partial(middle_kernel, rows, cols),
+        grid=(span // tile,),
+        in_specs=[
+            pl.BlockSpec((1, tile, model), lambda i: (g, i, 0)),
+            pl.BlockSpec((rows, cols, tile, PAIR), lambda i: (0, 0, i, 0)),
+            fixed(weight.shape),
+            fixed(vectors.shape),
+        ],
+        out_specs=[
+            pl.BlockSpec((tile, model), lambda i: (i, 0)),
+            pl.BlockSpec((tile, model), lambda i: (i, 0)),
+            pl.BlockSpec((model, tile), lambda i: (0, i)),
+        ],
+        out_shape=[
+            jax.ShapeDtypeStruct((span, model), jnp.float32),
+            jax.ShapeDtypeStruct((span, model), jnp.bfloat16),
+            jax.ShapeDtypeStruct((model, span), jnp.bfloat16),
+        ],
+        compiler_params=params(),
+        cost_estimate=cost(2 * span * model * model, 2 * model * model + 12 * span * model),
+        name="out_norm",
+    )(tokens, att, weight, vectors)
+
+
+def hidden_kernel(rows, dps, groups, *refs):
+    normed_refs = refs[:groups]
+    turned_refs = refs[groups : 2 * groups]
+    middle_refs = refs[2 * groups : 3 * groups]
+    (cot_ref, cot_turned_ref, fc_ref, fc_bias_ref, proj_ref, proj_bias_ref) = refs[
+        3 * groups : 3 * groups + 6
+    ]
+    (out_ref, back_ref, grad_fc_ref, grad_proj_ref, bias_ref) = refs[
+        3 * groups + 6 : 3 * groups + 11
+    ]
+    normed_all, turned_all, out_acc, back_acc = refs[3 * groups + 11 :]
+    step = pl.program_id(0) * pl.num_programs(1) + pl.program_id(1)
+    last = pl.num_programs(0) * pl.num_programs(1) - 1
+    span = normed_refs[0].shape[0]
+    model = normed_all.shape[1]
+    depth = model // rows
+    tile = fc_ref.shape[3]
+
+    @pl.when(step == 0)
+    def _():
+        for g in range(groups):
+            normed_all[g * span : (g + 1) * span, :] = normed_refs[g][...]
+            turned_all[:, g * span : (g + 1) * span] = turned_refs[g][...]
+
+    fc_weight = fc_ref[:, 0].reshape(model, tile)
+    hidden = dot(normed_all[...], fc_weight) + fc_bias_ref[0]
+    root = 0.7978845608028654
+    square = hidden * hidden
+    inner = jnp.tanh(hidden * (root + (root * 0.044715) * square))
+    plus = 0.5 + 0.5 * inner
+    active = (hidden * plus).astype(jnp.bfloat16)
+    slope = plus + hidden * (0.5 - 0.5 * inner * inner) * (root + (3 * root * 0.044715) * square)
+    cot = cot_ref[...]
+    grad_active = None
+    for r in range(rows):
+        part = dot_nt(cot[:, r * depth : (r + 1) * depth], proj_ref[r, 0])
+        grad_active = part if grad_active is None else grad_active + part
+    grad_hidden = grad_active * slope
+    grad_low = grad_hidden.astype(jnp.bfloat16)
+    bias_ref[0] = jnp.sum(grad_low.astype(jnp.float32), axis=0, keepdims=True)
+    grad_fc = dot(turned_all[...], grad_low).astype(jnp.bfloat16)
+    grad_proj = dot(cot_turned_ref[...], active).astype(jnp.bfloat16)
+    cut = model // (rows * dps)
+    for r in range(rows):
+        for d in range(dps):
+            at = (d * rows + r) * cut
+            grad_fc_ref[r, 0, d] = grad_fc[at : at + cut]
+            grad_proj_ref[r, 0, d] = grad_proj[at : at + cut]
+    for r in range(rows):
+        lanes = slice(r * depth, (r + 1) * depth)
+        forward = dot(active, proj_ref[r, 0])
+        backward = dot_nt(grad_low, fc_ref[r, 0])
+
+        @pl.when(step == 0)
+        def _():
+            out_acc[:, lanes] = forward
+            back_acc[:, lanes] = backward
+
+        @pl.when(step > 0)
+        def _():
+            out_acc[:, lanes] += forward
+            back_acc[:, lanes] += backward
+
+    @pl.when(step == last)
+    def _():
+        for g in range(groups):
+            at = slice(g * span, (g + 1) * span)
+            out_ref[g] = (middle_refs[g][...] + out_acc[at] + proj_bias_ref[...]).astype(
+                out_ref.dtype
+            )
+            back_ref[g] = back_acc[at]
+
+
+def feed_forward(normed, turned, middle, cot, cot_turned, fc, fc_bias, proj, proj_bias, dps):
+    groups = len(normed)
+    span, model = normed[0].shape
+    tokens = groups * span
+    rows, cols, depth, local = fc.shape
+    tile = min(HIDDEN_TILE, local)
+    cut = model // (rows * dps)
+    grad_spec = pl.BlockSpec((rows, 1, dps, cut, tile), lambda c, i: (0, c, 0, 0, i))
+    grad_shape = jax.ShapeDtypeStruct((rows, cols, dps, cut, local), jnp.bfloat16)
+    return pl.pallas_call(
+        functools.partial(hidden_kernel, rows, dps, groups),
+        grid=(cols, local // tile),
+        in_specs=[fixed((span, model))] * groups
+        + [fixed((model, span))] * groups
+        + [fixed((span, model))] * groups
+        + [
+            fixed((tokens, model)),
+            fixed((model, tokens)),
+            pl.BlockSpec((rows, 1, depth, tile), lambda c, i: (0, c, 0, i)),
+            pl.BlockSpec((1, 1, tile), lambda c, i: (c, 0, i)),
+            pl.BlockSpec((rows, 1, tile, depth), lambda c, i: (0, c, i, 0)),
+            fixed((1, model)),
+        ],
+        out_specs=[
+            fixed((groups, span, model)),
+            fixed((groups, span, model)),
+            grad_spec,
+            grad_spec,
+            pl.BlockSpec((1, 1, tile), lambda c, i: (c, 0, i)),
+        ],
+        out_shape=[
+            jax.ShapeDtypeStruct((groups, span, model), jnp.bfloat16),
+            jax.ShapeDtypeStruct((groups, span, model), jnp.float32),
+            grad_shape,
+            grad_shape,
+            jax.ShapeDtypeStruct((cols, 1, local), jnp.float32),
+        ],
+        scratch_shapes=[
+            pltpu.VMEM((tokens, model), jnp.bfloat16),
+            pltpu.VMEM((model, tokens), jnp.bfloat16),
+            pltpu.VMEM((tokens, model), jnp.float32),
+            pltpu.VMEM((tokens, model), jnp.float32),
+        ],
+        compiler_params=params(),
+        cost_estimate=cost(
+            12 * tokens * model * cols * local, 8 * model * cols * local, tokens * cols * local
+        ),
+        name="feed_forward",
+    )(*normed, *turned, *middle, cot, cot_turned, fc, fc_bias, proj, proj_bias)
+
+
+def middle_back_kernel(
+    rows, cols, grad_ref, middle_ref, cot_ref, w_ref, vec_ref, dx_ref, turned_ref, datt_ref, sum_ref
+):
+    grad = grad_ref[0]
+    unit, inverse = centered(middle_ref[...])
+    total = cot_ref[0].astype(jnp.float32) + norm_back(grad, vec_ref[1:2], unit, inverse)
+    dx_ref[...] = total
+    low = total.astype(jnp.bfloat16)
+    turned_ref[...] = jnp.transpose(low)
+    depth = w_ref.shape[3]
+    for c in range(cols):
+        part = dot_nt(low[:, :depth], w_ref[0, c])
+        for r in range(1, rows):
+            part = part + dot_nt(low[:, r * depth : (r + 1) * depth], w_ref[r, c])
+        part = part.astype(jnp.bfloat16)
+        for r in range(rows):
+            datt_ref[r, c] = part[:, r * PAIR : (r + 1) * PAIR]
+
+    @pl.when(pl.program_id(0) == 0)
+    def _():
+        sum_ref[...] = jnp.zeros_like(sum_ref)
+
+    sum_ref[0:1] += jnp.sum(grad * unit, axis=0, keepdims=True)
+    sum_ref[1:2] += jnp.sum(grad, axis=0, keepdims=True)
+    sum_ref[2:3] += jnp.sum(low.astype(jnp.float32), axis=0, keepdims=True)
+
+
+def middle_back(grad, middle, cot, weight, vectors, g):
+    span, model = middle.shape
+    rows, cols = weight.shape[:2]
+    tile = min(256, span)
+    return pl.pallas_call(
+        functools.partial(middle_back_kernel, rows, cols),
+        grid=(span // tile,),
+        in_specs=[
+            pl.BlockSpec((1, tile, model), lambda i: (g, i, 0)),
+            pl.BlockSpec((tile, model), lambda i: (i, 0)),
+            pl.BlockSpec((1, tile, model), lambda i: (g, i, 0)),
+            fixed(weight.shape),
+            fixed(vectors.shape),
+        ],
+        out_specs=[
+            pl.BlockSpec((tile, model), lambda i: (i, 0)),
+            pl.BlockSpec((model, tile), lambda i: (0, i)),
+            pl.BlockSpec((rows, cols, tile, PAIR), lambda i: (0, 0, i, 0)),
+            pl.BlockSpec((8, model), lambda i: (0, 0)),
+        ],
+        out_shape=[
+            jax.ShapeDtypeStruct((span, model), jnp.float32),
+            jax.ShapeDtypeStruct((model, span), jnp.bfloat16),
+            jax.ShapeDtypeStruct((rows, cols, span, PAIR), jnp.bfloat16),
+            jax.ShapeDtypeStruct((8, model), jnp.float32),
+        ],
+        compiler_params=params(),
+        cost_estimate=cost(2 * span * model * model, 2 * model * model + 18 * span * model),
+        name="out_norm_back",
+    )(grad, middle, cot, weight, vectors)
+
+
+def out_grad_kernel(rows, dps, groups, *refs):
+    out_ref = refs[2 * groups]
+    total = None
+    for g in range(groups):
+        att = jnp.concatenate([refs[groups + g][r, 0] for r in range(rows)], axis=1)
+        part = dot(refs[g][...], att)
+        total = part if total is None else total + part
+    total = total.astype(jnp.bfloat16)
+    cut = out_ref.shape[3]
+    for r in range(rows):
+        for d in range(dps):
+            at = (d * rows + r) * cut
+            out_ref[r, 0, d] = total[at : at + cut]
+
+
+def out_grad(turned, att, dps):
+    groups = len(turned)
+    model, span = turned[0].shape
+    rows, cols = att[0].shape[:2]
+    cut = model // (rows * dps)
+    return pl.pallas_call(
+        functools.partial(out_grad_kernel, rows, dps, groups),
+        grid=(cols,),
+        in_specs=[fixed((model, span))] * groups
+        + [pl.BlockSpec((rows, 1, span, PAIR), lambda c: (0, c, 0, 0))] * groups,
+        out_specs=pl.BlockSpec((rows, 1, dps, cut, rows * PAIR), lambda c: (0, c, 0, 0, 0)),
+        out_shape=jax.ShapeDtypeStruct((rows, cols, dps, cut, rows * PAIR), jnp.bfloat16),
+        compiler_params=params(),
+        cost_estimate=cost(2 * groups * span * model * model, 2 * model * model),
+        name="out_grad",
+    )(*turned, *att)
+
+
+def input_kernel(rows, dps, groups, *refs):
+    grad_refs = refs[:groups]
+    dx_refs = refs[groups : 2 * groups]
+    (turned_ref, tok_ref, w_ref, gain_ref) = refs[2 * groups : 2 * groups + 4]
+    (out_ref, grad_ref, bias_ref, sum_ref) = refs[2 * groups + 4 : 2 * groups + 8]
+    acc = refs[2 * groups + 8]
+    step = pl.program_id(0) * pl.num_programs(1) + pl.program_id(1)
+    last = pl.num_programs(0) * pl.num_programs(1) - 1
+    span = dx_refs[0].shape[0]
+    depth = w_ref.shape[3]
+    cut = grad_ref.shape[4]
+    grads = []
+    for part in range(3):
+        lanes = slice(part * PAIR, (part + 1) * PAIR)
+        grads.append(
+            jnp.concatenate(
+                [
+                    jnp.concatenate([ref[half, 0, :, lanes] for half in range(2)], axis=1)
+                    for ref in grad_refs
+                ],
+                axis=0,
+            )
+        )
+    for part in range(3):
+        weight_grad = dot(turned_ref[...], grads[part]).astype(jnp.bfloat16)
+        for r in range(rows):
+            for d in range(dps):
+                at = (d * rows + r) * cut
+                grad_ref[r, 0, d, part] = weight_grad[at : at + cut]
+        bias_ref[0, part] = jnp.sum(grads[part].astype(jnp.float32), axis=0, keepdims=True)
+    for r in range(rows):
+        lanes = slice(r * depth, (r + 1) * depth)
+        piece = dot_nt(grads[0], w_ref[r, 0, 0])
+        for part in range(1, 3):
+            piece = piece + dot_nt(grads[part], w_ref[r, 0, part])
+
+        @pl.when(step == 0)
+        def _():
+            acc[:, lanes] = piece
+
+        @pl.when(step > 0)
+        def _():
+            acc[:, lanes] += piece
+
+    @pl.when(step == last)
+    def _():
+        gain_sum = None
+        for g in range(groups):
+            grad = acc[g * span : (g + 1) * span]
+            unit, inverse = centered(tok_ref[g].astype(jnp.float32))
+            out_ref[g] = dx_refs[g][...] + norm_back(grad, gain_ref[...], unit, inverse)
+            gains = jnp.sum(grad * unit, axis=0, keepdims=True)
+            shifts = jnp.sum(grad, axis=0, keepdims=True)
+            gain_sum = gains if gain_sum is None else gain_sum + gains
+            shift_sum = shifts if g == 0 else shift_sum + shifts
+        sum_ref[0:1] = gain_sum
+        sum_ref[1:2] = shift_sum
+
+
+def input_back(grads, dx, normed_turned, tokens, weight, gain, dps):
+    groups = len(grads)
+    rows, cols, _, depth, width = weight.shape
+    span, model = dx[0].shape
+    cut = model // (rows * dps)
+    count = groups * span
+    return pl.pallas_call(
+        functools.partial(input_kernel, rows, dps, groups),
+        grid=(rows // 2, cols),
+        in_specs=[pl.BlockSpec((2, 1, span, 3 * PAIR), lambda i, c: (i, c, 0, 0))] * groups
+        + [fixed((span, model))] * groups
+        + [
+            fixed((model, count)),
+            fixed((groups, span, model)),
+            pl.BlockSpec((rows, 1, 3, depth, 2 * PAIR), lambda i, c: (0, c, 0, 0, i)),
+            fixed((1, model)),
+        ],
+        out_specs=[
+            fixed((groups, span, model)),
+            pl.BlockSpec((rows, 1, dps, 3, cut, 2 * PAIR), lambda i, c: (0, c, 0, 0, 0, i)),
+            pl.BlockSpec((1, 3, 1, 2 * PAIR), lambda i, c: (c, 0, 0, i)),
+            fixed((8, model)),
+        ],
+        out_shape=[
+            jax.ShapeDtypeStruct((groups, span, model), jnp.float32),
+            jax.ShapeDtypeStruct((rows, cols, dps, 3, cut, width), jnp.bfloat16),
+            jax.ShapeDtypeStruct((cols, 3, 1, width), jnp.float32),
+            jax.ShapeDtypeStruct((8, model), jnp.float32),
+        ],
+        scratch_shapes=[pltpu.VMEM((count, model), jnp.float32)],
+        compiler_params=params(),
+        cost_estimate=cost(12 * count * model * model, 12 * model * model + 20 * count * model),
+        name="input_back",
+    )(*grads, *dx, normed_turned, tokens, weight, gain)
+
+
+def head_body(
+    tokens,
+    cotangent,
+    branch,
+    ln1_gain,
+    ln1_bias,
+    qkv_weight,
+    qv_bias,
+    out_weight,
+    out_bias,
+    ln2_gain,
+    ln2_bias,
+    fc_weight,
+    fc_bias,
+    proj_weight,
+    proj_bias,
+):
+    groups, span, model = tokens.shape
+    rows = lax.axis_size("row")
+    cols = lax.axis_size("col")
+    dps = lax.axis_size("dp")
+    members = rows * cols
+    count = groups * span
+    head_cols = qv_bias.shape[1]
+    hidden_cols = fc_bias.shape[0]
+
+    def spread(shard):
+        whole = lax.all_gather(shard, MESH_AXES, axis=0, tiled=False)
+        return whole.reshape((rows, cols) + shard.shape)
+
+    def swap(blocks):
+        return lax.all_to_all(blocks, MESH_AXES, 0, 0, tiled=True)
+
+    def collect(partial):
+        partial = partial.reshape((members,) + partial.shape[2:])
+        partial = lax.psum_scatter(partial, MESH_AXES, scatter_dimension=0, tiled=True)
+        partial = lax.psum_scatter(partial, "dp", scatter_dimension=1, tiled=True)
+        return partial.reshape(partial.shape[2:]).astype(jnp.float32)
+
+    w_qkv = spread(jnp.transpose(qkv_weight, (1, 0, 2)))
+    biases = lax.all_gather(jnp.concatenate([qv_bias.reshape(-1), fc_bias]), "col", axis=0)
+    w_out = spread(out_weight)
+    w_fc = spread(fc_weight)
+    w_proj = spread(proj_weight)
+    qv_full = biases[:, : 2 * head_cols].reshape(cols, 2, 1, head_cols)
+    fc_full = biases[:, 2 * head_cols :].reshape(cols, 1, hidden_cols)
+
+    residual = tokens.astype(jnp.float32)
+    normed = normalize(residual, ln1_gain, ln1_bias).astype(jnp.bfloat16).reshape(count, model)
+    normed_turned = normed.T
+    cot_flat = cotangent.reshape(count, model)
+    cot_turned = cot_flat.T
+    proj_bias_sum = jnp.sum(cot_flat.astype(jnp.float32), axis=0)
+
+    blocks = project_qkv(normed, w_qkv, qv_full, groups)
+    vectors = jnp.stack([out_bias, ln2_gain, ln2_bias] + [out_bias] * 5)
+    gains = jnp.stack([ln2_gain] * 8)
+    qkv, att, att_own, log_totals, middle, normed_two, turned_two = [], [], [], [], [], [], []
+    for g in range(groups):
+        received = swap(blocks[g].reshape(members, span, 3 * PAIR))
+        qkv.append(received.reshape(members * span, 3 * PAIR))
+    for g in range(groups):
+        mixed, totals = attend(branch[g], qkv[g])
+        att_own.append(mixed)
+        log_totals.append(totals)
+        att.append(swap(mixed.reshape(members, span, PAIR)).reshape(rows, cols, span, PAIR))
+    for g in range(groups):
+        mid, low, turned = project_out(tokens, att[g], w_out, vectors, g)
+        middle.append(mid)
+        normed_two.append(low)
+        turned_two.append(turned)
+    block_out, grad_two, grad_fc, grad_proj, fc_bias_sum = feed_forward(
+        normed_two,
+        turned_two,
+        middle,
+        cot_flat,
+        cot_turned,
+        w_fc,
+        fc_full,
+        w_proj,
+        proj_bias[None],
+        dps,
+    )
+    d_fc = collect(grad_fc)
+    d_proj = collect(grad_proj).T
+    dx, dx_turned, grad_att, sums_two = [], [], [], []
+    for g in range(groups):
+        total, turned, datt, sums = middle_back(
+            grad_two, middle[g], cotangent, w_out, gains, g
+        )
+        dx.append(total)
+        dx_turned.append(turned)
+        sums_two.append(sums)
+        grad_att.append(
+            swap(datt.reshape(members, span, PAIR)).reshape(members * span, PAIR)
+        )
+    d_out = collect(out_grad(dx_turned, att, dps)).T
+    grads = []
+    for g in range(groups):
+        grad = attend_back(branch[g], qkv[g], att_own[g], grad_att[g], log_totals[g])
+        grads.append(
+            swap(grad.reshape(members, span, 3 * PAIR)).reshape(rows, cols, span, 3 * PAIR)
+        )
+    input_grad, grad_qkv, qkv_bias_sum, sums_one = input_back(
+        grads, dx, normed_turned, tokens, w_qkv, ln1_gain[None], dps
+    )
+    d_qkv = jnp.transpose(collect(grad_qkv), (1, 0, 2))
+    sums_two = functools.reduce(jnp.add, sums_two)
+    bias_rows = jnp.transpose(qkv_bias_sum[:, :, 0], (1, 0, 2)).reshape(3, cols * head_cols)
+    small = (
+        sums_one[0],
+        sums_one[1],
+        bias_rows[0],
+        bias_rows[2],
+        sums_two[2],
+        sums_two[0],
+        sums_two[1],
+        fc_bias_sum.reshape(-1),
+        proj_bias_sum,
+    )
+    ends = []
+    for item in small:
+        ends.append((ends[-1] if ends else 0) + item.shape[0])
+    packed = lax.psum(jnp.concatenate(small), ("dp",) + MESH_AXES)
+    (s_gain1, s_bias1, s_q, s_v, s_out, s_gain2, s_bias2, s_fc, s_proj) = jnp.split(
+        packed, ends[:-1]
+    )
+    return (
+        block_out,
+        input_grad,
+        s_gain1,
+        s_bias1,
+        d_qkv,
+        jnp.stack([s_q, s_v]),
+        d_out,
+        s_out,
+        s_gain2,
+        s_bias2,
+        d_fc,
+        s_fc,
+        d_proj,
+        s_proj,
+    )
+
+
+def by_heads(mesh):
+    rows, cols = mesh.shape["row"], mesh.shape["col"]
+
+    def body(tokens, cotangent, branch, ln1_gain, ln1_bias, qkv_weight, *rest):
+        width = qkv_weight.shape[2] * cols
+        whole = tokens.shape[1] * rows * cols
+        fits = width == rows * cols * PAIR and rows % 2 == 0
+        fits = fits and whole == PLEN + CONTS * CLEN and tokens.shape[1] % BQ == 0
+        chosen = head_body if fits else gathered_body
+        return chosen(tokens, cotangent, branch, ln1_gain, ln1_bias, qkv_weight, *rest)
+
+    return body
+
+
 def solution(mesh):
     placed = (
         P("dp", ("row", "col"), None),
@@ -329,7 +1133,7 @@
         P(),
     )
     return jax.shard_map(
-        body,
+        by_heads(mesh),
         mesh=mesh,
         in_specs=placed,
         out_specs=(

time: 2770 us -> 884 us (0.32)
  matrix products: 959 us -> 0 us
  waiting for transfers between devices: 1190 us -> 435 us
  other arithmetic: 432 us -> 11 us
  Pallas kernels: 0 us -> 323 us
  local copies, waits for them, and re-layouts: 83 us -> 16.5 us
  loops' own time: 39.9 us -> 0 us
  starting transfers between devices: 1.88 us -> 32.3 us
    dot_general x52 -> x0, matrix products: 959 us -> none  [the longest x8 219 us: block_scores(): jnp.einsum('qhd,khd->hqk', q_part, keys3, preferred_element_type=jnp.floa...]
    all_gather x16 -> x4, waiting for transfers between devices: 499 us -> 38.8 us  [spread(): whole = lax.all_gather(shard, MESH_AXES, axis=0, tiled=False)]
    reduce_scatter x16 -> x8, waiting for transfers between devices: 686 us -> 265 us  [the longest x4 208 us: collect(): lax.psum_scatter(partial, MESH_AXES, scatter_dimension=0, tiled=True)]
    pallas_call x0 -> x12, Pallas kernels: none -> 323 us  [the longest x2 95.7 us: attend_back(): pl.pallas_call(functools.partial(attend_back_kernel, BK_BACK), grid=(toke...]
    convert_element_type x18 -> x2, other arithmetic: 262 us -> 3.92 us  [the longest x1 2.15 us: head_body(): normalize(residual, ln1_gain, ln1_bias).astype(jnp.bfloat16)]
    all_to_all x0 -> x8, waiting for transfers between devices: none -> 127 us  [swap(): return lax.all_to_all(blocks, MESH_AXES, 0, 0, tiled=True)]
    reduce_sum x22 -> x1, other arithmetic: 109 us -> 0.37 us  [head_body(): proj_bias_sum = jnp.sum(cot_flat.astype(jnp.float32), axis=0)]
    another operation x5 -> x0, loops' own time: 39.9 us -> none  [the longest x2 22.7 us: micro_step(): attended, log_totals = lax.map(attend, block_starts)]
  transfers between devices with their start and end apart: 32 -> 20, of which waited for: 31 -> 12; matrix products, arithmetic and copies ran while one was open for 7% -> 2% of each run, Pallas kernels for 0% -> 27%
where the time goes in v1:
time: 884 us; the launch traced here: 879 us
  waiting for transfers between devices  435 us (49%)
  Pallas kernels  323 us (37%)
  blocking collectives  45.1 us (5%)
  starting transfers between devices  32.3 us (4%)
  local copies, waits for them, and re-layouts  16.5 us (2%)
  between operations  15.1 us (2%)
  other arithmetic  11 us (1%)
    reduce_scatter x4, waiting for transfers between devices, collect(): lax.psum_scatter(partial, MESH_AXES, scatter_dimension=0, tiled=True)  208 us
    all_to_all x8, waiting for transfers between devices, swap(): return lax.all_to_all(blocks, MESH_AXES, 0, 0, tiled=True)  127 us
    pallas_call x2, Pallas kernels, attend_back(): pl.pallas_call(functools.partial(attend_back_kernel, BK_BACK), grid=(toke...  95.7 us
    pallas_call x1, Pallas kernels, feed_forward(): pl.pallas_call(functools.partial(hidden_kernel, rows, dps, groups), grid=...  78.1 us
    pallas_call x2, Pallas kernels, attend(): pl.pallas_call(functools.partial(attend_kernel, BK), grid=(blocks,), in_s...  74 us
    reduce_scatter x4, waiting for transfers between devices, collect(): partial = lax.psum_scatter(partial, 'dp', scatter_dimension=1, tiled=True)  56.4 us
    psum x1, blocking collectives, head_body(): packed = lax.psum(jnp.concatenate(small), ('dp',) + MESH_AXES)  39.8 us
    all_gather x4, waiting for transfers between devices, spread(): whole = lax.all_gather(shard, MESH_AXES, axis=0, tiled=False)  38.8 us
  transfers between devices with their start and end apart: 20, of which 12 were waited for; matrix products, arithmetic and copies ran while one was open for 2% of the time, Pallas kernels for 27%

profile of v1, /device:TPU:0, one launch (start us, length us, event | category | flops | bytes accessed | tf_op | source)
XLA Modules:
  0.0 879.0 jit_solution(17363348348821321856)
XLA Ops:
  10.1 5.3 all-gather.1
  16.4 0.7 fusion.2
  17.2 2.1 fusion.5
  19.3 38.7 %all-gather.10.cloned.1.call-done = bf16[24,256,512]{2,1,0:T(8,128)(2,1)} async-done(((bf16[3,256,512]{2,1,0:T(8,128)(2,1)}), bf16[24,256,512]{2,1,0:T(8,128)(2,1)}) %all-gather.10.cloned.1.call-update) | async-done | bytes 6291472 | tf_op jit(solution)/shard_map/all_gather | solution.py:985
  58.0 10.8 %qkv.1 = (bf16[4,2,512,384]{3,2,1,0:T(8,128)(2,1)}, bf16[4,2,512,384]{3,2,1,0:T(8,128)(2,1)}) custom-call(bf16[1024,1024]{1,0:T(8,128)(2,1)} %bitcast.85, bf16[4,2,3,256,512]{4,3,2,1,0:T(8,128)(2,1)} %bitcast.133, f32[2,2,1,512]{3,2,1,0:T(1,128)} %reshape.194.bias_ref), custom_call_target="tpu_custom_call" | custom-call | flops 6442450944 | bytes 14680064 | tf_op jit(solution)/shard_map/qkv/pallas_call | solution.py:381
  68.8 3.8 all-to-all-start.2
  73.1 48.2 %all-to-all-done.2 = bf16[8,512,384]{2,1,0:T(8,128)(2,1)S(1)} async-done(((bf16[8,512,384]{2,1,0:T(8,128)(2,1)}), bf16[8,512,384]{2,1,0:T(8,128)(2,1)S(1)}, u32[]{:S(2)}, u32[]{:S(2)}) %all-to-all-start.2) | async-done | bytes 3145760 | tf_op jit(solution)/shard_map/all_to_all | solution.py:989
  121.4 1.7 copy-done.6
  123.0 3.7 all-to-all-start
  126.7 38.5 %attend.3 = (bf16[4096,128]{1,0:T(8,128)(2,1)}, f32[16,8,512]{2,1,0:T(8,128)}) custom-call(s32[8]{0:T(128)} %get-tuple-element.87.cut_ref, bf16[4096,384]{1,0:T(8,128)(2,1)} %bitcast.92), custom_call_target="tpu_custom_call" | custom-call | flops 34359738368 | bytes 4194304 | tf_op jit(solution)/shard_map/attend/pallas_call | solution.py:464
  165.2 20.8 %all-to-all-done = bf16[8,512,384]{2,1,0:T(8,128)(2,1)S(1)} async-done(((bf16[8,512,384]{2,1,0:T(8,128)(2,1)}), bf16[8,512,384]{2,1,0:T(8,128)(2,1)S(1)}, u32[]{:S(2)}, u32[]{:S(2)}) %all-to-all-start) | async-done | bytes 3145760 | tf_op jit(solution)/shard_map/all_to_all | solution.py:989
  186.1 1.7 copy-done.5
  187.7 3.6 all-to-all-start.3
  191.3 35.5 %attend.2 = (bf16[4096,128]{1,0:T(8,128)(2,1)}, f32[16,8,512]{2,1,0:T(8,128)}) custom-call(s32[8]{0:T(128)} %get-tuple-element.88.cut_ref, bf16[4096,384]{1,0:T(8,128)(2,1)} %bitcast.90), custom_call_target="tpu_custom_call" | custom-call | flops 34359738368 | bytes 4194304 | tf_op jit(solution)/shard_map/attend/pallas_call | solution.py:464
  226.8 4.7 all-to-all-start.1
  231.5 2.6 copy.47
  235.4 5.4 out_norm.3
  240.8 16.7 %all-to-all-done.1 = bf16[8,512,128]{2,1,0:T(8,128)(2,1)} async-done(((bf16[8,512,128]{2,1,0:T(8,128)(2,1)}), bf16[8,512,128]{2,1,0:T(8,128)(2,1)}, u32[]{:S(2)}, u32[]{:S(2)}) %all-to-all-start.1) | async-done | bytes 1048608 | tf_op jit(solution)/shard_map/all_to_all | solution.py:989
  257.6 5.4 out_norm.2
  263.0 78.1 %feed_forward.1 = (bf16[2,512,1024]{2,1,0:T(8,128)(2,1)}, f32[2,512,1024]{2,1,0:T(8,128)}, bf16[4,2,4,64,2048]{4,3,2,1,0:T(8,128)(2,1)}, bf16[4,2,4,64,2048]{4,3,2,1,0:T(8,128)(2,1)}, f32[2,1,2048]{2,1,0:T(1,128)}) custom-call(bf16[512,1024]{1,0:T(8,128)(2,1)} %get-tuple-element.45.refs_0_, bf16[512,1024]{1,0:T(8,128)(2,1)} %get-tuple-element.48.refs_1_, ...), custom_call_target="tpu_custom_call" | custom-call | flops 51539607552 | bytes 33554432 | tf_op jit(solution)/shard_map/feed_forward/pallas_call | solution.py:729
  341.7 6.9 out_norm_back.3
  348.6 3.8 all-to-all-start.6
  352.4 7.0 out_norm_back.2
  359.4 7.5 all-to-all-done.6
  366.8 3.6 all-to-all-start.4
  370.4 49.8 %attend_back.3 = bf16[4096,384]{1,0:T(8,128)(2,1)} custom-call(s32[8]{0:T(128)} %get-tuple-element.87.cut_ref, bf16[4096,384]{1,0:T(8,128)(2,1)} %bitcast.93, bf16[4096,128]{1,0:T(8,128)(2,1)} %get-tuple-element.47.o_ref, bf16[4096,128]{1,0:T(8,128)(2,1)} %bitcast.104, f32[16,8,512]{2,1,0:T(8,128)} %get-tuple-element.58.lse_ref), custom_call_target="tpu_custom_call" | custom-call | flops 42949672960 | bytes 8388608 | tf_op jit(solution)/shard_map/attend_back/pallas_call | solution.py:562
  420.2 1.0 copy-done.9
  421.2 4.1 all-to-all-start.7
  425.3 45.9 %attend_back.2 = bf16[4096,384]{1,0:T(8,128)(2,1)} custom-call(s32[8]{0:T(128)} %get-tuple-element.88.cut_ref, bf16[4096,384]{1,0:T(8,128)(2,1)} %bitcast.91, bf16[4096,128]{1,0:T(8,128)(2,1)} %get-tuple-element.44.o_ref, bf16[4096,128]{1,0:T(8,128)(2,1)} %bitcast.105, f32[16,8,512]{2,1,0:T(8,128)} %get-tuple-element.56.lse_ref), custom_call_target="tpu_custom_call" | custom-call | flops 42949672960 | bytes 8388608 | tf_op jit(solution)/shard_map/attend_back/pallas_call | solution.py:562
  471.2 1.8 copy-done.7
  473.0 4.5 all-to-all-start.5
  477.5 5.5 out_grad.1
  483.4 2.6 copy.46
  485.9 34.1 %all-to-all-done.5 = bf16[8,512,384]{2,1,0:T(8,128)(2,1)} async-done(((bf16[8,512,384]{2,1,0:T(8,128)(2,1)}), bf16[8,512,384]{2,1,0:T(8,128)(2,1)}, u32[]{:S(2)}, u32[]{:S(2)}) %all-to-all-start.5) | async-done | bytes 3145760 | tf_op jit(solution)/shard_map/all_to_all | solution.py:989
  520.1 34.7 %input_back.1 = (f32[2,512,1024]{2,1,0:T(8,128)}, bf16[4,2,4,3,64,512]{5,4,3,2,1,0:T(8,128)(2,1)}, f32[2,3,1,512]{3,2,1,0:T(1,128)}, f32[8,1024]{1,0:T(8,128)}) custom-call(bf16[4,2,512,384]{3,2,1,0:T(8,128)(2,1)} %bitcast.25.refs_0_, bf16[4,2,512,384]{3,2,1,0:T(8,128)(2,1)} %bitcast.94, f32[512,1024]{1,0:T(8,128)} %get-tuple-element.59.refs_2_, ...), custom_call_target="tpu_custom_call" | custom-call | flops 12884901888 | bytes 33554432 | tf_op jit(solution)/shard_map/input_back/pallas_call | solution.py:928
  555.5 0.7 reduce-scatter.21.cloned.1.call-update
  557.1 59.7 %reduce-scatter.9.cloned.1.call-done = bf16[1,4,3,64,512]{4,3,2,1,0:T(8,128)(2,1)} async-done(((bf16[8,4,3,64,512]{4,3,2,1,0:T(8,128)(2,1)}), bf16[1,4,3,64,512]{4,3,2,1,0:T(8,128)(2,1)}) %reduce-scatter.9.cloned.1.call-update) | async-done | bytes 786448 | tf_op jit(solution)/shard_map/reduce_scatter | solution.py:993
  616.9 74.9 %reduce-scatter.17.cloned.1.call-done = bf16[1,4,64,2048]{3,2,1,0:T(8,128)(2,1)} async-done(((bf16[8,4,64,2048]{3,2,1,0:T(8,128)(2,1)}), bf16[1,4,64,2048]{3,2,1,0:T(8,128)(2,1)}) %reduce-scatter.17.cloned.1.call-update) | async-done | bytes 1048592 | tf_op jit(solution)/shard_map/reduce_scatter | solution.py:993
  692.3 0.8 fusion.8
  693.2 73.6 %reduce-scatter.21.cloned.1.call-done = bf16[1,4,64,2048]{3,2,1,0:T(8,128)(2,1)} async-done(((bf16[8,4,64,2048]{3,2,1,0:T(8,128)(2,1)}), bf16[1,4,64,2048]{3,2,1,0:T(8,128)(2,1)}) %reduce-scatter.21.cloned.1.call-update) | async-done | bytes 1048592 | tf_op jit(solution)/shard_map/reduce_scatter | solution.py:993
  766.9 39.8 %psum.7 = f32[12288]{0:T(1024)S(1)} all-reduce(f32[12288]{0:T(1024)S(1)} %constant_dynamic-update-slice_fusion), channel_id=1, replica_groups=mesh['dp'=4,'row'=4,'col'=2] {'dp','row','col'}, use_global_device_ids=true, to_apply=%region_3.0 | all-reduce | flops 12288 | bytes 98304 | tf_op jit(solution)/shard_map/psum | solution.py:1081
  808.5 1.5 convert_bitcast_fusion.2
  810.0 2.8 reduce-scatter.11.cloned.1.call-done
  812.8 1.7 convert_bitcast_fusion.1
  814.5 27.4 %reduce-scatter.19.cloned.1.call-done = bf16[1,1,64,2048]{3,2,1,0:T(8,128)(2,1)} async-done(((bf16[1,4,64,2048]{3,2,1,0:T(8,128)(2,1)}), bf16[1,1,64,2048]{3,2,1,0:T(8,128)(2,1)}) %reduce-scatter.19.cloned.1.call-update) | async-done | bytes 262160 | tf_op jit(solution)/shard_map/reduce_scatter | solution.py:994
  841.9 1.8 bitcast_convert_fusion
  843.7 26.2 %reduce-scatter.23.cloned.1.call-done = bf16[1,1,64,2048]{3,2,1,0:T(8,128)(2,1)} async-done(((bf16[1,4,64,2048]{3,2,1,0:T(8,128)(2,1)}), bf16[1,1,64,2048]{3,2,1,0:T(8,128)(2,1)}) %reduce-scatter.23.cloned.1.call-update) | async-done | bytes 262160 | tf_op jit(solution)/shard_map/reduce_scatter | solution.py:994
  869.9 1.8 convert_bitcast_fusion
  (106 shorter events, 10.6 us)
Async XLA Ops:
  7.2 2.9 copy-start.19
  7.2 2.9 copy-start.17
  7.2 8.9 %copy-start = (bf16[2,512,1024]{2,1,0:T(8,128)(2,1)S(1)}, bf16[2,512,1024]{2,1,0:T(8,128)(2,1)}, u32[]{:S(2)}) copy-start(bf16[2,512,1024]{2,1,0:T(8,128)(2,1)} %refs_5_.1) | copy-start | bytes 6291460
  7.2 50.8 %all-gather.10.cloned.1.call-start = ((), (), s32[]{:S(2)}) async-start(), calls=%async_computation.24 | async-start | bytes 7077888 | tf_op jit(solution)/shard_map/all_gather | solution.py:985
  7.9 227.5 %all-gather.12.cloned.1.call-start = ((), (), s32[]{:S(2)}) async-start(), calls=%async_computation.25 | async-start | bytes 2359296 | tf_op jit(solution)/shard_map/all_gather | solution.py:985
  8.7 8.5 copy-start.20
  8.7 8.5 copy-start.21
  8.7 254.2 %all-gather.14.cloned.1.call-start = ((), (), s32[]{:S(2)}) async-start(), calls=%async_computation.26 | async-start | bytes 9437184 | tf_op jit(solution)/shard_map/all_gather | solution.py:985
  9.5 253.5 %all-gather.16.cloned.1.call-start = ((), (), s32[]{:S(2)}) async-start(), calls=%async_computation.27 | async-start | bytes 9437184 | tf_op jit(solution)/shard_map/all_gather | solution.py:985
  15.4 216.1 %copy-start.11 = (f32[2,3072]{1,0:T(2,128)}, f32[2,3072]{1,0:T(2,128)S(1)}, u32[]{:S(2)}) copy-start(f32[2,3072]{1,0:T(2,128)S(1)} %reshape.186) | copy-start | bytes 73732
  68.8 3.8 copy-start.22
  68.8 52.6 %all-to-all-start.2 = ((bf16[8,512,384]{2,1,0:T(8,128)(2,1)}), bf16[8,512,384]{2,1,0:T(8,128)(2,1)S(1)}, u32[]{:S(2)}, u32[]{:S(2)}) async-start(bf16[8,512,384]{2,1,0:T(8,128)(2,1)} %bitcast.98), calls=%async_computation.2 | async-start | bytes 6291456 | tf_op jit(solution)/shard_map/all_to_all | solution.py:989
  121.4 1.7 copy-start.6
  123.0 63.0 %all-to-all-start = ((bf16[8,512,384]{2,1,0:T(8,128)(2,1)}), bf16[8,512,384]{2,1,0:T(8,128)(2,1)S(1)}, u32[]{:S(2)}, u32[]{:S(2)}) async-start(bf16[8,512,384]{2,1,0:T(8,128)(2,1)} %bitcast.96), calls=%async_computation | async-start | bytes 6291456 | tf_op jit(solution)/shard_map/all_to_all | solution.py:989
  186.1 1.7 copy-start.5
  187.7 39.0 %all-to-all-start.3 = ((bf16[8,512,128]{2,1,0:T(8,128)(2,1)}), bf16[8,512,128]{2,1,0:T(8,128)(2,1)S(1)}, u32[]{:S(2)}, u32[]{:S(2)}) async-start(bf16[8,512,128]{2,1,0:T(8,128)(2,1)} %bitcast.103), calls=%async_computation.3 | async-start | bytes 2097152 | tf_op jit(solution)/shard_map/all_to_all | solution.py:989
  226.7 4.8 copy-start.1
  226.7 7.4 copy-start.4
  226.8 8.0 copy-start.10
  226.8 8.0 copy-start.14
  226.8 8.0 copy-start.18
  226.8 30.8 %all-to-all-start.1 = ((bf16[8,512,128]{2,1,0:T(8,128)(2,1)}), bf16[8,512,128]{2,1,0:T(8,128)(2,1)}, u32[]{:S(2)}, u32[]{:S(2)}) async-start(bf16[8,512,128]{2,1,0:T(8,128)(2,1)} %bitcast.102), calls=%async_computation.1 | async-start | bytes 2097152 | tf_op jit(solution)/shard_map/all_to_all | solution.py:989
  231.5 2.6 slice-start
  348.6 18.2 %all-to-all-start.6 = ((bf16[8,512,128]{2,1,0:T(8,128)(2,1)}), bf16[8,512,128]{2,1,0:T(8,128)(2,1)S(1)}, u32[]{:S(2)}, u32[]{:S(2)}) async-start(bf16[8,512,128]{2,1,0:T(8,128)(2,1)} %bitcast.107), calls=%async_computation.6 | async-start | bytes 2097152 | tf_op jit(solution)/shard_map/all_to_all | solution.py:989
  366.8 3.6 copy-start.8
  366.8 53.4 %all-to-all-start.4 = ((bf16[8,512,128]{2,1,0:T(8,128)(2,1)}), bf16[8,512,128]{2,1,0:T(8,128)(2,1)S(1)}, u32[]{:S(2)}, u32[]{:S(2)}) async-start(bf16[8,512,128]{2,1,0:T(8,128)(2,1)} %bitcast.106), calls=%async_computation.4 | async-start | bytes 2097152 | tf_op jit(solution)/shard_map/all_to_all | solution.py:989
  420.2 1.0 copy-start.9
  421.2 50.0 %all-to-all-start.7 = ((bf16[8,512,384]{2,1,0:T(8,128)(2,1)}), bf16[8,512,384]{2,1,0:T(8,128)(2,1)S(1)}, u32[]{:S(2)}, u32[]{:S(2)}) async-start(bf16[8,512,384]{2,1,0:T(8,128)(2,1)} %bitcast.97), calls=%async_computation.7 | async-start | bytes 6291456 | tf_op jit(solution)/shard_map/all_to_all | solution.py:989
  471.2 1.8 copy-start.7
  473.0 47.1 %all-to-all-start.5 = ((bf16[8,512,384]{2,1,0:T(8,128)(2,1)}), bf16[8,512,384]{2,1,0:T(8,128)(2,1)}, u32[]{:S(2)}, u32[]{:S(2)}) async-start(bf16[8,512,384]{2,1,0:T(8,128)(2,1)} %bitcast.95), calls=%async_computation.5 | async-start | bytes 6291456 | tf_op jit(solution)/shard_map/all_to_all | solution.py:989
  477.4 78.9 %reduce-scatter.13.cloned.1.call-start = ((), (), s32[]{:S(2)}) async-start(), calls=%async_computation.18 | async-start | bytes 2359296 | tf_op jit(solution)/shard_map/reduce_scatter | solution.py:993
  477.5 5.9 copy-start.3
  483.1 133.7 %reduce-scatter.9.cloned.1.call-start = ((), (), s32[]{:S(2)}) async-start(), calls=%async_computation.16 | async-start | bytes 7077888 | tf_op jit(solution)/shard_map/reduce_scatter | solution.py:993
  554.7 137.0 %reduce-scatter.17.cloned.1.call-start = ((), (), s32[]{:S(2)}) async-start(), calls=%async_computation.20 | async-start | bytes 9437184 | tf_op jit(solution)/shard_map/reduce_scatter | solution.py:993
  555.5 211.3 %reduce-scatter.21.cloned.1.call-start = ((), (), s32[]{:S(2)}) async-start(), calls=%async_computation.22 | async-start | bytes 9437184 | tf_op jit(solution)/shard_map/reduce_scatter | solution.py:993
  556.2 135.6 %copy-start.2 = (bf16[2,512,1024]{2,1,0:T(8,128)(2,1)S(1)}, bf16[2,512,1024]{2,1,0:T(8,128)(2,1)}, u32[]{:S(2)}) copy-start(bf16[2,512,1024]{2,1,0:T(8,128)(2,1)} %cot_ref.3) | copy-start | bytes 6291460
  556.3 136.0 %copy-start.12 = (f32[8,1024]{1,0:T(8,128)S(1)}, f32[8,1024]{1,0:T(8,128)}, u32[]{:S(2)}) copy-start(f32[8,1024]{1,0:T(8,128)} %get-tuple-element.65) | copy-start | bytes 98308
  556.3 136.0 %copy-start.13 = (f32[8,1024]{1,0:T(8,128)S(1)}, f32[8,1024]{1,0:T(8,128)}, u32[]{:S(2)}) copy-start(f32[8,1024]{1,0:T(8,128)} %get-tuple-element.64) | copy-start | bytes 98308
  556.3 136.0 %copy-start.16 = (f32[2,3,1,512]{3,2,1,0:T(1,128)S(1)}, f32[2,3,1,512]{3,2,1,0:T(1,128)}, u32[]{:S(2)}) copy-start(f32[2,3,1,512]{3,2,1,0:T(1,128)} %get-tuple-element.63) | copy-start | bytes 36868
  556.3 210.6 %copy-start.15 = (f32[2,1,2048]{2,1,0:T(1,128)S(1)}, f32[2,1,2048]{2,1,0:T(1,128)}, u32[]{:S(2)}) copy-start(f32[2,1,2048]{2,1,0:T(1,128)} %get-tuple-element.66) | copy-start | bytes 49156
  556.3 252.2 %reduce-scatter.15.cloned.1.call-start = ((), (), s32[]{:S(2)}) async-start(), calls=%async_computation.19 | async-start | bytes 327680 | tf_op jit(solution)/shard_map/reduce_scatter | solution.py:994
  557.0 255.8 %reduce-scatter.11.cloned.1.call-start = ((), (), s32[]{:S(2)}) async-start(), calls=%async_computation.17 | async-start | bytes 983040 | tf_op jit(solution)/shard_map/reduce_scatter | solution.py:994
  616.8 225.1 %reduce-scatter.19.cloned.1.call-start = ((), (), s32[]{:S(2)}) async-start(), calls=%async_computation.21 | async-start | bytes 1310720 | tf_op jit(solution)/shard_map/reduce_scatter | solution.py:994
  691.8 178.1 %reduce-scatter.23.cloned.1.call-start = ((), (), s32[]{:S(2)}) async-start(), calls=%async_computation.23 | async-start | bytes 1310720 | tf_op jit(solution)/shard_map/reduce_scatter | solution.py:994
Sparse Core Ops, SparseCore 0:
  9.9 48.1 all-gather.9
  59.9 37.9 all-gather.11
  99.8 88.0 all-gather.13
  189.7 70.4 all-gather.15
  483.2 48.3 reduce-scatter.12
  554.9 61.8 reduce-scatter.8
  620.3 71.4 reduce-scatter.16
  695.2 71.4 reduce-scatter.20
  769.0 19.9 reduce-scatter.14
  791.2 21.5 reduce-scatter.10
  815.1 26.7 reduce-scatter.18
  844.1 25.7 reduce-scatter.22

commit v2 on v1

--- a/solution.py
+++ b/solution.py
@@ -21,7 +21,6 @@
 BK = 512
 BK_BACK = 512
 HIDDEN_TILE = 512
-VMEM_BYTES = 60 * 2**20
 NT = (((1,), (1,)), ((), ()))
 TN = (((0,), (0,)), ((), ()))
 MESH_AXES = ("row", "col")
@@ -336,8 +335,8 @@
     return pl.CostEstimate(flops=int(flops), bytes_accessed=int(moved), transcendentals=int(exps))
 
 
-def params():
-    return pltpu.CompilerParams(vmem_limit_bytes=VMEM_BYTES)
+def params(mebibytes):
+    return pltpu.CompilerParams(vmem_limit_bytes=mebibytes * 2**20)
 
 
 def fixed(shape):
@@ -388,7 +387,7 @@
         ],
         out_specs=[pl.BlockSpec((2, 1, span, 3 * PAIR), lambda i, c: (i, c, 0, 0))] * groups,
         out_shape=[jax.ShapeDtypeStruct((rows, cols, span, 3 * PAIR), jnp.bfloat16)] * groups,
-        compiler_params=params(),
+        compiler_params=params(24),
         cost_estimate=cost(6 * tokens * model * model, 8 * tokens * model + 6 * model * model),
         name="qkv",
     )(normed, weight, bias)
@@ -480,7 +479,7 @@
             pltpu.VMEM((2 * BQ, PAIR), jnp.float32),
             pltpu.VMEM((2 * BQ, 2 * PAIR), jnp.float32),
         ],
-        compiler_params=params(),
+        compiler_params=params(24),
         cost_estimate=cost(8 * 2 * pairs * 256, 2 * tokens * 4 * PAIR, pairs),
         name="attend",
     )(cut, qkv)
@@ -576,7 +575,7 @@
             pltpu.VMEM((tokens, PAIR), jnp.float32),
             pltpu.VMEM((PAIR, 2 * BQ), jnp.float32),
         ],
-        compiler_params=params(),
+        compiler_params=params(32),
         cost_estimate=cost(10 * 2 * pairs * 256, 2 * tokens * 8 * PAIR, pairs),
         name="attend_back",
     )(cut, qkv, att, grad_att, log_totals)
@@ -638,134 +637,141 @@
             jax.ShapeDtypeStruct((span, model), jnp.bfloat16),
             jax.ShapeDtypeStruct((model, span), jnp.bfloat16),
         ],
-        compiler_params=params(),
+        compiler_params=params(24),
         cost_estimate=cost(2 * span * model * model, 2 * model * model + 12 * span * model),
         name="out_norm",
     )(tokens, att, weight, vectors)
 
 
-def hidden_kernel(rows, dps, groups, *refs):
+def hidden_kernel(rows, dps, groups, first, *refs):
     normed_refs = refs[:groups]
     turned_refs = refs[groups : 2 * groups]
-    middle_refs = refs[2 * groups : 3 * groups]
-    (cot_ref, cot_turned_ref, fc_ref, fc_bias_ref, proj_ref, proj_bias_ref) = refs[
-        3 * groups : 3 * groups + 6
-    ]
-    (out_ref, back_ref, grad_fc_ref, grad_proj_ref, bias_ref) = refs[
-        3 * groups + 6 : 3 * groups + 11
-    ]
-    normed_all, turned_all, out_acc, back_acc = refs[3 * groups + 11 :]
+    cot_ref, cot_turned_ref, w_ref, fc_bias_ref = refs[2 * groups : 2 * groups + 4]
+    if first:
+        middle_refs = refs[2 * groups + 4 : 3 * groups + 4]
+        out_acc, back_acc, grad_ref, bias_ref, sems = refs[3 * groups + 4 :]
+    else:
+        (prev_out_ref, prev_back_ref, proj_bias_ref) = refs[2 * groups + 4 : 2 * groups + 7]
+        out_ref, back_acc, grad_ref, bias_ref, out_acc, sems = refs[2 * groups + 7 :]
     step = pl.program_id(0) * pl.num_programs(1) + pl.program_id(1)
     last = pl.num_programs(0) * pl.num_programs(1) - 1
-    span = normed_refs[0].shape[0]
-    model = normed_all.shape[1]
-    depth = model // rows
-    tile = fc_ref.shape[3]
+    span, model = normed_refs[0].shape
+    tile = w_ref.shape[4]
+    if first:
+        copies = [
+            pltpu.make_async_copy(
+                middle_refs[g], out_acc.at[pl.ds(g * span, span)], sems.at[g]
+            )
+            for g in range(groups)
+        ]
+    else:
+        copies = [
+            pltpu.make_async_copy(prev_out_ref, out_acc, sems.at[0]),
+            pltpu.make_async_copy(prev_back_ref, back_acc, sems.at[1]),
+        ]
 
     @pl.when(step == 0)
     def _():
-        for g in range(groups):
-            normed_all[g * span : (g + 1) * span, :] = normed_refs[g][...]
-            turned_all[:, g * span : (g + 1) * span] = turned_refs[g][...]
-
-    fc_weight = fc_ref[:, 0].reshape(model, tile)
-    hidden = dot(normed_all[...], fc_weight) + fc_bias_ref[0]
+        for copy in copies:
+            copy.start()
+        if first:
+            back_acc[...] = jnp.zeros_like(back_acc)
+
+    fc_weight = w_ref[:, 0, 0].reshape(model, tile)
+    proj_turned = w_ref[:, 0, 1].reshape(model, tile)
     root = 0.7978845608028654
-    square = hidden * hidden
-    inner = jnp.tanh(hidden * (root + (root * 0.044715) * square))
-    plus = 0.5 + 0.5 * inner
-    active = (hidden * plus).astype(jnp.bfloat16)
-    slope = plus + hidden * (0.5 - 0.5 * inner * inner) * (root + (3 * root * 0.044715) * square)
-    cot = cot_ref[...]
-    grad_active = None
-    for r in range(rows):
-        part = dot_nt(cot[:, r * depth : (r + 1) * depth], proj_ref[r, 0])
-        grad_active = part if grad_active is None else grad_active + part
-    grad_hidden = grad_active * slope
-    grad_low = grad_hidden.astype(jnp.bfloat16)
-    bias_ref[0] = jnp.sum(grad_low.astype(jnp.float32), axis=0, keepdims=True)
-    grad_fc = dot(turned_all[...], grad_low).astype(jnp.bfloat16)
-    grad_proj = dot(cot_turned_ref[...], active).astype(jnp.bfloat16)
+    actives, lows = [], []
+    for g in range(groups):
+        hidden = dot(normed_refs[g][...], fc_weight) + fc_bias_ref[0]
+        square = hidden * hidden
+        inner = jnp.tanh(hidden * (root + (root * 0.044715) * square))
+        plus = 0.5 + 0.5 * inner
+        actives.append((hidden * plus).astype(jnp.bfloat16))
+        bend = 0.5 - 0.5 * inner * inner
+        slope = plus + hidden * bend * (root + (3 * root * 0.044715) * square)
+        grad_active = dot(cot_ref[g * span : (g + 1) * span], proj_turned)
+        lows.append((grad_active * slope).astype(jnp.bfloat16))
+    bias_ref[0] = functools.reduce(
+        jnp.add, [jnp.sum(low.astype(jnp.float32), axis=0, keepdims=True) for low in lows]
+    )
+    low_all = jnp.concatenate(lows, axis=0)
+    active_all = jnp.concatenate(actives, axis=0)
+    turned_all = jnp.concatenate([ref[...] for ref in turned_refs], axis=1)
     cut = model // (rows * dps)
-    for r in range(rows):
-        for d in range(dps):
-            at = (d * rows + r) * cut
-            grad_fc_ref[r, 0, d] = grad_fc[at : at + cut]
-            grad_proj_ref[r, 0, d] = grad_proj[at : at + cut]
-    for r in range(rows):
-        lanes = slice(r * depth, (r + 1) * depth)
-        forward = dot(active, proj_ref[r, 0])
-        backward = dot_nt(grad_low, fc_ref[r, 0])
-
-        @pl.when(step == 0)
+    for which, weight_grad in enumerate(
+        (dot(turned_all, low_all), dot(cot_turned_ref[...], active_all))
+    ):
+        weight_grad = weight_grad.astype(jnp.bfloat16)
+        for r in range(rows):
+            for d in range(dps):
+                at = (d * rows + r) * cut
+                grad_ref[r, 0, d, which] = weight_grad[at : at + cut]
+
+    @pl.when(step == 0)
+    def _():
+        for copy in copies:
+            copy.wait()
+
+    out_acc[...] += dot_nt(active_all, proj_turned)
+    back_acc[...] += dot_nt(low_all, fc_weight)
+    if not first:
+
+        @pl.when(step == last)
         def _():
-            out_acc[:, lanes] = forward
-            back_acc[:, lanes] = backward
-
-        @pl.when(step > 0)
-        def _():
-            out_acc[:, lanes] += forward
-            back_acc[:, lanes] += backward
-
-    @pl.when(step == last)
-    def _():
-        for g in range(groups):
-            at = slice(g * span, (g + 1) * span)
-            out_ref[g] = (middle_refs[g][...] + out_acc[at] + proj_bias_ref[...]).astype(
-                out_ref.dtype
-            )
-            back_ref[g] = back_acc[at]
-
-
-def feed_forward(normed, turned, middle, cot, cot_turned, fc, fc_bias, proj, proj_bias, dps):
+            for g in range(groups):
+                at = slice(g * span, (g + 1) * span)
+                out_ref[g] = (out_acc[at] + proj_bias_ref[...]).astype(out_ref.dtype)
+
+
+def feed_forward(first, normed, turned, cot, cot_turned, weight, fc_bias, rest, dps):
     groups = len(normed)
     span, model = normed[0].shape
     tokens = groups * span
-    rows, cols, depth, local = fc.shape
+    rows, cols, _, depth, local = weight.shape
     tile = min(HIDDEN_TILE, local)
     cut = model // (rows * dps)
-    grad_spec = pl.BlockSpec((rows, 1, dps, cut, tile), lambda c, i: (0, c, 0, 0, i))
-    grad_shape = jax.ShapeDtypeStruct((rows, cols, dps, cut, local), jnp.bfloat16)
+    acc_shape = jax.ShapeDtypeStruct((tokens, model), jnp.float32)
+    anywhere = pl.BlockSpec(memory_space=pl.ANY)
+    if first:
+        rest_specs = [anywhere] * groups
+        out_spec, out_shape = fixed((tokens, model)), acc_shape
+        scratch = [pltpu.SemaphoreType.DMA((groups,))]
+    else:
+        rest_specs = [anywhere, anywhere, fixed((1, model))]
+        out_spec = fixed((groups, span, model))
+        out_shape = jax.ShapeDtypeStruct((groups, span, model), jnp.bfloat16)
+        scratch = [pltpu.VMEM((tokens, model), jnp.float32), pltpu.SemaphoreType.DMA((2,))]
     return pl.pallas_call(
-        functools.partial(hidden_kernel, rows, dps, groups),
+        functools.partial(hidden_kernel, rows, dps, groups, first),
         grid=(cols, local // tile),
         in_specs=[fixed((span, model))] * groups
         + [fixed((model, span))] * groups
-        + [fixed((span, model))] * groups
         + [
             fixed((tokens, model)),
             fixed((model, tokens)),
-            pl.BlockSpec((rows, 1, depth, tile), lambda c, i: (0, c, 0, i)),
+            pl.BlockSpec((rows, 1, 2, depth, tile), lambda c, i: (0, c, 0, 0, i)),
             pl.BlockSpec((1, 1, tile), lambda c, i: (c, 0, i)),
-            pl.BlockSpec((rows, 1, tile, depth), lambda c, i: (0, c, i, 0)),
-            fixed((1, model)),
-        ],
+        ]
+        + rest_specs,
         out_specs=[
-            fixed((groups, span, model)),
-            fixed((groups, span, model)),
-            grad_spec,
-            grad_spec,
+            out_spec,
+            fixed((tokens, model)),
+            pl.BlockSpec((rows, 1, dps, 2, cut, tile), lambda c, i: (0, c, 0, 0, 0, i)),
             pl.BlockSpec((1, 1, tile), lambda c, i: (c, 0, i)),
         ],
         out_shape=[
-            jax.ShapeDtypeStruct((groups, span, model), jnp.bfloat16),
-            jax.ShapeDtypeStruct((groups, span, model), jnp.float32),
-            grad_shape,
-            grad_shape,
+            out_shape,
+            acc_shape,
+            jax.ShapeDtypeStruct((rows, cols, dps, 2, cut, local), jnp.bfloat16),
             jax.ShapeDtypeStruct((cols, 1, local), jnp.float32),
         ],
-        scratch_shapes=[
-            pltpu.VMEM((tokens, model), jnp.bfloat16),
-            pltpu.VMEM((model, tokens), jnp.bfloat16),
-            pltpu.VMEM((tokens, model), jnp.float32),
-            pltpu.VMEM((tokens, model), jnp.float32),
-        ],
-        compiler_params=params(),
+        scratch_shapes=scratch,
+        compiler_params=params(60),
         cost_estimate=cost(
             12 * tokens * model * cols * local, 8 * model * cols * local, tokens * cols * local
         ),
-        name="feed_forward",
-    )(*normed, *turned, *middle, cot, cot_turned, fc, fc_bias, proj, proj_bias)
+        name="feed_forward_first" if first else "feed_forward_second",
+    )(*normed, *turned, cot, cot_turned, weight, fc_bias, *rest)
 
 
 def middle_back_kernel(
@@ -821,7 +827,7 @@
             jax.ShapeDtypeStruct((rows, cols, span, PAIR), jnp.bfloat16),
             jax.ShapeDtypeStruct((8, model), jnp.float32),
         ],
-        compiler_params=params(),
+        compiler_params=params(24),
         cost_estimate=cost(2 * span * model * model, 2 * model * model + 18 * span * model),
         name="out_norm_back",
     )(grad, middle, cot, weight, vectors)
@@ -854,105 +860,111 @@
         + [pl.BlockSpec((rows, 1, span, PAIR), lambda c: (0, c, 0, 0))] * groups,
         out_specs=pl.BlockSpec((rows, 1, dps, cut, rows * PAIR), lambda c: (0, c, 0, 0, 0)),
         out_shape=jax.ShapeDtypeStruct((rows, cols, dps, cut, rows * PAIR), jnp.bfloat16),
-        compiler_params=params(),
+        compiler_params=params(24),
         cost_estimate=cost(2 * groups * span * model * model, 2 * model * model),
         name="out_grad",
     )(*turned, *att)
 
 
-def input_kernel(rows, dps, groups, *refs):
-    grad_refs = refs[:groups]
-    dx_refs = refs[groups : 2 * groups]
-    (turned_ref, tok_ref, w_ref, gain_ref) = refs[2 * groups : 2 * groups + 4]
-    (out_ref, grad_ref, bias_ref, sum_ref) = refs[2 * groups + 4 : 2 * groups + 8]
-    acc = refs[2 * groups + 8]
-    step = pl.program_id(0) * pl.num_programs(1) + pl.program_id(1)
-    last = pl.num_programs(0) * pl.num_programs(1) - 1
-    span = dx_refs[0].shape[0]
-    depth = w_ref.shape[3]
+def qkv_grad_kernel(rows, dps, turned_ref, dqkv_ref, *refs):
+    grad_ref, bias_ref = refs[-2:]
     cut = grad_ref.shape[4]
-    grads = []
     for part in range(3):
         lanes = slice(part * PAIR, (part + 1) * PAIR)
-        grads.append(
-            jnp.concatenate(
-                [
-                    jnp.concatenate([ref[half, 0, :, lanes] for half in range(2)], axis=1)
-                    for ref in grad_refs
-                ],
-                axis=0,
-            )
-        )
-    for part in range(3):
-        weight_grad = dot(turned_ref[...], grads[part]).astype(jnp.bfloat16)
+        grads = jnp.concatenate([dqkv_ref[half, 0, :, lanes] for half in range(2)], axis=1)
+        weight_grad = dot(turned_ref[...], grads)
         for r in range(rows):
             for d in range(dps):
                 at = (d * rows + r) * cut
-                grad_ref[r, 0, d, part] = weight_grad[at : at + cut]
-        bias_ref[0, part] = jnp.sum(grads[part].astype(jnp.float32), axis=0, keepdims=True)
-    for r in range(rows):
-        lanes = slice(r * depth, (r + 1) * depth)
-        piece = dot_nt(grads[0], w_ref[r, 0, 0])
-        for part in range(1, 3):
-            piece = piece + dot_nt(grads[part], w_ref[r, 0, part])
-
-        @pl.when(step == 0)
-        def _():
-            acc[:, lanes] = piece
-
-        @pl.when(step > 0)
-        def _():
-            acc[:, lanes] += piece
-
-    @pl.when(step == last)
+                piece = weight_grad[at : at + cut]
+                if len(refs) == 3:
+                    piece = piece + refs[0][r, 0, d, part]
+                grad_ref[r, 0, d, part] = piece.astype(grad_ref.dtype)
+        bias_ref[0, part] = jnp.sum(grads.astype(jnp.float32), axis=0, keepdims=True)
+
+
+def qkv_grad(dqkv, normed_turned, before, g, final, dps):
+    rows, cols, span, _ = dqkv.shape
+    model = normed_turned.shape[0]
+    width = rows * PAIR
+    cut = model // (rows * dps)
+    grad_spec = pl.BlockSpec((rows, 1, dps, 3, cut, 2 * PAIR), lambda i, c: (0, c, 0, 0, 0, i))
+    grad_type = jnp.bfloat16 if final else jnp.float32
+    return pl.pallas_call(
+        functools.partial(qkv_grad_kernel, rows, dps),
+        grid=(rows // 2, cols),
+        in_specs=[
+            pl.BlockSpec((model, span), lambda i, c: (0, g), pipeline_mode=pl.Buffered(1)),
+            pl.BlockSpec((2, 1, span, 3 * PAIR), lambda i, c: (i, c, 0, 0)),
+        ]
+        + [grad_spec] * len(before),
+        out_specs=[grad_spec, pl.BlockSpec((1, 3, 1, 2 * PAIR), lambda i, c: (c, 0, 0, i))],
+        out_shape=[
+            jax.ShapeDtypeStruct((rows, cols, dps, 3, cut, width), grad_type),
+            jax.ShapeDtypeStruct((cols, 3, 1, width), jnp.float32),
+        ],
+        compiler_params=params(40),
+        cost_estimate=cost(6 * span * model * model, 24 * model * model),
+        name="qkv_grad",
+    )(normed_turned, dqkv, *before)
+
+
+def input_kernel(rows, dqkv_ref, w_ref, dx_ref, tok_ref, gain_ref, *refs):
+    out_ref, sum_ref, acc = refs[-3:]
+    step = pl.program_id(0) * pl.num_programs(1) + pl.program_id(1)
+    model = acc.shape[1]
+    grads, weights = [], []
+    for part in range(3):
+        lanes = slice(part * PAIR, (part + 1) * PAIR)
+        grads += [dqkv_ref[half, 0, :, lanes] for half in range(2)]
+        weights.append(w_ref[:, 0, part].reshape(model, 2 * PAIR))
+    piece = dot_nt(jnp.concatenate(grads, axis=1), jnp.concatenate(weights, axis=1))
+
+    @pl.when(step == 0)
     def _():
-        gain_sum = None
-        for g in range(groups):
-            grad = acc[g * span : (g + 1) * span]
-            unit, inverse = centered(tok_ref[g].astype(jnp.float32))
-            out_ref[g] = dx_refs[g][...] + norm_back(grad, gain_ref[...], unit, inverse)
-            gains = jnp.sum(grad * unit, axis=0, keepdims=True)
-            shifts = jnp.sum(grad, axis=0, keepdims=True)
-            gain_sum = gains if gain_sum is None else gain_sum + gains
-            shift_sum = shifts if g == 0 else shift_sum + shifts
-        sum_ref[0:1] = gain_sum
-        sum_ref[1:2] = shift_sum
-
-
-def input_back(grads, dx, normed_turned, tokens, weight, gain, dps):
-    groups = len(grads)
+        acc[...] = piece
+
+    @pl.when(step > 0)
+    def _():
+        acc[...] += piece
+
+    @pl.when(step == pl.num_programs(0) * pl.num_programs(1) - 1)
+    def _():
+        grad = acc[...]
+        unit, inverse = centered(tok_ref[0].astype(jnp.float32))
+        out_ref[0] = dx_ref[...] + norm_back(grad, gain_ref[...], unit, inverse)
+        sum_ref[0:1] = jnp.sum(grad * unit, axis=0, keepdims=True)
+        sum_ref[1:2] = jnp.sum(grad, axis=0, keepdims=True)
+
+
+def input_back(dqkv, dx, tokens, weight, gain, before, g):
     rows, cols, _, depth, width = weight.shape
-    span, model = dx[0].shape
-    cut = model // (rows * dps)
-    count = groups * span
+    span, model = dx.shape
     return pl.pallas_call(
-        functools.partial(input_kernel, rows, dps, groups),
+        functools.partial(input_kernel, rows),
         grid=(rows // 2, cols),
-        in_specs=[pl.BlockSpec((2, 1, span, 3 * PAIR), lambda i, c: (i, c, 0, 0))] * groups
-        + [fixed((span, model))] * groups
-        + [
-            fixed((model, count)),
-            fixed((groups, span, model)),
+        in_specs=[
+            pl.BlockSpec((2, 1, span, 3 * PAIR), lambda i, c: (i, c, 0, 0)),
             pl.BlockSpec((rows, 1, 3, depth, 2 * PAIR), lambda i, c: (0, c, 0, 0, i)),
+            fixed((span, model)),
+            pl.BlockSpec((1, span, model), lambda i, c: (g, 0, 0), pipeline_mode=pl.Buffered(1)),
             fixed((1, model)),
-        ],
+        ]
+        + [pl.BlockSpec(memory_space=pl.ANY)] * len(before),
         out_specs=[
-            fixed((groups, span, model)),
-            pl.BlockSpec((rows, 1, dps, 3, cut, 2 * PAIR), lambda i, c: (0, c, 0, 0, 0, i)),
-            pl.BlockSpec((1, 3, 1, 2 * PAIR), lambda i, c: (c, 0, 0, i)),
+            pl.BlockSpec((1, span, model), lambda i, c: (g, 0, 0), pipeline_mode=pl.Buffered(1)),
             fixed((8, model)),
         ],
         out_shape=[
-            jax.ShapeDtypeStruct((groups, span, model), jnp.float32),
-            jax.ShapeDtypeStruct((rows, cols, dps, 3, cut, width), jnp.bfloat16),
-            jax.ShapeDtypeStruct((cols, 3, 1, width), jnp.float32),
+            jax.ShapeDtypeStruct(tokens.shape, jnp.float32),
             jax.ShapeDtypeStruct((8, model), jnp.float32),
         ],
-        scratch_shapes=[pltpu.VMEM((count, model), jnp.float32)],
-        compiler_params=params(),
-        cost_estimate=cost(12 * count * model * model, 12 * model * model + 20 * count * model),
+        scratch_shapes=[pltpu.VMEM((span, model), jnp.float32)],
+        compiler_params=params(32),
+        cost_estimate=cost(6 * span * model * model, 6 * model * model + 12 * span * model),
+        input_output_aliases={5: 0} if before else {},
         name="input_back",
-    )(*grads, *dx, normed_turned, tokens, weight, gain)
+    )(dqkv, weight, dx, tokens, gain, *before)
 
 
 def head_body(
@@ -988,17 +1000,33 @@
     def swap(blocks):
         return lax.all_to_all(blocks, MESH_AXES, 0, 0, tiled=True)
 
-    def collect(partial):
+    def collect_plane(partial):
         partial = partial.reshape((members,) + partial.shape[2:])
         partial = lax.psum_scatter(partial, MESH_AXES, scatter_dimension=0, tiled=True)
-        partial = lax.psum_scatter(partial, "dp", scatter_dimension=1, tiled=True)
-        return partial.reshape(partial.shape[2:]).astype(jnp.float32)
-
+        return partial.reshape(partial.shape[1:])
+
+    def collect_dp(partial):
+        pieces = lax.all_to_all(partial, "dp", 0, 0, tiled=True)
+        return jnp.sum(pieces.astype(jnp.float32), axis=0)
+
+    def total(values):
+        for axis in ("row", "col", "dp"):
+            size = lax.axis_size(axis)
+            step = 1
+            while step < size:
+                pairs = [(i, i ^ step) for i in range(size)]
+                values = values + lax.ppermute(values, axis, pairs)
+                step *= 2
+        return values
+
+    half = hidden_cols // 2
+    proj_turned = proj_weight.T
+    shards = [
+        jnp.stack([fc_weight[:, at : at + half], proj_turned[:, at : at + half]])
+        for at in (0, half)
+    ]
     w_qkv = spread(jnp.transpose(qkv_weight, (1, 0, 2)))
     biases = lax.all_gather(jnp.concatenate([qv_bias.reshape(-1), fc_bias]), "col", axis=0)
-    w_out = spread(out_weight)
-    w_fc = spread(fc_weight)
-    w_proj = spread(proj_weight)
     qv_full = biases[:, : 2 * head_cols].reshape(cols, 2, 1, head_cols)
     fc_full = biases[:, 2 * head_cols :].reshape(cols, 1, hidden_cols)
 
@@ -1016,6 +1044,12 @@
     for g in range(groups):
         received = swap(blocks[g].reshape(members, span, 3 * PAIR))
         qkv.append(received.reshape(members * span, 3 * PAIR))
+    qkv[-1], out_weight, shards[0], shards[1] = lax.optimization_barrier(
+        (qkv[-1], out_weight, shards[0], shards[1])
+    )
+    w_out = spread(out_weight)
+    w_first = spread(shards[0])
+    w_second = spread(shards[1])
     for g in range(groups):
         mixed, totals = attend(branch[g], qkv[g])
         att_own.append(mixed)
@@ -1026,76 +1060,85 @@
         middle.append(mid)
         normed_two.append(low)
         turned_two.append(turned)
-    block_out, grad_two, grad_fc, grad_proj, fc_bias_sum = feed_forward(
-        normed_two,
-        turned_two,
-        middle,
-        cot_flat,
-        cot_turned,
-        w_fc,
-        fc_full,
-        w_proj,
-        proj_bias[None],
+    shared = (normed_two, turned_two, cot_flat, cot_turned)
+    out_part, back_part, grad_first, fc_sum_first = feed_forward(
+        True, *shared, w_first, fc_full[:, :, :half], middle, dps
+    )
+    plane_first = collect_plane(grad_first)
+    block_out, grad_two, grad_second, fc_sum_second = feed_forward(
+        False,
+        *shared,
+        w_second,
+        fc_full[:, :, half:],
+        (out_part, back_part, proj_bias[None]),
         dps,
     )
-    d_fc = collect(grad_fc)
-    d_proj = collect(grad_proj).T
+    plane_second = collect_plane(grad_second)
+    grad_two = grad_two.reshape(groups, span, model)
     dx, dx_turned, grad_att, sums_two = [], [], [], []
     for g in range(groups):
-        total, turned, datt, sums = middle_back(
+        rows_grad, turned, datt, sums = middle_back(
             grad_two, middle[g], cotangent, w_out, gains, g
         )
-        dx.append(total)
+        dx.append(rows_grad)
         dx_turned.append(turned)
         sums_two.append(sums)
         grad_att.append(
             swap(datt.reshape(members, span, PAIR)).reshape(members * span, PAIR)
         )
-    d_out = collect(out_grad(dx_turned, att, dps)).T
+    plane_out = collect_plane(out_grad(dx_turned, att, dps))
+    grad_att[-1], plane_first = lax.optimization_barrier((grad_att[-1], plane_first))
     grads = []
     for g in range(groups):
         grad = attend_back(branch[g], qkv[g], att_own[g], grad_att[g], log_totals[g])
         grads.append(
             swap(grad.reshape(members, span, 3 * PAIR)).reshape(rows, cols, span, 3 * PAIR)
         )
-    input_grad, grad_qkv, qkv_bias_sum, sums_one = input_back(
-        grads, dx, normed_turned, tokens, w_qkv, ln1_gain[None], dps
-    )
-    d_qkv = jnp.transpose(collect(grad_qkv), (1, 0, 2))
     sums_two = functools.reduce(jnp.add, sums_two)
-    bias_rows = jnp.transpose(qkv_bias_sum[:, :, 0], (1, 0, 2)).reshape(3, cols * head_cols)
-    small = (
-        sums_one[0],
-        sums_one[1],
-        bias_rows[0],
-        bias_rows[2],
-        sums_two[2],
-        sums_two[0],
-        sums_two[1],
-        fc_bias_sum.reshape(-1),
-        proj_bias_sum,
-    )
-    ends = []
-    for item in small:
-        ends.append((ends[-1] if ends else 0) + item.shape[0])
-    packed = lax.psum(jnp.concatenate(small), ("dp",) + MESH_AXES)
-    (s_gain1, s_bias1, s_q, s_v, s_out, s_gain2, s_bias2, s_fc, s_proj) = jnp.split(
-        packed, ends[:-1]
-    )
+    fc_sum = jnp.concatenate([fc_sum_first, fc_sum_second], axis=2).reshape(-1)
+    early = (sums_two[2], sums_two[0], sums_two[1], fc_sum, proj_bias_sum)
+    grads[0], plane_second, early = lax.optimization_barrier((grads[0], plane_second, early))
+    early = total(jnp.concatenate(early))
+    input_grads, sums_one, bias_sums, before = [], [], [], []
+    for g in range(groups):
+        grad_qkv, bias_sum = qkv_grad(
+            grads[g], normed_turned, before, g, g == groups - 1, dps
+        )
+        before = [grad_qkv]
+        bias_sums.append(bias_sum)
+        rows_grad, sums = input_back(
+            grads[g], dx[g], tokens, w_qkv, ln1_gain[None], input_grads, g
+        )
+        input_grads = [rows_grad]
+        sums_one.append(sums)
+        if g < groups - 1:
+            grads[g + 1], input_grads, early = lax.optimization_barrier(
+                (grads[g + 1], input_grads, early)
+            )
+    d_qkv = jnp.transpose(collect_dp(collect_plane(grad_qkv)), (1, 0, 2))
+    d_out = collect_dp(plane_out).T
+    d_hidden = jnp.concatenate([collect_dp(plane_first), collect_dp(plane_second)], axis=2)
+    sums_one = functools.reduce(jnp.add, sums_one)
+    bias_sum = functools.reduce(jnp.add, bias_sums)
+    bias_rows = jnp.transpose(bias_sum[:, :, 0], (1, 0, 2)).reshape(3, model)
+    late = total(jnp.stack([sums_one[0], sums_one[1], bias_rows[0], bias_rows[2]]))
+    s_out, s_gain_two, s_bias_two = (early[i * model : (i + 1) * model] for i in range(3))
+    s_fc = early[3 * model : 3 * model + hidden_cols * cols]
+    s_proj = early[3 * model + hidden_cols * cols :]
     return (
         block_out,
-        input_grad,
-        s_gain1,
-        s_bias1,
+        input_grads[0],
+        late[0],
+        late[1],
         d_qkv,
-        jnp.stack([s_q, s_v]),
+        late[2:],
         d_out,
         s_out,
-        s_gain2,
-        s_bias2,
-        d_fc,
+        s_gain_two,
+        s_bias_two,
+        d_hidden[0],
         s_fc,
-        d_proj,
+        d_hidden[1].T,
         s_proj,
     )
 
@@ -1107,6 +1150,7 @@
         width = qkv_weight.shape[2] * cols
         whole = tokens.shape[1] * rows * cols
         fits = width == rows * cols * PAIR and rows % 2 == 0
+        fits = fits and all(size & (size - 1) == 0 for size in mesh.shape.values())
         fits = fits and whole == PLEN + CONTS * CLEN and tokens.shape[1] % BQ == 0
         chosen = head_body if fits else gathered_body
         return chosen(tokens, cotangent, branch, ln1_gain, ln1_bias, qkv_weight, *rest)

time: 884 us -> 680 us (0.77)
  waiting for transfers between devices: 435 us -> 171 us
  local copies, waits for them, and re-layouts: 16.5 us -> 71.3 us
  starting transfers between devices: 32.3 us -> 62.7 us
  Pallas kernels: 323 us -> 295 us
    reduce_scatter x8 -> x4, waiting for transfers between devices: 265 us -> 0.06 us  [collect_plane(): lax.psum_scatter(partial, MESH_AXES, scatter_dimension=0, tiled=True)]
    all_to_all x8, waiting for transfers between devices: 127 us -> 59.5 us  [swap(): return lax.all_to_all(blocks, MESH_AXES, 0, 0, tiled=True)]
    unnamed x58 -> x121, local copies, waits for them, and re-layouts: 6.2 us -> 58.9 us
    ppermute x0 -> x10, waiting for transfers between devices: none -> 47.4 us  [total(): values = values + lax.ppermute(values, axis, pairs)]
    psum x1 -> x0, blocking collectives: 39.8 us -> none  [head_body(): packed = lax.psum(jnp.concatenate(small), ('dp',) + MESH_AXES)]
    all_to_all x0 -> x2, blocking collectives: none -> 39.5 us  [collect_dp(): pieces = lax.all_to_all(partial, 'dp', 0, 0, tiled=True)]
    ppermute x0 -> x10, starting transfers between devices: none -> 19.9 us  [total(): values = values + lax.ppermute(values, axis, pairs)]
    all_gather x4, waiting for transfers between devices: 38.8 us -> 51.4 us  [spread(): whole = lax.all_gather(shard, MESH_AXES, axis=0, tiled=False)]
  transfers between devices with their start and end apart: 20 -> 28, of which waited for: 12 -> 14; matrix products, arithmetic and copies ran while one was open for 2% -> 4% of each run, Pallas kernels for 27% -> 43%
where the time goes in v2:
time: 680 us; the launch traced here: 673 us
  Pallas kernels  295 us (43%)
  waiting for transfers between devices  171 us (25%)
  local copies, waits for them, and re-layouts  71.3 us (10%)
  starting transfers between devices  62.7 us (9%)
  blocking collectives  44.9 us (7%)
  between operations  15.4 us (2%)
  other arithmetic  13.3 us (2%)
    pallas_call x2, Pallas kernels, attend_back(): pl.pallas_call(functools.partial(attend_back_kernel, BK_BACK), grid=(toke...  90.7 us
    pallas_call x2, Pallas kernels, feed_forward(): pl.pallas_call(functools.partial(hidden_kernel, rows, dps, groups, first)...  72.5 us
    pallas_call x2, Pallas kernels, attend(): pl.pallas_call(functools.partial(attend_kernel, BK), grid=(blocks,), in_s...  72.2 us
    all_to_all x8, waiting for transfers between devices, swap(): return lax.all_to_all(blocks, MESH_AXES, 0, 0, tiled=True)  59.5 us
    unnamed x121, local copies, waits for them, and re-layouts  58.9 us
    all_gather x4, waiting for transfers between devices, spread(): whole = lax.all_gather(shard, MESH_AXES, axis=0, tiled=False)  51.4 us
    ppermute x10, waiting for transfers between devices, total(): values = values + lax.ppermute(values, axis, pairs)  47.4 us
    all_to_all x2, blocking collectives, collect_dp(): pieces = lax.all_to_all(partial, 'dp', 0, 0, tiled=True)  39.5 us
  transfers between devices with their start and end apart: 28, of which 14 were waited for; matrix products, arithmetic and copies ran while one was open for 4% of the time, Pallas kernels for 43%

profile of v2, /device:TPU:0, one launch (start us, length us, event | category | flops | bytes accessed | tf_op | source)
XLA Modules:
  0.0 673.1 jit_solution(14827069095473498847)
XLA Ops:
  9.3 5.3 all-gather.1
  19.6 38.5 %all-gather.10.cloned.1.call-done = bf16[24,256,512]{2,1,0:T(8,128)(2,1)} async-done(((bf16[3,256,512]{2,1,0:T(8,128)(2,1)}), bf16[24,256,512]{2,1,0:T(8,128)(2,1)}) %all-gather.10.cloned.1.call-update) | async-done | bytes 6291472 | tf_op jit(solution)/shard_map/all_gather | solution.py:997
  58.1 2.8 copy-done.7
  62.4 8.3 %qkv.1 = (bf16[4,2,512,384]{3,2,1,0:T(8,128)(2,1)S(1)}, bf16[4,2,512,384]{3,2,1,0:T(8,128)(2,1)S(1)}) custom-call(bf16[1024,1024]{1,0:T(8,128)(2,1)S(1)} %bitcast.94, bf16[4,2,3,256,512]{4,3,2,1,0:T(8,128)(2,1)S(1)} %bitcast.86, f32[2,2,1,512]{3,2,1,0:T(1,128)S(1)} %reshape.196.bias_ref), custom_call_target="tpu_custom_call" | custom-call | flops 6442450944 | bytes 14680064 | tf_op jit(solution)/shard_map/qkv/pallas_call | solution.py:380
  74.0 4.4 all-to-all-start.2
  82.8 32.6 %all-to-all-done.2 = bf16[8,512,384]{2,1,0:T(8,128)(2,1)} async-done(((bf16[8,512,384]{2,1,0:T(8,128)(2,1)}), bf16[8,512,384]{2,1,0:T(8,128)(2,1)}, u32[]{:S(2)}, u32[]{:S(2)}) %all-to-all-start.2) | async-done | bytes 3145760 | tf_op jit(solution)/shard_map/all_to_all | solution.py:1001
  116.8 4.5 all-to-all-start
  121.3 36.8 %attend.3 = (bf16[4096,128]{1,0:T(8,128)(2,1)S(1)}, f32[16,8,512]{2,1,0:T(8,128)S(1)}) custom-call(s32[8]{0:T(128)S(1)} %get-tuple-element.137.cut_ref, bf16[4096,384]{1,0:T(8,128)(2,1)} %bitcast.9.qkv_ref), custom_call_target="tpu_custom_call" | custom-call | flops 34359738368 | bytes 4194304 | tf_op jit(solution)/shard_map/attend/pallas_call | solution.py:463
  159.0 7.6 %all-to-all-done = bf16[8,512,384]{2,1,0:T(8,128)(2,1)} async-done(((bf16[8,512,384]{2,1,0:T(8,128)(2,1)}), bf16[8,512,384]{2,1,0:T(8,128)(2,1)}, u32[]{:S(2)}, u32[]{:S(2)}) %all-to-all-start) | async-done | bytes 3145760 | tf_op jit(solution)/shard_map/all_to_all | solution.py:1001
  166.7 3.6 all-to-all-start.3
  170.2 35.4 %attend.2 = (bf16[4096,128]{1,0:T(8,128)(2,1)S(1)}, f32[16,8,512]{2,1,0:T(8,128)S(1)}) custom-call(s32[8]{0:T(128)S(1)} %get-tuple-element.138.cut_ref, bf16[4096,384]{1,0:T(8,128)(2,1)} %bitcast.5.qkv_ref), custom_call_target="tpu_custom_call" | custom-call | flops 34359738368 | bytes 4194304 | tf_op jit(solution)/shard_map/attend/pallas_call | solution.py:463
  207.4 4.4 all-to-all-start.1
  212.1 3.9 copy.60
  218.3 2.3 out_norm.3
  224.0 13.5 %all-to-all-done.1 = bf16[8,512,128]{2,1,0:T(8,128)(2,1)} async-done(((bf16[8,512,128]{2,1,0:T(8,128)(2,1)}), bf16[8,512,128]{2,1,0:T(8,128)(2,1)}, u32[]{:S(2)}, u32[]{:S(2)}) %all-to-all-start.1) | async-done | bytes 1048608 | tf_op jit(solution)/shard_map/all_to_all | solution.py:1001
  239.2 3.3 out_norm.2
  245.7 36.4 %feed_forward_first.1 = (f32[1024,1024]{1,0:T(8,128)}, f32[1024,1024]{1,0:T(8,128)}, bf16[4,2,4,2,64,1024]{5,4,3,2,1,0:T(8,128)(2,1)}, f32[2,1,1024]{2,1,0:T(1,128)}) custom-call(bf16[512,1024]{1,0:T(8,128)(2,1)} %copy-done.41, bf16[512,1024]{1,0:T(8,128)(2,1)} %copy-done.39, bf16[1024,512]{1,0:T(8,128)(2,1)} %copy-done.42, bf16[1024,512]{1,0:T(8,128)(2,1)} %copy-done.40, ...), custom_call_target="tpu_custom_call" | custom-call | flops 25769803776 | bytes 16777216 | tf_op jit(solution)/shard_map/feed_forward_first/pallas_call | solution.py:744
  282.4 12.9 %all-gather.14.cloned.1.call-done = bf16[16,256,1024]{2,1,0:T(8,128)(2,1)} async-done(((bf16[2,256,1024]{2,1,0:T(8,128)(2,1)}), bf16[16,256,1024]{2,1,0:T(8,128)(2,1)}) %all-gather.14.cloned.1.call-update) | async-done | bytes 8388624 | tf_op jit(solution)/shard_map/all_gather | solution.py:997
  295.3 36.1 %feed_forward_second.1 = (bf16[2,512,1024]{2,1,0:T(8,128)(2,1)}, f32[1024,1024]{1,0:T(8,128)}, bf16[4,2,4,2,64,1024]{5,4,3,2,1,0:T(8,128)(2,1)}, f32[2,1,1024]{2,1,0:T(1,128)}) custom-call(bf16[512,1024]{1,0:T(8,128)(2,1)} %copy-done.41, bf16[512,1024]{1,0:T(8,128)(2,1)} %copy-done.39, bf16[1024,512]{1,0:T(8,128)(2,1)} %copy-done.42, ...), custom_call_target="tpu_custom_call" | custom-call | flops 25769803776 | bytes 16777216 | tf_op jit(solution)/shard_map/feed_forward_second/pallas_call | solution.py:744
  334.8 2.4 copy-done.10
  338.8 3.2 out_norm_back.3
  345.3 4.3 all-to-all-start.6
  356.9 3.2 out_norm_back.2
  360.2 4.1 out_grad.1
  365.6 5.5 all-to-all-done.6
  371.1 4.5 all-to-all-start.4
  376.6 44.5 %attend_back.3 = bf16[4096,384]{1,0:T(8,128)(2,1)S(1)} custom-call(s32[8]{0:T(128)S(1)} %get-tuple-element.138.cut_ref, bf16[4096,384]{1,0:T(8,128)(2,1)} %bitcast.5.qkv_ref, bf16[4096,128]{1,0:T(8,128)(2,1)S(1)} %copy-done.32, bf16[4096,128]{1,0:T(8,128)(2,1)} %bitcast.35.do_ref, f32[16,8,512]{2,1,0:T(8,128)S(1)} %copy-done.46), custom_call_target="tpu_custom_call" | custom-call | flops 42949672960 | bytes 8388608 | tf_op jit(solution)/shard_map/attend_back/pallas_call | solution.py:561
  422.8 4.6 all-to-all-start.7
  427.5 46.2 %attend_back.2 = bf16[4096,384]{1,0:T(8,128)(2,1)S(1)} custom-call(s32[8]{0:T(128)S(1)} %copy-done.38, bf16[4096,384]{1,0:T(8,128)(2,1)} %bitcast.9.qkv_ref, bf16[4096,128]{1,0:T(8,128)(2,1)S(1)} %copy-done.30, bf16[4096,128]{1,0:T(8,128)(2,1)} %bitcast.29.do_ref, f32[16,8,512]{2,1,0:T(8,128)S(1)} %get-tuple-element.87.lse_ref), custom_call_target="tpu_custom_call" | custom-call | flops 42949672960 | bytes 8388608 | tf_op jit(solution)/shard_map/attend_back/pallas_call | solution.py:561
  475.6 4.6 all-to-all-start.5
  485.5 37.9 %collective-permute-done.1 = f32[8192]{0:T(1024)S(1)} collective-permute-done((f32[8192]{0:T(1024)S(1)}, f32[8192]{0:T(1024)S(1)}, u32[]{:S(2)}, u32[]{:S(2)}) %collective-permute-start.1) | collective-permute-done | bytes 32800 | tf_op jit(solution)/shard_map/ppermute | solution.py:1018
  524.8 4.0 copy.59
  528.8 2.4 collective-permute-start.3
  532.8 8.5 %qkv_grad.2 = (f32[4,2,4,3,64,512]{5,4,3,2,1,0:T(8,128)}, f32[2,3,1,512]{3,2,1,0:T(1,128)S(1)}) custom-call(bf16[1024,1024]{1,0:T(8,128)(2,1)S(1)} %bitcast.91, bf16[4,2,512,384]{3,2,1,0:T(8,128)(2,1)} %bitcast.37.dqkv_ref), custom_call_target="tpu_custom_call" | custom-call | flops 3221225472 | bytes 25165824 | tf_op jit(solution)/shard_map/qkv_grad/pallas_call | solution.py:893
  541.3 6.1 collective-permute-start.4
  547.4 2.8 copy-done.8
  550.2 9.1 %input_back.2 = (f32[2,512,1024]{2,1,0:T(8,128)}, f32[8,1024]{1,0:T(8,128)S(1)}) custom-call(bf16[4,2,512,384]{3,2,1,0:T(8,128)(2,1)} %bitcast.37.dqkv_ref, bf16[4,2,3,256,512]{4,3,2,1,0:T(8,128)(2,1)S(1)} %bitcast.87, f32[512,1024]{1,0:T(8,128)S(1)} %copy-done.23, bf16[2,512,1024]{2,1,0:T(8,128)(2,1)S(1)} %copy-done, f32[1,1024]{1,0:T(1,128)S(1)} %bitcast.107), custom_call_target="tpu_custom_call" | custom-call | flops 3221225472 | bytes 12582912 | tf_op jit(solution)/shard_map/input_back/pallas_call | solution.py:943
  561.0 8.1 %qkv_grad.3 = (bf16[4,2,4,3,64,512]{5,4,3,2,1,0:T(8,128)(2,1)S(1)}, f32[2,3,1,512]{3,2,1,0:T(1,128)S(1)}) custom-call(bf16[1024,1024]{1,0:T(8,128)(2,1)S(1)} %bitcast.92, bf16[4,2,512,384]{3,2,1,0:T(8,128)(2,1)} %bitcast.33.dqkv_ref, f32[4,2,4,3,64,512]{5,4,3,2,1,0:T(8,128)} %get-tuple-element.110.refs_0_), custom_call_target="tpu_custom_call" | custom-call | flops 3221225472 | bytes 25165824 | tf_op jit(solution)/shard_map/qkv_grad/pallas_call | solution.py:893
  569.0 2.6 copy-done.15
  571.7 11.7 %all_to_all.60 = bf16[4,64,512]{2,1,0:T(8,128)(2,1)S(1)} all-to-all(bf16[4,64,512]{2,1,0:T(8,128)(2,1)} %bitcast.119), channel_id=1, replica_groups=mesh['dp'=4,'row'=4,'col'=2] {'dp'}, dimensions={0} | all-to-all | bytes 524288 | tf_op jit(solution)/shard_map/all_to_all | solution.py:1009
  583.3 27.9 %all_to_all.61 = bf16[4,2,64,1024]{3,2,1,0:T(8,128)(2,1)} all-to-all(bf16[4,2,64,1024]{3,2,1,0:T(8,128)(2,1)S(1)} %bitcast.115), channel_id=1, replica_groups=mesh['dp'=4,'row'=4,'col'=2] {'dp'}, dimensions={0} | all-to-all | bytes 2097152 | tf_op jit(solution)/shard_map/all_to_all | solution.py:1009
  611.2 3.8 all-to-all-start.10
  615.1 2.8 copy-done.9
  619.6 9.1 %input_back.3 = (f32[2,512,1024]{2,1,0:T(8,128)}, f32[8,1024]{1,0:T(8,128)S(1)}) custom-call(bf16[4,2,512,384]{3,2,1,0:T(8,128)(2,1)} %bitcast.33.dqkv_ref, bf16[4,2,3,256,512]{4,3,2,1,0:T(8,128)(2,1)S(1)} %bitcast.88, f32[512,1024]{1,0:T(8,128)S(1)} %copy-done.21, bf16[2,512,1024]{2,1,0:T(8,128)(2,1)S(1)} %copy-done, ...), custom_call_target="tpu_custom_call", output_to_operand_aliasing={{0}: (5, {})} | custom-call | flops 3221225472 | bytes 12582912 | tf_op jit(solution)/shard_map/input_back/pallas_call | solution.py:943
  629.4 10.4 %all-to-all-done.10 = bf16[4,2,64,1024]{3,2,1,0:T(8,128)(2,1)S(1)} async-done(((bf16[4,2,64,1024]{3,2,1,0:T(8,128)(2,1)}), bf16[4,2,64,1024]{3,2,1,0:T(8,128)(2,1)S(1)}, u32[]{:S(2)}, u32[]{:S(2)}) %all-to-all-start.10) | async-done | bytes 1048608 | tf_op jit(solution)/shard_map/all_to_all | solution.py:1009
  639.8 3.5 all-to-all-start.8
  647.9 3.0 collective-permute-done.7
  656.1 4.6 collective-permute-start.9
  (205 shorter events, 79.9 us)
Async XLA Ops:
  7.2 9.5 %copy-start = (bf16[2,512,1024]{2,1,0:T(8,128)(2,1)S(1)}, bf16[2,512,1024]{2,1,0:T(8,128)(2,1)}, u32[]{:S(2)}) copy-start(bf16[2,512,1024]{2,1,0:T(8,128)(2,1)} %tok_ref.7) | copy-start | bytes 6291460
  7.2 10.2 %copy-start.35 = (f32[1024]{0:T(1024)S(1)}, f32[1024]{0:T(1024)}, u32[]{:S(2)}) copy-start(f32[1024]{0:T(1024)} %param.18) | copy-start | bytes 12292
  7.2 10.2 %copy-start.54 = (f32[1024]{0:T(1024)S(1)}, f32[1024]{0:T(1024)}, u32[]{:S(2)}) copy-start(f32[1024]{0:T(1024)} %param.19) | copy-start | bytes 12292
  7.2 50.8 %all-gather.10.cloned.1.call-start = ((), (), s32[]{:S(2)}) async-start(), calls=%async_computation.20 | async-start | bytes 7077888 | tf_op jit(solution)/shard_map/all_gather | solution.py:997
  14.7 197.3 %copy-start.49 = (f32[2,3072]{1,0:T(2,128)}, f32[2,3072]{1,0:T(2,128)S(1)}, u32[]{:S(2)}) copy-start(f32[2,3072]{1,0:T(2,128)S(1)} %reshape.188) | copy-start | bytes 73732
  74.0 41.4 %all-to-all-start.2 = ((bf16[8,512,384]{2,1,0:T(8,128)(2,1)}), bf16[8,512,384]{2,1,0:T(8,128)(2,1)}, u32[]{:S(2)}, u32[]{:S(2)}) async-start(bf16[8,512,384]{2,1,0:T(8,128)(2,1)} %bitcast.100), calls=%async_computation.2 | async-start | bytes 6291456 | tf_op jit(solution)/shard_map/all_to_all | solution.py:1001
  78.4 138.3 %all-gather.12.cloned.1.call-start = ((), (), s32[]{:S(2)}) async-start(), calls=%async_computation.21 | async-start | bytes 2359296 | tf_op jit(solution)/shard_map/all_gather | solution.py:997
  81.3 35.4 %copy-start.55 = (s32[2,8]{1,0:T(2,128)S(1)}, s32[2,8]{1,0:T(2,128)}, u32[]{:S(2)}) copy-start(s32[2,8]{1,0:T(2,128)} %param.17) | copy-start | bytes 196
  115.4 130.3 %all-gather.16.cloned.1.call-start = ((), (), s32[]{:S(2)}) async-start(), calls=%async_computation.23 | async-start | bytes 9437184 | tf_op jit(solution)/shard_map/all_gather | solution.py:997
  116.2 179.1 %all-gather.14.cloned.1.call-start = ((), (), s32[]{:S(2)}) async-start(), calls=%async_computation.22 | async-start | bytes 9437184 | tf_op jit(solution)/shard_map/all_gather | solution.py:997
  116.8 4.5 copy-start.37
  116.8 49.9 %all-to-all-start = ((bf16[8,512,384]{2,1,0:T(8,128)(2,1)}), bf16[8,512,384]{2,1,0:T(8,128)(2,1)}, u32[]{:S(2)}, u32[]{:S(2)}) async-start(bf16[8,512,384]{2,1,0:T(8,128)(2,1)} %bitcast.99), calls=%async_computation | async-start | bytes 6291456 | tf_op jit(solution)/shard_map/all_to_all | solution.py:1001
  166.7 40.7 %all-to-all-start.3 = ((bf16[8,512,128]{2,1,0:T(8,128)(2,1)}), bf16[8,512,128]{2,1,0:T(8,128)(2,1)S(1)}, u32[]{:S(2)}, u32[]{:S(2)}) async-start(bf16[8,512,128]{2,1,0:T(8,128)(2,1)} %bitcast.103), calls=%async_computation.3 | async-start | bytes 2097152 | tf_op jit(solution)/shard_map/all_to_all | solution.py:1001
  207.4 8.6 %copy-start.48 = (f32[1024]{0:T(1024)S(1)}, f32[1024]{0:T(1024)}, u32[]{:S(2)}) copy-start(f32[1024]{0:T(1024)} %param.23) | copy-start | bytes 12292
  207.4 8.6 %copy-start.50 = (f32[1024]{0:T(1024)S(1)}, f32[1024]{0:T(1024)}, u32[]{:S(2)}) copy-start(f32[1024]{0:T(1024)} %param.24) | copy-start | bytes 12292
  207.4 8.6 %copy-start.53 = (f32[1024]{0:T(1024)S(1)}, f32[1024]{0:T(1024)}, u32[]{:S(2)}) copy-start(f32[1024]{0:T(1024)} %param.25) | copy-start | bytes 12292
  207.4 30.0 %all-to-all-start.1 = ((bf16[8,512,128]{2,1,0:T(8,128)(2,1)}), bf16[8,512,128]{2,1,0:T(8,128)(2,1)}, u32[]{:S(2)}, u32[]{:S(2)}) async-start(bf16[8,512,128]{2,1,0:T(8,128)(2,1)} %bitcast.104), calls=%async_computation.1 | async-start | bytes 2097152 | tf_op jit(solution)/shard_map/all_to_all | solution.py:1001
  211.8 215.6 %reduce-scatter.5.cloned.1.call-start = ((), (), s32[]{:S(2)}) async-start(), calls=%async_computation.16 | async-start | bytes 9437184 | tf_op jit(solution)/shard_map/reduce_scatter | solution.py:1005
  212.0 4.0 slice-start
  282.2 200.1 %reduce-scatter.7.cloned.1.call-start = ((), (), s32[]{:S(2)}) async-start(), calls=%async_computation.17 | async-start | bytes 9437184 | tf_op jit(solution)/shard_map/reduce_scatter | solution.py:1005
  345.3 25.8 %all-to-all-start.6 = ((bf16[8,512,128]{2,1,0:T(8,128)(2,1)}), bf16[8,512,128]{2,1,0:T(8,128)(2,1)}, u32[]{:S(2)}, u32[]{:S(2)}) async-start(bf16[8,512,128]{2,1,0:T(8,128)(2,1)} %bitcast.106), calls=%async_computation.7 | async-start | bytes 2097152 | tf_op jit(solution)/shard_map/all_to_all | solution.py:1001
  349.6 222.1 %reduce-scatter.11.cloned.1.call-start = ((), (), s32[]{:S(2)}) async-start(), calls=%async_computation.19 | async-start | bytes 2359296 | tf_op jit(solution)/shard_map/reduce_scatter | solution.py:1005
  360.2 4.1 copy-start.20
  360.2 4.1 copy-start.33
  365.6 10.0 %copy-start.32 = (bf16[4096,128]{1,0:T(8,128)(2,1)S(1)}, bf16[4096,128]{1,0:T(8,128)(2,1)}, u32[]{:S(2)}) copy-start(bf16[4096,128]{1,0:T(8,128)(2,1)} %copy-done.31) | copy-start | bytes 3145732
  371.1 51.7 %all-to-all-start.4 = ((bf16[8,512,128]{2,1,0:T(8,128)(2,1)}), bf16[8,512,128]{2,1,0:T(8,128)(2,1)}, u32[]{:S(2)}, u32[]{:S(2)}) async-start(bf16[8,512,128]{2,1,0:T(8,128)(2,1)} %bitcast.105), calls=%async_computation.4 | async-start | bytes 2097152 | tf_op jit(solution)/shard_map/all_to_all | solution.py:1001
  422.8 4.6 copy-start.30
  422.8 4.6 copy-start.38
  422.8 52.8 %all-to-all-start.7 = ((bf16[8,512,384]{2,1,0:T(8,128)(2,1)}), bf16[8,512,384]{2,1,0:T(8,128)(2,1)}, u32[]{:S(2)}, u32[]{:S(2)}) async-start(bf16[8,512,384]{2,1,0:T(8,128)(2,1)} %bitcast.101), calls=%async_computation.8 | async-start | bytes 6291456 | tf_op jit(solution)/shard_map/all_to_all | solution.py:1001
  475.6 6.6 copy-start.51
  475.6 6.6 copy-start.52
  475.6 83.7 %all-to-all-start.5 = ((bf16[8,512,384]{2,1,0:T(8,128)(2,1)}), bf16[8,512,384]{2,1,0:T(8,128)(2,1)}, u32[]{:S(2)}, u32[]{:S(2)}) async-start(bf16[8,512,384]{2,1,0:T(8,128)(2,1)} %bitcast.98), calls=%async_computation.6 | async-start | bytes 6291456 | tf_op jit(solution)/shard_map/all_to_all | solution.py:1001
  480.2 159.6 %reduce-scatter.9.cloned.1.call-start = ((), (), s32[]{:S(2)}) async-start(), calls=%async_computation.18 | async-start | bytes 7077888 | tf_op jit(solution)/shard_map/reduce_scatter | solution.py:1005
  482.4 1.3 collective-permute-start
  483.6 39.7 %collective-permute-start.1 = (f32[8192]{0:T(1024)S(1)}, f32[8192]{0:T(1024)S(1)}, u32[]{:S(2)}, u32[]{:S(2)}) collective-permute-start(f32[8192]{0:T(1024)S(1)} %add.71), channel_id=1, source_target_pairs={{0,4},{2,6},{4,0},{6,2},{1,5},{3,7},{5,1},{7,3},{8,12},{10,14},{12... | collective-permute-start | bytes 98312 | tf_op jit(solution)/shard_map/ppermute | solution.py:1018
  523.4 5.4 collective-permute-start.2
  528.8 12.5 %collective-permute-start.3 = (f32[8192]{0:T(1024)S(1)}, f32[8192]{0:T(1024)S(1)}, u32[]{:S(2)}, u32[]{:S(2)}) collective-permute-start(f32[8192]{0:T(1024)S(1)} %add.73), channel_id=1, source_target_pairs={{0,8},{8,0},{16,24},{24,16},{1,9},{9,1},{17,25},{25,17},{2,10},{10... | collective-permute-start | bytes 98312 | tf_op jit(solution)/shard_map/ppermute | solution.py:1018
  532.8 14.6 %copy-start.23 = (f32[512,1024]{1,0:T(8,128)S(1)}, f32[512,1024]{1,0:T(8,128)}, u32[]{:S(2)}) copy-start(f32[512,1024]{1,0:T(8,128)} %copy-done.22) | copy-start | bytes 6291460
  532.8 14.6 %copy-start.36 = (f32[1024]{0:T(1024)S(1)}, f32[1024]{0:T(1024)}, u32[]{:S(2)}) copy-start(f32[1024]{0:T(1024)} %param.18) | copy-start | bytes 12292
  541.3 18.0 %collective-permute-start.4 = (f32[8192]{0:T(1024)S(1)}, f32[8192]{0:T(1024)S(1)}, u32[]{:S(2)}, u32[]{:S(2)}) collective-permute-start(f32[8192]{0:T(1024)S(1)} %add.74), channel_id=1, source_target_pairs={{0,16},{8,24},{16,0},{24,8},{1,17},{9,25},{17,1},{25,9},{2,18},{10... | collective-permute-start | bytes 98312 | tf_op jit(solution)/shard_map/ppermute | solution.py:1018
  571.6 11.7 %copy-start.47 = (bf16[1,4,2,64,1024]{4,3,2,1,0:T(8,128)(2,1)S(1)}, bf16[1,4,2,64,1024]{4,3,2,1,0:T(8,128)(2,1)}, u32[]{:S(2)}) copy-start(bf16[1,4,2,64,1024]{4,3,2,1,0:T(8,128)(2,1)} %reduce-scatter.7.cloned.1.call-done) | copy-start | bytes 3145732
  611.2 28.6 %all-to-all-start.10 = ((bf16[4,2,64,1024]{3,2,1,0:T(8,128)(2,1)}), bf16[4,2,64,1024]{3,2,1,0:T(8,128)(2,1)S(1)}, u32[]{:S(2)}, u32[]{:S(2)}) async-start(bf16[4,2,64,1024]{3,2,1,0:T(8,128)(2,1)} %bitcast.114), calls=%async_computation.14 | async-start | bytes 2097152 | tf_op jit(solution)/shard_map/all_to_all | solution.py:1009
  628.7 14.7 %collective-permute-start.5 = (f32[4,1024]{1,0:T(4,128)S(1)}, f32[4,1024]{1,0:T(4,128)S(1)}, u32[]{:S(2)}, u32[]{:S(2)}) collective-permute-start(f32[4,1024]{1,0:T(4,128)S(1)} %pad_maximum_fusion.4), channel_id=1, source_target_pairs={{0,2},{2,0},{4,6},{6,4},{1,3},{3,1},{5,7},{7,5},{8,10},{10,8},{12,... | collective-permute-start | bytes 49160 | tf_op jit(solution)/shard_map/ppermute | solution.py:1018
  639.8 25.1 %all-to-all-start.8 = ((bf16[4,3,64,512]{3,2,1,0:T(8,128)(2,1)}), bf16[4,3,64,512]{3,2,1,0:T(8,128)(2,1)S(1)}, u32[]{:S(2)}, u32[]{:S(2)}) async-start(bf16[4,3,64,512]{3,2,1,0:T(8,128)(2,1)} %bitcast.117), calls=%async_computation.11 | async-start | bytes 1572864 | tf_op jit(solution)/shard_map/all_to_all | solution.py:1009
  643.4 3.8 collective-permute-start.6
  647.2 3.7 collective-permute-start.7
  650.9 5.1 collective-permute-start.8
  656.1 7.6 %collective-permute-start.9 = (f32[4,1024]{1,0:T(4,128)S(1)}, f32[4,1024]{1,0:T(4,128)S(1)}, u32[]{:S(2)}, u32[]{:S(2)}) collective-permute-start(f32[4,1024]{1,0:T(4,128)S(1)} %add.81), channel_id=1, source_target_pairs={{0,16},{8,24},{16,0},{24,8},{1,17},{9,25},{17,1},{25,9},{2,18},{10... | collective-permute-start | bytes 49160 | tf_op jit(solution)/shard_map/ppermute | solution.py:1018
  (37 other events, 60.0 us)
Sparse Core Ops, SparseCore 0:
  9.9 48.1 all-gather.9
  115.6 50.6 all-gather.11
  168.8 70.4 all-gather.15
  241.0 54.2 all-gather.13
  298.6 78.0 reduce-scatter.4
  380.0 92.2 reduce-scatter.6
  475.6 56.6 reduce-scatter.10
  571.8 58.0 reduce-scatter.8

commit v3 on v2

--- a/solution.py
+++ b/solution.py
@@ -355,42 +355,56 @@
     return jnp.where(low, stacked[:half], stacked[half:])
 
 
-def qkv_kernel(rows, groups, x_ref, w_ref, bias_ref, *out_refs):
-    depth = w_ref.shape[3]
-    for part in range(3):
-        weight = w_ref[:, 0, part].reshape(rows * depth, 2 * PAIR)
-        values = dot(x_ref[...], weight)
-        if part != 1:
-            values = values + bias_ref[0, 0 if part == 0 else 1]
-        if part == 0:
-            values = values * HEAD**-0.5
-        values = values.astype(jnp.bfloat16)
-        span = values.shape[0] // groups
-        for g in range(groups):
-            for half in range(2):
-                out_refs[g][half, 0, :, part * PAIR : (part + 1) * PAIR] = values[
-                    g * span : (g + 1) * span, half * PAIR : (half + 1) * PAIR
-                ]
-
-
-def project_qkv(normed, weight, bias, groups):
-    rows, cols, _, depth, width = weight.shape
-    tokens, model = normed.shape
-    span = tokens // groups
+def pack_kernel(fc_ref, proj_ref, out_ref, first_ref, second_ref):
+    depth, hidden = fc_ref.shape
+    half = hidden // 2
+    turned = jnp.transpose(proj_ref[...])
+    for at, ref in ((0, first_ref), (half, second_ref)):
+        ref[:depth] = fc_ref[:, at : at + half]
+        ref[depth : 2 * depth] = turned[:, at : at + half]
+    for h in range(out_ref.shape[0] // PAIR):
+        first_ref[2 * depth :, h * depth : (h + 1) * depth] = out_ref[h * PAIR : (h + 1) * PAIR]
+
+
+def pack_weights(fc_weight, proj_weight, out_weight):
+    depth, hidden = fc_weight.shape
+    shapes = [(2 * depth + PAIR, hidden // 2), (2 * depth, hidden // 2)]
     return pl.pallas_call(
-        functools.partial(qkv_kernel, rows, groups),
-        grid=(rows // 2, cols),
+        pack_kernel,
+        in_specs=[pl.BlockSpec(memory_space=pltpu.VMEM)] * 3,
+        out_specs=[pl.BlockSpec(memory_space=pltpu.VMEM)] * 2,
+        out_shape=[jax.ShapeDtypeStruct(shape, jnp.bfloat16) for shape in shapes],
+        compiler_params=params(60),
+        cost_estimate=cost(1, 8 * depth * hidden),
+        name="pack_weights",
+    )(fc_weight, proj_weight, out_weight)
+
+
+def qkv_kernel(x_ref, w_ref, vec_ref, out_ref):
+    rows = x_ref[...].reshape(out_ref.shape[0], x_ref.shape[2])
+    values = (dot(rows, w_ref[...]) + vec_ref[0:1]) * vec_ref[1:2]
+    out_ref[...] = values.astype(out_ref.dtype)
+
+
+def project_qkv(normed, weight, bias, span):
+    members, _, model = normed.shape
+    width = weight.shape[1]
+    tokens = members * span
+    vectors = jnp.stack([bias, jnp.where(jnp.arange(width) < PAIR, HEAD**-0.5, 1.0)])
+    return pl.pallas_call(
+        qkv_kernel,
+        grid=(members // 2,),
         in_specs=[
-            fixed((tokens, model)),
-            pl.BlockSpec((rows, 1, 3, depth, 2 * PAIR), lambda i, c: (0, c, 0, 0, i)),
-            pl.BlockSpec((1, 2, 1, 2 * PAIR), lambda i, c: (c, 0, 0, i)),
-        ],
-        out_specs=[pl.BlockSpec((2, 1, span, 3 * PAIR), lambda i, c: (i, c, 0, 0))] * groups,
-        out_shape=[jax.ShapeDtypeStruct((rows, cols, span, 3 * PAIR), jnp.bfloat16)] * groups,
-        compiler_params=params(24),
-        cost_estimate=cost(6 * tokens * model * model, 8 * tokens * model + 6 * model * model),
+            pl.BlockSpec((2, span, model), lambda i: (i, 0, 0)),
+            fixed((model, width)),
+            fixed((2, width)),
+        ],
+        out_specs=pl.BlockSpec((2 * span, width), lambda i: (i, 0)),
+        out_shape=jax.ShapeDtypeStruct((tokens, width), jnp.bfloat16),
+        compiler_params=params(60),
+        cost_estimate=cost(2 * tokens * model * width, 2 * tokens * (model + width)),
         name="qkv",
-    )(normed, weight, bias)
+    )(normed, weight, vectors)
 
 
 def attend_kernel(
@@ -479,7 +493,7 @@
             pltpu.VMEM((2 * BQ, PAIR), jnp.float32),
             pltpu.VMEM((2 * BQ, 2 * PAIR), jnp.float32),
         ],
-        compiler_params=params(24),
+        compiler_params=params(60),
         cost_estimate=cost(8 * 2 * pairs * 256, 2 * tokens * 4 * PAIR, pairs),
         name="attend",
     )(cut, qkv)
@@ -575,7 +589,7 @@
             pltpu.VMEM((tokens, PAIR), jnp.float32),
             pltpu.VMEM((PAIR, 2 * BQ), jnp.float32),
         ],
-        compiler_params=params(32),
+        compiler_params=params(60),
         cost_estimate=cost(10 * 2 * pairs * 256, 2 * tokens * 8 * PAIR, pairs),
         name="attend_back",
     )(cut, qkv, att, grad_att, log_totals)
@@ -593,6 +607,21 @@
     mean_one = jnp.mean(scaled, axis=-1, keepdims=True)
     mean_two = jnp.mean(scaled * unit, axis=-1, keepdims=True)
     return (scaled - mean_one - unit * mean_two) * inverse
+
+
+def out_block(w_ref, r, c, rows):
+    width = w_ref.shape[3] // rows
+    return jnp.concatenate(
+        [w_ref[r, c, :, h * width : (h + 1) * width] for h in range(rows)], axis=0
+    )
+
+
+def out_weight_spec(weight):
+    rows, cols, depth, width = weight.shape
+    at = 4
+    return pl.BlockSpec(
+        (rows, cols, PAIR, width), lambda *_: (0, 0, at, 0), pipeline_mode=pl.Buffered(1)
+    )
 
 
 def middle_kernel(
@@ -603,9 +632,9 @@
         parts.append(jnp.concatenate([att_ref[r, c] for r in range(rows)], axis=1))
     pieces = []
     for r in range(rows):
-        total = dot(parts[0], w_ref[r, 0])
+        total = dot(parts[0], out_block(w_ref, r, 0, rows))
         for c in range(1, cols):
-            total = total + dot(parts[c], w_ref[r, c])
+            total = total + dot(parts[c], out_block(w_ref, r, c, rows))
         pieces.append(total)
     middle = tok_ref[0].astype(jnp.float32) + jnp.concatenate(pieces, axis=1) + vec_ref[0:1]
     middle_ref[...] = middle
@@ -624,7 +653,7 @@
         in_specs=[
             pl.BlockSpec((1, tile, model), lambda i: (g, i, 0)),
             pl.BlockSpec((rows, cols, tile, PAIR), lambda i: (0, 0, i, 0)),
-            fixed(weight.shape),
+            out_weight_spec(weight),
             fixed(vectors.shape),
         ],
         out_specs=[
@@ -637,26 +666,67 @@
             jax.ShapeDtypeStruct((span, model), jnp.bfloat16),
             jax.ShapeDtypeStruct((model, span), jnp.bfloat16),
         ],
-        compiler_params=params(24),
+        compiler_params=params(60),
         cost_estimate=cost(2 * span * model * model, 2 * model * model + 12 * span * model),
         name="out_norm",
     )(tokens, att, weight, vectors)
 
 
+def store_grads(rows, dps, turned_refs, cot_turned_ref, low_all, active_all, grad_ref):
+    turned_all = jnp.concatenate([ref[...] for ref in turned_refs], axis=1)
+    cut = turned_all.shape[0] // (rows * dps)
+    for which, weight_grad in enumerate(
+        (dot(turned_all, low_all), dot(cot_turned_ref[...], active_all))
+    ):
+        weight_grad = weight_grad.astype(jnp.bfloat16)
+        for r in range(rows):
+            for d in range(dps):
+                at = (d * rows + r) * cut
+                grad_ref[r, 0, d, which * cut : (which + 1) * cut] = weight_grad[at : at + cut]
+
+
+def hidden_grad_kernel(rows, dps, *refs):
+    low_ref, active_ref, grad_ref = refs[-3:]
+    store_grads(rows, dps, refs[:-4], refs[-4], low_ref[0], active_ref[0], grad_ref)
+
+
+def hidden_grad(turned, cot_turned, low, active, dps, rows):
+    cols, tokens, local = low.shape
+    model = cot_turned.shape[0]
+    tile = min(HIDDEN_TILE, local)
+    cut = model // (rows * dps)
+    piece = pl.BlockSpec((1, tokens, tile), lambda c, i: (c, 0, i))
+    return pl.pallas_call(
+        functools.partial(hidden_grad_kernel, rows, dps),
+        grid=(cols, local // tile),
+        in_specs=[fixed(part.shape) for part in turned]
+        + [fixed(cot_turned.shape), piece, piece],
+        out_specs=pl.BlockSpec((rows, 1, dps, 2 * cut, tile), lambda c, i: (0, c, 0, 0, i)),
+        out_shape=jax.ShapeDtypeStruct(
+            (rows, cols, dps, 2 * cut + cut // 2, local), jnp.bfloat16
+        ),
+        compiler_params=params(60),
+        cost_estimate=cost(4 * tokens * model * cols * local, 8 * model * cols * local),
+        name="hidden_grad",
+    )(*turned, cot_turned, low, active)
+
+
 def hidden_kernel(rows, dps, groups, first, *refs):
-    normed_refs = refs[:groups]
-    turned_refs = refs[groups : 2 * groups]
-    cot_ref, cot_turned_ref, w_ref, fc_bias_ref = refs[2 * groups : 2 * groups + 4]
+    normed_refs, refs = refs[:groups], refs[groups:]
     if first:
-        middle_refs = refs[2 * groups + 4 : 3 * groups + 4]
-        out_acc, back_acc, grad_ref, bias_ref, sems = refs[3 * groups + 4 :]
+        turned_refs, cot_turned_ref, refs = refs[:groups], refs[groups], refs[groups + 1 :]
+    cot_ref, w_ref, fc_bias_ref = refs[:3]
+    if first:
+        middle_refs = refs[3 : groups + 3]
+        out_acc, back_acc, grad_ref, bias_ref, sems = refs[groups + 3 :]
     else:
-        (prev_out_ref, prev_back_ref, proj_bias_ref) = refs[2 * groups + 4 : 2 * groups + 7]
-        out_ref, back_acc, grad_ref, bias_ref, out_acc, sems = refs[2 * groups + 7 :]
+        prev_out_ref, prev_back_ref, proj_bias_ref = refs[3:6]
+        out_ref, back_acc, low_ref, active_ref, bias_ref, out_acc, sems = refs[6:]
     step = pl.program_id(0) * pl.num_programs(1) + pl.program_id(1)
     last = pl.num_programs(0) * pl.num_programs(1) - 1
     span, model = normed_refs[0].shape
-    tile = w_ref.shape[4]
+    tile = w_ref.shape[3]
+    depth = model // rows
     if first:
         copies = [
             pltpu.make_async_copy(
@@ -677,8 +747,8 @@
         if first:
             back_acc[...] = jnp.zeros_like(back_acc)
 
-    fc_weight = w_ref[:, 0, 0].reshape(model, tile)
-    proj_turned = w_ref[:, 0, 1].reshape(model, tile)
+    fc_weight = w_ref[:, 0, :depth].reshape(model, tile)
+    proj_turned = w_ref[:, 0, depth:].reshape(model, tile)
     root = 0.7978845608028654
     actives, lows = [], []
     for g in range(groups):
@@ -696,16 +766,13 @@
     )
     low_all = jnp.concatenate(lows, axis=0)
     active_all = jnp.concatenate(actives, axis=0)
-    turned_all = jnp.concatenate([ref[...] for ref in turned_refs], axis=1)
-    cut = model // (rows * dps)
-    for which, weight_grad in enumerate(
-        (dot(turned_all, low_all), dot(cot_turned_ref[...], active_all))
-    ):
-        weight_grad = weight_grad.astype(jnp.bfloat16)
-        for r in range(rows):
-            for d in range(dps):
-                at = (d * rows + r) * cut
-                grad_ref[r, 0, d, which] = weight_grad[at : at + cut]
+    if first:
+        store_grads(
+            rows, dps, turned_refs, cot_turned_ref, low_all, active_all, grad_ref
+        )
+    else:
+        low_ref[0] = low_all
+        active_ref[0] = active_all
 
     @pl.when(step == 0)
     def _():
@@ -723,11 +790,12 @@
                 out_ref[g] = (out_acc[at] + proj_bias_ref[...]).astype(out_ref.dtype)
 
 
-def feed_forward(first, normed, turned, cot, cot_turned, weight, fc_bias, rest, dps):
+def feed_forward(first, normed, turned, cot, weight, fc_bias, rest, dps):
     groups = len(normed)
     span, model = normed[0].shape
     tokens = groups * span
-    rows, cols, _, depth, local = weight.shape
+    rows, cols, _, local = weight.shape
+    depth = model // rows
     tile = min(HIDDEN_TILE, local)
     cut = model // (rows * dps)
     acc_shape = jax.ShapeDtypeStruct((tokens, model), jnp.float32)
@@ -736,42 +804,42 @@
         rest_specs = [anywhere] * groups
         out_spec, out_shape = fixed((tokens, model)), acc_shape
         scratch = [pltpu.SemaphoreType.DMA((groups,))]
+        grad_specs = [pl.BlockSpec((rows, 1, dps, 2 * cut, tile), lambda c, i: (0, c, 0, 0, i))]
+        grad_shapes = [jax.ShapeDtypeStruct((rows, cols, dps, 2 * cut, local), jnp.bfloat16)]
     else:
         rest_specs = [anywhere, anywhere, fixed((1, model))]
         out_spec = fixed((groups, span, model))
         out_shape = jax.ShapeDtypeStruct((groups, span, model), jnp.bfloat16)
         scratch = [pltpu.VMEM((tokens, model), jnp.float32), pltpu.SemaphoreType.DMA((2,))]
+        grad_specs = [pl.BlockSpec((1, tokens, tile), lambda c, i: (c, 0, i))] * 2
+        grad_shapes = [jax.ShapeDtypeStruct((cols, tokens, local), jnp.bfloat16)] * 2
+    products = 12 if first else 8
     return pl.pallas_call(
         functools.partial(hidden_kernel, rows, dps, groups, first),
         grid=(cols, local // tile),
         in_specs=[fixed((span, model))] * groups
-        + [fixed((model, span))] * groups
+        + [fixed(part.shape) for part in turned]
         + [
             fixed((tokens, model)),
-            fixed((model, tokens)),
-            pl.BlockSpec((rows, 1, 2, depth, tile), lambda c, i: (0, c, 0, 0, i)),
+            pl.BlockSpec((rows, 1, 2 * depth, tile), lambda c, i: (0, c, 0, i)),
             pl.BlockSpec((1, 1, tile), lambda c, i: (c, 0, i)),
         ]
         + rest_specs,
-        out_specs=[
-            out_spec,
-            fixed((tokens, model)),
-            pl.BlockSpec((rows, 1, dps, 2, cut, tile), lambda c, i: (0, c, 0, 0, 0, i)),
-            pl.BlockSpec((1, 1, tile), lambda c, i: (c, 0, i)),
-        ],
-        out_shape=[
-            out_shape,
-            acc_shape,
-            jax.ShapeDtypeStruct((rows, cols, dps, 2, cut, local), jnp.bfloat16),
-            jax.ShapeDtypeStruct((cols, 1, local), jnp.float32),
-        ],
+        out_specs=[out_spec, fixed((tokens, model))]
+        + grad_specs
+        + [pl.BlockSpec((1, 1, tile), lambda c, i: (c, 0, i))],
+        out_shape=[out_shape, acc_shape]
+        + grad_shapes
+        + [jax.ShapeDtypeStruct((cols, 1, local), jnp.float32)],
         scratch_shapes=scratch,
         compiler_params=params(60),
         cost_estimate=cost(
-            12 * tokens * model * cols * local, 8 * model * cols * local, tokens * cols * local
+            products * tokens * model * cols * local,
+            8 * model * cols * local,
+            tokens * cols * local,
         ),
         name="feed_forward_first" if first else "feed_forward_second",
-    )(*normed, *turned, cot, cot_turned, weight, fc_bias, *rest)
+    )(*normed, *turned, cot, weight, fc_bias, *rest)
 
 
 def middle_back_kernel(
@@ -783,11 +851,11 @@
     dx_ref[...] = total
     low = total.astype(jnp.bfloat16)
     turned_ref[...] = jnp.transpose(low)
-    depth = w_ref.shape[3]
+    depth = w_ref.shape[3] // rows
     for c in range(cols):
-        part = dot_nt(low[:, :depth], w_ref[0, c])
+        part = dot_nt(low[:, :depth], out_block(w_ref, 0, c, rows))
         for r in range(1, rows):
-            part = part + dot_nt(low[:, r * depth : (r + 1) * depth], w_ref[r, c])
+            part = part + dot_nt(low[:, r * depth : (r + 1) * depth], out_block(w_ref, r, c, rows))
         part = part.astype(jnp.bfloat16)
         for r in range(rows):
             datt_ref[r, c] = part[:, r * PAIR : (r + 1) * PAIR]
@@ -812,7 +880,7 @@
             pl.BlockSpec((1, tile, model), lambda i: (g, i, 0)),
             pl.BlockSpec((tile, model), lambda i: (i, 0)),
             pl.BlockSpec((1, tile, model), lambda i: (g, i, 0)),
-            fixed(weight.shape),
+            out_weight_spec(weight),
             fixed(vectors.shape),
         ],
         out_specs=[
@@ -827,28 +895,30 @@
             jax.ShapeDtypeStruct((rows, cols, span, PAIR), jnp.bfloat16),
             jax.ShapeDtypeStruct((8, model), jnp.float32),
         ],
-        compiler_params=params(24),
+        compiler_params=params(60),
         cost_estimate=cost(2 * span * model * model, 2 * model * model + 18 * span * model),
         name="out_norm_back",
     )(grad, middle, cot, weight, vectors)
 
 
 def out_grad_kernel(rows, dps, groups, *refs):
-    out_ref = refs[2 * groups]
+    out_ref = refs[-1]
     total = None
     for g in range(groups):
         att = jnp.concatenate([refs[groups + g][r, 0] for r in range(rows)], axis=1)
         part = dot(refs[g][...], att)
         total = part if total is None else total + part
     total = total.astype(jnp.bfloat16)
-    cut = out_ref.shape[3]
+    half = out_ref.shape[3]
     for r in range(rows):
         for d in range(dps):
-            at = (d * rows + r) * cut
-            out_ref[r, 0, d] = total[at : at + cut]
-
-
-def out_grad(turned, att, dps):
+            at = (d * rows + r) * 2 * half
+            out_ref[r, 0, d] = jnp.concatenate(
+                [total[at : at + half], total[at + half : at + 2 * half]], axis=1
+            )
+
+
+def out_grad(turned, att, before, dps):
     groups = len(turned)
     model, span = turned[0].shape
     rows, cols = att[0].shape[:2]
@@ -857,68 +927,87 @@
         functools.partial(out_grad_kernel, rows, dps, groups),
         grid=(cols,),
         in_specs=[fixed((model, span))] * groups
-        + [pl.BlockSpec((rows, 1, span, PAIR), lambda c: (0, c, 0, 0))] * groups,
-        out_specs=pl.BlockSpec((rows, 1, dps, cut, rows * PAIR), lambda c: (0, c, 0, 0, 0)),
-        out_shape=jax.ShapeDtypeStruct((rows, cols, dps, cut, rows * PAIR), jnp.bfloat16),
-        compiler_params=params(24),
+        + [pl.BlockSpec((rows, 1, span, PAIR), lambda c: (0, c, 0, 0))] * groups
+        + [pl.BlockSpec(memory_space=pl.ANY)],
+        out_specs=pl.BlockSpec(
+            (rows, 1, dps, cut // 2, 2 * rows * PAIR), lambda c: (0, c, 0, 4, 0)
+        ),
+        out_shape=jax.ShapeDtypeStruct(before.shape, before.dtype),
+        compiler_params=params(60),
         cost_estimate=cost(2 * groups * span * model * model, 2 * model * model),
+        input_output_aliases={2 * groups: 0},
         name="out_grad",
-    )(*turned, *att)
-
-
-def qkv_grad_kernel(rows, dps, turned_ref, dqkv_ref, *refs):
-    grad_ref, bias_ref = refs[-2:]
-    cut = grad_ref.shape[4]
-    for part in range(3):
-        lanes = slice(part * PAIR, (part + 1) * PAIR)
-        grads = jnp.concatenate([dqkv_ref[half, 0, :, lanes] for half in range(2)], axis=1)
-        weight_grad = dot(turned_ref[...], grads)
-        for r in range(rows):
-            for d in range(dps):
-                at = (d * rows + r) * cut
-                piece = weight_grad[at : at + cut]
-                if len(refs) == 3:
-                    piece = piece + refs[0][r, 0, d, part]
-                grad_ref[r, 0, d, part] = piece.astype(grad_ref.dtype)
-        bias_ref[0, part] = jnp.sum(grads.astype(jnp.float32), axis=0, keepdims=True)
-
-
-def qkv_grad(dqkv, normed_turned, before, g, final, dps):
-    rows, cols, span, _ = dqkv.shape
-    model = normed_turned.shape[0]
-    width = rows * PAIR
-    cut = model // (rows * dps)
-    grad_spec = pl.BlockSpec((rows, 1, dps, 3, cut, 2 * PAIR), lambda i, c: (0, c, 0, 0, 0, i))
-    grad_type = jnp.bfloat16 if final else jnp.float32
+    )(*turned, *att, before)
+
+
+def qkv_grad_kernel(final, dqkv_ref, x_ref, *refs):
+    grad_ref, bias_ref, acc = refs[-3:]
+    step = pl.program_id(0)
+    grads = dqkv_ref[...]
+    part = lax.dot_general(grads, x_ref[0], TN, preferred_element_type=jnp.float32)
+    sums = jnp.sum(grads.astype(jnp.float32), axis=0, keepdims=True)
+
+    @pl.when(step == 0)
+    def _():
+        acc[...] = refs[0][...] + part if final else part
+        bias_ref[...] = jnp.zeros_like(bias_ref)
+
+    @pl.when(step > 0)
+    def _():
+        acc[...] += part
+
+    bias_ref[0:1] += sums
+
+    @pl.when(step == pl.num_programs(0) - 1)
+    def _():
+        grad_ref[...] = jnp.transpose(acc[...]).astype(grad_ref.dtype) if final else acc[...]
+
+
+def qkv_grad(dqkv, normed, before):
+    tokens, width = dqkv.shape
+    members, _, model = normed.shape
+    final = len(before) == 1
+    tile = tokens // members
+    grad_type = (
+        jax.ShapeDtypeStruct((model, width), jnp.bfloat16)
+        if final
+        else jax.ShapeDtypeStruct((width, model), jnp.float32)
+    )
     return pl.pallas_call(
-        functools.partial(qkv_grad_kernel, rows, dps),
-        grid=(rows // 2, cols),
+        functools.partial(qkv_grad_kernel, final),
+        grid=(tokens // tile,),
         in_specs=[
-            pl.BlockSpec((model, span), lambda i, c: (0, g), pipeline_mode=pl.Buffered(1)),
-            pl.BlockSpec((2, 1, span, 3 * PAIR), lambda i, c: (i, c, 0, 0)),
+            pl.BlockSpec((tile, width), lambda i: (i, 0)),
+            pl.BlockSpec((1, tile, model), lambda i: (i, 0, 0)),
         ]
-        + [grad_spec] * len(before),
-        out_specs=[grad_spec, pl.BlockSpec((1, 3, 1, 2 * PAIR), lambda i, c: (c, 0, 0, i))],
-        out_shape=[
-            jax.ShapeDtypeStruct((rows, cols, dps, 3, cut, width), grad_type),
-            jax.ShapeDtypeStruct((cols, 3, 1, width), jnp.float32),
-        ],
-        compiler_params=params(40),
-        cost_estimate=cost(6 * span * model * model, 24 * model * model),
+        + [fixed((width, model))] * len(before),
+        out_specs=[fixed(grad_type.shape), fixed((8, width))],
+        out_shape=[grad_type, jax.ShapeDtypeStruct((8, width), jnp.float32)],
+        scratch_shapes=[pltpu.VMEM((width, model), jnp.float32)],
+        compiler_params=params(60),
+        cost_estimate=cost(2 * tokens * model * width, 2 * tokens * (model + width)),
         name="qkv_grad",
-    )(normed_turned, dqkv, *before)
-
-
-def input_kernel(rows, dqkv_ref, w_ref, dx_ref, tok_ref, gain_ref, *refs):
+    )(dqkv, normed, *before)
+
+
+def input_kernel(rows, dps, plane_ref, dqkv_ref, left_ref, right_ref, dx_ref, tok_ref, *refs):
+    gain_ref = refs[0]
     out_ref, sum_ref, acc = refs[-3:]
     step = pl.program_id(0) * pl.num_programs(1) + pl.program_id(1)
-    model = acc.shape[1]
-    grads, weights = [], []
+    short = left_ref.shape[3] * 2 // 3
+    grads = []
     for part in range(3):
         lanes = slice(part * PAIR, (part + 1) * PAIR)
         grads += [dqkv_ref[half, 0, :, lanes] for half in range(2)]
-        weights.append(w_ref[:, 0, part].reshape(model, 2 * PAIR))
-    piece = dot_nt(jnp.concatenate(grads, axis=1), jnp.concatenate(weights, axis=1))
+    pieces = []
+    for r in range(rows):
+        for d in range(dps):
+            at = (plane_ref[0] - d) & (dps - 1)
+            left, right = left_ref[at, r, 0], right_ref[at, r, 0]
+            last = jnp.concatenate([left[short:], right[short:]], axis=0)
+            pieces.append(jnp.concatenate([left[:short], right[:short], last], axis=1))
+    weights = jnp.concatenate(pieces, axis=0)
+    piece = dot_nt(jnp.concatenate(grads, axis=1), weights)
 
     @pl.when(step == 0)
     def _():
@@ -937,15 +1026,17 @@
         sum_ref[1:2] = jnp.sum(grad, axis=0, keepdims=True)
 
 
-def input_back(dqkv, dx, tokens, weight, gain, before, g):
-    rows, cols, _, depth, width = weight.shape
+def input_back(plane, dqkv, dx, tokens, weight, gain, before, g):
+    dps, rows, cols, high, _ = weight.shape
     span, model = dx.shape
     return pl.pallas_call(
-        functools.partial(input_kernel, rows),
+        functools.partial(input_kernel, rows, dps),
         grid=(rows // 2, cols),
         in_specs=[
+            pl.BlockSpec(memory_space=pltpu.SMEM),
             pl.BlockSpec((2, 1, span, 3 * PAIR), lambda i, c: (i, c, 0, 0)),
-            pl.BlockSpec((rows, 1, 3, depth, 2 * PAIR), lambda i, c: (0, c, 0, 0, i)),
+            pl.BlockSpec((dps, rows, 1, high, 2 * PAIR), lambda i, c: (0, 0, c, 0, i)),
+            pl.BlockSpec((dps, rows, 1, high, 2 * PAIR), lambda i, c: (0, 0, c, 0, rows // 2 + i)),
             fixed((span, model)),
             pl.BlockSpec((1, span, model), lambda i, c: (g, 0, 0), pipeline_mode=pl.Buffered(1)),
             fixed((1, model)),
@@ -960,11 +1051,11 @@
             jax.ShapeDtypeStruct((8, model), jnp.float32),
         ],
         scratch_shapes=[pltpu.VMEM((span, model), jnp.float32)],
-        compiler_params=params(32),
+        compiler_params=params(60),
         cost_estimate=cost(6 * span * model * model, 6 * model * model + 12 * span * model),
-        input_output_aliases={5: 0} if before else {},
+        input_output_aliases={7: 0} if before else {},
         name="input_back",
-    )(dqkv, weight, dx, tokens, gain, *before)
+    )(plane, dqkv, weight, weight, dx, tokens, gain, *before)
 
 
 def head_body(
@@ -1005,9 +1096,18 @@
         partial = lax.psum_scatter(partial, MESH_AXES, scatter_dimension=0, tiled=True)
         return partial.reshape(partial.shape[1:])
 
+    def exchange_dp(partial):
+        me = lax.axis_index("dp")
+        summed = lax.dynamic_index_in_dim(partial, me, 0, False).astype(jnp.float32)
+        for shift in range(1, dps):
+            piece = lax.dynamic_index_in_dim(partial, (me + shift) % dps, 0, False)
+            pairs = [(i, (i + shift) % dps) for i in range(dps)]
+            summed = summed + lax.ppermute(piece, "dp", pairs).astype(jnp.float32)
+        return summed
+
     def collect_dp(partial):
-        pieces = lax.all_to_all(partial, "dp", 0, 0, tiled=True)
-        return jnp.sum(pieces.astype(jnp.float32), axis=0)
+        partial = lax.psum_scatter(partial, "dp", scatter_dimension=0, tiled=True)
+        return partial[0].astype(jnp.float32)
 
     def total(values):
         for axis in ("row", "col", "dp"):
@@ -1020,125 +1120,177 @@
         return values
 
     half = hidden_cols // 2
-    proj_turned = proj_weight.T
-    shards = [
-        jnp.stack([fc_weight[:, at : at + half], proj_turned[:, at : at + half]])
-        for at in (0, half)
-    ]
-    w_qkv = spread(jnp.transpose(qkv_weight, (1, 0, 2)))
-    biases = lax.all_gather(jnp.concatenate([qv_bias.reshape(-1), fc_bias]), "col", axis=0)
-    qv_full = biases[:, : 2 * head_cols].reshape(cols, 2, 1, head_cols)
-    fc_full = biases[:, 2 * head_cols :].reshape(cols, 1, hidden_cols)
-
     residual = tokens.astype(jnp.float32)
-    normed = normalize(residual, ln1_gain, ln1_bias).astype(jnp.bfloat16).reshape(count, model)
-    normed_turned = normed.T
+    normed = normalize(residual, ln1_gain, ln1_bias).astype(jnp.bfloat16)
+    row = lax.axis_index("row")
+    col = lax.axis_index("col")
+    own = qkv_weight.reshape(-1, 3, rows, PAIR).transpose(2, 0, 1, 3)
+    own = lax.all_to_all(own.reshape(rows, -1, 3 * PAIR), "row", 0, 0, tiled=True)
+    own = own.reshape(model, 3 * PAIR)
+    own_bias = lax.dynamic_slice_in_dim(qv_bias, row * PAIR, PAIR, 1)
+    own_bias = jnp.concatenate([own_bias[0], jnp.zeros((PAIR,), jnp.float32), own_bias[1]])
+    fc_full = lax.all_gather(fc_bias, "col", axis=0).reshape(cols, 1, hidden_cols)
+
+    normed_all = [lax.all_gather(normed[0], MESH_AXES, axis=0, tiled=False)]
     cot_flat = cotangent.reshape(count, model)
     cot_turned = cot_flat.T
     proj_bias_sum = jnp.sum(cot_flat.astype(jnp.float32), axis=0)
-
-    blocks = project_qkv(normed, w_qkv, qv_full, groups)
+    plane = lax.axis_index("dp")
+    short = qkv_weight.shape[0] // dps
+    part = lax.dynamic_slice_in_dim(qkv_weight, plane * short, short, 0)
+    last = jnp.concatenate([part[: short // 2, 2], part[short // 2 :, 2]], axis=1)
+    part = jnp.concatenate([part[:, 0], part[:, 1]], axis=1)
+    later = jnp.concatenate([normed[1], part, last], axis=0)
+    shards = pack_weights(fc_weight, proj_weight, out_weight)
+    normed_all[0], later, cot_turned, proj_bias_sum, shards, own, fc_full = (
+        lax.optimization_barrier(
+            (normed_all[0], later, cot_turned, proj_bias_sum, shards, own, fc_full)
+        )
+    )
+    later = lax.all_gather(later, MESH_AXES, axis=0, tiled=False)
+    normed_all.append(later)
     vectors = jnp.stack([out_bias, ln2_gain, ln2_bias] + [out_bias] * 5)
     gains = jnp.stack([ln2_gain] * 8)
     qkv, att, att_own, log_totals, middle, normed_two, turned_two = [], [], [], [], [], [], []
-    for g in range(groups):
-        received = swap(blocks[g].reshape(members, span, 3 * PAIR))
-        qkv.append(received.reshape(members * span, 3 * PAIR))
-    qkv[-1], out_weight, shards[0], shards[1] = lax.optimization_barrier(
-        (qkv[-1], out_weight, shards[0], shards[1])
-    )
-    w_out = spread(out_weight)
     w_first = spread(shards[0])
     w_second = spread(shards[1])
+    def step_up(value):
+        return lax.ppermute(value, "dp", [(i, i + 1) for i in range(dps - 1)])
+
+    def step_down(value):
+        return lax.ppermute(value, "dp", [(i + 1, i) for i in range(dps - 1)])
+
     for g in range(groups):
+        qkv.append(project_qkv(normed_all[g], own, own_bias, span))
         mixed, totals = attend(branch[g], qkv[g])
+        if g < groups - 1:
+            mixed, normed_all[g + 1] = lax.optimization_barrier((mixed, normed_all[g + 1]))
         att_own.append(mixed)
+        if g > 0:
+            quarter = normed_all[1][:, span:].reshape(rows, cols, -1, model)
+            ups, downs = [step_up(quarter)], [step_down(quarter)]
+            mixed, att[g - 1], ups, downs = lax.optimization_barrier(
+                (mixed, att[g - 1], ups, downs)
+            )
+            ups.append(step_up(ups[-1]))
+            downs.append(step_down(downs[-1]))
         log_totals.append(totals)
         att.append(swap(mixed.reshape(members, span, PAIR)).reshape(rows, cols, span, PAIR))
     for g in range(groups):
-        mid, low, turned = project_out(tokens, att[g], w_out, vectors, g)
+        mid, low, turned = project_out(tokens, att[g], w_first, vectors, g)
         middle.append(mid)
         normed_two.append(low)
         turned_two.append(turned)
-    shared = (normed_two, turned_two, cot_flat, cot_turned)
+    all_turned = turned_two + [cot_turned]
+    normed_two[-1], ups, downs = lax.optimization_barrier((normed_two[-1], ups, downs))
+    ups.append(step_up(ups[-1]))
+    downs.append(step_down(downs[-1]))
     out_part, back_part, grad_first, fc_sum_first = feed_forward(
-        True, *shared, w_first, fc_full[:, :, :half], middle, dps
+        True, normed_two, all_turned, cot_flat, w_first, fc_full[:, :, :half], middle, dps
     )
     plane_first = collect_plane(grad_first)
-    block_out, grad_two, grad_second, fc_sum_second = feed_forward(
+    block_out, grad_two, low, active, fc_sum_second = feed_forward(
         False,
-        *shared,
+        normed_two,
+        [],
+        cot_flat,
         w_second,
         fc_full[:, :, half:],
         (out_part, back_part, proj_bias[None]),
         dps,
     )
-    plane_second = collect_plane(grad_second)
     grad_two = grad_two.reshape(groups, span, model)
     dx, dx_turned, grad_att, sums_two = [], [], [], []
     for g in range(groups):
         rows_grad, turned, datt, sums = middle_back(
-            grad_two, middle[g], cotangent, w_out, gains, g
+            grad_two, middle[g], cotangent, w_first, gains, g
         )
         dx.append(rows_grad)
         dx_turned.append(turned)
         sums_two.append(sums)
+        if g == 0:
+            datt, low, active = lax.optimization_barrier((datt, low, active))
         grad_att.append(
             swap(datt.reshape(members, span, PAIR)).reshape(members * span, PAIR)
         )
-    plane_out = collect_plane(out_grad(dx_turned, att, dps))
-    grad_att[-1], plane_first = lax.optimization_barrier((grad_att[-1], plane_first))
-    grads = []
+    grad_second = hidden_grad(turned_two, cot_turned, low, active, dps, rows)
+    grad_att[0], grad_second = lax.optimization_barrier((grad_att[0], grad_second))
+    plane_second = collect_plane(out_grad(dx_turned, att, grad_second, dps))
+    grads, bias_sums, before = [], [], []
     for g in range(groups):
         grad = attend_back(branch[g], qkv[g], att_own[g], grad_att[g], log_totals[g])
+        if g == 0:
+            grad, grad_att[1], plane_first, ups, downs = lax.optimization_barrier(
+                (grad, grad_att[1], plane_first, ups, downs)
+            )
+            hidden_first = exchange_dp(plane_first)
+        else:
+            grad, hidden_first, grads[0] = lax.optimization_barrier(
+                (grad, hidden_first, grads[0])
+            )
+        grad_qkv, bias_sum = qkv_grad(grad, normed_all[g], before)
+        before = [grad_qkv]
+        bias_sums.append(bias_sum[0])
         grads.append(
             swap(grad.reshape(members, span, 3 * PAIR)).reshape(rows, cols, span, 3 * PAIR)
         )
+    grads[-1], grad_qkv, plane_second = lax.optimization_barrier(
+        (grads[-1], grad_qkv, plane_second)
+    )
+    hidden_second = collect_dp(plane_second)
+    grad_qkv = exchange_dp(grad_qkv.reshape(dps, rows, -1, 3 * PAIR))
+    quarters = [quarter]
+    for shift in range(1, dps):
+        quarters.append(jnp.where(plane >= shift, ups[shift - 1], downs[dps - shift - 1]))
+    w_qkv = jnp.stack(quarters)
+    input_grads, sums_one = [], []
+    for g in range(groups):
+        rows_grad, sums = input_back(
+            plane[None], grads[g], dx[g], tokens, w_qkv, ln1_gain[None], input_grads, g
+        )
+        input_grads = [rows_grad]
+        sums_one.append(sums)
     sums_two = functools.reduce(jnp.add, sums_two)
     fc_sum = jnp.concatenate([fc_sum_first, fc_sum_second], axis=2).reshape(-1)
-    early = (sums_two[2], sums_two[0], sums_two[1], fc_sum, proj_bias_sum)
-    grads[0], plane_second, early = lax.optimization_barrier((grads[0], plane_second, early))
-    early = total(jnp.concatenate(early))
-    input_grads, sums_one, bias_sums, before = [], [], [], []
-    for g in range(groups):
-        grad_qkv, bias_sum = qkv_grad(
-            grads[g], normed_turned, before, g, g == groups - 1, dps
-        )
-        before = [grad_qkv]
-        bias_sums.append(bias_sum)
-        rows_grad, sums = input_back(
-            grads[g], dx[g], tokens, w_qkv, ln1_gain[None], input_grads, g
-        )
-        input_grads = [rows_grad]
-        sums_one.append(sums)
-        if g < groups - 1:
-            grads[g + 1], input_grads, early = lax.optimization_barrier(
-                (grads[g + 1], input_grads, early)
-            )
-    d_qkv = jnp.transpose(collect_dp(collect_plane(grad_qkv)), (1, 0, 2))
-    d_out = collect_dp(plane_out).T
-    d_hidden = jnp.concatenate([collect_dp(plane_first), collect_dp(plane_second)], axis=2)
     sums_one = functools.reduce(jnp.add, sums_one)
     bias_sum = functools.reduce(jnp.add, bias_sums)
-    bias_rows = jnp.transpose(bias_sum[:, :, 0], (1, 0, 2)).reshape(3, model)
-    late = total(jnp.stack([sums_one[0], sums_one[1], bias_rows[0], bias_rows[2]]))
-    s_out, s_gain_two, s_bias_two = (early[i * model : (i + 1) * model] for i in range(3))
-    s_fc = early[3 * model : 3 * model + hidden_cols * cols]
-    s_proj = early[3 * model + hidden_cols * cols :]
+    qv_sum = jnp.zeros((2, model), jnp.float32)
+    qv_sum = lax.dynamic_update_slice(
+        qv_sum,
+        jnp.stack([bias_sum[:PAIR], bias_sum[2 * PAIR :]]),
+        (0, col * head_cols + row * PAIR),
+    )
+    small = (sums_two[2], sums_two[0], sums_two[1], fc_sum, proj_bias_sum)
+    small += (sums_one[0], sums_one[1], qv_sum.reshape(-1))
+    small = total(jnp.concatenate(small))
+    grad_qkv = lax.all_to_all(grad_qkv, "row", 0, 0, tiled=True)
+    d_qkv = grad_qkv.reshape(rows, -1, 3, PAIR).transpose(1, 2, 0, 3).reshape(-1, 3, head_cols)
+    cut = model // (rows * dps)
+    d_fc, d_proj = (
+        jnp.concatenate([hidden_first[at : at + cut], hidden_second[at : at + cut]], axis=1)
+        for at in (0, cut)
+    )
+    packed_out = hidden_second[2 * cut :]
+    d_out = jnp.concatenate([packed_out[:, :head_cols], packed_out[:, head_cols:]], axis=0).T
+    parts, at = [], 0
+    for size in (model, model, model, hidden_cols * cols, model, model, model, 2 * model):
+        parts.append(small[at : at + size])
+        at += size
+    s_out, s_gain_two, s_bias_two, s_fc, s_proj, s_gain_one, s_bias_one, s_qv = parts
     return (
         block_out,
         input_grads[0],
-        late[0],
-        late[1],
+        s_gain_one,
+        s_bias_one,
         d_qkv,
-        late[2:],
+        s_qv.reshape(2, model),
         d_out,
         s_out,
         s_gain_two,
         s_bias_two,
-        d_hidden[0],
+        d_fc,
         s_fc,
-        d_hidden[1].T,
+        d_proj.T,
         s_proj,
     )
 
@@ -1149,7 +1301,9 @@
     def body(tokens, cotangent, branch, ln1_gain, ln1_bias, qkv_weight, *rest):
         width = qkv_weight.shape[2] * cols
         whole = tokens.shape[1] * rows * cols
-        fits = width == rows * cols * PAIR and rows % 2 == 0
+        fits = width == rows * cols * PAIR and rows == 4 and mesh.shape["dp"] == 4 and tokens.shape[0] == 2
+        fits = fits and qkv_weight.shape[0] * 4 == qkv_weight.shape[2] * cols
+        fits = fits and rest[6].shape[0] == 4 * rows * PAIR
         fits = fits and all(size & (size - 1) == 0 for size in mesh.shape.values())
         fits = fits and whole == PLEN + CONTS * CLEN and tokens.shape[1] % BQ == 0
         chosen = head_body if fits else gathered_body

time: 680 us -> 605 us (0.89)
  waiting for transfers between devices: 171 us -> 117 us
  local copies, waits for them, and re-layouts: 71.3 us -> 25 us
  Pallas kernels: 295 us -> 337 us
  blocking collectives: 44.9 us -> 5.32 us
  starting transfers between devices: 62.7 us -> 75.3 us
    unnamed x121 -> x68, local copies, waits for them, and re-layouts: 58.9 us -> 5.22 us
    all_gather x0 -> x2, waiting for transfers between devices: none -> 51.1 us  [the longest x1 34.6 us: head_body(): normed_all = [lax.all_gather(normed[0], MESH_AXES, axis=0, tiled=False)]]
    all_to_all x8 -> x6, waiting for transfers between devices: 59.5 us -> 9.54 us  [swap(): return lax.all_to_all(blocks, MESH_AXES, 0, 0, tiled=True)]
    all_to_all x2 -> x0, blocking collectives: 39.5 us -> none  [collect_dp(): pieces = lax.all_to_all(partial, 'dp', 0, 0, tiled=True)]
    ppermute x10 -> x5, waiting for transfers between devices: 47.4 us -> 8.87 us  [total(): values = values + lax.ppermute(values, axis, pairs)]
    pallas_call x5 -> x8, Pallas kernels: 43 us -> 79 us  [the longest x2 22.5 us: qkv_grad(): pl.pallas_call(functools.partial(qkv_grad_kernel, final), grid=(tokens //...]
    ppermute x0 -> x12, starting transfers between devices: none -> 33.1 us  [the longest x3 14.8 us: step_up(): return lax.ppermute(value, 'dp', [(i, i + 1) for i in range(dps - 1)])]
    all_gather x4 -> x2, waiting for transfers between devices: 51.4 us -> 23.5 us  [spread(): whole = lax.all_gather(shard, MESH_AXES, axis=0, tiled=False)]
  transfers between devices with their start and end apart: 28 -> 32, of which waited for: 14 -> 16; matrix products, arithmetic and copies ran while one was open for 4% -> 6% of each run, Pallas kernels for 43% -> 57%
where the time goes in v3:
time: 605 us; the launch traced here: 595 us
  Pallas kernels  337 us (56%)
  waiting for transfers between devices  117 us (19%)
  starting transfers between devices  75.3 us (12%)
  local copies, waits for them, and re-layouts  25 us (4%)
  other arithmetic  19.5 us (3%)
  between operations  15.3 us (3%)
    pallas_call x2, Pallas kernels, attend_back(): pl.pallas_call(functools.partial(attend_back_kernel, BK_BACK), grid=(toke...  91.8 us
    pallas_call x2, Pallas kernels, attend(): pl.pallas_call(functools.partial(attend_kernel, BK), grid=(blocks,), in_s...  71 us
    pallas_call x2, Pallas kernels, feed_forward(): pl.pallas_call(functools.partial(hidden_kernel, rows, dps, groups, first)...  64 us
    all_gather x1, waiting for transfers between devices, head_body(): normed_all = [lax.all_gather(normed[0], MESH_AXES, axis=0, tiled=False)]  34.6 us
    all_to_all x6, starting transfers between devices, swap(): return lax.all_to_all(blocks, MESH_AXES, 0, 0, tiled=True)  24 us
    all_gather x2, waiting for transfers between devices, spread(): whole = lax.all_gather(shard, MESH_AXES, axis=0, tiled=False)  23.5 us
    pallas_call x2, Pallas kernels, qkv_grad(): pl.pallas_call(functools.partial(qkv_grad_kernel, final), grid=(tokens //...  22.5 us
    pallas_call x2, Pallas kernels, input_back(): pl.pallas_call(functools.partial(input_kernel, rows, dps), grid=(rows //...  22 us
  transfers between devices with their start and end apart: 32, of which 16 were waited for; matrix products, arithmetic and copies ran while one was open for 6% of the time, Pallas kernels for 57%

profile of v3, /device:TPU:0, one launch (start us, length us, event | category | flops | bytes accessed | tf_op | source)
XLA Modules:
  0.0 594.6 jit_solution(17236746742411576736)
XLA Ops:
  15.6 4.2 all-to-all-start
  19.8 5.3 all-gather
  25.2 3.4 pack_weights.1
  28.5 2.5 copy.54
  34.8 4.7 all-to-all-done
  41.8 34.6 %all-gather.9.cloned.1.call-done.x_ref = bf16[8,512,1024]{2,1,0:T(8,128)(2,1)} async-done(((bf16[1,512,1024]{2,1,0:T(8,128)(2,1)}), bf16[8,512,1024]{2,1,0:T(8,128)(2,1)}) %all-gather.9.cloned.1.call-update) | async-done | bytes 8388624 | tf_op jit(solution)/shard_map/all_gather | solution.py:1134
  79.0 8.5 %qkv.2.qkv_ref = bf16[4096,384]{1,0:T(8,128)(2,1)} custom-call(bf16[8,512,1024]{2,1,0:T(8,128)(2,1)} %all-gather.9.cloned.1.call-done.x_ref, bf16[1024,384]{1,0:T(8,128)(2,1)} %bitcast.122, f32[2,384]{1,0:T(2,128)} %pad_maximum_fusion.3.vec_ref), custom_call_target="tpu_custom_call" | custom-call | flops 3221225472 | bytes 11534336 | tf_op jit(solution)/shard_map/qkv/pallas_call | solution.py:394
  87.5 36.0 %attend.2 = (bf16[4096,128]{1,0:T(8,128)(2,1)}, f32[16,8,512]{2,1,0:T(8,128)}) custom-call(s32[8]{0:T(128)} %get-tuple-element.203.cut_ref, bf16[4096,384]{1,0:T(8,128)(2,1)} %qkv.2.qkv_ref), custom_call_target="tpu_custom_call" | custom-call | flops 34359738368 | bytes 4194304 | tf_op jit(solution)/shard_map/attend/pallas_call | solution.py:477
  123.5 16.4 %all-gather.11.cloned.1.call-done = bf16[4864,1024]{1,0:T(8,128)(2,1)} async-done(((bf16[608,1024]{1,0:T(8,128)(2,1)}), bf16[4864,1024]{1,0:T(8,128)(2,1)}) %all-gather.11.cloned.1.call-update) | async-done | bytes 9961488 | tf_op jit(solution)/shard_map/all_gather | solution.py:1150
  141.5 4.7 collective-permute-start
  147.5 3.6 all-to-all-start.1
  151.1 8.9 %qkv.3.qkv_ref = bf16[4096,384]{1,0:T(8,128)(2,1)} custom-call(bf16[8,608,1024]{2,1,0:T(8,128)(2,1)} %bitcast.107, bf16[1024,384]{1,0:T(8,128)(2,1)} %bitcast.123, f32[2,384]{1,0:T(2,128)} %pad_maximum_fusion.3.vec_ref), custom_call_target="tpu_custom_call" | custom-call | flops 3221225472 | bytes 11534336 | tf_op jit(solution)/shard_map/qkv/pallas_call | solution.py:394
  160.0 35.0 %attend.3 = (bf16[4096,128]{1,0:T(8,128)(2,1)}, f32[16,8,512]{2,1,0:T(8,128)}) custom-call(s32[8]{0:T(128)} %get-tuple-element.204.cut_ref, bf16[4096,384]{1,0:T(8,128)(2,1)} %qkv.3.qkv_ref), custom_call_target="tpu_custom_call" | custom-call | flops 34359738368 | bytes 4194304 | tf_op jit(solution)/shard_map/attend/pallas_call | solution.py:477
  195.0 6.7 %collective-permute-start.2 = (bf16[4,2,96,1024]{3,2,1,0:T(8,128)(2,1)}, bf16[4,2,96,1024]{3,2,1,0:T(8,128)(2,1)}, u32[]{:S(2)}, u32[]{:S(2)}) collective-permute-start(bf16[4,2,96,1024]{3,2,1,0:T(8,128)(2,1)} %collective-permute-done), channel_id=1, source_target_pairs={{0,8},{8,16},{16,24},{1,9},{9,17},{17,25},{2,10},{10,18},{18,26},{... | collective-permute-start | bytes 4718600 | tf_op jit(solution)/shard_map/ppermute | solution.py:1158
  203.0 4.0 all-to-all-start.2
  208.3 18.7 %all-gather.13.cloned.1.call-done = bf16[5120,1024]{1,0:T(8,128)(2,1)} async-done(((bf16[640,1024]{1,0:T(8,128)(2,1)}), bf16[5120,1024]{1,0:T(8,128)(2,1)}) %all-gather.13.cloned.1.call-update) | async-done | bytes 10485776 | tf_op jit(solution)/shard_map/all_gather | solution.py:1088
  227.0 5.6 out_norm.2
  233.6 5.7 out_norm.3
  240.2 35.8 %feed_forward_first.1 = (f32[1024,1024]{1,0:T(8,128)}, f32[1024,1024]{1,0:T(8,128)}, bf16[4,2,4,128,1024]{4,3,2,1,0:T(8,128)(2,1)}, f32[2,1,1024]{2,1,0:T(1,128)}) custom-call(bf16[512,1024]{1,0:T(8,128)(2,1)} %get-tuple-element.101.refs_0_, bf16[512,1024]{1,0:T(8,128)(2,1)} %get-tuple-element.106.refs_1_, ...), custom_call_target="tpu_custom_call" | custom-call | flops 25769803776 | bytes 16777216 | tf_op jit(solution)/shard_map/feed_forward_first/pallas_call | solution.py:817
  276.0 4.8 all-gather.15.cloned.1.call-done
  280.8 28.3 %feed_forward_second.1 = (bf16[2,512,1024]{2,1,0:T(8,128)(2,1)}, f32[1024,1024]{1,0:T(8,128)}, bf16[2,1024,1024]{2,1,0:T(8,128)(2,1)}, bf16[2,1024,1024]{2,1,0:T(8,128)(2,1)}, f32[2,1,1024]{2,1,0:T(1,128)}) custom-call(bf16[512,1024]{1,0:T(8,128)(2,1)} %get-tuple-element.101.refs_0_, bf16[512,1024]{1,0:T(8,128)(2,1)} %get-tuple-element.106.refs_1_, ...), custom_call_target="tpu_custom_call" | custom-call | flops 17179869184 | bytes 16777216 | tf_op jit(solution)/shard_map/feed_forward_second/pallas_call | solution.py:817
  309.7 7.0 %out_norm_back.2 = (f32[512,1024]{1,0:T(8,128)}, bf16[1024,512]{1,0:T(8,128)(2,1)}, bf16[4,2,512,128]{3,2,1,0:T(8,128)(2,1)}, f32[8,1024]{1,0:T(8,128)}) custom-call(f32[2,512,1024]{2,1,0:T(8,128)} %bitcast.113, f32[512,1024]{1,0:T(8,128)} %get-tuple-element.112.refs_8_.middle_ref, bf16[2,512,1024]{2,1,0:T(8,128)(2,1)} %cot_ref.3, ...), custom_call_target="tpu_custom_call" | custom-call | flops 1073741824 | bytes 11534336 | tf_op jit(solution)/shard_map/out_norm_back/pallas_call | solution.py:876
  316.6 3.6 all-to-all-start.3
  320.3 7.0 %out_norm_back.3 = (f32[512,1024]{1,0:T(8,128)}, bf16[1024,512]{1,0:T(8,128)(2,1)}, bf16[4,2,512,128]{3,2,1,0:T(8,128)(2,1)}, f32[8,1024]{1,0:T(8,128)}) custom-call(f32[2,512,1024]{2,1,0:T(8,128)} %bitcast.114, f32[512,1024]{1,0:T(8,128)} %get-tuple-element.113.refs_9_.middle_ref, bf16[2,512,1024]{2,1,0:T(8,128)(2,1)} %cot_ref.3, ...), custom_call_target="tpu_custom_call" | custom-call | flops 1073741824 | bytes 11534336 | tf_op jit(solution)/shard_map/out_norm_back/pallas_call | solution.py:876
  327.3 13.7 %hidden_grad.1.refs_4_ = bf16[4,2,4,160,1024]{4,3,2,1,0:T(8,128)(2,1)} custom-call(bf16[1024,512]{1,0:T(8,128)(2,1)} %get-tuple-element.109.refs_2_.refs_0_, bf16[1024,512]{1,0:T(8,128)(2,1)} %get-tuple-element.110.refs_3_.refs_1_, bf16[1024,1024]{1,0:T(8,128)(2,1)} %bitcast.132, bf16[2,1024,1024]{2,1,0:T(8,128)(2,1)} %get-tuple-element.122.refs_3_, ...), custom_call_target="tpu_custom_call" | custom-call | flops 8589934592 | bytes 16777216 | tf_op jit(solution)/shard_map/hidden_grad/pallas_call | solution.py:699
  341.0 4.2 all-to-all-done.3
  345.3 5.9 out_grad.1
  351.3 4.3 all-to-all-start.4
  355.5 3.5 collective-permute-start.4
  360.4 46.1 %attend_back.2.dqkv_ref = bf16[4096,384]{1,0:T(8,128)(2,1)} custom-call(s32[8]{0:T(128)} %get-tuple-element.203.cut_ref, bf16[4096,384]{1,0:T(8,128)(2,1)} %qkv.2.qkv_ref, bf16[4096,128]{1,0:T(8,128)(2,1)} %get-tuple-element.98.o_ref, bf16[4096,128]{1,0:T(8,128)(2,1)} %bitcast.138, f32[16,8,512]{2,1,0:T(8,128)} %get-tuple-element.125.lse_ref), custom_call_target="tpu_custom_call" | custom-call | flops 42949672960 | bytes 8388608 | tf_op jit(solution)/shard_map/attend_back/pallas_call | solution.py:575
  406.6 2.6 dynamic-slice_bitcast_fusion.2
  411.0 7.1 %collective-permute-start.7 = (bf16[128,1024]{1,0:T(8,128)(2,1)}, bf16[128,1024]{1,0:T(8,128)(2,1)}, u32[]{:S(2)}, u32[]{:S(2)}) collective-permute-start(bf16[128,1024]{1,0:T(8,128)(2,1)} %get-tuple-element.170), channel_id=1, source_target_pairs={{0,16},{8,24},{16,0},{24,8},{1,17},{9,25},{17,1},{25,9},{2,18},{10... | collective-permute-start | bytes 786440 | tf_op jit(solution)/shard_map/ppermute | solution.py:1105
  418.1 4.1 all-to-all-start.5
  422.2 45.7 %attend_back.3.dqkv_ref = bf16[4096,384]{1,0:T(8,128)(2,1)} custom-call(s32[8]{0:T(128)} %get-tuple-element.204.cut_ref, bf16[4096,384]{1,0:T(8,128)(2,1)} %qkv.3.qkv_ref, bf16[4096,128]{1,0:T(8,128)(2,1)} %get-tuple-element.102.o_ref, bf16[4096,128]{1,0:T(8,128)(2,1)} %bitcast.33.do_ref, f32[16,8,512]{2,1,0:T(8,128)} %get-tuple-element.133.lse_ref), custom_call_target="tpu_custom_call" | custom-call | flops 42949672960 | bytes 8388608 | tf_op jit(solution)/shard_map/attend_back/pallas_call | solution.py:575
  470.0 2.5 all-to-all-done.5
  474.1 4.4 all-to-all-start.6
  478.8 11.2 %qkv_grad.2 = (f32[384,1024]{1,0:T(8,128)}, f32[8,384]{1,0:T(8,128)}) custom-call(bf16[4096,384]{1,0:T(8,128)(2,1)} %attend_back.2.dqkv_ref, bf16[8,512,1024]{2,1,0:T(8,128)(2,1)} %all-gather.9.cloned.1.call-done.x_ref), custom_call_target="tpu_custom_call" | custom-call | flops 3221225472 | bytes 11534336 | tf_op jit(solution)/shard_map/qkv_grad/pallas_call | solution.py:976
  493.8 3.2 pad_maximum_fusion.left_ref.right_ref
  497.0 11.3 %qkv_grad.3 = (bf16[1024,384]{1,0:T(8,128)(2,1)}, f32[8,384]{1,0:T(8,128)}) custom-call(bf16[4096,384]{1,0:T(8,128)(2,1)} %attend_back.3.dqkv_ref, bf16[8,608,1024]{2,1,0:T(8,128)(2,1)} %bitcast.108, f32[384,1024]{1,0:T(8,128)} %get-tuple-element.137.refs_0_), custom_call_target="tpu_custom_call" | custom-call | flops 3221225472 | bytes 11534336 | tf_op jit(solution)/shard_map/qkv_grad/pallas_call | solution.py:976
  508.3 16.9 %reduce-scatter.6.cloned.1.call-done = bf16[1,4,160,1024]{3,2,1,0:T(8,128)(2,1)} async-done(((bf16[8,4,160,1024]{3,2,1,0:T(8,128)(2,1)}), bf16[1,4,160,1024]{3,2,1,0:T(8,128)(2,1)}) %reduce-scatter.6.cloned.1.call-update) | async-done | bytes 1310736 | tf_op jit(solution)/shard_map/reduce_scatter | solution.py:1096
  525.1 2.8 all-to-all-done.6
  528.7 11.1 %input_back.2 = (f32[2,512,1024]{2,1,0:T(8,128)}, f32[8,1024]{1,0:T(8,128)}) custom-call(s32[1]{0:T(128)} %bitcast.28.plane_ref, bf16[4,2,512,384]{3,2,1,0:T(8,128)(2,1)} %bitcast.115, bf16[4,4,2,96,1024]{4,3,2,1,0:T(8,128)(2,1)} %pad_maximum_fusion.left_ref.right_ref, bf16[4,4,2,96,1024]{4,3,2,1,0:T(8,128)(2,1)} %pad_maximum_fusion.left_ref.right_ref, ...), custom_call_target="tpu_custom_call" | custom-call | flops 3221225472 | bytes 12582912 | tf_op jit(solution)/shard_map/input_back/pallas_call | solution.py:1032
  541.5 2.4 collective-permute-start.15
  545.3 11.0 %input_back.3 = (f32[2,512,1024]{2,1,0:T(8,128)}, f32[8,1024]{1,0:T(8,128)}) custom-call(s32[1]{0:T(128)} %bitcast.28.plane_ref, bf16[4,2,512,384]{3,2,1,0:T(8,128)(2,1)} %bitcast.43.dqkv_ref, bf16[4,4,2,96,1024]{4,3,2,1,0:T(8,128)(2,1)} %pad_maximum_fusion.left_ref.right_ref, ...), custom_call_target="tpu_custom_call", output_to_operand_aliasing={{0}: (7, {})} | custom-call | flops 3221225472 | bytes 12582912 | tf_op jit(solution)/shard_map/input_back/pallas_call | solution.py:1032
  559.9 2.7 collective-permute-done.10
  564.2 2.6 collective-permute-done.11
  568.7 3.5 all-to-all-start.7
  572.2 6.7 %collective-permute-start.13 = (f32[12288]{0:T(1024)S(1)}, f32[12288]{0:T(1024)S(1)}, u32[]{:S(2)}, u32[]{:S(2)}) collective-permute-start(f32[12288]{0:T(1024)S(1)} %add.150), channel_id=1, source_target_pairs={{0,16},{8,24},{16,0},{24,8},{1,17},{9,25},{17,1},{25,9},{2,18},{10... | collective-permute-start | bytes 147464 | tf_op jit(solution)/shard_map/ppermute | solution.py:1118
  (171 shorter events, 55.1 us)
Async XLA Ops:
  7.2 70.6 %copy-start = (f32[2,512]{1,0:T(2,128)S(1)}, f32[2,512]{1,0:T(2,128)}, u32[]{:S(2)}) copy-start(f32[2,512]{1,0:T(2,128)} %param.21) | copy-start | bytes 12292
  7.2 69.2 %all-gather.9.cloned.1.call-start = ((), (), s32[]{:S(2)}) async-start(), calls=%async_computation.11 | async-start | bytes 9437184 | tf_op jit(solution)/shard_map/all_gather | solution.py:1134
  13.4 15.2 %copy-start.3 = (bf16[2,512,1024]{2,1,0:T(8,128)(2,1)S(1)}, bf16[2,512,1024]{2,1,0:T(8,128)(2,1)}, u32[]{:S(2)}) copy-start(bf16[2,512,1024]{2,1,0:T(8,128)(2,1)} %cot_ref.3) | copy-start | bytes 6291460
  15.6 23.9 %all-to-all-start = ((bf16[4,256,384]{1,2,0:T(8,128)(2,1)}), bf16[4,256,384]{1,2,0:T(8,128)(2,1)}, u32[]{:S(2)}, u32[]{:S(2)}) async-start(bf16[4,256,384]{1,2,0:T(8,128)(2,1)} %bitcast.128), calls=%async_computation | async-start | bytes 1572864 | tf_op jit(solution)/shard_map/all_to_all | solution.py:1128
  19.8 120.1 %all-gather.11.cloned.1.call-start = ((), (), s32[]{:S(2)}) async-start(), calls=%async_computation.15 | async-start | bytes 11206656 | tf_op jit(solution)/shard_map/all_gather | solution.py:1150
  34.8 43.7 %copy-start.29 = (s32[2,8]{1,0:T(2,128)S(1)}, s32[2,8]{1,0:T(2,128)}, u32[]{:S(2)}) copy-start(s32[2,8]{1,0:T(2,128)} %param.17) | copy-start | bytes 196
  76.5 150.5 %all-gather.13.cloned.1.call-start = ((), (), s32[]{:S(2)}) async-start(), calls=%async_computation.16 | async-start | bytes 11796480 | tf_op jit(solution)/shard_map/all_gather | solution.py:1088
  77.2 203.6 %all-gather.15.cloned.1.call-start = ((), (), s32[]{:S(2)}) async-start(), calls=%async_computation.17 | async-start | bytes 9437184 | tf_op jit(solution)/shard_map/all_gather | solution.py:1088
  141.5 18.5 %copy-start.7 = (bf16[8,96,1024]{2,1,0:T(8,128)(2,1)}, bf16[8,96,1024]{2,1,0:T(8,128)(2,1)S(1)}, u32[]{:S(2)}) copy-start(bf16[8,96,1024]{2,1,0:T(8,128)(2,1)S(1)} %slice.141) | copy-start | bytes 4718596
  141.5 53.5 %collective-permute-start = (bf16[4,2,96,1024]{3,2,1,0:T(8,128)(2,1)S(1)}, bf16[4,2,96,1024]{3,2,1,0:T(8,128)(2,1)}, u32[]{:S(2)}, u32[]{:S(2)}) collective-permute-start(bf16[4,2,96,1024]{3,2,1,0:T(8,128)(2,1)S(1)} %bitcast.124), channel_id=1, source_target_pairs={{0,8},{8,16},{16,24},{1,9},{9,17},{17,25},{2,10},{10,18},{18,26},{... | collective-permute-start | bytes 4718600 | tf_op jit(solution)/shard_map/ppermute | solution.py:1158
  146.2 48.9 %collective-permute-start.1 = (bf16[4,2,96,1024]{3,2,1,0:T(8,128)(2,1)S(1)}, bf16[4,2,96,1024]{3,2,1,0:T(8,128)(2,1)}, u32[]{:S(2)}, u32[]{:S(2)}) collective-permute-start(bf16[4,2,96,1024]{3,2,1,0:T(8,128)(2,1)S(1)} %bitcast.125), channel_id=1, source_target_pairs={{8,0},{16,8},{24,16},{9,1},{17,9},{25,17},{10,2},{18,10},{26,18},{... | collective-permute-start | bytes 4718600 | tf_op jit(solution)/shard_map/ppermute | solution.py:1161
  147.5 47.6 %all-to-all-start.1 = ((bf16[8,512,128]{2,1,0:T(8,128)(2,1)}), bf16[8,512,128]{2,1,0:T(8,128)(2,1)S(1)}, u32[]{:S(2)}, u32[]{:S(2)}) async-start(bf16[8,512,128]{2,1,0:T(8,128)(2,1)} %bitcast.135), calls=%async_computation.1 | async-start | bytes 2097152 | tf_op jit(solution)/shard_map/all_to_all | solution.py:1092
  160.0 47.1 %copy-start.17 = (f32[1024]{0:T(1024)S(1)}, f32[1024]{0:T(1024)}, u32[]{:S(2)}) copy-start(f32[1024]{0:T(1024)} %param.23) | copy-start | bytes 12292
  160.0 47.1 %copy-start.23 = (f32[1024]{0:T(1024)S(1)}, f32[1024]{0:T(1024)}, u32[]{:S(2)}) copy-start(f32[1024]{0:T(1024)} %param.24) | copy-start | bytes 12292
  160.0 47.1 %copy-start.27 = (f32[1024]{0:T(1024)S(1)}, f32[1024]{0:T(1024)}, u32[]{:S(2)}) copy-start(f32[1024]{0:T(1024)} %param.25) | copy-start | bytes 12292
  195.0 32.0 %copy-start.5 = (bf16[8,512,128]{2,1,0:T(8,128)(2,1)}, bf16[8,512,128]{2,1,0:T(8,128)(2,1)S(1)}, u32[]{:S(2)}) copy-start(bf16[8,512,128]{2,1,0:T(8,128)(2,1)S(1)} %all-to-all-done.1) | copy-start | bytes 3145732
  195.0 44.3 %collective-permute-start.2 = (bf16[4,2,96,1024]{3,2,1,0:T(8,128)(2,1)}, bf16[4,2,96,1024]{3,2,1,0:T(8,128)(2,1)}, u32[]{:S(2)}, u32[]{:S(2)}) collective-permute-start(bf16[4,2,96,1024]{3,2,1,0:T(8,128)(2,1)} %collective-permute-done), channel_id=1, source_target_pairs={{0,8},{8,16},{16,24},{1,9},{9,17},{17,25},{2,10},{10,18},{18,26},{... | collective-permute-start | bytes 4718600 | tf_op jit(solution)/shard_map/ppermute | solution.py:1158
  201.7 38.5 %collective-permute-start.3 = (bf16[4,2,96,1024]{3,2,1,0:T(8,128)(2,1)}, bf16[4,2,96,1024]{3,2,1,0:T(8,128)(2,1)}, u32[]{:S(2)}, u32[]{:S(2)}) collective-permute-start(bf16[4,2,96,1024]{3,2,1,0:T(8,128)(2,1)} %collective-permute-done.1), channel_id=1, source_target_pairs={{8,0},{16,8},{24,16},{9,1},{17,9},{25,17},{10,2},{18,10},{26,18},{... | collective-permute-start | bytes 4718600 | tf_op jit(solution)/shard_map/ppermute | solution.py:1161
  203.0 29.6 %all-to-all-start.2 = ((bf16[8,512,128]{2,1,0:T(8,128)(2,1)}), bf16[8,512,128]{2,1,0:T(8,128)(2,1)S(1)}, u32[]{:S(2)}, u32[]{:S(2)}) async-start(bf16[8,512,128]{2,1,0:T(8,128)(2,1)} %bitcast.134), calls=%async_computation.2 | async-start | bytes 2097152 | tf_op jit(solution)/shard_map/all_to_all | solution.py:1092
  207.0 199.6 %reduce-scatter.4.cloned.1.call-start = ((), (), s32[]{:S(2)}) async-start(), calls=%async_computation.12 | async-start | bytes 9437184 | tf_op jit(solution)/shard_map/reduce_scatter | solution.py:1096
  316.6 28.6 %all-to-all-start.3 = ((bf16[8,512,128]{2,1,0:T(8,128)(2,1)}), bf16[8,512,128]{2,1,0:T(8,128)(2,1)S(1)}, u32[]{:S(2)}, u32[]{:S(2)}) async-start(bf16[8,512,128]{2,1,0:T(8,128)(2,1)} %bitcast.139), calls=%async_computation.3 | async-start | bytes 2097152 | tf_op jit(solution)/shard_map/all_to_all | solution.py:1092
  320.2 204.9 %reduce-scatter.6.cloned.1.call-start = ((), (), s32[]{:S(2)}) async-start(), calls=%async_computation.13 | async-start | bytes 11796480 | tf_op jit(solution)/shard_map/reduce_scatter | solution.py:1096
  351.2 9.2 %copy-start.19 = (f32[8,1024]{1,0:T(8,128)S(1)}, f32[8,1024]{1,0:T(8,128)}, u32[]{:S(2)}) copy-start(f32[8,1024]{1,0:T(8,128)} %get-tuple-element.154) | copy-start | bytes 98308
  351.2 9.2 %copy-start.20 = (f32[8,1024]{1,0:T(8,128)S(1)}, f32[8,1024]{1,0:T(8,128)}, u32[]{:S(2)}) copy-start(f32[8,1024]{1,0:T(8,128)} %get-tuple-element.155) | copy-start | bytes 98308
  351.3 55.2 %all-to-all-start.4 = ((bf16[8,512,128]{2,1,0:T(8,128)(2,1)}), bf16[8,512,128]{2,1,0:T(8,128)(2,1)}, u32[]{:S(2)}, u32[]{:S(2)}) async-start(bf16[8,512,128]{2,1,0:T(8,128)(2,1)} %bitcast.32), calls=%async_computation.4 | async-start | bytes 2097152 | tf_op jit(solution)/shard_map/all_to_all | solution.py:1092
  355.5 51.0 %collective-permute-start.4 = (bf16[4,2,96,1024]{3,2,1,0:T(8,128)(2,1)}, bf16[4,2,96,1024]{3,2,1,0:T(8,128)(2,1)S(1)}, u32[]{:S(2)}, u32[]{:S(2)}) collective-permute-start(bf16[4,2,96,1024]{3,2,1,0:T(8,128)(2,1)} %collective-permute-done.2), channel_id=1, source_target_pairs={{0,8},{8,16},{16,24},{1,9},{9,17},{17,25},{2,10},{10,18},{18,26},{... | collective-permute-start | bytes 4718600 | tf_op jit(solution)/shard_map/ppermute | solution.py:1158
  359.0 47.5 %collective-permute-start.5 = (bf16[4,2,96,1024]{3,2,1,0:T(8,128)(2,1)}, bf16[4,2,96,1024]{3,2,1,0:T(8,128)(2,1)S(1)}, u32[]{:S(2)}, u32[]{:S(2)}) collective-permute-start(bf16[4,2,96,1024]{3,2,1,0:T(8,128)(2,1)} %collective-permute-done.3), channel_id=1, source_target_pairs={{8,0},{16,8},{24,16},{9,1},{17,9},{25,17},{10,2},{18,10},{26,18},{... | collective-permute-start | bytes 4718600 | tf_op jit(solution)/shard_map/ppermute | solution.py:1161
  406.5 11.6 %copy-start.10 = (bf16[4,2,96,1024]{3,2,1,0:T(8,128)(2,1)}, bf16[4,2,96,1024]{3,2,1,0:T(8,128)(2,1)S(1)}, u32[]{:S(2)}) copy-start(bf16[4,2,96,1024]{3,2,1,0:T(8,128)(2,1)S(1)} %collective-permute-done.4) | copy-start | bytes 4718596
  406.5 11.6 %copy-start.12 = (bf16[4,2,96,1024]{3,2,1,0:T(8,128)(2,1)}, bf16[4,2,96,1024]{3,2,1,0:T(8,128)(2,1)S(1)}, u32[]{:S(2)}) copy-start(bf16[4,2,96,1024]{3,2,1,0:T(8,128)(2,1)S(1)} %collective-permute-done.5) | copy-start | bytes 4718596
  409.1 58.7 %collective-permute-start.6 = (bf16[128,1024]{1,0:T(8,128)(2,1)}, bf16[128,1024]{1,0:T(8,128)(2,1)}, u32[]{:S(2)}, u32[]{:S(2)}) collective-permute-start(bf16[128,1024]{1,0:T(8,128)(2,1)} %get-tuple-element.168), channel_id=1, source_target_pairs={{0,8},{8,16},{16,24},{24,0},{1,9},{9,17},{17,25},{25,1},{2,10},{10... | collective-permute-start | bytes 786440 | tf_op jit(solution)/shard_map/ppermute | solution.py:1105
  411.0 56.9 %collective-permute-start.7 = (bf16[128,1024]{1,0:T(8,128)(2,1)}, bf16[128,1024]{1,0:T(8,128)(2,1)}, u32[]{:S(2)}, u32[]{:S(2)}) collective-permute-start(bf16[128,1024]{1,0:T(8,128)(2,1)} %get-tuple-element.170), channel_id=1, source_target_pairs={{0,16},{8,24},{16,0},{24,8},{1,17},{9,25},{17,1},{25,9},{2,18},{10... | collective-permute-start | bytes 786440 | tf_op jit(solution)/shard_map/ppermute | solution.py:1105
  418.1 49.8 %collective-permute-start.8 = (bf16[128,1024]{1,0:T(8,128)(2,1)S(1)}, bf16[128,1024]{1,0:T(8,128)(2,1)}, u32[]{:S(2)}, u32[]{:S(2)}) collective-permute-start(bf16[128,1024]{1,0:T(8,128)(2,1)S(1)} %get-tuple-element.169), channel_id=1, source_target_pairs={{0,24},{8,0},{16,8},{24,16},{1,25},{9,1},{17,9},{25,17},{2,26},{10... | collective-permute-start | bytes 786440 | tf_op jit(solution)/shard_map/ppermute | solution.py:1105
  418.1 54.4 %all-to-all-start.5 = ((bf16[8,512,384]{2,1,0:T(8,128)(2,1)}), bf16[8,512,384]{2,1,0:T(8,128)(2,1)S(1)}, u32[]{:S(2)}, u32[]{:S(2)}) async-start(bf16[8,512,384]{2,1,0:T(8,128)(2,1)} %bitcast.127), calls=%async_computation.6 | async-start | bytes 6291456 | tf_op jit(solution)/shard_map/all_to_all | solution.py:1092
  474.1 53.8 %all-to-all-start.6 = ((bf16[8,512,384]{2,1,0:T(8,128)(2,1)}), bf16[8,512,384]{2,1,0:T(8,128)(2,1)}, u32[]{:S(2)}, u32[]{:S(2)}) async-start(bf16[8,512,384]{2,1,0:T(8,128)(2,1)} %bitcast.116), calls=%async_computation.7 | async-start | bytes 6291456 | tf_op jit(solution)/shard_map/all_to_all | solution.py:1092
  478.6 105.8 %reduce-scatter.8.cloned.1.call-start = ((), (), s32[]{:S(2)}) async-start(), calls=%async_computation.14 | async-start | bytes 1638400 | tf_op jit(solution)/shard_map/reduce_scatter | solution.py:1109
  478.7 11.2 %copy-start.13 = (bf16[4,2,96,1024]{3,2,1,0:T(8,128)(2,1)S(1)}, bf16[4,2,96,1024]{3,2,1,0:T(8,128)(2,1)}, u32[]{:S(2)}) copy-start(bf16[4,2,96,1024]{3,2,1,0:T(8,128)(2,1)} %copy-done.12) | copy-start | bytes 4718596
  528.7 11.1 %copy-start.16 = (bf16[1024,384]{1,0:T(8,128)(2,1)S(1)}, bf16[1024,384]{1,0:T(8,128)(2,1)}, u32[]{:S(2)}) copy-start(bf16[1024,384]{1,0:T(8,128)(2,1)} %get-tuple-element.163) | copy-start | bytes 2359300
  539.9 27.6 %collective-permute-start.14 = (bf16[4,64,384]{2,1,0:T(8,128)(2,1)S(1)}, bf16[4,64,384]{2,1,0:T(8,128)(2,1)S(1)}, u32[]{:S(2)}, u32[]{:S(2)}) collective-permute-start(bf16[4,64,384]{2,1,0:T(8,128)(2,1)S(1)} %get-tuple-element.171), channel_id=1, source_target_pairs={{0,8},{8,16},{16,24},{24,0},{1,9},{9,17},{17,25},{25,1},{2,10},{10... | collective-permute-start | bytes 589832 | tf_op jit(solution)/shard_map/ppermute | solution.py:1105
  541.5 26.2 %collective-permute-start.15 = (bf16[4,64,384]{2,1,0:T(8,128)(2,1)S(1)}, bf16[4,64,384]{2,1,0:T(8,128)(2,1)S(1)}, u32[]{:S(2)}, u32[]{:S(2)}) collective-permute-start(bf16[4,64,384]{2,1,0:T(8,128)(2,1)S(1)} %get-tuple-element.173), channel_id=1, source_target_pairs={{0,16},{8,24},{16,0},{24,8},{1,17},{9,25},{17,1},{25,9},{2,18},{10... | collective-permute-start | bytes 589832 | tf_op jit(solution)/shard_map/ppermute | solution.py:1105
  543.9 24.0 %collective-permute-start.16 = (bf16[4,64,384]{2,1,0:T(8,128)(2,1)S(1)}, bf16[4,64,384]{2,1,0:T(8,128)(2,1)S(1)}, u32[]{:S(2)}, u32[]{:S(2)}) collective-permute-start(bf16[4,64,384]{2,1,0:T(8,128)(2,1)S(1)} %get-tuple-element.172), channel_id=1, source_target_pairs={{0,24},{8,0},{16,8},{24,16},{1,25},{9,1},{17,9},{25,17},{2,26},{10... | collective-permute-start | bytes 589832 | tf_op jit(solution)/shard_map/ppermute | solution.py:1105
  545.3 11.0 %copy-start.21 = (f32[8,1024]{1,0:T(8,128)S(1)}, f32[8,1024]{1,0:T(8,128)}, u32[]{:S(2)}) copy-start(f32[8,1024]{1,0:T(8,128)} %get-tuple-element.159) | copy-start | bytes 98308
  556.3 22.6 %copy-start.9 = (f32[128,1024]{1,0:T(8,128)S(1)}, f32[128,1024]{1,0:T(8,128)}, u32[]{:S(2)}) copy-start(f32[128,1024]{1,0:T(8,128)} %fusion.7) | copy-start | bytes 1572868
  557.2 1.3 collective-permute-start.9
  558.5 4.2 collective-permute-start.10
  562.6 4.2 collective-permute-start.11
  566.8 5.4 collective-permute-start.12
  568.7 14.4 %all-to-all-start.7 = ((f32[4,64,384]{2,1,0:T(8,128)}), f32[4,64,384]{2,1,0:T(8,128)S(1)}, u32[]{:S(2)}, u32[]{:S(2)}) async-start(f32[4,64,384]{2,1,0:T(8,128)} %fusion.9), calls=%async_computation.9 | async-start | bytes 786432 | tf_op jit(solution)/shard_map/all_to_all | solution.py:1266
  572.2 9.0 %collective-permute-start.13 = (f32[12288]{0:T(1024)S(1)}, f32[12288]{0:T(1024)S(1)}, u32[]{:S(2)}, u32[]{:S(2)}) collective-permute-start(f32[12288]{0:T(1024)S(1)} %add.150), channel_id=1, source_target_pairs={{0,16},{8,24},{16,0},{24,8},{1,17},{9,25},{17,1},{25,9},{2,18},{10... | collective-permute-start | bytes 147464 | tf_op jit(solution)/shard_map/ppermute | solution.py:1118
  (14 other events, 51.6 us)
Sparse Core Ops, SparseCore 0:
  12.3 64.1 all-gather.8
  78.9 60.9 all-gather.10
  142.4 84.6 all-gather.12
  228.8 51.9 all-gather.14
  284.1 93.9 reduce-scatter.3
  381.5 143.6 reduce-scatter.5
  528.1 44.8 reduce-scatter.7

commit v4 on v3

--- a/solution.py
+++ b/solution.py
@@ -636,22 +636,22 @@
         for c in range(1, cols):
             total = total + dot(parts[c], out_block(w_ref, r, c, rows))
         pieces.append(total)
-    middle = tok_ref[0].astype(jnp.float32) + jnp.concatenate(pieces, axis=1) + vec_ref[0:1]
+    middle = tok_ref[...].astype(jnp.float32) + jnp.concatenate(pieces, axis=1) + vec_ref[0:1]
     middle_ref[...] = middle
     normed = (centered(middle)[0] * vec_ref[1:2] + vec_ref[2:3]).astype(jnp.bfloat16)
     normed_ref[...] = normed
     turned_ref[...] = jnp.transpose(normed)
 
 
-def project_out(tokens, att, weight, vectors, g):
+def project_out(tokens, att, weight, vectors):
     rows, cols, span, _ = att.shape
-    model = tokens.shape[2]
+    model = tokens.shape[1]
     tile = min(256, span)
     return pl.pallas_call(
         functools.partial(middle_kernel, rows, cols),
         grid=(span // tile,),
         in_specs=[
-            pl.BlockSpec((1, tile, model), lambda i: (g, i, 0)),
+            pl.BlockSpec((tile, model), lambda i: (i, 0)),
             pl.BlockSpec((rows, cols, tile, PAIR), lambda i: (0, 0, i, 0)),
             out_weight_spec(weight),
             fixed(vectors.shape),
@@ -685,22 +685,27 @@
                 grad_ref[r, 0, d, which * cut : (which + 1) * cut] = weight_grad[at : at + cut]
 
 
-def hidden_grad_kernel(rows, dps, *refs):
-    low_ref, active_ref, grad_ref = refs[-3:]
-    store_grads(rows, dps, refs[:-4], refs[-4], low_ref[0], active_ref[0], grad_ref)
+def hidden_grad_kernel(rows, dps, groups, *refs):
+    lows, actives = refs[groups + 1 : 2 * groups + 1], refs[2 * groups + 1 : -1]
+    low_all = jnp.concatenate([ref[0] for ref in lows], axis=0)
+    active_all = jnp.concatenate([ref[0] for ref in actives], axis=0)
+    store_grads(rows, dps, refs[:groups], refs[groups], low_all, active_all, refs[-1])
 
 
 def hidden_grad(turned, cot_turned, low, active, dps, rows):
-    cols, tokens, local = low.shape
+    groups = len(low)
+    cols, span, local = low[0].shape
+    tokens = groups * span
     model = cot_turned.shape[0]
     tile = min(HIDDEN_TILE, local)
     cut = model // (rows * dps)
-    piece = pl.BlockSpec((1, tokens, tile), lambda c, i: (c, 0, i))
+    piece = pl.BlockSpec((1, span, tile), lambda c, i: (c, 0, i))
     return pl.pallas_call(
-        functools.partial(hidden_grad_kernel, rows, dps),
+        functools.partial(hidden_grad_kernel, rows, dps, groups),
         grid=(cols, local // tile),
         in_specs=[fixed(part.shape) for part in turned]
-        + [fixed(cot_turned.shape), piece, piece],
+        + [fixed(cot_turned.shape)]
+        + [piece] * (2 * groups),
         out_specs=pl.BlockSpec((rows, 1, dps, 2 * cut, tile), lambda c, i: (0, c, 0, 0, i)),
         out_shape=jax.ShapeDtypeStruct(
             (rows, cols, dps, 2 * cut + cut // 2, local), jnp.bfloat16
@@ -708,44 +713,43 @@
         compiler_params=params(60),
         cost_estimate=cost(4 * tokens * model * cols * local, 8 * model * cols * local),
         name="hidden_grad",
-    )(*turned, cot_turned, low, active)
+    )(*turned, cot_turned, *low, *active)
 
 
 def hidden_kernel(rows, dps, groups, first, *refs):
     normed_refs, refs = refs[:groups], refs[groups:]
     if first:
         turned_refs, cot_turned_ref, refs = refs[:groups], refs[groups], refs[groups + 1 :]
-    cot_ref, w_ref, fc_bias_ref = refs[:3]
+    cot_refs, refs = refs[:groups], refs[groups:]
+    w_ref, fc_bias_ref = refs[:2]
     if first:
-        middle_refs = refs[3 : groups + 3]
-        out_acc, back_acc, grad_ref, bias_ref, sems = refs[groups + 3 :]
+        starts = refs[2 : groups + 2]
+        out_accs = refs[groups + 2 : 2 * groups + 2]
+        back_accs = refs[2 * groups + 2 : 3 * groups + 2]
+        grad_ref, bias_ref, sems = refs[3 * groups + 2 :]
+        ends = out_accs
     else:
-        prev_out_ref, prev_back_ref, proj_bias_ref = refs[3:6]
-        out_ref, back_acc, low_ref, active_ref, bias_ref, out_acc, sems = refs[6:]
+        proj_bias_ref = refs[4]
+        out_ref, back_acc, low_ref, active_ref, bias_ref, out_acc, sems = refs[5:]
+        starts, ends = refs[2:4], (out_acc, back_acc)
+        out_accs, back_accs = (out_acc,), (back_acc,)
     step = pl.program_id(0) * pl.num_programs(1) + pl.program_id(1)
     last = pl.num_programs(0) * pl.num_programs(1) - 1
-    span, model = normed_refs[0].shape
+    model = normed_refs[0].shape[1]
     tile = w_ref.shape[3]
     depth = model // rows
-    if first:
-        copies = [
-            pltpu.make_async_copy(
-                middle_refs[g], out_acc.at[pl.ds(g * span, span)], sems.at[g]
-            )
-            for g in range(groups)
-        ]
-    else:
-        copies = [
-            pltpu.make_async_copy(prev_out_ref, out_acc, sems.at[0]),
-            pltpu.make_async_copy(prev_back_ref, back_acc, sems.at[1]),
-        ]
+    copies = [
+        pltpu.make_async_copy(start, end, sems.at[at])
+        for at, (start, end) in enumerate(zip(starts, ends))
+    ]
 
     @pl.when(step == 0)
     def _():
         for copy in copies:
             copy.start()
         if first:
-            back_acc[...] = jnp.zeros_like(back_acc)
+            for back_acc in back_accs:
+                back_acc[...] = jnp.zeros_like(back_acc)
 
     fc_weight = w_ref[:, 0, :depth].reshape(model, tile)
     proj_turned = w_ref[:, 0, depth:].reshape(model, tile)
@@ -759,35 +763,38 @@
         actives.append((hidden * plus).astype(jnp.bfloat16))
         bend = 0.5 - 0.5 * inner * inner
         slope = plus + hidden * bend * (root + (3 * root * 0.044715) * square)
-        grad_active = dot(cot_ref[g * span : (g + 1) * span], proj_turned)
+        grad_active = dot(cot_refs[g][...], proj_turned)
         lows.append((grad_active * slope).astype(jnp.bfloat16))
     bias_ref[0] = functools.reduce(
         jnp.add, [jnp.sum(low.astype(jnp.float32), axis=0, keepdims=True) for low in lows]
     )
-    low_all = jnp.concatenate(lows, axis=0)
-    active_all = jnp.concatenate(actives, axis=0)
     if first:
         store_grads(
-            rows, dps, turned_refs, cot_turned_ref, low_all, active_all, grad_ref
+            rows,
+            dps,
+            turned_refs,
+            cot_turned_ref,
+            jnp.concatenate(lows, axis=0),
+            jnp.concatenate(actives, axis=0),
+            grad_ref,
         )
     else:
-        low_ref[0] = low_all
-        active_ref[0] = active_all
+        low_ref[0] = lows[0]
+        active_ref[0] = actives[0]
 
     @pl.when(step == 0)
     def _():
         for copy in copies:
             copy.wait()
 
-    out_acc[...] += dot_nt(active_all, proj_turned)
-    back_acc[...] += dot_nt(low_all, fc_weight)
+    for g in range(groups):
+        out_accs[g][...] += dot_nt(actives[g], proj_turned)
+        back_accs[g][...] += dot_nt(lows[g], fc_weight)
     if not first:
 
         @pl.when(step == last)
         def _():
-            for g in range(groups):
-                at = slice(g * span, (g + 1) * span)
-                out_ref[g] = (out_acc[at] + proj_bias_ref[...]).astype(out_ref.dtype)
+            out_ref[...] = (out_acc[...] + proj_bias_ref[...]).astype(out_ref.dtype)
 
 
 def feed_forward(first, normed, turned, cot, weight, fc_bias, rest, dps):
@@ -798,37 +805,37 @@
     depth = model // rows
     tile = min(HIDDEN_TILE, local)
     cut = model // (rows * dps)
-    acc_shape = jax.ShapeDtypeStruct((tokens, model), jnp.float32)
+    acc_shape = jax.ShapeDtypeStruct((span, model), jnp.float32)
     anywhere = pl.BlockSpec(memory_space=pl.ANY)
+    whole = fixed((span, model))
     if first:
         rest_specs = [anywhere] * groups
-        out_spec, out_shape = fixed((tokens, model)), acc_shape
+        out_shape = [acc_shape] * (2 * groups)
         scratch = [pltpu.SemaphoreType.DMA((groups,))]
         grad_specs = [pl.BlockSpec((rows, 1, dps, 2 * cut, tile), lambda c, i: (0, c, 0, 0, i))]
         grad_shapes = [jax.ShapeDtypeStruct((rows, cols, dps, 2 * cut, local), jnp.bfloat16)]
     else:
         rest_specs = [anywhere, anywhere, fixed((1, model))]
-        out_spec = fixed((groups, span, model))
-        out_shape = jax.ShapeDtypeStruct((groups, span, model), jnp.bfloat16)
-        scratch = [pltpu.VMEM((tokens, model), jnp.float32), pltpu.SemaphoreType.DMA((2,))]
-        grad_specs = [pl.BlockSpec((1, tokens, tile), lambda c, i: (c, 0, i))] * 2
-        grad_shapes = [jax.ShapeDtypeStruct((cols, tokens, local), jnp.bfloat16)] * 2
+        out_shape = [jax.ShapeDtypeStruct((span, model), jnp.bfloat16), acc_shape]
+        scratch = [pltpu.VMEM((span, model), jnp.float32), pltpu.SemaphoreType.DMA((2,))]
+        grad_specs = [pl.BlockSpec((1, span, tile), lambda c, i: (c, 0, i))] * 2
+        grad_shapes = [jax.ShapeDtypeStruct((cols, span, local), jnp.bfloat16)] * 2
     products = 12 if first else 8
     return pl.pallas_call(
         functools.partial(hidden_kernel, rows, dps, groups, first),
         grid=(cols, local // tile),
-        in_specs=[fixed((span, model))] * groups
+        in_specs=[whole] * groups
         + [fixed(part.shape) for part in turned]
+        + [whole] * groups
         + [
-            fixed((tokens, model)),
             pl.BlockSpec((rows, 1, 2 * depth, tile), lambda c, i: (0, c, 0, i)),
             pl.BlockSpec((1, 1, tile), lambda c, i: (c, 0, i)),
         ]
         + rest_specs,
-        out_specs=[out_spec, fixed((tokens, model))]
+        out_specs=[whole] * len(out_shape)
         + grad_specs
         + [pl.BlockSpec((1, 1, tile), lambda c, i: (c, 0, i))],
-        out_shape=[out_shape, acc_shape]
+        out_shape=out_shape
         + grad_shapes
         + [jax.ShapeDtypeStruct((cols, 1, local), jnp.float32)],
         scratch_shapes=scratch,
@@ -839,15 +846,15 @@
             tokens * cols * local,
         ),
         name="feed_forward_first" if first else "feed_forward_second",
-    )(*normed, *turned, cot, weight, fc_bias, *rest)
+    )(*normed, *turned, *cot, weight, fc_bias, *rest)
 
 
 def middle_back_kernel(
     rows, cols, grad_ref, middle_ref, cot_ref, w_ref, vec_ref, dx_ref, turned_ref, datt_ref, sum_ref
 ):
-    grad = grad_ref[0]
+    grad = grad_ref[...]
     unit, inverse = centered(middle_ref[...])
-    total = cot_ref[0].astype(jnp.float32) + norm_back(grad, vec_ref[1:2], unit, inverse)
+    total = cot_ref[...].astype(jnp.float32) + norm_back(grad, vec_ref[1:2], unit, inverse)
     dx_ref[...] = total
     low = total.astype(jnp.bfloat16)
     turned_ref[...] = jnp.transpose(low)
@@ -869,7 +876,7 @@
     sum_ref[2:3] += jnp.sum(low.astype(jnp.float32), axis=0, keepdims=True)
 
 
-def middle_back(grad, middle, cot, weight, vectors, g):
+def middle_back(grad, middle, cot, weight, vectors):
     span, model = middle.shape
     rows, cols = weight.shape[:2]
     tile = min(256, span)
@@ -877,9 +884,9 @@
         functools.partial(middle_back_kernel, rows, cols),
         grid=(span // tile,),
         in_specs=[
-            pl.BlockSpec((1, tile, model), lambda i: (g, i, 0)),
             pl.BlockSpec((tile, model), lambda i: (i, 0)),
-            pl.BlockSpec((1, tile, model), lambda i: (g, i, 0)),
+            pl.BlockSpec((tile, model), lambda i: (i, 0)),
+            pl.BlockSpec((tile, model), lambda i: (i, 0)),
             out_weight_spec(weight),
             fixed(vectors.shape),
         ],
@@ -1134,6 +1141,8 @@
     normed_all = [lax.all_gather(normed[0], MESH_AXES, axis=0, tiled=False)]
     cot_flat = cotangent.reshape(count, model)
     cot_turned = cot_flat.T
+    toks = [tokens[g] for g in range(groups)]
+    cots = [cotangent[g] for g in range(groups)]
     proj_bias_sum = jnp.sum(cot_flat.astype(jnp.float32), axis=0)
     plane = lax.axis_index("dp")
     short = qkv_weight.shape[0] // dps
@@ -1177,7 +1186,7 @@
         log_totals.append(totals)
         att.append(swap(mixed.reshape(members, span, PAIR)).reshape(rows, cols, span, PAIR))
     for g in range(groups):
-        mid, low, turned = project_out(tokens, att[g], w_first, vectors, g)
+        mid, low, turned = project_out(toks[g], att[g], w_first, vectors)
         middle.append(mid)
         normed_two.append(low)
         turned_two.append(turned)
@@ -1185,59 +1194,64 @@
     normed_two[-1], ups, downs = lax.optimization_barrier((normed_two[-1], ups, downs))
     ups.append(step_up(ups[-1]))
     downs.append(step_down(downs[-1]))
-    out_part, back_part, grad_first, fc_sum_first = feed_forward(
-        True, normed_two, all_turned, cot_flat, w_first, fc_full[:, :, :half], middle, dps
-    )
+    first_parts = feed_forward(
+        True, normed_two, all_turned, cots, w_first, fc_full[:, :, :half], middle, dps
+    )
+    grad_first, fc_sum_first = first_parts[2 * groups :]
     plane_first = collect_plane(grad_first)
-    block_out, grad_two, low, active, fc_sum_second = feed_forward(
-        False,
-        normed_two,
-        [],
-        cot_flat,
-        w_second,
-        fc_full[:, :, half:],
-        (out_part, back_part, proj_bias[None]),
-        dps,
-    )
-    grad_two = grad_two.reshape(groups, span, model)
+    block_out, low, active, fc_sums = [], [], [], []
     dx, dx_turned, grad_att, sums_two = [], [], [], []
     for g in range(groups):
+        output_rows, grad_two, low_part, active_part, fc_part = feed_forward(
+            False,
+            [normed_two[g]],
+            [],
+            [cots[g]],
+            w_second,
+            fc_full[:, :, half:],
+            (first_parts[g], first_parts[groups + g], proj_bias[None]),
+            dps,
+        )
+        block_out.append(output_rows)
+        low.append(low_part)
+        active.append(active_part)
+        fc_sums.append(fc_part)
         rows_grad, turned, datt, sums = middle_back(
-            grad_two, middle[g], cotangent, w_first, gains, g
+            grad_two, middle[g], cots[g], w_first, gains
         )
         dx.append(rows_grad)
         dx_turned.append(turned)
         sums_two.append(sums)
         if g == 0:
-            datt, low, active = lax.optimization_barrier((datt, low, active))
+            datt, normed_two[1] = lax.optimization_barrier((datt, normed_two[1]))
         grad_att.append(
             swap(datt.reshape(members, span, PAIR)).reshape(members * span, PAIR)
         )
+    fc_sum_second = functools.reduce(jnp.add, fc_sums)
     grad_second = hidden_grad(turned_two, cot_turned, low, active, dps, rows)
     grad_att[0], grad_second = lax.optimization_barrier((grad_att[0], grad_second))
     plane_second = collect_plane(out_grad(dx_turned, att, grad_second, dps))
-    grads, bias_sums, before = [], [], []
+    rows_back, grads, bias_sums, before = [], [], [], []
     for g in range(groups):
         grad = attend_back(branch[g], qkv[g], att_own[g], grad_att[g], log_totals[g])
         if g == 0:
-            grad, grad_att[1], plane_first, ups, downs = lax.optimization_barrier(
-                (grad, grad_att[1], plane_first, ups, downs)
+            grad, grad_att[1], plane_first = lax.optimization_barrier(
+                (grad, grad_att[1], plane_first)
             )
-            hidden_first = exchange_dp(plane_first)
         else:
-            grad, hidden_first, grads[0] = lax.optimization_barrier(
-                (grad, hidden_first, grads[0])
+            grad, rows_back[0], plane_first, grads[0], ups, downs = lax.optimization_barrier(
+                (grad, rows_back[0], plane_first, grads[0], ups, downs)
             )
-        grad_qkv, bias_sum = qkv_grad(grad, normed_all[g], before)
+        rows_back.append(grad)
+        grads.append(
+            swap(grad.reshape(members, span, 3 * PAIR)).reshape(rows, cols, span, 3 * PAIR)
+        )
+    hidden_first = exchange_dp(plane_first)
+    for g in range(groups):
+        grad_qkv, bias_sum = qkv_grad(rows_back[g], normed_all[g], before)
         before = [grad_qkv]
         bias_sums.append(bias_sum[0])
-        grads.append(
-            swap(grad.reshape(members, span, 3 * PAIR)).reshape(rows, cols, span, 3 * PAIR)
-        )
-    grads[-1], grad_qkv, plane_second = lax.optimization_barrier(
-        (grads[-1], grad_qkv, plane_second)
-    )
-    hidden_second = collect_dp(plane_second)
+    grad_qkv, hidden_first = lax.optimization_barrier((grad_qkv, hidden_first))
     grad_qkv = exchange_dp(grad_qkv.reshape(dps, rows, -1, 3 * PAIR))
     quarters = [quarter]
     for shift in range(1, dps):
@@ -1250,6 +1264,11 @@
         )
         input_grads = [rows_grad]
         sums_one.append(sums)
+        if g == 0:
+            input_grads, grad_qkv, plane_second = lax.optimization_barrier(
+                (input_grads, grad_qkv, plane_second)
+            )
+            hidden_second = collect_dp(plane_second)
     sums_two = functools.reduce(jnp.add, sums_two)
     fc_sum = jnp.concatenate([fc_sum_first, fc_sum_second], axis=2).reshape(-1)
     sums_one = functools.reduce(jnp.add, sums_one)
@@ -1278,7 +1297,7 @@
         at += size
     s_out, s_gain_two, s_bias_two, s_fc, s_proj, s_gain_one, s_bias_one, s_qv = parts
     return (
-        block_out,
+        jnp.stack(block_out),
         input_grads[0],
         s_gain_one,
         s_bias_one,

time: 605 us -> 586 us (0.969)
  waiting for transfers between devices: 117 us -> 86.5 us
  Pallas kernels: 337 us -> 350 us
  starting transfers between devices: 75.3 us -> 63.2 us
  local copies, waits for them, and re-layouts: 25 us -> 31.5 us
  other arithmetic: 19.5 us -> 25.6 us
    reduce_scatter x2, waiting for transfers between devices: 16.9 us -> 0.02 us  [collect_plane(): lax.psum_scatter(partial, MESH_AXES, scatter_dimension=0, tiled=True)]
    all_gather x2, waiting for transfers between devices: 23.5 us -> 10.2 us  [spread(): whole = lax.all_gather(shard, MESH_AXES, axis=0, tiled=False)]
    all_to_all x6, waiting for transfers between devices: 9.54 us -> 0.02 us  [swap(): return lax.all_to_all(blocks, MESH_AXES, 0, 0, tiled=True)]
    pallas_call x2 -> x3, Pallas kernels: 64 us -> 68.9 us  [feed_forward(): pl.pallas_call(functools.partial(hidden_kernel, rows, dps, groups, first)...]
  transfers between devices with their start and end apart: 32 -> 32, of which waited for: 16 -> 13; matrix products, arithmetic and copies ran while one was open for 6% -> 8% of each run, Pallas kernels for 57% -> 61%
where the time goes in v4:
time: 586 us; the launch traced here: 578 us
  Pallas kernels  350 us (60%)
  waiting for transfers between devices  86.5 us (15%)
  starting transfers between devices  63.2 us (11%)
  local copies, waits for them, and re-layouts  31.5 us (5%)
  other arithmetic  25.6 us (4%)
  between operations  15.3 us (3%)
    pallas_call x2, Pallas kernels, attend_back(): pl.pallas_call(functools.partial(attend_back_kernel, BK_BACK), grid=(toke...  97 us
    pallas_call x2, Pallas kernels, attend(): pl.pallas_call(functools.partial(attend_kernel, BK), grid=(blocks,), in_s...  75.4 us
    pallas_call x3, Pallas kernels, feed_forward(): pl.pallas_call(functools.partial(hidden_kernel, rows, dps, groups, first)...  68.9 us
    all_gather x1, waiting for transfers between devices, head_body(): normed_all = [lax.all_gather(normed[0], MESH_AXES, axis=0, tiled=False)]  33.5 us
    all_to_all x6, starting transfers between devices, swap(): return lax.all_to_all(blocks, MESH_AXES, 0, 0, tiled=True)  24.1 us
    pallas_call x2, Pallas kernels, qkv_grad(): pl.pallas_call(functools.partial(qkv_grad_kernel, final), grid=(tokens //...  22.1 us
    pallas_call x2, Pallas kernels, input_back(): pl.pallas_call(functools.partial(input_kernel, rows, dps), grid=(rows //...  22 us
    pallas_call x2, Pallas kernels, project_qkv(): pl.pallas_call(qkv_kernel, grid=(members // 2,), in_specs=[pl.BlockSpec((...  17 us
  transfers between devices with their start and end apart: 32, of which 13 were waited for; matrix products, arithmetic and copies ran while one was open for 8% of the time, Pallas kernels for 61%

profile of v4, /device:TPU:0, one launch (start us, length us, event | category | flops | bytes accessed | tf_op | source)
XLA Modules:
  0.0 577.9 jit_solution(11666192324526008650)
XLA Ops:
  16.5 4.2 all-to-all-start
  20.8 5.3 all-gather
  26.1 3.4 pack_weights.1
  29.5 4.0 copy.46
  36.3 2.5 convert_reduce_fusion.1
  38.8 2.6 all-to-all-done
  43.7 33.5 %all-gather.9.cloned.1.call-done.x_ref = bf16[8,512,1024]{2,1,0:T(8,128)(2,1)} async-done(((bf16[1,512,1024]{2,1,0:T(8,128)(2,1)}), bf16[8,512,1024]{2,1,0:T(8,128)(2,1)}) %all-gather.9.cloned.1.call-update) | async-done | bytes 8388624 | tf_op jit(solution)/shard_map/all_gather | solution.py:1141
  79.7 8.5 %qkv.2.qkv_ref = bf16[4096,384]{1,0:T(8,128)(2,1)} custom-call(bf16[8,512,1024]{2,1,0:T(8,128)(2,1)} %all-gather.9.cloned.1.call-done.x_ref, bf16[1024,384]{1,0:T(8,128)(2,1)} %bitcast.125, f32[2,384]{1,0:T(2,128)} %pad_maximum_fusion.4.vec_ref), custom_call_target="tpu_custom_call" | custom-call | flops 3221225472 | bytes 11534336 | tf_op jit(solution)/shard_map/qkv/pallas_call | solution.py:394
  88.2 37.3 %attend.2 = (bf16[4096,128]{1,0:T(8,128)(2,1)}, f32[16,8,512]{2,1,0:T(8,128)}) custom-call(s32[8]{0:T(128)} %get-tuple-element.225.cut_ref, bf16[4096,384]{1,0:T(8,128)(2,1)} %qkv.2.qkv_ref), custom_call_target="tpu_custom_call" | custom-call | flops 34359738368 | bytes 4194304 | tf_op jit(solution)/shard_map/attend/pallas_call | solution.py:477
  125.5 15.2 %all-gather.11.cloned.1.call-done = bf16[4864,1024]{1,0:T(8,128)(2,1)} async-done(((bf16[608,1024]{1,0:T(8,128)(2,1)}), bf16[4864,1024]{1,0:T(8,128)(2,1)}) %all-gather.11.cloned.1.call-update) | async-done | bytes 9961488 | tf_op jit(solution)/shard_map/all_gather | solution.py:1159
  140.7 2.7 slice.155
  144.6 5.8 collective-permute-start
  150.4 3.6 all-to-all-start.1
  154.0 8.5 %qkv.3.qkv_ref = bf16[4096,384]{1,0:T(8,128)(2,1)} custom-call(bf16[8,608,1024]{2,1,0:T(8,128)(2,1)} %bitcast.116, bf16[1024,384]{1,0:T(8,128)(2,1)} %bitcast.126, f32[2,384]{1,0:T(2,128)} %pad_maximum_fusion.4.vec_ref), custom_call_target="tpu_custom_call" | custom-call | flops 3221225472 | bytes 11534336 | tf_op jit(solution)/shard_map/qkv/pallas_call | solution.py:394
  162.5 38.2 %attend.3 = (bf16[4096,128]{1,0:T(8,128)(2,1)}, f32[16,8,512]{2,1,0:T(8,128)}) custom-call(s32[8]{0:T(128)} %get-tuple-element.226.cut_ref, bf16[4096,384]{1,0:T(8,128)(2,1)} %qkv.3.qkv_ref), custom_call_target="tpu_custom_call" | custom-call | flops 34359738368 | bytes 4194304 | tf_op jit(solution)/shard_map/attend/pallas_call | solution.py:477
  200.7 2.4 collective-permute-start.2
  205.1 4.2 all-to-all-start.2
  209.6 3.1 slice_bitcast_fusion.1
  214.8 8.5 %all-gather.13.cloned.1.call-done = bf16[5120,1024]{1,0:T(8,128)(2,1)} async-done(((bf16[640,1024]{1,0:T(8,128)(2,1)}), bf16[5120,1024]{1,0:T(8,128)(2,1)}) %all-gather.13.cloned.1.call-update) | async-done | bytes 10485776 | tf_op jit(solution)/shard_map/all_gather | solution.py:1095
  223.2 5.4 out_norm.2
  228.6 5.4 out_norm.3
  234.1 2.7 collective-permute-done.2
  236.8 5.2 collective-permute-done.3
  242.0 35.6 %feed_forward_first.1 = (f32[512,1024]{1,0:T(8,128)}, f32[512,1024]{1,0:T(8,128)}, f32[512,1024]{1,0:T(8,128)}, f32[512,1024]{1,0:T(8,128)}, bf16[4,2,4,128,1024...) custom-call(bf16[512,1024]{1,0:T(8,128)(2,1)} %get-tuple-element.110.refs_0_, ...), custom_call_target="tpu_custom_call" | custom-call | flops 25769803776 | bytes 16777216 | tf_op jit(solution)/shard_map/feed_forward_first/pallas_call | solution.py:824
  279.4 16.6 %feed_forward_second.2 = (bf16[512,1024]{1,0:T(8,128)(2,1)}, f32[512,1024]{1,0:T(8,128)}, bf16[2,512,1024]{2,1,0:T(8,128)(2,1)}, bf16[2,512,1024]{2,1,0:T(8,128)(2,1)}, f32[2,1,1024]{2,1,0:T(1,128)}) custom-call(bf16[512,1024]{1,0:T(8,128)(2,1)} %get-tuple-element.110.refs_0_, bf16[512,1024]{1,0:T(8,128)(2,1)} %get-tuple-element.185.refs_5_.refs_1_.cot_ref, ...), custom_call_target="tpu_custom_call" | custom-call | flops 8589934592 | bytes 16777216 | tf_op jit(solution)/shard_map/feed_forward_second/pallas_call | solution.py:824
  296.6 7.2 %out_norm_back.2 = (f32[512,1024]{1,0:T(8,128)}, bf16[1024,512]{1,0:T(8,128)(2,1)}, bf16[4,2,512,128]{3,2,1,0:T(8,128)(2,1)}, f32[8,1024]{1,0:T(8,128)}) custom-call(f32[512,1024]{1,0:T(8,128)} %get-tuple-element.126.grad_ref, f32[512,1024]{1,0:T(8,128)} %get-tuple-element.121.refs_9_.middle_ref, ...), custom_call_target="tpu_custom_call" | custom-call | flops 1073741824 | bytes 11534336 | tf_op jit(solution)/shard_map/out_norm_back/pallas_call | solution.py:883
  303.8 3.8 all-to-all-start.3
  307.7 16.7 %feed_forward_second.3 = (bf16[512,1024]{1,0:T(8,128)(2,1)}, f32[512,1024]{1,0:T(8,128)}, bf16[2,512,1024]{2,1,0:T(8,128)(2,1)}, bf16[2,512,1024]{2,1,0:T(8,128)(2,1)}, f32[2,1,1024]{2,1,0:T(1,128)}) custom-call(bf16[512,1024]{1,0:T(8,128)(2,1)} %get-tuple-element.128.refs_1_.refs_0_, bf16[512,1024]{1,0:T(8,128)(2,1)} %get-tuple-element.184.refs_6_.refs_1_.cot_ref, ...), custom_call_target="tpu_custom_call" | custom-call | flops 8589934592 | bytes 16777216 | tf_op jit(solution)/shard_map/feed_forward_second/pallas_call | solution.py:824
  324.4 6.8 %out_norm_back.3 = (f32[512,1024]{1,0:T(8,128)}, bf16[1024,512]{1,0:T(8,128)(2,1)}, bf16[4,2,512,128]{3,2,1,0:T(8,128)(2,1)}, f32[8,1024]{1,0:T(8,128)}) custom-call(f32[512,1024]{1,0:T(8,128)} %get-tuple-element.139.grad_ref, f32[512,1024]{1,0:T(8,128)} %get-tuple-element.122.refs_10_.middle_ref, ...), custom_call_target="tpu_custom_call" | custom-call | flops 1073741824 | bytes 11534336 | tf_op jit(solution)/shard_map/out_norm_back/pallas_call | solution.py:883
  331.2 14.0 %hidden_grad.1.refs_4_ = bf16[4,2,4,160,1024]{4,3,2,1,0:T(8,128)(2,1)} custom-call(bf16[1024,512]{1,0:T(8,128)(2,1)} %get-tuple-element.118.refs_2_.refs_0_, bf16[1024,512]{1,0:T(8,128)(2,1)} %get-tuple-element.119.refs_3_.refs_1_, bf16[1024,1024]{1,0:T(8,128)(2,1)} %bitcast.132, bf16[2,512,1024]{2,1,0:T(8,128)(2,1)} %get-tuple-element.133.refs_3_, ...), custom_call_target="tpu_custom_call" | custom-call | flops 8589934592 | bytes 16777216 | tf_op jit(solution)/shard_map/hidden_grad/pallas_call | solution.py:703
  345.2 5.8 %out_grad.1 = bf16[4,2,4,160,1024]{4,3,2,1,0:T(8,128)(2,1)} custom-call(bf16[1024,512]{1,0:T(8,128)(2,1)} %get-tuple-element.166.refs_0_, bf16[1024,512]{1,0:T(8,128)(2,1)} %get-tuple-element.167.refs_1_, bf16[4,2,512,128]{3,2,1,0:T(8,128)(2,1)} %bitcast.123, bf16[4,2,512,128]{3,2,1,0:T(8,128)(2,1)} %bitcast.29.att_ref.refs_3_, ...), custom_call_target="tpu_custom_call", output_to_operand_aliasing={{}: (4, {})} | custom-call | flops 2147483648 | bytes 2097152 | tf_op jit(solution)/shard_map/out_grad/pallas_call | solution.py:933
  351.2 4.9 collective-permute-start.4
  357.3 3.9 all-to-all-start.4
  361.4 47.8 %attend_back.2.dqkv_ref = bf16[4096,384]{1,0:T(8,128)(2,1)} custom-call(s32[8]{0:T(128)} %get-tuple-element.225.cut_ref, bf16[4096,384]{1,0:T(8,128)(2,1)} %qkv.2.qkv_ref, bf16[4096,128]{1,0:T(8,128)(2,1)} %get-tuple-element.107.o_ref, bf16[4096,128]{1,0:T(8,128)(2,1)} %bitcast.138, f32[16,8,512]{2,1,0:T(8,128)} %get-tuple-element.138.lse_ref), custom_call_target="tpu_custom_call" | custom-call | flops 42949672960 | bytes 8388608 | tf_op jit(solution)/shard_map/attend_back/pallas_call | solution.py:575
  410.1 4.1 all-to-all-start.5
  414.2 49.2 %attend_back.3.dqkv_ref = bf16[4096,384]{1,0:T(8,128)(2,1)} custom-call(s32[8]{0:T(128)} %get-tuple-element.226.cut_ref, bf16[4096,384]{1,0:T(8,128)(2,1)} %qkv.3.qkv_ref, bf16[4096,128]{1,0:T(8,128)(2,1)} %get-tuple-element.113.o_ref, bf16[4096,128]{1,0:T(8,128)(2,1)} %bitcast.139, f32[16,8,512]{2,1,0:T(8,128)} %get-tuple-element.143.lse_ref), custom_call_target="tpu_custom_call" | custom-call | flops 42949672960 | bytes 8388608 | tf_op jit(solution)/shard_map/attend_back/pallas_call | solution.py:575
  465.1 4.5 all-to-all-start.6
  471.1 3.8 collective-permute-start.8
  476.5 10.8 %qkv_grad.2 = (f32[384,1024]{1,0:T(8,128)}, f32[8,384]{1,0:T(8,128)}) custom-call(bf16[4096,384]{1,0:T(8,128)(2,1)} %attend_back.2.dqkv_ref, bf16[8,512,1024]{2,1,0:T(8,128)(2,1)} %all-gather.9.cloned.1.call-done.x_ref), custom_call_target="tpu_custom_call" | custom-call | flops 3221225472 | bytes 11534336 | tf_op jit(solution)/shard_map/qkv_grad/pallas_call | solution.py:983
  491.1 4.4 pad_maximum_fusion.left_ref.right_ref
  495.5 11.2 %qkv_grad.3 = (bf16[1024,384]{1,0:T(8,128)(2,1)}, f32[8,384]{1,0:T(8,128)}) custom-call(bf16[4096,384]{1,0:T(8,128)(2,1)} %attend_back.3.dqkv_ref, bf16[8,608,1024]{2,1,0:T(8,128)(2,1)} %bitcast.117, f32[384,1024]{1,0:T(8,128)} %get-tuple-element.162.refs_0_), custom_call_target="tpu_custom_call" | custom-call | flops 3221225472 | bytes 11534336 | tf_op jit(solution)/shard_map/qkv_grad/pallas_call | solution.py:983
  509.1 3.8 collective-permute-start.11
  512.9 11.0 %input_back.2 = (f32[2,512,1024]{2,1,0:T(8,128)}, f32[8,1024]{1,0:T(8,128)}) custom-call(s32[1]{0:T(128)} %bitcast.34.plane_ref, bf16[4,2,512,384]{3,2,1,0:T(8,128)(2,1)} %bitcast.121, bf16[4,4,2,96,1024]{4,3,2,1,0:T(8,128)(2,1)} %pad_maximum_fusion.left_ref.right_ref, bf16[4,4,2,96,1024]{4,3,2,1,0:T(8,128)(2,1)} %pad_maximum_fusion.left_ref.right_ref, ...), custom_call_target="tpu_custom_call" | custom-call | flops 3221225472 | bytes 12582912 | tf_op jit(solution)/shard_map/input_back/pallas_call | solution.py:1039
  523.9 5.4 collective-permute-done.10
  531.9 11.0 %input_back.3 = (f32[2,512,1024]{2,1,0:T(8,128)}, f32[8,1024]{1,0:T(8,128)}) custom-call(s32[1]{0:T(128)} %bitcast.34.plane_ref, bf16[4,2,512,384]{3,2,1,0:T(8,128)(2,1)} %bitcast.44.dqkv_ref, bf16[4,4,2,96,1024]{4,3,2,1,0:T(8,128)(2,1)} %pad_maximum_fusion.left_ref.right_ref, ...), custom_call_target="tpu_custom_call", output_to_operand_aliasing={{0}: (7, {})} | custom-call | flops 3221225472 | bytes 12582912 | tf_op jit(solution)/shard_map/input_back/pallas_call | solution.py:1039
  546.9 2.4 collective-permute-done.13
  551.0 3.5 all-to-all-start.7
  556.1 3.0 collective-permute-done.15
  (163 shorter events, 59.3 us)
Async XLA Ops:
  7.2 71.4 %copy-start = (f32[2,512]{1,0:T(2,128)S(1)}, f32[2,512]{1,0:T(2,128)}, u32[]{:S(2)}) copy-start(f32[2,512]{1,0:T(2,128)} %param.21) | copy-start | bytes 12292
  7.2 70.0 %all-gather.9.cloned.1.call-start = ((), (), s32[]{:S(2)}) async-start(), calls=%async_computation.11 | async-start | bytes 9437184 | tf_op jit(solution)/shard_map/all_gather | solution.py:1141
  12.2 8.6 %copy-start.16 = (f32[2048]{0:T(1024)S(1)}, f32[2048]{0:T(1024)}, u32[]{:S(2)}) copy-start(f32[2048]{0:T(1024)} %param.27) | copy-start | bytes 24580
  16.5 24.9 %all-to-all-start = ((bf16[4,256,384]{1,2,0:T(8,128)(2,1)}), bf16[4,256,384]{1,2,0:T(8,128)(2,1)}, u32[]{:S(2)}, u32[]{:S(2)}) async-start(bf16[4,256,384]{1,2,0:T(8,128)(2,1)} %bitcast.128), calls=%async_computation | async-start | bytes 1572864 | tf_op jit(solution)/shard_map/all_to_all | solution.py:1135
  20.8 119.9 %all-gather.11.cloned.1.call-start = ((), (), s32[]{:S(2)}) async-start(), calls=%async_computation.15 | async-start | bytes 11206656 | tf_op jit(solution)/shard_map/all_gather | solution.py:1159
  43.7 35.5 %copy-start.22 = (s32[2,8]{1,0:T(2,128)S(1)}, s32[2,8]{1,0:T(2,128)}, u32[]{:S(2)}) copy-start(s32[2,8]{1,0:T(2,128)} %param.17) | copy-start | bytes 196
  77.2 146.0 %all-gather.13.cloned.1.call-start = ((), (), s32[]{:S(2)}) async-start(), calls=%async_computation.16 | async-start | bytes 11796480 | tf_op jit(solution)/shard_map/all_gather | solution.py:1095
  78.0 201.4 %all-gather.15.cloned.1.call-start = ((), (), s32[]{:S(2)}) async-start(), calls=%async_computation.17 | async-start | bytes 9437184 | tf_op jit(solution)/shard_map/all_gather | solution.py:1095
  143.4 57.3 %collective-permute-start.1 = (bf16[4,2,96,1024]{3,2,1,0:T(8,128)(2,1)}, bf16[4,2,96,1024]{3,2,1,0:T(8,128)(2,1)}, u32[]{:S(2)}, u32[]{:S(2)}) collective-permute-start(bf16[4,2,96,1024]{3,2,1,0:T(8,128)(2,1)} %bitcast.20), channel_id=1, source_target_pairs={{8,0},{16,8},{24,16},{9,1},{17,9},{25,17},{10,2},{18,10},{26,18},{... | collective-permute-start | bytes 4718600 | tf_op jit(solution)/shard_map/ppermute | solution.py:1170
  144.6 56.0 %collective-permute-start = (bf16[4,2,96,1024]{3,2,1,0:T(8,128)(2,1)}, bf16[4,2,96,1024]{3,2,1,0:T(8,128)(2,1)}, u32[]{:S(2)}, u32[]{:S(2)}) collective-permute-start(bf16[4,2,96,1024]{3,2,1,0:T(8,128)(2,1)} %bitcast.20), channel_id=1, source_target_pairs={{0,8},{8,16},{16,24},{1,9},{9,17},{17,25},{2,10},{10,18},{18,26},{... | collective-permute-start | bytes 4718600 | tf_op jit(solution)/shard_map/ppermute | solution.py:1167
  150.4 50.3 %all-to-all-start.1 = ((bf16[8,512,128]{2,1,0:T(8,128)(2,1)}), bf16[8,512,128]{2,1,0:T(8,128)(2,1)S(1)}, u32[]{:S(2)}, u32[]{:S(2)}) async-start(bf16[8,512,128]{2,1,0:T(8,128)(2,1)} %bitcast.134), calls=%async_computation.1 | async-start | bytes 2097152 | tf_op jit(solution)/shard_map/all_to_all | solution.py:1099
  162.5 41.9 %copy-start.9 = (f32[1024]{0:T(1024)S(1)}, f32[1024]{0:T(1024)}, u32[]{:S(2)}) copy-start(f32[1024]{0:T(1024)} %param.23) | copy-start | bytes 12292
  162.5 41.9 %copy-start.15 = (f32[1024]{0:T(1024)S(1)}, f32[1024]{0:T(1024)}, u32[]{:S(2)}) copy-start(f32[1024]{0:T(1024)} %param.24) | copy-start | bytes 12292
  162.5 41.9 %copy-start.20 = (f32[1024]{0:T(1024)S(1)}, f32[1024]{0:T(1024)}, u32[]{:S(2)}) copy-start(f32[1024]{0:T(1024)} %param.25) | copy-start | bytes 12292
  200.7 12.0 %copy-start.4 = (bf16[8,512,128]{2,1,0:T(8,128)(2,1)}, bf16[8,512,128]{2,1,0:T(8,128)(2,1)S(1)}, u32[]{:S(2)}) copy-start(bf16[8,512,128]{2,1,0:T(8,128)(2,1)S(1)} %all-to-all-done.1) | copy-start | bytes 3145732
  200.7 36.1 %collective-permute-start.2 = (bf16[4,2,96,1024]{3,2,1,0:T(8,128)(2,1)}, bf16[4,2,96,1024]{3,2,1,0:T(8,128)(2,1)}, u32[]{:S(2)}, u32[]{:S(2)}) collective-permute-start(bf16[4,2,96,1024]{3,2,1,0:T(8,128)(2,1)} %collective-permute-done), channel_id=1, source_target_pairs={{0,8},{8,16},{16,24},{1,9},{9,17},{17,25},{2,10},{10,18},{18,26},{... | collective-permute-start | bytes 4718600 | tf_op jit(solution)/shard_map/ppermute | solution.py:1167
  203.1 38.9 %collective-permute-start.3 = (bf16[4,2,96,1024]{3,2,1,0:T(8,128)(2,1)}, bf16[4,2,96,1024]{3,2,1,0:T(8,128)(2,1)}, u32[]{:S(2)}, u32[]{:S(2)}) collective-permute-start(bf16[4,2,96,1024]{3,2,1,0:T(8,128)(2,1)} %collective-permute-done.1), channel_id=1, source_target_pairs={{8,0},{16,8},{24,16},{9,1},{17,9},{25,17},{10,2},{18,10},{26,18},{... | collective-permute-start | bytes 4718600 | tf_op jit(solution)/shard_map/ppermute | solution.py:1170
  205.1 23.5 %all-to-all-start.2 = ((bf16[8,512,128]{2,1,0:T(8,128)(2,1)}), bf16[8,512,128]{2,1,0:T(8,128)(2,1)}, u32[]{:S(2)}, u32[]{:S(2)}) async-start(bf16[8,512,128]{2,1,0:T(8,128)(2,1)} %bitcast.137), calls=%async_computation.2 | async-start | bytes 2097152 | tf_op jit(solution)/shard_map/all_to_all | solution.py:1099
  209.3 199.8 %reduce-scatter.4.cloned.1.call-start = ((), (), s32[]{:S(2)}) async-start(), calls=%async_computation.12 | async-start | bytes 9437184 | tf_op jit(solution)/shard_map/reduce_scatter | solution.py:1103
  303.8 41.4 %all-to-all-start.3 = ((bf16[8,512,128]{2,1,0:T(8,128)(2,1)}), bf16[8,512,128]{2,1,0:T(8,128)(2,1)S(1)}, u32[]{:S(2)}, u32[]{:S(2)}) async-start(bf16[8,512,128]{2,1,0:T(8,128)(2,1)} %bitcast.140), calls=%async_computation.3 | async-start | bytes 2097152 | tf_op jit(solution)/shard_map/all_to_all | solution.py:1099
  307.6 223.4 %reduce-scatter.6.cloned.1.call-start = ((), (), s32[]{:S(2)}) async-start(), calls=%async_computation.13 | async-start | bytes 11796480 | tf_op jit(solution)/shard_map/reduce_scatter | solution.py:1103
  351.0 10.2 %copy-start.17 = (f32[2,1,1024]{2,1,0:T(1,128)S(1)}, f32[2,1,1024]{2,1,0:T(1,128)}, u32[]{:S(2)}) copy-start(f32[2,1,1024]{2,1,0:T(1,128)} %get-tuple-element.174) | copy-start | bytes 24580
  351.1 10.2 %copy-start.18 = (f32[2,1,1024]{2,1,0:T(1,128)S(1)}, f32[2,1,1024]{2,1,0:T(1,128)}, u32[]{:S(2)}) copy-start(f32[2,1,1024]{2,1,0:T(1,128)} %get-tuple-element.175) | copy-start | bytes 24580
  351.1 10.2 %copy-start.11 = (f32[8,1024]{1,0:T(8,128)S(1)}, f32[8,1024]{1,0:T(8,128)}, u32[]{:S(2)}) copy-start(f32[8,1024]{1,0:T(8,128)} %get-tuple-element.171) | copy-start | bytes 98308
  351.1 10.2 %copy-start.12 = (f32[8,1024]{1,0:T(8,128)S(1)}, f32[8,1024]{1,0:T(8,128)}, u32[]{:S(2)}) copy-start(f32[8,1024]{1,0:T(8,128)} %get-tuple-element.172) | copy-start | bytes 98308
  351.1 10.2 %copy-start.19 = (f32[2,1,1024]{2,1,0:T(1,128)S(1)}, f32[2,1,1024]{2,1,0:T(1,128)}, u32[]{:S(2)}) copy-start(f32[2,1,1024]{2,1,0:T(1,128)} %get-tuple-element.173) | copy-start | bytes 24580
  351.2 112.3 %collective-permute-start.4 = (bf16[4,2,96,1024]{3,2,1,0:T(8,128)(2,1)}, bf16[4,2,96,1024]{3,2,1,0:T(8,128)(2,1)}, u32[]{:S(2)}, u32[]{:S(2)}) collective-permute-start(bf16[4,2,96,1024]{3,2,1,0:T(8,128)(2,1)} %collective-permute-done.2), channel_id=1, source_target_pairs={{0,8},{8,16},{16,24},{1,9},{9,17},{17,25},{2,10},{10,18},{18,26},{... | collective-permute-start | bytes 4718600 | tf_op jit(solution)/shard_map/ppermute | solution.py:1167
  356.0 107.4 %collective-permute-start.5 = (bf16[4,2,96,1024]{3,2,1,0:T(8,128)(2,1)}, bf16[4,2,96,1024]{3,2,1,0:T(8,128)(2,1)}, u32[]{:S(2)}, u32[]{:S(2)}) collective-permute-start(bf16[4,2,96,1024]{3,2,1,0:T(8,128)(2,1)} %collective-permute-done.3), channel_id=1, source_target_pairs={{8,0},{16,8},{24,16},{9,1},{17,9},{25,17},{10,2},{18,10},{26,18},{... | collective-permute-start | bytes 4718600 | tf_op jit(solution)/shard_map/ppermute | solution.py:1170
  357.3 51.8 %all-to-all-start.4 = ((bf16[8,512,128]{2,1,0:T(8,128)(2,1)}), bf16[8,512,128]{2,1,0:T(8,128)(2,1)S(1)}, u32[]{:S(2)}, u32[]{:S(2)}) async-start(bf16[8,512,128]{2,1,0:T(8,128)(2,1)} %bitcast.37), calls=%async_computation.4 | async-start | bytes 2097152 | tf_op jit(solution)/shard_map/all_to_all | solution.py:1099
  410.1 53.3 %all-to-all-start.5 = ((bf16[8,512,384]{2,1,0:T(8,128)(2,1)}), bf16[8,512,384]{2,1,0:T(8,128)(2,1)S(1)}, u32[]{:S(2)}, u32[]{:S(2)}) async-start(bf16[8,512,384]{2,1,0:T(8,128)(2,1)} %bitcast.127), calls=%async_computation.6 | async-start | bytes 6291456 | tf_op jit(solution)/shard_map/all_to_all | solution.py:1099
  465.1 66.8 %all-to-all-start.6 = ((bf16[8,512,384]{2,1,0:T(8,128)(2,1)}), bf16[8,512,384]{2,1,0:T(8,128)(2,1)}, u32[]{:S(2)}, u32[]{:S(2)}) async-start(bf16[8,512,384]{2,1,0:T(8,128)(2,1)} %bitcast.120), calls=%async_computation.7 | async-start | bytes 6291456 | tf_op jit(solution)/shard_map/all_to_all | solution.py:1099
  469.6 97.5 %reduce-scatter.8.cloned.1.call-start = ((), (), s32[]{:S(2)}) async-start(), calls=%async_computation.14 | async-start | bytes 1638400 | tf_op jit(solution)/shard_map/reduce_scatter | solution.py:1116
  470.8 35.9 %collective-permute-start.6 = (bf16[128,1024]{1,0:T(8,128)(2,1)S(1)}, bf16[128,1024]{1,0:T(8,128)(2,1)S(1)}, u32[]{:S(2)}, u32[]{:S(2)}) collective-permute-start(bf16[128,1024]{1,0:T(8,128)(2,1)S(1)} %get-tuple-element.190), channel_id=1, source_target_pairs={{0,8},{8,16},{16,24},{24,0},{1,9},{9,17},{17,25},{25,1},{2,10},{10... | collective-permute-start | bytes 786440 | tf_op jit(solution)/shard_map/ppermute | solution.py:1112
  471.1 35.6 %collective-permute-start.8 = (bf16[128,1024]{1,0:T(8,128)(2,1)S(1)}, bf16[128,1024]{1,0:T(8,128)(2,1)S(1)}, u32[]{:S(2)}, u32[]{:S(2)}) collective-permute-start(bf16[128,1024]{1,0:T(8,128)(2,1)S(1)} %get-tuple-element.191), channel_id=1, source_target_pairs={{0,24},{8,0},{16,8},{24,16},{1,25},{9,1},{17,9},{25,17},{2,26},{10... | collective-permute-start | bytes 786440 | tf_op jit(solution)/shard_map/ppermute | solution.py:1112
  474.9 31.8 %collective-permute-start.7 = (bf16[128,1024]{1,0:T(8,128)(2,1)S(1)}, bf16[128,1024]{1,0:T(8,128)(2,1)S(1)}, u32[]{:S(2)}, u32[]{:S(2)}) collective-permute-start(bf16[128,1024]{1,0:T(8,128)(2,1)S(1)} %get-tuple-element.192), channel_id=1, source_target_pairs={{0,16},{8,24},{16,0},{24,8},{1,17},{9,25},{17,1},{25,9},{2,18},{10... | collective-permute-start | bytes 786440 | tf_op jit(solution)/shard_map/ppermute | solution.py:1112
  509.0 14.8 %collective-permute-start.9 = (bf16[4,64,384]{2,1,0:T(8,128)(2,1)S(1)}, bf16[4,64,384]{2,1,0:T(8,128)(2,1)S(1)}, u32[]{:S(2)}, u32[]{:S(2)}) collective-permute-start(bf16[4,64,384]{2,1,0:T(8,128)(2,1)S(1)} %get-tuple-element.193), channel_id=1, source_target_pairs={{0,8},{8,16},{16,24},{24,0},{1,9},{9,17},{17,25},{25,1},{2,10},{10... | collective-permute-start | bytes 589832 | tf_op jit(solution)/shard_map/ppermute | solution.py:1112
  509.1 14.8 %collective-permute-start.11 = (bf16[4,64,384]{2,1,0:T(8,128)(2,1)S(1)}, bf16[4,64,384]{2,1,0:T(8,128)(2,1)S(1)}, u32[]{:S(2)}, u32[]{:S(2)}) collective-permute-start(bf16[4,64,384]{2,1,0:T(8,128)(2,1)S(1)} %get-tuple-element.194), channel_id=1, source_target_pairs={{0,24},{8,0},{16,8},{24,16},{1,25},{9,1},{17,9},{25,17},{2,26},{10... | collective-permute-start | bytes 589832 | tf_op jit(solution)/shard_map/ppermute | solution.py:1112
  512.9 16.3 %collective-permute-start.10 = (bf16[4,64,384]{2,1,0:T(8,128)(2,1)S(1)}, bf16[4,64,384]{2,1,0:T(8,128)(2,1)S(1)}, u32[]{:S(2)}, u32[]{:S(2)}) collective-permute-start(bf16[4,64,384]{2,1,0:T(8,128)(2,1)S(1)} %get-tuple-element.195), channel_id=1, source_target_pairs={{0,16},{8,24},{16,0},{24,8},{1,17},{9,25},{17,1},{25,9},{2,18},{10... | collective-permute-start | bytes 589832 | tf_op jit(solution)/shard_map/ppermute | solution.py:1112
  523.9 7.2 %copy-start.14 = (f32[1024]{0:T(1024)S(1)}, f32[1024]{0:T(1024)}, u32[]{:S(2)}) copy-start(f32[1024]{0:T(1024)} %convert_reduce_fusion.1) | copy-start | bytes 12292
  531.9 11.1 %copy-start.13 = (f32[8,1024]{1,0:T(8,128)S(1)}, f32[8,1024]{1,0:T(8,128)}, u32[]{:S(2)}) copy-start(f32[8,1024]{1,0:T(8,128)} %get-tuple-element.177) | copy-start | bytes 98308
  531.9 22.7 %copy-start.8 = (bf16[512,1024]{1,0:T(8,128)(2,1)S(1)}, bf16[512,1024]{1,0:T(8,128)(2,1)}, u32[]{:S(2)}) copy-start(bf16[512,1024]{1,0:T(8,128)(2,1)} %get-tuple-element.131) | copy-start | bytes 3145732
  543.0 11.7 %copy-start.7 = (bf16[512,1024]{1,0:T(8,128)(2,1)S(1)}, bf16[512,1024]{1,0:T(8,128)(2,1)}, u32[]{:S(2)}) copy-start(bf16[512,1024]{1,0:T(8,128)(2,1)} %get-tuple-element.125) | copy-start | bytes 3145732
  543.9 1.3 collective-permute-start.12
  545.2 4.2 collective-permute-start.13
  549.3 5.2 collective-permute-start.14
  551.0 10.8 %all-to-all-start.7 = ((f32[4,64,384]{2,1,0:T(8,128)}), f32[4,64,384]{2,1,0:T(8,128)S(1)}, u32[]{:S(2)}, u32[]{:S(2)}) async-start(f32[4,64,384]{2,1,0:T(8,128)} %fusion.9), calls=%async_computation.9 | async-start | bytes 786432 | tf_op jit(solution)/shard_map/all_to_all | solution.py:1285
  554.5 4.7 collective-permute-start.15
  559.2 6.0 %collective-permute-start.16 = (f32[12288]{0:T(1024)S(1)}, f32[12288]{0:T(1024)S(1)}, u32[]{:S(2)}, u32[]{:S(2)}) collective-permute-start(f32[12288]{0:T(1024)S(1)} %add.157), channel_id=1, source_target_pairs={{0,16},{8,24},{16,0},{24,8},{1,17},{9,25},{17,1},{25,9},{2,18},{10... | collective-permute-start | bytes 147464 | tf_op jit(solution)/shard_map/ppermute | solution.py:1125
  (7 other events, 20.0 us)
Sparse Core Ops, SparseCore 0:
  12.3 64.8 all-gather.8
  79.7 60.9 all-gather.10
  143.1 80.0 all-gather.12
  225.0 54.3 all-gather.14
  282.7 82.7 reduce-scatter.3
  368.8 108.6 reduce-scatter.5
  531.2 31.3 reduce-scatter.7

commit v5 on v4

--- a/solution.py
+++ b/solution.py
@@ -951,7 +951,8 @@
     grad_ref, bias_ref, acc = refs[-3:]
     step = pl.program_id(0)
     grads = dqkv_ref[...]
-    part = lax.dot_general(grads, x_ref[0], TN, preferred_element_type=jnp.float32)
+    rows = x_ref[...].reshape(grads.shape[0], x_ref.shape[2])
+    part = lax.dot_general(grads, rows, TN, preferred_element_type=jnp.float32)
     sums = jnp.sum(grads.astype(jnp.float32), axis=0, keepdims=True)
 
     @pl.when(step == 0)
@@ -974,7 +975,7 @@
     tokens, width = dqkv.shape
     members, _, model = normed.shape
     final = len(before) == 1
-    tile = tokens // members
+    tile = 2 * tokens // members
     grad_type = (
         jax.ShapeDtypeStruct((model, width), jnp.bfloat16)
         if final
@@ -985,7 +986,7 @@
         grid=(tokens // tile,),
         in_specs=[
             pl.BlockSpec((tile, width), lambda i: (i, 0)),
-            pl.BlockSpec((1, tile, model), lambda i: (i, 0, 0)),
+            pl.BlockSpec((2, tile // 2, model), lambda i: (i, 0, 0)),
         ]
         + [fixed((width, model))] * len(before),
         out_specs=[fixed(grad_type.shape), fixed((8, width))],
@@ -1238,20 +1239,19 @@
             grad, grad_att[1], plane_first = lax.optimization_barrier(
                 (grad, grad_att[1], plane_first)
             )
+            hidden_first = exchange_dp(plane_first)
         else:
-            grad, rows_back[0], plane_first, grads[0], ups, downs = lax.optimization_barrier(
-                (grad, rows_back[0], plane_first, grads[0], ups, downs)
+            grad, rows_back[0], hidden_first, grads[0], ups, downs = lax.optimization_barrier(
+                (grad, rows_back[0], hidden_first, grads[0], ups, downs)
             )
         rows_back.append(grad)
         grads.append(
             swap(grad.reshape(members, span, 3 * PAIR)).reshape(rows, cols, span, 3 * PAIR)
         )
-    hidden_first = exchange_dp(plane_first)
     for g in range(groups):
         grad_qkv, bias_sum = qkv_grad(rows_back[g], normed_all[g], before)
         before = [grad_qkv]
         bias_sums.append(bias_sum[0])
-    grad_qkv, hidden_first = lax.optimization_barrier((grad_qkv, hidden_first))
     grad_qkv = exchange_dp(grad_qkv.reshape(dps, rows, -1, 3 * PAIR))
     quarters = [quarter]
     for shift in range(1, dps):

time: 586 us -> 585 us (level)
  starting transfers between devices: 63.2 us -> 75.7 us
  Pallas kernels: 350 us -> 341 us
    all_gather x2, waiting for transfers between devices: 10.2 us -> 25.1 us  [spread(): whole = lax.all_gather(shard, MESH_AXES, axis=0, tiled=False)]
    all_to_all x6, starting transfers between devices: 24.1 us -> 35 us  [swap(): return lax.all_to_all(blocks, MESH_AXES, 0, 0, tiled=True)]
  transfers between devices with their start and end apart: 32 -> 32, of which waited for: 13 -> 9; matrix products, arithmetic and copies ran while one was open for 8% -> 8% of each run, Pallas kernels for 61% -> 59%
where the time goes in v5:
time: 585 us; the launch traced here: 582 us
  Pallas kernels  341 us (58%)
  waiting for transfers between devices  87.4 us (15%)
  starting transfers between devices  75.7 us (13%)
  local copies, waits for them, and re-layouts  31.6 us (5%)
  other arithmetic  26.6 us (5%)
  between operations  15.1 us (3%)
    pallas_call x2, Pallas kernels, attend_back(): pl.pallas_call(functools.partial(attend_back_kernel, BK_BACK), grid=(toke...  94.3 us
    pallas_call x2, Pallas kernels, attend(): pl.pallas_call(functools.partial(attend_kernel, BK), grid=(blocks,), in_s...  72.9 us
    pallas_call x3, Pallas kernels, feed_forward(): pl.pallas_call(functools.partial(hidden_kernel, rows, dps, groups, first)...  68.6 us
    all_to_all x6, starting transfers between devices, swap(): return lax.all_to_all(blocks, MESH_AXES, 0, 0, tiled=True)  35 us
    all_gather x1, waiting for transfers between devices, head_body(): normed_all = [lax.all_gather(normed[0], MESH_AXES, axis=0, tiled=False)]  33.5 us
    all_gather x2, waiting for transfers between devices, spread(): whole = lax.all_gather(shard, MESH_AXES, axis=0, tiled=False)  25.1 us
    pallas_call x2, Pallas kernels, input_back(): pl.pallas_call(functools.partial(input_kernel, rows, dps), grid=(rows //...  22.2 us
    pallas_call x2, Pallas kernels, qkv_grad(): pl.pallas_call(functools.partial(qkv_grad_kernel, final), grid=(tokens //...  17.6 us
  transfers between devices with their start and end apart: 32, of which 9 were waited for; matrix products, arithmetic and copies ran while one was open for 8% of the time, Pallas kernels for 59%

profile of v5, /device:TPU:0, one launch (start us, length us, event | category | flops | bytes accessed | tf_op | source)
XLA Modules:
  0.0 582.5 jit_solution(17564098338337034942)
XLA Ops:
  12.2 2.3 copy.42
  16.5 4.2 all-to-all-start
  20.8 5.3 all-gather
  26.1 3.3 pack_weights.1
  29.4 4.0 copy.46
  36.2 2.5 convert_reduce_fusion.1
  38.7 2.7 all-to-all-done
  41.4 2.3 copy.44
  43.7 33.5 %all-gather.9.cloned.1.call-done.x_ref = bf16[8,512,1024]{2,1,0:T(8,128)(2,1)} async-done(((bf16[1,512,1024]{2,1,0:T(8,128)(2,1)}), bf16[8,512,1024]{2,1,0:T(8,128)(2,1)}) %all-gather.9.cloned.1.call-update) | async-done | bytes 8388624 | tf_op jit(solution)/shard_map/all_gather | solution.py:1142
  79.7 8.5 %qkv.2.qkv_ref = bf16[4096,384]{1,0:T(8,128)(2,1)} custom-call(bf16[8,512,1024]{2,1,0:T(8,128)(2,1)} %all-gather.9.cloned.1.call-done.x_ref, bf16[1024,384]{1,0:T(8,128)(2,1)} %bitcast.125, f32[2,384]{1,0:T(2,128)} %pad_maximum_fusion.4.vec_ref), custom_call_target="tpu_custom_call" | custom-call | flops 3221225472 | bytes 11534336 | tf_op jit(solution)/shard_map/qkv/pallas_call | solution.py:394
  88.2 37.2 %attend.2 = (bf16[4096,128]{1,0:T(8,128)(2,1)}, f32[16,8,512]{2,1,0:T(8,128)}) custom-call(s32[8]{0:T(128)} %get-tuple-element.221.cut_ref, bf16[4096,384]{1,0:T(8,128)(2,1)} %qkv.2.qkv_ref), custom_call_target="tpu_custom_call" | custom-call | flops 34359738368 | bytes 4194304 | tf_op jit(solution)/shard_map/attend/pallas_call | solution.py:477
  125.5 15.1 %all-gather.11.cloned.1.call-done = bf16[4864,1024]{1,0:T(8,128)(2,1)} async-done(((bf16[608,1024]{1,0:T(8,128)(2,1)}), bf16[4864,1024]{1,0:T(8,128)(2,1)}) %all-gather.11.cloned.1.call-update) | async-done | bytes 9961488 | tf_op jit(solution)/shard_map/all_gather | solution.py:1160
  140.6 2.7 slice.155
  144.6 5.7 collective-permute-start
  150.3 3.6 all-to-all-start.1
  153.9 8.5 %qkv.3.qkv_ref = bf16[4096,384]{1,0:T(8,128)(2,1)} custom-call(bf16[8,608,1024]{2,1,0:T(8,128)(2,1)} %bitcast.116, bf16[1024,384]{1,0:T(8,128)(2,1)} %bitcast.126, f32[2,384]{1,0:T(2,128)} %pad_maximum_fusion.4.vec_ref), custom_call_target="tpu_custom_call" | custom-call | flops 3221225472 | bytes 11534336 | tf_op jit(solution)/shard_map/qkv/pallas_call | solution.py:394
  162.4 35.7 %attend.3 = (bf16[4096,128]{1,0:T(8,128)(2,1)}, f32[16,8,512]{2,1,0:T(8,128)}) custom-call(s32[8]{0:T(128)} %get-tuple-element.222.cut_ref, bf16[4096,384]{1,0:T(8,128)(2,1)} %qkv.3.qkv_ref), custom_call_target="tpu_custom_call" | custom-call | flops 34359738368 | bytes 4194304 | tf_op jit(solution)/shard_map/attend/pallas_call | solution.py:477
  198.1 2.4 collective-permute-start.2
  202.5 4.2 all-to-all-start.2
  207.1 3.2 slice_bitcast_fusion.1
  212.3 16.3 %all-gather.13.cloned.1.call-done = bf16[5120,1024]{1,0:T(8,128)(2,1)} async-done(((bf16[640,1024]{1,0:T(8,128)(2,1)}), bf16[5120,1024]{1,0:T(8,128)(2,1)}) %all-gather.13.cloned.1.call-update) | async-done | bytes 10485776 | tf_op jit(solution)/shard_map/all_gather | solution.py:1096
  228.7 5.4 out_norm.2
  234.1 5.4 out_norm.3
  239.5 35.6 %feed_forward_first.1 = (f32[512,1024]{1,0:T(8,128)}, f32[512,1024]{1,0:T(8,128)}, f32[512,1024]{1,0:T(8,128)}, f32[512,1024]{1,0:T(8,128)}, bf16[4,2,4,128,1024...) custom-call(bf16[512,1024]{1,0:T(8,128)(2,1)} %get-tuple-element.108.refs_0_, ...), custom_call_target="tpu_custom_call" | custom-call | flops 25769803776 | bytes 16777216 | tf_op jit(solution)/shard_map/feed_forward_first/pallas_call | solution.py:824
  275.1 8.8 %all-gather.15.cloned.1.call-done = bf16[4096,1024]{1,0:T(8,128)(2,1)} async-done(((bf16[512,1024]{1,0:T(8,128)(2,1)}), bf16[4096,1024]{1,0:T(8,128)(2,1)}) %all-gather.15.cloned.1.call-update) | async-done | bytes 8388624 | tf_op jit(solution)/shard_map/all_gather | solution.py:1096
  283.9 16.6 %feed_forward_second.2 = (bf16[512,1024]{1,0:T(8,128)(2,1)}, f32[512,1024]{1,0:T(8,128)}, bf16[2,512,1024]{2,1,0:T(8,128)(2,1)}, bf16[2,512,1024]{2,1,0:T(8,128)(2,1)}, f32[2,1,1024]{2,1,0:T(1,128)}) custom-call(bf16[512,1024]{1,0:T(8,128)(2,1)} %get-tuple-element.108.refs_0_, bf16[512,1024]{1,0:T(8,128)(2,1)} %get-tuple-element.181.refs_5_.refs_1_.cot_ref, ...), custom_call_target="tpu_custom_call" | custom-call | flops 8589934592 | bytes 16777216 | tf_op jit(solution)/shard_map/feed_forward_second/pallas_call | solution.py:824
  301.1 7.2 %out_norm_back.2 = (f32[512,1024]{1,0:T(8,128)}, bf16[1024,512]{1,0:T(8,128)(2,1)}, bf16[4,2,512,128]{3,2,1,0:T(8,128)(2,1)}, f32[8,1024]{1,0:T(8,128)}) custom-call(f32[512,1024]{1,0:T(8,128)} %get-tuple-element.124.grad_ref, f32[512,1024]{1,0:T(8,128)} %get-tuple-element.119.refs_9_.middle_ref, ...), custom_call_target="tpu_custom_call" | custom-call | flops 1073741824 | bytes 11534336 | tf_op jit(solution)/shard_map/out_norm_back/pallas_call | solution.py:883
  308.4 14.3 %all-to-all-start.3 = ((bf16[8,512,128]{2,1,0:T(8,128)(2,1)}), bf16[8,512,128]{2,1,0:T(8,128)(2,1)S(1)}, u32[]{:S(2)}, u32[]{:S(2)}) async-start(bf16[8,512,128]{2,1,0:T(8,128)(2,1)} %bitcast.140), calls=%async_computation.3 | async-start | bytes 2097152 | tf_op jit(solution)/shard_map/all_to_all | solution.py:1100
  322.7 16.4 %feed_forward_second.3 = (bf16[512,1024]{1,0:T(8,128)(2,1)}, f32[512,1024]{1,0:T(8,128)}, bf16[2,512,1024]{2,1,0:T(8,128)(2,1)}, bf16[2,512,1024]{2,1,0:T(8,128)(2,1)}, f32[2,1,1024]{2,1,0:T(1,128)}) custom-call(bf16[512,1024]{1,0:T(8,128)(2,1)} %get-tuple-element.126.refs_1_.refs_0_, bf16[512,1024]{1,0:T(8,128)(2,1)} %get-tuple-element.180.refs_6_.refs_1_.cot_ref, ...), custom_call_target="tpu_custom_call" | custom-call | flops 8589934592 | bytes 16777216 | tf_op jit(solution)/shard_map/feed_forward_second/pallas_call | solution.py:824
  339.1 6.7 %out_norm_back.3 = (f32[512,1024]{1,0:T(8,128)}, bf16[1024,512]{1,0:T(8,128)(2,1)}, bf16[4,2,512,128]{3,2,1,0:T(8,128)(2,1)}, f32[8,1024]{1,0:T(8,128)}) custom-call(f32[512,1024]{1,0:T(8,128)} %get-tuple-element.137.grad_ref, f32[512,1024]{1,0:T(8,128)} %get-tuple-element.120.refs_10_.middle_ref, ...), custom_call_target="tpu_custom_call" | custom-call | flops 1073741824 | bytes 11534336 | tf_op jit(solution)/shard_map/out_norm_back/pallas_call | solution.py:883
  345.9 14.3 %hidden_grad.1.refs_4_ = bf16[4,2,4,160,1024]{4,3,2,1,0:T(8,128)(2,1)} custom-call(bf16[1024,512]{1,0:T(8,128)(2,1)} %get-tuple-element.116.refs_2_.refs_0_, bf16[1024,512]{1,0:T(8,128)(2,1)} %get-tuple-element.117.refs_3_.refs_1_, bf16[1024,1024]{1,0:T(8,128)(2,1)} %bitcast.132, bf16[2,512,1024]{2,1,0:T(8,128)(2,1)} %get-tuple-element.131.refs_3_, ...), custom_call_target="tpu_custom_call" | custom-call | flops 8589934592 | bytes 16777216 | tf_op jit(solution)/shard_map/hidden_grad/pallas_call | solution.py:703
  360.2 5.8 %out_grad.1 = bf16[4,2,4,160,1024]{4,3,2,1,0:T(8,128)(2,1)} custom-call(bf16[1024,512]{1,0:T(8,128)(2,1)} %get-tuple-element.162.refs_0_, bf16[1024,512]{1,0:T(8,128)(2,1)} %get-tuple-element.163.refs_1_, bf16[4,2,512,128]{3,2,1,0:T(8,128)(2,1)} %bitcast.123, bf16[4,2,512,128]{3,2,1,0:T(8,128)(2,1)} %bitcast.29.att_ref.refs_3_, ...), custom_call_target="tpu_custom_call", output_to_operand_aliasing={{}: (4, {})} | custom-call | flops 2147483648 | bytes 2097152 | tf_op jit(solution)/shard_map/out_grad/pallas_call | solution.py:933
  366.1 4.6 collective-permute-start.7
  372.1 4.1 all-to-all-start.4
  376.3 47.8 %attend_back.2.dqkv_ref = bf16[4096,384]{1,0:T(8,128)(2,1)} custom-call(s32[8]{0:T(128)} %get-tuple-element.221.cut_ref, bf16[4096,384]{1,0:T(8,128)(2,1)} %qkv.2.qkv_ref, bf16[4096,128]{1,0:T(8,128)(2,1)} %get-tuple-element.105.o_ref, bf16[4096,128]{1,0:T(8,128)(2,1)} %bitcast.138, f32[16,8,512]{2,1,0:T(8,128)} %get-tuple-element.136.lse_ref), custom_call_target="tpu_custom_call" | custom-call | flops 42949672960 | bytes 8388608 | tf_op jit(solution)/shard_map/attend_back/pallas_call | solution.py:575
  425.1 4.3 all-to-all-start.5
  430.6 3.3 collective-permute-start.4
  435.4 46.4 %attend_back.3.dqkv_ref = bf16[4096,384]{1,0:T(8,128)(2,1)} custom-call(s32[8]{0:T(128)} %get-tuple-element.222.cut_ref, bf16[4096,384]{1,0:T(8,128)(2,1)} %qkv.3.qkv_ref, bf16[4096,128]{1,0:T(8,128)(2,1)} %get-tuple-element.111.o_ref, bf16[4096,128]{1,0:T(8,128)(2,1)} %bitcast.139, f32[16,8,512]{2,1,0:T(8,128)} %get-tuple-element.141.lse_ref), custom_call_target="tpu_custom_call" | custom-call | flops 42949672960 | bytes 8388608 | tf_op jit(solution)/shard_map/attend_back/pallas_call | solution.py:575
  485.7 4.4 all-to-all-start.6
  490.2 8.6 %qkv_grad.2 = (f32[384,1024]{1,0:T(8,128)}, f32[8,384]{1,0:T(8,128)}) custom-call(bf16[4096,384]{1,0:T(8,128)(2,1)} %attend_back.2.dqkv_ref, bf16[8,512,1024]{2,1,0:T(8,128)(2,1)} %all-gather.9.cloned.1.call-done.x_ref), custom_call_target="tpu_custom_call" | custom-call | flops 3221225472 | bytes 11534336 | tf_op jit(solution)/shard_map/qkv_grad/pallas_call | solution.py:984
  498.8 9.0 %qkv_grad.3 = (bf16[1024,384]{1,0:T(8,128)(2,1)}, f32[8,384]{1,0:T(8,128)}) custom-call(bf16[4096,384]{1,0:T(8,128)(2,1)} %attend_back.3.dqkv_ref, bf16[8,608,1024]{2,1,0:T(8,128)(2,1)} %bitcast.117, f32[384,1024]{1,0:T(8,128)} %get-tuple-element.160.refs_0_), custom_call_target="tpu_custom_call" | custom-call | flops 3221225472 | bytes 11534336 | tf_op jit(solution)/shard_map/qkv_grad/pallas_call | solution.py:984
  509.0 4.0 collective-permute-start.11
  516.8 4.3 pad_maximum_fusion.left_ref.right_ref
  521.2 11.0 %input_back.2 = (f32[2,512,1024]{2,1,0:T(8,128)}, f32[8,1024]{1,0:T(8,128)}) custom-call(s32[1]{0:T(128)} %bitcast.34.plane_ref, bf16[4,2,512,384]{3,2,1,0:T(8,128)(2,1)} %bitcast.121, bf16[4,4,2,96,1024]{4,3,2,1,0:T(8,128)(2,1)} %pad_maximum_fusion.left_ref.right_ref, bf16[4,4,2,96,1024]{4,3,2,1,0:T(8,128)(2,1)} %pad_maximum_fusion.left_ref.right_ref, ...), custom_call_target="tpu_custom_call" | custom-call | flops 3221225472 | bytes 12582912 | tf_op jit(solution)/shard_map/input_back/pallas_call | solution.py:1040
  534.8 11.3 %input_back.3 = (f32[2,512,1024]{2,1,0:T(8,128)}, f32[8,1024]{1,0:T(8,128)}) custom-call(s32[1]{0:T(128)} %bitcast.34.plane_ref, bf16[4,2,512,384]{3,2,1,0:T(8,128)(2,1)} %bitcast.48.dqkv_ref, bf16[4,4,2,96,1024]{4,3,2,1,0:T(8,128)(2,1)} %pad_maximum_fusion.left_ref.right_ref, ...), custom_call_target="tpu_custom_call", output_to_operand_aliasing={{0}: (7, {})} | custom-call | flops 3221225472 | bytes 12582912 | tf_op jit(solution)/shard_map/input_back/pallas_call | solution.py:1040
  548.3 2.2 collective-permute-start.13
  554.6 3.5 all-to-all-start.7
  560.2 4.3 collective-permute-done.15
  (165 shorter events, 54.3 us)
Async XLA Ops:
  7.2 71.4 %copy-start = (f32[2,512]{1,0:T(2,128)S(1)}, f32[2,512]{1,0:T(2,128)}, u32[]{:S(2)}) copy-start(f32[2,512]{1,0:T(2,128)} %param.21) | copy-start | bytes 12292
  7.2 70.0 %all-gather.9.cloned.1.call-start = ((), (), s32[]{:S(2)}) async-start(), calls=%async_computation.11 | async-start | bytes 9437184 | tf_op jit(solution)/shard_map/all_gather | solution.py:1142
  12.2 8.6 %copy-start.17 = (f32[2048]{0:T(1024)S(1)}, f32[2048]{0:T(1024)}, u32[]{:S(2)}) copy-start(f32[2048]{0:T(1024)} %param.27) | copy-start | bytes 24580
  16.5 24.9 %all-to-all-start = ((bf16[4,256,384]{1,2,0:T(8,128)(2,1)}), bf16[4,256,384]{1,2,0:T(8,128)(2,1)}, u32[]{:S(2)}, u32[]{:S(2)}) async-start(bf16[4,256,384]{1,2,0:T(8,128)(2,1)} %bitcast.128), calls=%async_computation | async-start | bytes 1572864 | tf_op jit(solution)/shard_map/all_to_all | solution.py:1136
  20.8 119.8 %all-gather.11.cloned.1.call-start = ((), (), s32[]{:S(2)}) async-start(), calls=%async_computation.15 | async-start | bytes 11206656 | tf_op jit(solution)/shard_map/all_gather | solution.py:1160
  43.7 35.5 %copy-start.23 = (s32[2,8]{1,0:T(2,128)S(1)}, s32[2,8]{1,0:T(2,128)}, u32[]{:S(2)}) copy-start(s32[2,8]{1,0:T(2,128)} %param.17) | copy-start | bytes 196
  77.2 151.4 %all-gather.13.cloned.1.call-start = ((), (), s32[]{:S(2)}) async-start(), calls=%async_computation.16 | async-start | bytes 11796480 | tf_op jit(solution)/shard_map/all_gather | solution.py:1096
  78.0 205.9 %all-gather.15.cloned.1.call-start = ((), (), s32[]{:S(2)}) async-start(), calls=%async_computation.17 | async-start | bytes 9437184 | tf_op jit(solution)/shard_map/all_gather | solution.py:1096
  143.3 54.8 %collective-permute-start.1 = (bf16[4,2,96,1024]{3,2,1,0:T(8,128)(2,1)}, bf16[4,2,96,1024]{3,2,1,0:T(8,128)(2,1)}, u32[]{:S(2)}, u32[]{:S(2)}) collective-permute-start(bf16[4,2,96,1024]{3,2,1,0:T(8,128)(2,1)} %bitcast.20), channel_id=1, source_target_pairs={{8,0},{16,8},{24,16},{9,1},{17,9},{25,17},{10,2},{18,10},{26,18},{... | collective-permute-start | bytes 4718600 | tf_op jit(solution)/shard_map/ppermute | solution.py:1171
  144.6 53.5 %collective-permute-start = (bf16[4,2,96,1024]{3,2,1,0:T(8,128)(2,1)}, bf16[4,2,96,1024]{3,2,1,0:T(8,128)(2,1)}, u32[]{:S(2)}, u32[]{:S(2)}) collective-permute-start(bf16[4,2,96,1024]{3,2,1,0:T(8,128)(2,1)} %bitcast.20), channel_id=1, source_target_pairs={{0,8},{8,16},{16,24},{1,9},{9,17},{17,25},{2,10},{10,18},{18,26},{... | collective-permute-start | bytes 4718600 | tf_op jit(solution)/shard_map/ppermute | solution.py:1168
  150.3 47.8 %all-to-all-start.1 = ((bf16[8,512,128]{2,1,0:T(8,128)(2,1)}), bf16[8,512,128]{2,1,0:T(8,128)(2,1)S(1)}, u32[]{:S(2)}, u32[]{:S(2)}) async-start(bf16[8,512,128]{2,1,0:T(8,128)(2,1)} %bitcast.135), calls=%async_computation.1 | async-start | bytes 2097152 | tf_op jit(solution)/shard_map/all_to_all | solution.py:1100
  162.4 39.4 %copy-start.10 = (f32[1024]{0:T(1024)S(1)}, f32[1024]{0:T(1024)}, u32[]{:S(2)}) copy-start(f32[1024]{0:T(1024)} %param.23) | copy-start | bytes 12292
  162.4 39.4 %copy-start.16 = (f32[1024]{0:T(1024)S(1)}, f32[1024]{0:T(1024)}, u32[]{:S(2)}) copy-start(f32[1024]{0:T(1024)} %param.24) | copy-start | bytes 12292
  162.4 39.4 %copy-start.21 = (f32[1024]{0:T(1024)S(1)}, f32[1024]{0:T(1024)}, u32[]{:S(2)}) copy-start(f32[1024]{0:T(1024)} %param.25) | copy-start | bytes 12292
  198.1 12.2 %copy-start.4 = (bf16[8,512,128]{2,1,0:T(8,128)(2,1)}, bf16[8,512,128]{2,1,0:T(8,128)(2,1)S(1)}, u32[]{:S(2)}) copy-start(bf16[8,512,128]{2,1,0:T(8,128)(2,1)S(1)} %all-to-all-done.1) | copy-start | bytes 3145732
  198.1 41.4 %collective-permute-start.2 = (bf16[4,2,96,1024]{3,2,1,0:T(8,128)(2,1)}, bf16[4,2,96,1024]{3,2,1,0:T(8,128)(2,1)}, u32[]{:S(2)}, u32[]{:S(2)}) collective-permute-start(bf16[4,2,96,1024]{3,2,1,0:T(8,128)(2,1)} %collective-permute-done), channel_id=1, source_target_pairs={{0,8},{8,16},{16,24},{1,9},{9,17},{17,25},{2,10},{10,18},{18,26},{... | collective-permute-start | bytes 4718600 | tf_op jit(solution)/shard_map/ppermute | solution.py:1168
  200.5 38.9 %collective-permute-start.3 = (bf16[4,2,96,1024]{3,2,1,0:T(8,128)(2,1)}, bf16[4,2,96,1024]{3,2,1,0:T(8,128)(2,1)}, u32[]{:S(2)}, u32[]{:S(2)}) collective-permute-start(bf16[4,2,96,1024]{3,2,1,0:T(8,128)(2,1)} %collective-permute-done.1), channel_id=1, source_target_pairs={{8,0},{16,8},{24,16},{9,1},{17,9},{25,17},{10,2},{18,10},{26,18},{... | collective-permute-start | bytes 4718600 | tf_op jit(solution)/shard_map/ppermute | solution.py:1171
  202.5 31.5 %all-to-all-start.2 = ((bf16[8,512,128]{2,1,0:T(8,128)(2,1)}), bf16[8,512,128]{2,1,0:T(8,128)(2,1)}, u32[]{:S(2)}, u32[]{:S(2)}) async-start(bf16[8,512,128]{2,1,0:T(8,128)(2,1)} %bitcast.134), calls=%async_computation.2 | async-start | bytes 2097152 | tf_op jit(solution)/shard_map/all_to_all | solution.py:1100
  206.8 217.4 %reduce-scatter.4.cloned.1.call-start = ((), (), s32[]{:S(2)}) async-start(), calls=%async_computation.12 | async-start | bytes 9437184 | tf_op jit(solution)/shard_map/reduce_scatter | solution.py:1104
  308.4 51.8 %all-to-all-start.3 = ((bf16[8,512,128]{2,1,0:T(8,128)(2,1)}), bf16[8,512,128]{2,1,0:T(8,128)(2,1)S(1)}, u32[]{:S(2)}, u32[]{:S(2)}) async-start(bf16[8,512,128]{2,1,0:T(8,128)(2,1)} %bitcast.140), calls=%async_computation.3 | async-start | bytes 2097152 | tf_op jit(solution)/shard_map/all_to_all | solution.py:1100
  322.6 211.3 %reduce-scatter.6.cloned.1.call-start = ((), (), s32[]{:S(2)}) async-start(), calls=%async_computation.13 | async-start | bytes 11796480 | tf_op jit(solution)/shard_map/reduce_scatter | solution.py:1104
  366.0 10.2 %copy-start.18 = (f32[2,1,1024]{2,1,0:T(1,128)S(1)}, f32[2,1,1024]{2,1,0:T(1,128)}, u32[]{:S(2)}) copy-start(f32[2,1,1024]{2,1,0:T(1,128)} %get-tuple-element.170) | copy-start | bytes 24580
  366.0 10.2 %copy-start.19 = (f32[2,1,1024]{2,1,0:T(1,128)S(1)}, f32[2,1,1024]{2,1,0:T(1,128)}, u32[]{:S(2)}) copy-start(f32[2,1,1024]{2,1,0:T(1,128)} %get-tuple-element.171) | copy-start | bytes 24580
  366.1 10.2 %copy-start.12 = (f32[8,1024]{1,0:T(8,128)S(1)}, f32[8,1024]{1,0:T(8,128)}, u32[]{:S(2)}) copy-start(f32[8,1024]{1,0:T(8,128)} %get-tuple-element.167) | copy-start | bytes 98308
  366.1 10.2 %copy-start.13 = (f32[8,1024]{1,0:T(8,128)S(1)}, f32[8,1024]{1,0:T(8,128)}, u32[]{:S(2)}) copy-start(f32[8,1024]{1,0:T(8,128)} %get-tuple-element.168) | copy-start | bytes 98308
  366.1 10.2 %copy-start.20 = (f32[2,1,1024]{2,1,0:T(1,128)S(1)}, f32[2,1,1024]{2,1,0:T(1,128)}, u32[]{:S(2)}) copy-start(f32[2,1,1024]{2,1,0:T(1,128)} %get-tuple-element.169) | copy-start | bytes 24580
  366.1 117.9 %collective-permute-start.7 = (bf16[4,2,96,1024]{3,2,1,0:T(8,128)(2,1)}, bf16[4,2,96,1024]{3,2,1,0:T(8,128)(2,1)}, u32[]{:S(2)}, u32[]{:S(2)}) collective-permute-start(bf16[4,2,96,1024]{3,2,1,0:T(8,128)(2,1)} %collective-permute-done.2), channel_id=1, source_target_pairs={{0,8},{8,16},{16,24},{1,9},{9,17},{17,25},{2,10},{10,18},{18,26},{... | collective-permute-start | bytes 4718600 | tf_op jit(solution)/shard_map/ppermute | solution.py:1168
  370.8 113.2 %collective-permute-start.8 = (bf16[4,2,96,1024]{3,2,1,0:T(8,128)(2,1)}, bf16[4,2,96,1024]{3,2,1,0:T(8,128)(2,1)}, u32[]{:S(2)}, u32[]{:S(2)}) collective-permute-start(bf16[4,2,96,1024]{3,2,1,0:T(8,128)(2,1)} %collective-permute-done.3), channel_id=1, source_target_pairs={{8,0},{16,8},{24,16},{9,1},{17,9},{25,17},{10,2},{18,10},{26,18},{... | collective-permute-start | bytes 4718600 | tf_op jit(solution)/shard_map/ppermute | solution.py:1171
  372.1 52.1 %all-to-all-start.4 = ((bf16[8,512,128]{2,1,0:T(8,128)(2,1)}), bf16[8,512,128]{2,1,0:T(8,128)(2,1)S(1)}, u32[]{:S(2)}, u32[]{:S(2)}) async-start(bf16[8,512,128]{2,1,0:T(8,128)(2,1)} %bitcast.37), calls=%async_computation.4 | async-start | bytes 2097152 | tf_op jit(solution)/shard_map/all_to_all | solution.py:1100
  425.1 58.9 %all-to-all-start.5 = ((bf16[8,512,384]{2,1,0:T(8,128)(2,1)}), bf16[8,512,384]{2,1,0:T(8,128)(2,1)S(1)}, u32[]{:S(2)}, u32[]{:S(2)}) async-start(bf16[8,512,384]{2,1,0:T(8,128)(2,1)} %bitcast.127), calls=%async_computation.6 | async-start | bytes 6291456 | tf_op jit(solution)/shard_map/all_to_all | solution.py:1100
  430.6 51.2 %collective-permute-start.4 = (bf16[128,1024]{1,0:T(8,128)(2,1)S(1)}, bf16[128,1024]{1,0:T(8,128)(2,1)}, u32[]{:S(2)}, u32[]{:S(2)}) collective-permute-start(bf16[128,1024]{1,0:T(8,128)(2,1)S(1)} %get-tuple-element.186), channel_id=1, source_target_pairs={{0,8},{8,16},{16,24},{24,0},{1,9},{9,17},{17,25},{25,1},{2,10},{10... | collective-permute-start | bytes 786440 | tf_op jit(solution)/shard_map/ppermute | solution.py:1113
  433.9 48.0 %collective-permute-start.6 = (bf16[128,1024]{1,0:T(8,128)(2,1)S(1)}, bf16[128,1024]{1,0:T(8,128)(2,1)}, u32[]{:S(2)}, u32[]{:S(2)}) collective-permute-start(bf16[128,1024]{1,0:T(8,128)(2,1)S(1)} %get-tuple-element.187), channel_id=1, source_target_pairs={{0,24},{8,0},{16,8},{24,16},{1,25},{9,1},{17,9},{25,17},{2,26},{10... | collective-permute-start | bytes 786440 | tf_op jit(solution)/shard_map/ppermute | solution.py:1113
  434.5 47.4 %collective-permute-start.5 = (bf16[128,1024]{1,0:T(8,128)(2,1)S(1)}, bf16[128,1024]{1,0:T(8,128)(2,1)}, u32[]{:S(2)}, u32[]{:S(2)}) collective-permute-start(bf16[128,1024]{1,0:T(8,128)(2,1)S(1)} %get-tuple-element.188), channel_id=1, source_target_pairs={{0,16},{8,24},{16,0},{24,8},{1,17},{9,25},{17,1},{25,9},{2,18},{10... | collective-permute-start | bytes 786440 | tf_op jit(solution)/shard_map/ppermute | solution.py:1113
  485.7 49.1 %all-to-all-start.6 = ((bf16[8,512,384]{2,1,0:T(8,128)(2,1)}), bf16[8,512,384]{2,1,0:T(8,128)(2,1)}, u32[]{:S(2)}, u32[]{:S(2)}) async-start(bf16[8,512,384]{2,1,0:T(8,128)(2,1)} %bitcast.120), calls=%async_computation.7 | async-start | bytes 6291456 | tf_op jit(solution)/shard_map/all_to_all | solution.py:1100
  490.2 81.7 %reduce-scatter.8.cloned.1.call-start = ((), (), s32[]{:S(2)}) async-start(), calls=%async_computation.14 | async-start | bytes 1638400 | tf_op jit(solution)/shard_map/reduce_scatter | solution.py:1117
  509.0 23.1 %collective-permute-start.9 = (bf16[4,64,384]{2,1,0:T(8,128)(2,1)S(1)}, bf16[4,64,384]{2,1,0:T(8,128)(2,1)S(1)}, u32[]{:S(2)}, u32[]{:S(2)}) collective-permute-start(bf16[4,64,384]{2,1,0:T(8,128)(2,1)S(1)} %get-tuple-element.189), channel_id=1, source_target_pairs={{0,8},{8,16},{16,24},{24,0},{1,9},{9,17},{17,25},{25,1},{2,10},{10... | collective-permute-start | bytes 589832 | tf_op jit(solution)/shard_map/ppermute | solution.py:1113
  509.0 23.1 %collective-permute-start.11 = (bf16[4,64,384]{2,1,0:T(8,128)(2,1)S(1)}, bf16[4,64,384]{2,1,0:T(8,128)(2,1)S(1)}, u32[]{:S(2)}, u32[]{:S(2)}) collective-permute-start(bf16[4,64,384]{2,1,0:T(8,128)(2,1)S(1)} %get-tuple-element.190), channel_id=1, source_target_pairs={{0,24},{8,0},{16,8},{24,16},{1,25},{9,1},{17,9},{25,17},{2,26},{10... | collective-permute-start | bytes 589832 | tf_op jit(solution)/shard_map/ppermute | solution.py:1113
  513.0 19.1 %collective-permute-start.10 = (bf16[4,64,384]{2,1,0:T(8,128)(2,1)S(1)}, bf16[4,64,384]{2,1,0:T(8,128)(2,1)S(1)}, u32[]{:S(2)}, u32[]{:S(2)}) collective-permute-start(bf16[4,64,384]{2,1,0:T(8,128)(2,1)S(1)} %get-tuple-element.191), channel_id=1, source_target_pairs={{0,16},{8,24},{16,0},{24,8},{1,17},{9,25},{17,1},{25,9},{2,18},{10... | collective-permute-start | bytes 589832 | tf_op jit(solution)/shard_map/ppermute | solution.py:1113
  534.8 11.3 %copy-start.14 = (f32[8,1024]{1,0:T(8,128)S(1)}, f32[8,1024]{1,0:T(8,128)}, u32[]{:S(2)}) copy-start(f32[8,1024]{1,0:T(8,128)} %get-tuple-element.173) | copy-start | bytes 98308
  534.8 23.9 %copy-start.9 = (bf16[512,1024]{1,0:T(8,128)(2,1)S(1)}, bf16[512,1024]{1,0:T(8,128)(2,1)}, u32[]{:S(2)}) copy-start(bf16[512,1024]{1,0:T(8,128)(2,1)} %get-tuple-element.129) | copy-start | bytes 3145732
  546.1 12.6 %copy-start.8 = (bf16[512,1024]{1,0:T(8,128)(2,1)S(1)}, bf16[512,1024]{1,0:T(8,128)(2,1)}, u32[]{:S(2)}) copy-start(bf16[512,1024]{1,0:T(8,128)(2,1)} %get-tuple-element.123) | copy-start | bytes 3145732
  547.0 1.3 collective-permute-start.12
  548.3 4.3 collective-permute-start.13
  552.6 5.5 collective-permute-start.14
  554.6 12.0 %all-to-all-start.7 = ((f32[4,64,384]{2,1,0:T(8,128)}), f32[4,64,384]{2,1,0:T(8,128)S(1)}, u32[]{:S(2)}, u32[]{:S(2)}) async-start(f32[4,64,384]{2,1,0:T(8,128)} %fusion.9), calls=%async_computation.9 | async-start | bytes 786432 | tf_op jit(solution)/shard_map/all_to_all | solution.py:1285
  558.1 6.3 %collective-permute-start.15 = (f32[12288]{0:T(1024)S(1)}, f32[12288]{0:T(1024)S(1)}, u32[]{:S(2)}, u32[]{:S(2)}) collective-permute-start(f32[12288]{0:T(1024)S(1)} %add.156), channel_id=1, source_target_pairs={{0,8},{8,0},{16,24},{24,16},{1,9},{9,1},{17,25},{25,17},{2,10},{10... | collective-permute-start | bytes 147464 | tf_op jit(solution)/shard_map/ppermute | solution.py:1126
  558.6 7.9 %copy-start.5 = (f32[128,1024]{1,0:T(8,128)S(1)}, f32[128,1024]{1,0:T(8,128)}, u32[]{:S(2)}) copy-start(f32[128,1024]{1,0:T(8,128)} %fusion.7) | copy-start | bytes 1572868
  564.5 5.5 collective-permute-start.16
  (8 other events, 22.0 us)
Sparse Core Ops, SparseCore 0:
  12.3 64.8 all-gather.8
  79.7 60.8 all-gather.10
  143.1 85.5 all-gather.12
  230.4 53.4 all-gather.14
  287.2 82.7 reduce-scatter.3
  373.3 106.9 reduce-scatter.5
  534.1 33.5 reduce-scatter.7

commit v6 on v5

--- a/solution.py
+++ b/solution.py
@@ -1122,9 +1122,15 @@
             size = lax.axis_size(axis)
             step = 1
             while step < size:
-                pairs = [(i, i ^ step) for i in range(size)]
-                values = values + lax.ppermute(values, axis, pairs)
-                step *= 2
+                partners = (step, 2 * step, 3 * step) if 4 * step <= size else (step,)
+                parts = [values] + [
+                    lax.ppermute(values, axis, [(i, i ^ other) for i in range(size)])
+                    for other in partners
+                ]
+                values = parts[0] + parts[1]
+                if len(parts) == 4:
+                    values = values + (parts[2] + parts[3])
+                step *= len(parts)
         return values
 
     half = hidden_cols // 2
@@ -1252,6 +1258,10 @@
         grad_qkv, bias_sum = qkv_grad(rows_back[g], normed_all[g], before)
         before = [grad_qkv]
         bias_sums.append(bias_sum[0])
+        if g == 0:
+            before[0], plane_second = lax.optimization_barrier((before[0], plane_second))
+            hidden_second = collect_dp(plane_second)
+    grads[0], grad_qkv = lax.optimization_barrier((grads[0], grad_qkv))
     grad_qkv = exchange_dp(grad_qkv.reshape(dps, rows, -1, 3 * PAIR))
     quarters = [quarter]
     for shift in range(1, dps):
@@ -1264,11 +1274,6 @@
         )
         input_grads = [rows_grad]
         sums_one.append(sums)
-        if g == 0:
-            input_grads, grad_qkv, plane_second = lax.optimization_barrier(
-                (input_grads, grad_qkv, plane_second)
-            )
-            hidden_second = collect_dp(plane_second)
     sums_two = functools.reduce(jnp.add, sums_two)
     fc_sum = jnp.concatenate([fc_sum_first, fc_sum_second], axis=2).reshape(-1)
     sums_one = functools.reduce(jnp.add, sums_one)

time: 585 us -> 584 us (level)
  waiting for transfers between devices: 87.4 us -> 80 us
    all_gather x2, waiting for transfers between devices: 25.1 us -> 11.5 us  [spread(): whole = lax.all_gather(shard, MESH_AXES, axis=0, tiled=False)]
    all_to_all x6, starting transfers between devices: 35 us -> 24.2 us  [swap(): return lax.all_to_all(blocks, MESH_AXES, 0, 0, tiled=True)]
    ppermute x6, waiting for transfers between devices: 0.02 us -> 9.6 us  [exchange_dp(): summed = summed + lax.ppermute(piece, 'dp', pairs).astype(jnp.float32)]
    ppermute x5 -> x7, waiting for transfers between devices: 9.66 us -> 1.76 us  [total(): lax.ppermute(values, axis, [(i, i ^ other) for i in range(size)])]
  transfers between devices with their start and end apart: 32 -> 34, of which waited for: 9 -> 11; matrix products, arithmetic and copies ran while one was open for 8% -> 8% of each run, Pallas kernels for 59% -> 60%
where the time goes in v6:
time: 584 us; the launch traced here: 576 us
  Pallas kernels  343 us (59%)
  waiting for transfers between devices  80 us (14%)
  starting transfers between devices  73.8 us (13%)
  local copies, waits for them, and re-layouts  31.6 us (5%)
  other arithmetic  26.9 us (5%)
  between operations  15.1 us (3%)
    pallas_call x2, Pallas kernels, attend_back(): pl.pallas_call(functools.partial(attend_back_kernel, BK_BACK), grid=(toke...  95.4 us
    pallas_call x2, Pallas kernels, attend(): pl.pallas_call(functools.partial(attend_kernel, BK), grid=(blocks,), in_s...  74.2 us
    pallas_call x3, Pallas kernels, feed_forward(): pl.pallas_call(functools.partial(hidden_kernel, rows, dps, groups, first)...  68.8 us
    all_gather x1, waiting for transfers between devices, head_body(): normed_all = [lax.all_gather(normed[0], MESH_AXES, axis=0, tiled=False)]  33.5 us
    all_to_all x6, starting transfers between devices, swap(): return lax.all_to_all(blocks, MESH_AXES, 0, 0, tiled=True)  24.2 us
    pallas_call x2, Pallas kernels, input_back(): pl.pallas_call(functools.partial(input_kernel, rows, dps), grid=(rows //...  22.2 us
    pallas_call x2, Pallas kernels, qkv_grad(): pl.pallas_call(functools.partial(qkv_grad_kernel, final), grid=(tokens //...  17.7 us
    pallas_call x2, Pallas kernels, project_qkv(): pl.pallas_call(qkv_kernel, grid=(members // 2,), in_specs=[pl.BlockSpec((...  17 us
  transfers between devices with their start and end apart: 34, of which 11 were waited for; matrix products, arithmetic and copies ran while one was open for 8% of the time, Pallas kernels for 60%

profile of v6, /device:TPU:0, one launch (start us, length us, event | category | flops | bytes accessed | tf_op | source)
XLA Modules:
  0.0 576.0 jit_solution(16046645724817420560)
XLA Ops:
  16.5 4.2 all-to-all-start
  20.8 5.4 all-gather
  26.2 3.3 pack_weights.1
  29.5 4.0 copy.46
  36.3 2.5 convert_reduce_fusion.1
  38.8 2.6 all-to-all-done
  43.7 33.5 %all-gather.9.cloned.1.call-done.x_ref = bf16[8,512,1024]{2,1,0:T(8,128)(2,1)} async-done(((bf16[1,512,1024]{2,1,0:T(8,128)(2,1)}), bf16[8,512,1024]{2,1,0:T(8,128)(2,1)}) %all-gather.9.cloned.1.call-update) | async-done | bytes 8388624 | tf_op jit(solution)/shard_map/all_gather | solution.py:1148
  79.7 8.5 %qkv.2.qkv_ref = bf16[4096,384]{1,0:T(8,128)(2,1)} custom-call(bf16[8,512,1024]{2,1,0:T(8,128)(2,1)} %all-gather.9.cloned.1.call-done.x_ref, bf16[1024,384]{1,0:T(8,128)(2,1)} %bitcast.125, f32[2,384]{1,0:T(2,128)} %pad_maximum_fusion.4.vec_ref), custom_call_target="tpu_custom_call" | custom-call | flops 3221225472 | bytes 11534336 | tf_op jit(solution)/shard_map/qkv/pallas_call | solution.py:394
  88.2 39.7 %attend.2 = (bf16[4096,128]{1,0:T(8,128)(2,1)}, f32[16,8,512]{2,1,0:T(8,128)}) custom-call(s32[8]{0:T(128)} %get-tuple-element.223.cut_ref, bf16[4096,384]{1,0:T(8,128)(2,1)} %qkv.2.qkv_ref), custom_call_target="tpu_custom_call" | custom-call | flops 34359738368 | bytes 4194304 | tf_op jit(solution)/shard_map/attend/pallas_call | solution.py:477
  128.0 12.7 %all-gather.11.cloned.1.call-done = bf16[4864,1024]{1,0:T(8,128)(2,1)} async-done(((bf16[608,1024]{1,0:T(8,128)(2,1)}), bf16[4864,1024]{1,0:T(8,128)(2,1)}) %all-gather.11.cloned.1.call-update) | async-done | bytes 9961488 | tf_op jit(solution)/shard_map/all_gather | solution.py:1166
  140.6 2.7 slice.155
  144.6 5.8 collective-permute-start
  150.3 3.6 all-to-all-start.1
  153.9 8.5 %qkv.3.qkv_ref = bf16[4096,384]{1,0:T(8,128)(2,1)} custom-call(bf16[8,608,1024]{2,1,0:T(8,128)(2,1)} %bitcast.116, bf16[1024,384]{1,0:T(8,128)(2,1)} %bitcast.126, f32[2,384]{1,0:T(2,128)} %pad_maximum_fusion.4.vec_ref), custom_call_target="tpu_custom_call" | custom-call | flops 3221225472 | bytes 11534336 | tf_op jit(solution)/shard_map/qkv/pallas_call | solution.py:394
  162.4 34.4 %attend.3 = (bf16[4096,128]{1,0:T(8,128)(2,1)}, f32[16,8,512]{2,1,0:T(8,128)}) custom-call(s32[8]{0:T(128)} %get-tuple-element.224.cut_ref, bf16[4096,384]{1,0:T(8,128)(2,1)} %qkv.3.qkv_ref), custom_call_target="tpu_custom_call" | custom-call | flops 34359738368 | bytes 4194304 | tf_op jit(solution)/shard_map/attend/pallas_call | solution.py:477
  196.9 6.0 %collective-permute-start.2 = (bf16[4,2,96,1024]{3,2,1,0:T(8,128)(2,1)}, bf16[4,2,96,1024]{3,2,1,0:T(8,128)(2,1)}, u32[]{:S(2)}, u32[]{:S(2)}) collective-permute-start(bf16[4,2,96,1024]{3,2,1,0:T(8,128)(2,1)} %collective-permute-done), channel_id=1, source_target_pairs={{0,8},{8,16},{16,24},{1,9},{9,17},{17,25},{2,10},{10,18},{18,26},{... | collective-permute-start | bytes 4718600 | tf_op jit(solution)/shard_map/ppermute | solution.py:1174
  204.9 4.2 all-to-all-start.2
  209.4 3.2 slice_bitcast_fusion.1
  214.7 8.8 %all-gather.13.cloned.1.call-done = bf16[5120,1024]{1,0:T(8,128)(2,1)} async-done(((bf16[640,1024]{1,0:T(8,128)(2,1)}), bf16[5120,1024]{1,0:T(8,128)(2,1)}) %all-gather.13.cloned.1.call-update) | async-done | bytes 10485776 | tf_op jit(solution)/shard_map/all_gather | solution.py:1096
  223.5 5.4 out_norm.2
  228.9 5.4 out_norm.3
  236.2 5.2 collective-permute-done.3
  241.4 35.6 %feed_forward_first.1 = (f32[512,1024]{1,0:T(8,128)}, f32[512,1024]{1,0:T(8,128)}, f32[512,1024]{1,0:T(8,128)}, f32[512,1024]{1,0:T(8,128)}, bf16[4,2,4,128,1024...) custom-call(bf16[512,1024]{1,0:T(8,128)(2,1)} %get-tuple-element.109.refs_0_, ...), custom_call_target="tpu_custom_call" | custom-call | flops 25769803776 | bytes 16777216 | tf_op jit(solution)/shard_map/feed_forward_first/pallas_call | solution.py:824
  277.0 2.7 all-gather.15.cloned.1.call-done
  279.7 16.6 %feed_forward_second.2 = (bf16[512,1024]{1,0:T(8,128)(2,1)}, f32[512,1024]{1,0:T(8,128)}, bf16[2,512,1024]{2,1,0:T(8,128)(2,1)}, bf16[2,512,1024]{2,1,0:T(8,128)(2,1)}, f32[2,1,1024]{2,1,0:T(1,128)}) custom-call(bf16[512,1024]{1,0:T(8,128)(2,1)} %get-tuple-element.109.refs_0_, bf16[512,1024]{1,0:T(8,128)(2,1)} %get-tuple-element.183.refs_5_.refs_1_.cot_ref, ...), custom_call_target="tpu_custom_call" | custom-call | flops 8589934592 | bytes 16777216 | tf_op jit(solution)/shard_map/feed_forward_second/pallas_call | solution.py:824
  296.9 7.2 %out_norm_back.2 = (f32[512,1024]{1,0:T(8,128)}, bf16[1024,512]{1,0:T(8,128)(2,1)}, bf16[4,2,512,128]{3,2,1,0:T(8,128)(2,1)}, f32[8,1024]{1,0:T(8,128)}) custom-call(f32[512,1024]{1,0:T(8,128)} %get-tuple-element.125.grad_ref, f32[512,1024]{1,0:T(8,128)} %get-tuple-element.120.refs_9_.middle_ref, ...), custom_call_target="tpu_custom_call" | custom-call | flops 1073741824 | bytes 11534336 | tf_op jit(solution)/shard_map/out_norm_back/pallas_call | solution.py:883
  304.1 4.0 all-to-all-start.3
  308.1 16.6 %feed_forward_second.3 = (bf16[512,1024]{1,0:T(8,128)(2,1)}, f32[512,1024]{1,0:T(8,128)}, bf16[2,512,1024]{2,1,0:T(8,128)(2,1)}, bf16[2,512,1024]{2,1,0:T(8,128)(2,1)}, f32[2,1,1024]{2,1,0:T(1,128)}) custom-call(bf16[512,1024]{1,0:T(8,128)(2,1)} %get-tuple-element.127.refs_1_.refs_0_, bf16[512,1024]{1,0:T(8,128)(2,1)} %get-tuple-element.182.refs_6_.refs_1_.cot_ref, ...), custom_call_target="tpu_custom_call" | custom-call | flops 8589934592 | bytes 16777216 | tf_op jit(solution)/shard_map/feed_forward_second/pallas_call | solution.py:824
  324.8 6.8 %out_norm_back.3 = (f32[512,1024]{1,0:T(8,128)}, bf16[1024,512]{1,0:T(8,128)(2,1)}, bf16[4,2,512,128]{3,2,1,0:T(8,128)(2,1)}, f32[8,1024]{1,0:T(8,128)}) custom-call(f32[512,1024]{1,0:T(8,128)} %get-tuple-element.138.grad_ref, f32[512,1024]{1,0:T(8,128)} %get-tuple-element.121.refs_10_.middle_ref, ...), custom_call_target="tpu_custom_call" | custom-call | flops 1073741824 | bytes 11534336 | tf_op jit(solution)/shard_map/out_norm_back/pallas_call | solution.py:883
  331.6 14.0 %hidden_grad.1.refs_4_ = bf16[4,2,4,160,1024]{4,3,2,1,0:T(8,128)(2,1)} custom-call(bf16[1024,512]{1,0:T(8,128)(2,1)} %get-tuple-element.117.refs_2_.refs_0_, bf16[1024,512]{1,0:T(8,128)(2,1)} %get-tuple-element.118.refs_3_.refs_1_, bf16[1024,1024]{1,0:T(8,128)(2,1)} %bitcast.132, bf16[2,512,1024]{2,1,0:T(8,128)(2,1)} %get-tuple-element.132.refs_3_, ...), custom_call_target="tpu_custom_call" | custom-call | flops 8589934592 | bytes 16777216 | tf_op jit(solution)/shard_map/hidden_grad/pallas_call | solution.py:703
  345.6 5.8 %out_grad.1 = bf16[4,2,4,160,1024]{4,3,2,1,0:T(8,128)(2,1)} custom-call(bf16[1024,512]{1,0:T(8,128)(2,1)} %get-tuple-element.160.refs_0_, bf16[1024,512]{1,0:T(8,128)(2,1)} %get-tuple-element.161.refs_1_, bf16[4,2,512,128]{3,2,1,0:T(8,128)(2,1)} %bitcast.123, bf16[4,2,512,128]{3,2,1,0:T(8,128)(2,1)} %bitcast.29.att_ref.refs_3_, ...), custom_call_target="tpu_custom_call", output_to_operand_aliasing={{}: (4, {})} | custom-call | flops 2147483648 | bytes 2097152 | tf_op jit(solution)/shard_map/out_grad/pallas_call | solution.py:933
  351.6 5.1 collective-permute-start.7
  357.9 3.8 all-to-all-start.4
  361.9 50.9 %attend_back.2.dqkv_ref = bf16[4096,384]{1,0:T(8,128)(2,1)} custom-call(s32[8]{0:T(128)} %get-tuple-element.223.cut_ref, bf16[4096,384]{1,0:T(8,128)(2,1)} %qkv.2.qkv_ref, bf16[4096,128]{1,0:T(8,128)(2,1)} %get-tuple-element.106.o_ref, bf16[4096,128]{1,0:T(8,128)(2,1)} %bitcast.138, f32[16,8,512]{2,1,0:T(8,128)} %get-tuple-element.137.lse_ref), custom_call_target="tpu_custom_call" | custom-call | flops 42949672960 | bytes 8388608 | tf_op jit(solution)/shard_map/attend_back/pallas_call | solution.py:575
  413.8 4.1 all-to-all-start.5
  419.1 4.0 collective-permute-start.6
  423.1 44.5 %attend_back.3.dqkv_ref = bf16[4096,384]{1,0:T(8,128)(2,1)} custom-call(s32[8]{0:T(128)} %get-tuple-element.224.cut_ref, bf16[4096,384]{1,0:T(8,128)(2,1)} %qkv.3.qkv_ref, bf16[4096,128]{1,0:T(8,128)(2,1)} %get-tuple-element.112.o_ref, bf16[4096,128]{1,0:T(8,128)(2,1)} %bitcast.139, f32[16,8,512]{2,1,0:T(8,128)} %get-tuple-element.142.lse_ref), custom_call_target="tpu_custom_call" | custom-call | flops 42949672960 | bytes 8388608 | tf_op jit(solution)/shard_map/attend_back/pallas_call | solution.py:575
  471.4 4.5 all-to-all-start.6
  476.0 8.7 %qkv_grad.2 = (f32[384,1024]{1,0:T(8,128)}, f32[8,384]{1,0:T(8,128)}) custom-call(bf16[4096,384]{1,0:T(8,128)(2,1)} %attend_back.2.dqkv_ref, bf16[8,512,1024]{2,1,0:T(8,128)(2,1)} %all-gather.9.cloned.1.call-done.x_ref), custom_call_target="tpu_custom_call" | custom-call | flops 3221225472 | bytes 11534336 | tf_op jit(solution)/shard_map/qkv_grad/pallas_call | solution.py:984
  488.4 4.4 pad_maximum_fusion.left_ref.right_ref
  492.9 9.0 %qkv_grad.3 = (bf16[1024,384]{1,0:T(8,128)(2,1)}, f32[8,384]{1,0:T(8,128)}) custom-call(bf16[4096,384]{1,0:T(8,128)(2,1)} %attend_back.3.dqkv_ref, bf16[8,608,1024]{2,1,0:T(8,128)(2,1)} %bitcast.117, f32[384,1024]{1,0:T(8,128)} %get-tuple-element.163.refs_0_), custom_call_target="tpu_custom_call" | custom-call | flops 3221225472 | bytes 11534336 | tf_op jit(solution)/shard_map/qkv_grad/pallas_call | solution.py:984
  503.1 3.7 collective-permute-start.16
  506.8 4.2 collective-permute-start.18
  512.3 11.2 %input_back.2 = (f32[2,512,1024]{2,1,0:T(8,128)}, f32[8,1024]{1,0:T(8,128)}) custom-call(s32[1]{0:T(128)} %bitcast.34.plane_ref, bf16[4,2,512,384]{3,2,1,0:T(8,128)(2,1)} %bitcast.120, bf16[4,4,2,96,1024]{4,3,2,1,0:T(8,128)(2,1)} %pad_maximum_fusion.left_ref.right_ref, bf16[4,4,2,96,1024]{4,3,2,1,0:T(8,128)(2,1)} %pad_maximum_fusion.left_ref.right_ref, ...), custom_call_target="tpu_custom_call" | custom-call | flops 3221225472 | bytes 12582912 | tf_op jit(solution)/shard_map/input_back/pallas_call | solution.py:1040
  523.6 11.0 %input_back.3 = (f32[2,512,1024]{2,1,0:T(8,128)}, f32[8,1024]{1,0:T(8,128)}) custom-call(s32[1]{0:T(128)} %bitcast.34.plane_ref, bf16[4,2,512,384]{3,2,1,0:T(8,128)(2,1)} %bitcast.48.dqkv_ref, bf16[4,4,2,96,1024]{4,3,2,1,0:T(8,128)(2,1)} %pad_maximum_fusion.left_ref.right_ref, ...), custom_call_target="tpu_custom_call", output_to_operand_aliasing={{0}: (7, {})} | custom-call | flops 3221225472 | bytes 12582912 | tf_op jit(solution)/shard_map/input_back/pallas_call | solution.py:1040
  537.7 9.6 %collective-permute-done.17 = bf16[4,64,384]{2,1,0:T(8,128)(2,1)S(1)} collective-permute-done((bf16[4,64,384]{2,1,0:T(8,128)(2,1)S(1)}, bf16[4,64,384]{2,1,0:T(8,128)(2,1)S(1)}, u32[]{:S(2)}, u32[]{:S(2)}) %collective-permute-start.17) | collective-permute-done | bytes 196640 | tf_op jit(solution)/shard_map/ppermute | solution.py:1113
  549.0 3.5 all-to-all-start.7
  557.7 4.3 collective-permute-start.13
  (166 shorter events, 55.6 us)
Async XLA Ops:
  7.2 71.4 %copy-start = (f32[2,512]{1,0:T(2,128)S(1)}, f32[2,512]{1,0:T(2,128)}, u32[]{:S(2)}) copy-start(f32[2,512]{1,0:T(2,128)} %param.21) | copy-start | bytes 12292
  7.2 70.0 %all-gather.9.cloned.1.call-start = ((), (), s32[]{:S(2)}) async-start(), calls=%async_computation.11 | async-start | bytes 9437184 | tf_op jit(solution)/shard_map/all_gather | solution.py:1148
  16.5 24.9 %all-to-all-start = ((bf16[4,256,384]{1,2,0:T(8,128)(2,1)}), bf16[4,256,384]{1,2,0:T(8,128)(2,1)}, u32[]{:S(2)}, u32[]{:S(2)}) async-start(bf16[4,256,384]{1,2,0:T(8,128)(2,1)} %bitcast.128), calls=%async_computation | async-start | bytes 1572864 | tf_op jit(solution)/shard_map/all_to_all | solution.py:1142
  20.8 119.8 %all-gather.11.cloned.1.call-start = ((), (), s32[]{:S(2)}) async-start(), calls=%async_computation.15 | async-start | bytes 11206656 | tf_op jit(solution)/shard_map/all_gather | solution.py:1166
  43.7 35.5 %copy-start.23 = (s32[2,8]{1,0:T(2,128)S(1)}, s32[2,8]{1,0:T(2,128)}, u32[]{:S(2)}) copy-start(s32[2,8]{1,0:T(2,128)} %param.17) | copy-start | bytes 196
  77.2 146.3 %all-gather.13.cloned.1.call-start = ((), (), s32[]{:S(2)}) async-start(), calls=%async_computation.16 | async-start | bytes 11796480 | tf_op jit(solution)/shard_map/all_gather | solution.py:1096
  78.0 201.7 %all-gather.15.cloned.1.call-start = ((), (), s32[]{:S(2)}) async-start(), calls=%async_computation.17 | async-start | bytes 9437184 | tf_op jit(solution)/shard_map/all_gather | solution.py:1096
  143.3 53.6 %collective-permute-start.1 = (bf16[4,2,96,1024]{3,2,1,0:T(8,128)(2,1)}, bf16[4,2,96,1024]{3,2,1,0:T(8,128)(2,1)}, u32[]{:S(2)}, u32[]{:S(2)}) collective-permute-start(bf16[4,2,96,1024]{3,2,1,0:T(8,128)(2,1)} %bitcast.20), channel_id=1, source_target_pairs={{8,0},{16,8},{24,16},{9,1},{17,9},{25,17},{10,2},{18,10},{26,18},{... | collective-permute-start | bytes 4718600 | tf_op jit(solution)/shard_map/ppermute | solution.py:1177
  144.6 52.3 %collective-permute-start = (bf16[4,2,96,1024]{3,2,1,0:T(8,128)(2,1)}, bf16[4,2,96,1024]{3,2,1,0:T(8,128)(2,1)}, u32[]{:S(2)}, u32[]{:S(2)}) collective-permute-start(bf16[4,2,96,1024]{3,2,1,0:T(8,128)(2,1)} %bitcast.20), channel_id=1, source_target_pairs={{0,8},{8,16},{16,24},{1,9},{9,17},{17,25},{2,10},{10,18},{18,26},{... | collective-permute-start | bytes 4718600 | tf_op jit(solution)/shard_map/ppermute | solution.py:1174
  150.3 46.5 %all-to-all-start.1 = ((bf16[8,512,128]{2,1,0:T(8,128)(2,1)}), bf16[8,512,128]{2,1,0:T(8,128)(2,1)S(1)}, u32[]{:S(2)}, u32[]{:S(2)}) async-start(bf16[8,512,128]{2,1,0:T(8,128)(2,1)} %bitcast.135), calls=%async_computation.1 | async-start | bytes 2097152 | tf_op jit(solution)/shard_map/all_to_all | solution.py:1100
  162.4 41.8 %copy-start.10 = (f32[1024]{0:T(1024)S(1)}, f32[1024]{0:T(1024)}, u32[]{:S(2)}) copy-start(f32[1024]{0:T(1024)} %param.23) | copy-start | bytes 12292
  162.4 41.8 %copy-start.16 = (f32[1024]{0:T(1024)S(1)}, f32[1024]{0:T(1024)}, u32[]{:S(2)}) copy-start(f32[1024]{0:T(1024)} %param.24) | copy-start | bytes 12292
  162.4 41.8 %copy-start.21 = (f32[1024]{0:T(1024)S(1)}, f32[1024]{0:T(1024)}, u32[]{:S(2)}) copy-start(f32[1024]{0:T(1024)} %param.25) | copy-start | bytes 12292
  196.9 15.7 %copy-start.4 = (bf16[8,512,128]{2,1,0:T(8,128)(2,1)}, bf16[8,512,128]{2,1,0:T(8,128)(2,1)S(1)}, u32[]{:S(2)}) copy-start(bf16[8,512,128]{2,1,0:T(8,128)(2,1)S(1)} %all-to-all-done.1) | copy-start | bytes 3145732
  196.9 39.3 %collective-permute-start.2 = (bf16[4,2,96,1024]{3,2,1,0:T(8,128)(2,1)}, bf16[4,2,96,1024]{3,2,1,0:T(8,128)(2,1)}, u32[]{:S(2)}, u32[]{:S(2)}) collective-permute-start(bf16[4,2,96,1024]{3,2,1,0:T(8,128)(2,1)} %collective-permute-done), channel_id=1, source_target_pairs={{0,8},{8,16},{16,24},{1,9},{9,17},{17,25},{2,10},{10,18},{18,26},{... | collective-permute-start | bytes 4718600 | tf_op jit(solution)/shard_map/ppermute | solution.py:1174
  202.9 38.5 %collective-permute-start.3 = (bf16[4,2,96,1024]{3,2,1,0:T(8,128)(2,1)}, bf16[4,2,96,1024]{3,2,1,0:T(8,128)(2,1)}, u32[]{:S(2)}, u32[]{:S(2)}) collective-permute-start(bf16[4,2,96,1024]{3,2,1,0:T(8,128)(2,1)} %collective-permute-done.1), channel_id=1, source_target_pairs={{8,0},{16,8},{24,16},{9,1},{17,9},{25,17},{10,2},{18,10},{26,18},{... | collective-permute-start | bytes 4718600 | tf_op jit(solution)/shard_map/ppermute | solution.py:1177
  204.9 24.0 %all-to-all-start.2 = ((bf16[8,512,128]{2,1,0:T(8,128)(2,1)}), bf16[8,512,128]{2,1,0:T(8,128)(2,1)}, u32[]{:S(2)}, u32[]{:S(2)}) async-start(bf16[8,512,128]{2,1,0:T(8,128)(2,1)} %bitcast.134), calls=%async_computation.2 | async-start | bytes 2097152 | tf_op jit(solution)/shard_map/all_to_all | solution.py:1100
  209.2 203.7 %reduce-scatter.4.cloned.1.call-start = ((), (), s32[]{:S(2)}) async-start(), calls=%async_computation.12 | async-start | bytes 9437184 | tf_op jit(solution)/shard_map/reduce_scatter | solution.py:1104
  304.1 41.5 %all-to-all-start.3 = ((bf16[8,512,128]{2,1,0:T(8,128)(2,1)}), bf16[8,512,128]{2,1,0:T(8,128)(2,1)S(1)}, u32[]{:S(2)}, u32[]{:S(2)}) async-start(bf16[8,512,128]{2,1,0:T(8,128)(2,1)} %bitcast.140), calls=%async_computation.3 | async-start | bytes 2097152 | tf_op jit(solution)/shard_map/all_to_all | solution.py:1100
  308.1 184.8 %reduce-scatter.6.cloned.1.call-start = ((), (), s32[]{:S(2)}) async-start(), calls=%async_computation.13 | async-start | bytes 11796480 | tf_op jit(solution)/shard_map/reduce_scatter | solution.py:1104
  351.4 10.3 %copy-start.18 = (f32[2,1,1024]{2,1,0:T(1,128)S(1)}, f32[2,1,1024]{2,1,0:T(1,128)}, u32[]{:S(2)}) copy-start(f32[2,1,1024]{2,1,0:T(1,128)} %get-tuple-element.172) | copy-start | bytes 24580
  351.5 10.3 %copy-start.12 = (f32[8,1024]{1,0:T(8,128)S(1)}, f32[8,1024]{1,0:T(8,128)}, u32[]{:S(2)}) copy-start(f32[8,1024]{1,0:T(8,128)} %get-tuple-element.169) | copy-start | bytes 98308
  351.5 10.3 %copy-start.13 = (f32[8,1024]{1,0:T(8,128)S(1)}, f32[8,1024]{1,0:T(8,128)}, u32[]{:S(2)}) copy-start(f32[8,1024]{1,0:T(8,128)} %get-tuple-element.170) | copy-start | bytes 98308
  351.5 10.4 %copy-start.20 = (f32[2,1,1024]{2,1,0:T(1,128)S(1)}, f32[2,1,1024]{2,1,0:T(1,128)}, u32[]{:S(2)}) copy-start(f32[2,1,1024]{2,1,0:T(1,128)} %get-tuple-element.171) | copy-start | bytes 24580
  351.5 10.4 %copy-start.15 = (f32[1024]{0:T(1024)S(1)}, f32[1024]{0:T(1024)}, u32[]{:S(2)}) copy-start(f32[1024]{0:T(1024)} %convert_reduce_fusion.1) | copy-start | bytes 12292
  351.6 118.2 %collective-permute-start.7 = (bf16[4,2,96,1024]{3,2,1,0:T(8,128)(2,1)}, bf16[4,2,96,1024]{3,2,1,0:T(8,128)(2,1)}, u32[]{:S(2)}, u32[]{:S(2)}) collective-permute-start(bf16[4,2,96,1024]{3,2,1,0:T(8,128)(2,1)} %collective-permute-done.2), channel_id=1, source_target_pairs={{0,8},{8,16},{16,24},{1,9},{9,17},{17,25},{2,10},{10,18},{18,26},{... | collective-permute-start | bytes 4718600 | tf_op jit(solution)/shard_map/ppermute | solution.py:1174
  356.7 113.1 %collective-permute-start.8 = (bf16[4,2,96,1024]{3,2,1,0:T(8,128)(2,1)}, bf16[4,2,96,1024]{3,2,1,0:T(8,128)(2,1)}, u32[]{:S(2)}, u32[]{:S(2)}) collective-permute-start(bf16[4,2,96,1024]{3,2,1,0:T(8,128)(2,1)} %collective-permute-done.3), channel_id=1, source_target_pairs={{8,0},{16,8},{24,16},{9,1},{17,9},{25,17},{10,2},{18,10},{26,18},{... | collective-permute-start | bytes 4718600 | tf_op jit(solution)/shard_map/ppermute | solution.py:1177
  357.9 54.9 %all-to-all-start.4 = ((bf16[8,512,128]{2,1,0:T(8,128)(2,1)}), bf16[8,512,128]{2,1,0:T(8,128)(2,1)S(1)}, u32[]{:S(2)}, u32[]{:S(2)}) async-start(bf16[8,512,128]{2,1,0:T(8,128)(2,1)} %bitcast.37), calls=%async_computation.4 | async-start | bytes 2097152 | tf_op jit(solution)/shard_map/all_to_all | solution.py:1100
  413.8 56.0 %all-to-all-start.5 = ((bf16[8,512,384]{2,1,0:T(8,128)(2,1)}), bf16[8,512,384]{2,1,0:T(8,128)(2,1)S(1)}, u32[]{:S(2)}, u32[]{:S(2)}) async-start(bf16[8,512,384]{2,1,0:T(8,128)(2,1)} %bitcast.127), calls=%async_computation.6 | async-start | bytes 6291456 | tf_op jit(solution)/shard_map/all_to_all | solution.py:1100
  419.1 48.5 %collective-permute-start.4 = (bf16[128,1024]{1,0:T(8,128)(2,1)S(1)}, bf16[128,1024]{1,0:T(8,128)(2,1)}, u32[]{:S(2)}, u32[]{:S(2)}) collective-permute-start(bf16[128,1024]{1,0:T(8,128)(2,1)S(1)} %get-tuple-element.188), channel_id=1, source_target_pairs={{0,8},{8,16},{16,24},{24,0},{1,9},{9,17},{17,25},{25,1},{2,10},{10... | collective-permute-start | bytes 786440 | tf_op jit(solution)/shard_map/ppermute | solution.py:1113
  419.1 48.5 %collective-permute-start.6 = (bf16[128,1024]{1,0:T(8,128)(2,1)S(1)}, bf16[128,1024]{1,0:T(8,128)(2,1)}, u32[]{:S(2)}, u32[]{:S(2)}) collective-permute-start(bf16[128,1024]{1,0:T(8,128)(2,1)S(1)} %get-tuple-element.189), channel_id=1, source_target_pairs={{0,24},{8,0},{16,8},{24,16},{1,25},{9,1},{17,9},{25,17},{2,26},{10... | collective-permute-start | bytes 786440 | tf_op jit(solution)/shard_map/ppermute | solution.py:1113
  423.1 44.5 %collective-permute-start.5 = (bf16[128,1024]{1,0:T(8,128)(2,1)S(1)}, bf16[128,1024]{1,0:T(8,128)(2,1)}, u32[]{:S(2)}, u32[]{:S(2)}) collective-permute-start(bf16[128,1024]{1,0:T(8,128)(2,1)S(1)} %get-tuple-element.190), channel_id=1, source_target_pairs={{0,16},{8,24},{16,0},{24,8},{1,17},{9,25},{17,1},{25,9},{2,18},{10... | collective-permute-start | bytes 786440 | tf_op jit(solution)/shard_map/ppermute | solution.py:1113
  471.4 52.1 %all-to-all-start.6 = ((bf16[8,512,384]{2,1,0:T(8,128)(2,1)}), bf16[8,512,384]{2,1,0:T(8,128)(2,1)}, u32[]{:S(2)}, u32[]{:S(2)}) async-start(bf16[8,512,384]{2,1,0:T(8,128)(2,1)} %bitcast.121), calls=%async_computation.7 | async-start | bytes 6291456 | tf_op jit(solution)/shard_map/all_to_all | solution.py:1100
  475.9 90.2 %reduce-scatter.8.cloned.1.call-start = ((), (), s32[]{:S(2)}) async-start(), calls=%async_computation.14 | async-start | bytes 1638400 | tf_op jit(solution)/shard_map/reduce_scatter | solution.py:1117
  503.1 34.5 %collective-permute-start.16 = (bf16[4,64,384]{2,1,0:T(8,128)(2,1)S(1)}, bf16[4,64,384]{2,1,0:T(8,128)(2,1)S(1)}, u32[]{:S(2)}, u32[]{:S(2)}) collective-permute-start(bf16[4,64,384]{2,1,0:T(8,128)(2,1)S(1)} %get-tuple-element.191), channel_id=1, source_target_pairs={{0,8},{8,16},{16,24},{24,0},{1,9},{9,17},{17,25},{25,1},{2,10},{10... | collective-permute-start | bytes 589832 | tf_op jit(solution)/shard_map/ppermute | solution.py:1113
  506.8 30.9 %collective-permute-start.18 = (bf16[4,64,384]{2,1,0:T(8,128)(2,1)S(1)}, bf16[4,64,384]{2,1,0:T(8,128)(2,1)S(1)}, u32[]{:S(2)}, u32[]{:S(2)}) collective-permute-start(bf16[4,64,384]{2,1,0:T(8,128)(2,1)S(1)} %get-tuple-element.192), channel_id=1, source_target_pairs={{0,24},{8,0},{16,8},{24,16},{1,25},{9,1},{17,9},{25,17},{2,26},{10... | collective-permute-start | bytes 589832 | tf_op jit(solution)/shard_map/ppermute | solution.py:1113
  511.0 36.3 %collective-permute-start.17 = (bf16[4,64,384]{2,1,0:T(8,128)(2,1)S(1)}, bf16[4,64,384]{2,1,0:T(8,128)(2,1)S(1)}, u32[]{:S(2)}, u32[]{:S(2)}) collective-permute-start(bf16[4,64,384]{2,1,0:T(8,128)(2,1)S(1)} %get-tuple-element.193), channel_id=1, source_target_pairs={{0,16},{8,24},{16,0},{24,8},{1,17},{9,25},{17,1},{25,9},{2,18},{10... | collective-permute-start | bytes 589832 | tf_op jit(solution)/shard_map/ppermute | solution.py:1113
  523.6 11.0 %copy-start.14 = (f32[8,1024]{1,0:T(8,128)S(1)}, f32[8,1024]{1,0:T(8,128)}, u32[]{:S(2)}) copy-start(f32[8,1024]{1,0:T(8,128)} %get-tuple-element.175) | copy-start | bytes 98308
  534.6 20.5 %copy-start.8 = (bf16[512,1024]{1,0:T(8,128)(2,1)S(1)}, bf16[512,1024]{1,0:T(8,128)(2,1)}, u32[]{:S(2)}) copy-start(bf16[512,1024]{1,0:T(8,128)(2,1)} %get-tuple-element.124) | copy-start | bytes 3145732
  534.6 20.5 %copy-start.9 = (bf16[512,1024]{1,0:T(8,128)(2,1)S(1)}, bf16[512,1024]{1,0:T(8,128)(2,1)}, u32[]{:S(2)}) copy-start(bf16[512,1024]{1,0:T(8,128)(2,1)} %get-tuple-element.130) | copy-start | bytes 3145732
  535.5 17.0 %collective-permute-start.11 = (f32[12288]{0:T(1024)S(1)}, f32[12288]{0:T(1024)S(1)}, u32[]{:S(2)}, u32[]{:S(2)}) collective-permute-start(f32[12288]{0:T(1024)S(1)} %bitcast_dynamic-update-slice_fusion), channel_id=1, source_target_pairs={{0,6},{2,4},{4,2},{6,0},{1,7},{3,5},{5,3},{7,1},{8,14},{10,12},{12... | collective-permute-start | bytes 147464 | tf_op jit(solution)/shard_map/ppermute | solution.py:1127
  536.6 15.9 %collective-permute-start.10 = (f32[12288]{0:T(1024)S(1)}, f32[12288]{0:T(1024)}, u32[]{:S(2)}, u32[]{:S(2)}) collective-permute-start(f32[12288]{0:T(1024)S(1)} %bitcast_dynamic-update-slice_fusion), channel_id=1, source_target_pairs={{0,4},{2,6},{4,0},{6,2},{1,5},{3,7},{5,1},{7,3},{8,12},{10,14},{12... | collective-permute-start | bytes 147464 | tf_op jit(solution)/shard_map/ppermute | solution.py:1127
  537.6 14.9 %collective-permute-start.9 = (f32[12288]{0:T(1024)S(1)}, f32[12288]{0:T(1024)S(1)}, u32[]{:S(2)}, u32[]{:S(2)}) collective-permute-start(f32[12288]{0:T(1024)S(1)} %bitcast_dynamic-update-slice_fusion), channel_id=1, source_target_pairs={{0,2},{2,0},{4,6},{6,4},{1,3},{3,1},{5,7},{7,5},{8,10},{10,8},{12,... | collective-permute-start | bytes 147464 | tf_op jit(solution)/shard_map/ppermute | solution.py:1127
  549.0 13.0 %all-to-all-start.7 = ((f32[4,64,384]{2,1,0:T(8,128)}), f32[4,64,384]{2,1,0:T(8,128)S(1)}, u32[]{:S(2)}, u32[]{:S(2)}) async-start(f32[4,64,384]{2,1,0:T(8,128)} %fusion.9), calls=%async_computation.9 | async-start | bytes 786432 | tf_op jit(solution)/shard_map/all_to_all | solution.py:1290
  553.4 4.2 collective-permute-start.12
  557.5 6.2 %collective-permute-start.15 = (f32[12288]{0:T(1024)S(1)}, f32[12288]{0:T(1024)S(1)}, u32[]{:S(2)}, u32[]{:S(2)}) collective-permute-start(f32[12288]{0:T(1024)S(1)} %add.160), channel_id=1, source_target_pairs={{0,24},{8,16},{16,8},{24,0},{1,25},{9,17},{17,9},{25,1},{2,26},{10... | collective-permute-start | bytes 147464 | tf_op jit(solution)/shard_map/ppermute | solution.py:1127
  557.6 6.1 %collective-permute-start.14 = (f32[12288]{0:T(1024)S(1)}, f32[12288]{0:T(1024)S(1)}, u32[]{:S(2)}, u32[]{:S(2)}) collective-permute-start(f32[12288]{0:T(1024)S(1)} %add.160), channel_id=1, source_target_pairs={{0,16},{8,24},{16,0},{24,8},{1,17},{9,25},{17,1},{25,9},{2,18},{10... | collective-permute-start | bytes 147464 | tf_op jit(solution)/shard_map/ppermute | solution.py:1127
  557.7 6.5 %collective-permute-start.13 = (f32[12288]{0:T(1024)S(1)}, f32[12288]{0:T(1024)S(1)}, u32[]{:S(2)}, u32[]{:S(2)}) collective-permute-start(f32[12288]{0:T(1024)S(1)} %add.160), channel_id=1, source_target_pairs={{0,8},{8,0},{16,24},{24,16},{1,9},{9,1},{17,25},{25,17},{2,10},{10... | collective-permute-start | bytes 147464 | tf_op jit(solution)/shard_map/ppermute | solution.py:1127
  (10 other events, 45.2 us)
Sparse Core Ops, SparseCore 0:
  12.3 64.8 all-gather.8
  79.7 60.9 all-gather.10
  143.1 80.3 all-gather.12
  225.3 54.3 all-gather.14
  283.0 82.7 reduce-scatter.3
  369.1 108.0 reduce-scatter.5
  502.0 47.2 reduce-scatter.7
